TPU v7x, 256 devices: a whole 4x4x8 slice. The times are simulated.
256 devices in a mesh: ctx: 64 (over y, z, core), ch: 4 (over x).
Axes of the slice: x: 4, y: 4, z: 8, core: 2. Of those that a mesh axis runs over, the one named last changes fastest.
Arguments:
- gate_medium: bfloat16 [16384, 8192], P('ctx', 'ch'), may hold values from -6 to 6
- key_medium: bfloat16 [16384, 8192], P('ctx', 'ch'), may hold values from -6 to 6
- value_medium: bfloat16 [16384, 8192], P('ctx', 'ch'), may hold values from -16 to 16
- short_medium: float32 [3, 3, 8192], P(None, None, 'ch'), may hold values from -3.5 to 3.5
- filter_medium: float32 [128, 8192], P(None, 'ch'), may hold values from -2 to 2
- skip_medium: float32 [8192], P('ch'), may hold values from -4 to 4
- norm_gain: float32 [8192], P('ch'), may hold values from 0.5 to 1.5
- gate_long: bfloat16 [16384, 8192], P('ctx', 'ch'), may hold values from -6 to 6
- key_long: bfloat16 [16384, 8192], P('ctx', 'ch'), may hold values from -6 to 6
- short_long: float32 [3, 3, 8192], P(None, None, 'ch'), may hold values from -3.5 to 3.5
- decay_rates: float32 [16, 8192], P(None, 'ch'), may hold values from 6.1035156e-07 to 0.0625
- residues: float32 [16, 8192], P(None, 'ch'), may hold values from -1.5 to 1.5
- skip_long: float32 [8192], P('ch'), may hold values from -4 to 4
Outputs:
- mixed_medium: bfloat16 [16384, 8192], P('ctx', 'ch')
- mixed_long: bfloat16 [16384, 8192], P('ctx', 'ch')
All inputs are finite; a program needn't handle non-finite values.
Results may differ from a plain program's by a relative error of at most 0.0095.
Values may be sent and summed in bfloat16 or wider, within the bound.
A program may use at most 64 MiB of HBM per device.

v0:
```python
import jax
import jax.numpy as jnp
from jax import lax
from jax.sharding import PartitionSpec as P
from jax.experimental import pallas as pl
from jax.experimental.pallas import tpu as pltpu

TAPS = 128
SUB = 128
RB = 8


def medium_kernel(ext_ref, f_ref, skip_ref, gate_ref, out_ref, ss_ref, q_ref):
    rows = out_ref.shape[0]
    width = out_ref.shape[1]
    span = ext_ref.shape[0]

    @pl.when(pl.program_id(0) == 0)
    def _():
        ss_ref[...] = jnp.zeros_like(ss_ref)

    for h in range(width // SUB):
        lanes = pl.ds(h * SUB, SUB)
        ext = ext_ref[:, lanes].astype(jnp.float32)
        for b in range(8):
            q_ref[b, 8:, :] = ext[8 - b : span - b]

        def block(kb, carry):
            acc = [jnp.zeros((8, SUB), jnp.float32) for _ in range(RB)]
            start = pl.multiple_of(kb * (8 * RB) + 8, 8)
            for b in range(8):
                qv = q_ref[b, pl.ds(start, 8 * (RB + 15)), :]
                for a in range(16):
                    w = jnp.broadcast_to(f_ref[pl.ds(8 * a + b, 1), lanes], (8, SUB))
                    for kk in range(RB):
                        v = kk + 15 - a
                        acc[kk] = acc[kk] + w * qv[8 * v : 8 * v + 8]
            skip = jnp.broadcast_to(skip_ref[:, lanes], (8, SUB))
            for kk in range(RB):
                row = pl.multiple_of(kb * (8 * RB) + 8 * kk, 8)
                own = q_ref[0, pl.ds(row + TAPS, 8), :]
                conv = acc[kk] + skip * own
                mixed = (gate_ref[pl.ds(row, 8), lanes] * conv).astype(jnp.bfloat16)
                out_ref[pl.ds(row, 8), lanes] = mixed
                m = mixed.astype(jnp.float32)
                ss_ref[pl.ds(row, 8), :] += m * m
            return carry

        lax.fori_loop(0, rows // (8 * RB), block, 0)


def medium_call(ext, taps, skip, gate_feat, block=512, interpret=False):
    span, width = ext.shape
    rows = gate_feat.shape[0]
    grid = (width // block,)
    return pl.pallas_call(
        medium_kernel,
        grid=grid,
        in_specs=[
            pl.BlockSpec((span, block), lambda i: (0, i)),
            pl.BlockSpec((TAPS, block), lambda i: (0, i)),
            pl.BlockSpec((1, block), lambda i: (0, i)),
            pl.BlockSpec((rows, block), lambda i: (0, i)),
        ],
        out_specs=[
            pl.BlockSpec((rows, block), lambda i: (0, i)),
            pl.BlockSpec((rows, SUB), lambda i: (0, 0)),
        ],
        out_shape=[
            jax.ShapeDtypeStruct((rows, width), jnp.bfloat16),
            jax.ShapeDtypeStruct((rows, SUB), jnp.float32),
        ],
        scratch_shapes=[pltpu.VMEM((8, span, SUB), jnp.float32)],
        compiler_params=pltpu.CompilerParams(dimension_semantics=("arbitrary",)),
        interpret=interpret,
    )(ext, taps, skip, gate_feat)

D = 8192


def passed_along(value, axis, steps):
    count = lax.axis_size(axis)
    first, last = (max(0, -steps), min(count, count - steps))
    return lax.ppermute(value, axis, [(source, source + steps) for source in range(first, last)])


def short_filter(extended, weights):
    return weights[0] * extended[2:] + weights[1] * extended[1:-1] + weights[2] * extended[:-2]


def medium_conv(extended, taps, row_count):
    tap_count = taps.shape[0]
    total = jnp.zeros((row_count, taps.shape[1]), jnp.float32)
    for offset in range(tap_count):
        start = tap_count - 1 - offset
        total = total + taps[offset] * extended[start : start + row_count]
    return total


def body(
    gate_medium,
    key_medium,
    value_medium,
    short_medium,
    filter_medium,
    skip_medium,
    norm_gain,
    gate_long,
    key_long,
    short_long,
    decay_rates,
    residues,
    skip_long,
):
    row_count = gate_medium.shape[0]
    tap_count = filter_medium.shape[0]
    width_local = gate_medium.shape[1]
    late_product = (
        short_filter(key_medium, short_medium[1]) * short_filter(value_medium, short_medium[2])
    ).astype(jnp.bfloat16)
    rim_gate, rim_key, rim_value, rim_product = passed_along(
        (gate_medium[-2:], key_medium[-2:], value_medium[-2:], late_product[-(tap_count - 1) :]),
        "ctx",
        1,
    )
    head_key = short_filter(jnp.concatenate([rim_key, key_medium[:2]], 0), short_medium[1])
    head_value = short_filter(jnp.concatenate([rim_value, value_medium[:2]], 0), short_medium[2])
    head_product = (head_key * head_value).astype(jnp.bfloat16)
    product = jnp.concatenate([rim_product, head_product, late_product], 0)
    gate_feat = short_filter(jnp.concatenate([rim_gate, gate_medium], 0), short_medium[0])
    extended = jnp.concatenate([jnp.zeros((1, width_local), jnp.bfloat16), product], 0)
    mixed_medium, partial_squares = medium_call(
        extended, filter_medium, skip_medium[None, :], gate_feat
    )
    squares = jnp.sum(partial_squares, axis=1)
    total_squares = lax.psum(squares, "ch")
    inverse = lax.rsqrt(total_squares / D + 1e-06)
    normed = (mixed_medium * norm_gain * inverse[:, None]).astype(jnp.bfloat16)
    rim_gate_long, rim_key_long, rim_normed = passed_along(
        (gate_long[-2:], key_long[-2:], normed[-2:]), "ctx", 1
    )
    gate_feat_long = short_filter(jnp.concatenate([rim_gate_long, gate_long], 0), short_long[0])
    key_feat_long = short_filter(jnp.concatenate([rim_key_long, key_long], 0), short_long[1])
    value_feat_long = short_filter(jnp.concatenate([rim_normed, normed], 0), short_long[2])
    product_long = (key_feat_long * value_feat_long).astype(jnp.bfloat16)
    block_rows = 64
    block_count = row_count // block_rows
    positions = jnp.arange(block_rows).astype(jnp.float32)
    mode_weight = residues * jnp.sqrt(-jnp.expm1(-2.0 * decay_rates))
    rates_wide = decay_rates[:, None, :]
    to_end = jnp.exp(-rates_wide * (block_rows - 1.0 - positions)[None, :, None])
    from_start = mode_weight[:, None, :] * jnp.exp(-rates_wide * (positions + 1.0)[None, :, None])
    impulse = jnp.sum(
        mode_weight[:, None, :] * jnp.exp(-rates_wide * positions[None, :, None]), axis=0
    )
    blocks = product_long.reshape(block_count, block_rows, width_local)
    padded = jnp.pad(blocks, ((0, 0), (block_rows - 1, 0), (0, 0)))
    inner = jnp.zeros(blocks.shape, jnp.float32)
    for offset in range(block_rows):
        start = block_rows - 1 - offset
        inner = inner + impulse[offset] * padded[:, start : start + block_rows]
    ends = jnp.einsum(
        "bsc,msc->bmc", blocks.astype(jnp.float32), to_end, precision=lax.Precision.HIGHEST
    )
    block_decay = jnp.exp(-decay_rates * block_rows)

    def advance(state, end):
        return (block_decay * state + end, state)

    final_state, starts = lax.scan(advance, jnp.zeros(decay_rates.shape, jnp.float32), ends)
    position = lax.axis_index("ctx")
    piece = lax.all_gather(
        final_state[None].astype(jnp.bfloat16), "ctx", axis=0, tiled=True
    ).astype(jnp.float32)
    count = piece.shape[0]
    gaps = (position - 1 - jnp.arange(count, dtype=jnp.int32)).astype(jnp.float32)
    factors = jnp.where(
        gaps[:, None, None] >= 0.0,
        jnp.exp(-decay_rates[None] * row_count * jnp.maximum(gaps, 0.0)[:, None, None]),
        0.0,
    )
    incoming = jnp.zeros_like(final_state) + jnp.sum(factors * piece, axis=0)
    lead = jnp.exp(
        -decay_rates[None]
        * (block_rows * jnp.arange(block_count).astype(jnp.float32))[:, None, None]
    )
    states = starts + lead * incoming[None]
    outer = jnp.einsum("bmc,msc->bsc", states, from_start, precision=lax.Precision.HIGHEST)
    conv_long = (inner + outer).reshape(row_count, width_local) + skip_long * product_long
    mixed_long = (gate_feat_long * conv_long).astype(jnp.bfloat16)
    return (mixed_medium, mixed_long)


def solution(mesh):
    placed = (
        P("ctx", "ch"),
        P("ctx", "ch"),
        P("ctx", "ch"),
        P(None, None, "ch"),
        P(None, "ch"),
        P("ch"),
        P("ch"),
        P("ctx", "ch"),
        P("ctx", "ch"),
        P(None, None, "ch"),
        P(None, "ch"),
        P(None, "ch"),
        P("ch"),
    )
    return jax.shard_map(
        body,
        mesh=mesh,
        in_specs=placed,
        out_specs=(P("ctx", "ch"), P("ctx", "ch")),
        check_vma=False,
    )
```

profile of v0, /device:TPU:25, one launch (start us, length us, event | category | flops | bytes accessed | tf_op | source)
XLA Modules:
  0.0 256.3 jit_solution(1515355977605146537)
XLA Ops:
  7.2 0.0 all-gather.3.cloned.1.call-start
  7.2 0.8 fusion.22
  8.0 4.1 %collective-permute-start.1 = (bf16[2,2048]{1,0:T(2,128)(2,1)S(1)}, bf16[2,2048]{1,0:T(2,128)(2,1)S(1)}, u32[]{:S(2)}, u32[]{:S(2)}) collective-permute-start(bf16[2,2048]{1,0:T(2,128)(2,1)S(1)} %get-tuple-element.149), channel_id=1, source_target_pairs={{0,4},{4,8},{8,12},{12,16},{16,20},{20,24},{24,28},{28,32},{32,36}... | collective-permute-start | bytes 24584 | tf_op jit(solution)/shard_map/ppermute | solution.py:84
  12.1 0.8 fusion.23
  12.9 1.9 collective-permute-start.2
  14.8 1.0 fusion.25
  15.8 0.0 copy-start
  15.9 0.0 copy-start.1
  15.9 0.0 copy-start.6
  15.9 0.0 copy-start.7
  15.9 0.0 copy-start.8
  15.9 5.0 %multiply_convert_fusion.2 = bf16[254,2048]{1,0:T(8,128)(2,1)S(1)} fusion(bf16[256,2048]{1,0:T(8,128)(2,1)} %param.17, f32[2048]{0:T(1024)S(1)} %bitcast.46, f32[2048]{0:T(1024)S(1)} %bitcast.48, f32[2048]{0:T(1024)S(1)} %bitcast.50, bf16[256,2048]{1,0:T(8,128)(2,1)} %param.16, f32[2048]{0:T(1024)S(1)} %bitcast.52, f32[2048]{0:T(1024)S(1)} %bitcast.54, ...), kind=kLoop, calls=%fused_computation.88 | loop fusion | flops 9363456 | bytes 7331840 | tf_op jit(solution)/shard_map/convert_element_type | solution.py:120
  20.9 0.1 slice.731
  21.0 3.9 %collective-permute-start = (bf16[127,2048]{1,0:T(8,128)(2,1)S(1)}, bf16[127,2048]{1,0:T(8,128)(2,1)S(1)}, u32[]{:S(2)}, u32[]{:S(2)}) collective-permute-start(bf16[127,2048]{1,0:T(8,128)(2,1)S(1)} %slice.731), channel_id=1, source_target_pairs={{0,4},{4,8},{8,12},{12,16},{16,20},{20,24},{24,28},{28,32},{32,36}... | collective-permute-start | bytes 1560584 | tf_op jit(solution)/shard_map/ppermute | solution.py:84
  25.0 1.9 collective-permute-start.3
  26.9 0.6 slice.595
  27.5 3.9 %collective-permute-start.5 = (bf16[2,2048]{1,0:T(2,128)(2,1)}, bf16[2,2048]{1,0:T(2,128)(2,1)}, u32[]{:S(2)}, u32[]{:S(2)}) collective-permute-start(bf16[2,2048]{1,0:T(2,128)(2,1)} %slice.595), channel_id=1, source_target_pairs={{0,4},{4,8},{8,12},{12,16},{16,20},{20,24},{24,28},{28,32},{32,36}... | collective-permute-start | bytes 24584 | tf_op jit(solution)/shard_map/ppermute | solution.py:84
  31.5 0.8 sqrt_multiply_fusion
  32.3 0.7 fusion.24
  33.0 0.0 collective-permute-done.1
  33.0 0.0 collective-permute-done.2
  33.0 0.1 multiply_convert_fusion.3
  33.1 2.0 multiply_add_fusion.gate_ref
  35.1 1.8 pad_maximum_fusion.ext_ref
  36.9 32.4 %shard_map.140 = (bf16[256,2048]{1,0:T(8,128)(2,1)}, f32[256,128]{1,0:T(8,128)}) custom-call(bf16[384,2048]{1,0:T(8,128)(2,1)} %pad_maximum_fusion.ext_ref, f32[128,2048]{1,0:T(8,128)} %f_ref.1, f32[1,2048]{1,0:T(1,128)} %bitcast.70, f32[256,2048]{1,0:T(8,128)} %multiply_add_fusion.gate_ref), custom_call_target="tpu_custom_call" | custom-call | tf_op jit(solution)/shard_map/pallas_call | solution.py:56
  69.2 1.0 reduce_sum.28
  70.3 8.5 %psum.7 = f32[256]{0:T(256)S(1)} all-reduce(f32[256]{0:T(256)S(1)} %reduce_sum.28), channel_id=1, replica_groups=mesh['ctx'=64,'ch'=4] {'ch'}, use_global_device_ids=true, to_apply=%region_2.0 | all-reduce | flops 256 | bytes 2048 | tf_op jit(solution)/shard_map/psum | solution.py:136
  78.7 1.5 multiply_convert_fusion.1
  80.3 4.5 %collective-permute-start.6 = (bf16[2,2048]{1,0:T(2,128)(2,1)S(1)}, bf16[2,2048]{1,0:T(2,128)(2,1)S(1)}, u32[]{:S(2)}, u32[]{:S(2)}) collective-permute-start(bf16[2,2048]{1,0:T(2,128)(2,1)S(1)} %slice.739), channel_id=1, source_target_pairs={{0,4},{4,8},{8,12},{12,16},{16,20},{20,24},{24,28},{28,32},{32,36}... | collective-permute-start | bytes 24584 | tf_op jit(solution)/shard_map/ppermute | solution.py:84
  84.8 0.5 broadcast_subtract_fusion
  85.2 1.3 copy.40
  86.6 0.6 copy-done.49
  87.2 2.5 multiply_convert_fusion
  89.7 1.4 copy.41
  91.1 18.8 %fusion.13 = f32[4,16,2048]{1,0,2:T(4,128)} fusion(bf16[4,64,2048]{1,0,2:T(4,128)(2,1)S(1)} %copy.41, f32[64]{0:T(128)S(1)} %copy-done.52, f32[16,2048]{0,1:T(8,128)} %copy.40), kind=kOutput, calls=%fused_computation.80 | convolution fusion | flops 102760448 | bytes 1704192 | tf_op jit(solution)/shard_map/bsc,msc->bmc/dot_general | solution.py:162
  109.9 3.5 %copy.42 = f32[4,16,2048]{2,1,0:T(8,128)S(1)} copy(f32[4,16,2048]{1,0,2:T(4,128)} %fusion.13) | data formatting | bytes 1048576
  113.4 0.0 copy-start.3
  113.4 0.4 while.13
  113.4 0.1 bitcast_add_fusion.4
  113.6 0.1 bitcast_add_fusion.4
  113.7 0.1 bitcast_add_fusion.4
  113.8 0.1 bitcast_add_fusion.4
  113.8 0.6 convert_element_type.427
  114.5 0.0 all-gather.3.cloned.1.call-update
  114.5 1.4 slice.588
  115.9 3.3 %collective-permute-start.4 = (bf16[2,2048]{1,0:T(2,128)(2,1)}, bf16[2,2048]{1,0:T(2,128)(2,1)}, u32[]{:S(2)}, u32[]{:S(2)}) collective-permute-start(bf16[2,2048]{1,0:T(2,128)(2,1)} %slice.588), channel_id=1, source_target_pairs={{0,4},{4,8},{8,12},{12,16},{16,20},{20,24},{24,28},{28,32},{32,36}... | collective-permute-start | bytes 24584 | tf_op jit(solution)/shard_map/ppermute | solution.py:84
  119.2 2.3 copy.39
  121.5 0.6 convert_multiply_fusion.1
  122.1 0.5 broadcast_add_fusion
  122.6 12.7 %multiply_reduce_fusion = f32[64,2048]{0,1:T(8,128)S(1)} fusion(f32[64]{0:T(128)S(1)} %iota_convert_fusion, f32[16,2048]{0,1:T(8,128)S(1)} %copy-done.3, f32[16,2048]{0,1:T(8,128)} %copy.39), kind=kLoop, calls=%fused_computation.72 | loop fusion | flops 6160384 | bytes 786688 | tf_op jit(solution)/shard_map/reduce_sum | solution.py:153
  135.4 4.5 %slice_reduce_fusion.60 = (f32[2048]{0:T(1024)}, f32[2048]{0:T(1024)}, f32[2048]{0:T(1024)}, f32[2048]{0:T(1024)}, f32[2048]{0:T(1024)}, /*index=5*/f32[2048]{0:T(1024)}, f32[2048]{0:T(1024)}) fusion(f32[64,2048]{0,1:T(8,128)S(1)} %multiply_reduce_fusion), kind=kLoop, calls=%fused_computation.162 | loop fusion | bytes 114688 | tf_op jit(solution)/shard_map/slice | solution.py:161
  139.8 11.2 %slice_reduce_fusion.62 = (f32[2048]{0:T(1024)S(1)}, f32[2048]{0:T(1024)S(1)}, f32[2048]{0:T(1024)}, f32[2048]{0:T(1024)}, f32[2048]{0:T(1024)}, /*index=5*/f32[...) fusion(f32[64,2048]{0,1:T(8,128)S(1)} %multiply_reduce_fusion), kind=kLoop, calls=%fused_computation.164 | loop fusion | bytes 311296 | tf_op jit(solution)/shard_map/slice | solution.py:161
  151.0 11.4 %slice_reduce_fusion.61 = (f32[2048]{0:T(1024)}, f32[2048]{0:T(1024)}, f32[2048]{0:T(1024)}, f32[2048]{0:T(1024)}, f32[2048]{0:T(1024)}, /*index=5*/f32[2048]{0:...) fusion(f32[64,2048]{0,1:T(8,128)S(1)} %multiply_reduce_fusion), kind=kLoop, calls=%fused_computation.163 | loop fusion | bytes 311296 | tf_op jit(solution)/shard_map/slice | solution.py:161
  162.4 10.9 %slice_reduce_fusion.63 = (f32[2048]{0:T(1024)}, f32[2048]{0:T(1024)}, f32[2048]{0:T(1024)}, f32[2048]{0:T(1024)}, f32[2048]{0:T(1024)}, /*index=5*/f32[2048]{0:...) fusion(f32[64,2048]{0,1:T(8,128)S(1)} %multiply_reduce_fusion), kind=kLoop, calls=%fused_computation.167 | loop fusion | bytes 311296 | tf_op jit(solution)/shard_map/slice | solution.py:161
  173.2 20.6 %all-gather.3.cloned.1.call-done = bf16[1024,2048]{1,0:T(8,128)(2,1)} async-done(((bf16[16,2048]{1,0:T(8,128)(2,1)}), bf16[1024,2048]{1,0:T(8,128)(2,1)}) %all-gather.3.cloned.1.call-update) | async-done | bytes 4194320 | tf_op jit(solution)/shard_map/all_gather | solution.py:172
  193.9 3.9 %fusion.7 = f32[16,2048]{1,0:T(8,128)S(1)} fusion(bf16[64,16,2048]{2,1,0:T(8,128)(2,1)} %bitcast.45, f32[64]{0:T(128)S(1)} %convert_maximum_fusion, f32[16,2048]{1,0:T(8,128)S(1)} %copy-done.5, pred[64]{0:T(512)(128)(4,1)S(1)} %convert_compare_fusion), kind=kLoop, calls=%fused_computation.74 | loop fusion | flops 10452992 | bytes 4456768 | tf_op jit(solution)/shard_map/reduce_sum | solution.py:182
  197.8 0.2 multiply_add_fusion.1
  198.0 3.1 %copy.43 = f32[4,16,2048]{1,0,2:T(4,128)} copy(f32[4,16,2048]{2,1,0:T(8,128)S(1)} %multiply_add_fusion.1) | data formatting | bytes 1048576 | tf_op jit(solution)/shard_map/add | solution.py:187
  201.1 24.4 %fusion.3 = f32[2048,64,4]{1,2,0:T(4,128)} fusion(f32[4,16,2048]{1,0,2:T(4,128)} %copy.43, f32[64]{0:T(128)S(1)} %copy-done.51, f32[16,2048]{0,1:T(8,128)S(1)} %copy-done.3, f32[16,2048]{0,1:T(8,128)} %copy.39), kind=kOutput, calls=%fused_computation.68 | convolution fusion | flops 104857600 | bytes 2883840 | tf_op jit(solution)/shard_map/bmc,msc->bsc/dot_general | solution.py:188
  225.8 0.0 copy-start.45
  225.9 3.6 %copy.44 = f32[2048,64,4]{0,1,2:T(8,128)S(1)} copy(f32[2048,64,4]{1,2,0:T(4,128)} %fusion.3) | data formatting | bytes 4194304 | tf_op jit(solution)/shard_map/bmc,msc->bsc/dot_general | solution.py:188
  229.8 0.0 copy-start.2
  229.9 16.8 %bitcast_add_fusion.2 = f32[4,64,2048]{2,1,0:T(8,128)S(1)} fusion(f32[2048,64,4]{0,1,2:T(8,128)S(1)} %copy.44, bf16[4,64,2048]{2,1,0:T(8,128)(2,1)S(1)} %bitcast.44, f32[2048]{0:T(1024)S(1)} %copy-done.46, f32[2048]{0:T(1024)S(1)} %copy-done.47, f32[2048]{0:T(1024)} %get-tuple-element.77, f32[2048]{0:T(1024)} %get-tuple-element.78, ...), kind=kLoop, calls=%fused_computation.84 | loop fusion | flops 100663296 | bytes 5767168 | tf_op jit(solution)/shard_map/add | solution.py:189
  246.7 2.8 %fusion.17 = bf16[256,2048]{1,0:T(8,128)(2,1)} fusion(f32[4,64,2048]{2,1,0:T(8,128)S(1)} %bitcast_add_fusion.2, bf16[256,2048]{1,0:T(8,128)(2,1)S(1)} %multiply_convert_fusion, bf16[256,2048]{1,0:T(8,128)(2,1)S(1)} %copy-done.2, bf16[2,2048]{1,0:T(2,128)(2,1)} %collective-permute-done.4, f32[2048]{0:T(1024)} %param.27, f32[2048]{0:T(1024)} %bitcast.59, ...), kind=kLoop, calls=%fused_computation.83 | loop fusion | flops 9961472 | bytes 5283840 | tf_op jit(solution)/shard_map/convert_element_type | solution.py:190
  (115 shorter events, 0.3 us)
Async XLA Ops:
  7.2 186.7 %all-gather.3.cloned.1.call-start = ((), (), s32[]{:S(2)}) async-start(), calls=%async_computation | async-start | bytes 4259840 | tf_op jit(solution)/shard_map/all_gather | solution.py:172
  8.0 24.9 %collective-permute-start.1 = (bf16[2,2048]{1,0:T(2,128)(2,1)S(1)}, bf16[2,2048]{1,0:T(2,128)(2,1)S(1)}, u32[]{:S(2)}, u32[]{:S(2)}) collective-permute-start(bf16[2,2048]{1,0:T(2,128)(2,1)S(1)} %get-tuple-element.149), channel_id=1, source_target_pairs={{0,4},{4,8},{8,12},{12,16},{16,20},{20,24},{24,28},{28,32},{32,36}... | collective-permute-start | bytes 24584 | tf_op jit(solution)/shard_map/ppermute | solution.py:84
  12.9 20.0 %collective-permute-start.2 = (bf16[2,2048]{1,0:T(2,128)(2,1)S(1)}, bf16[2,2048]{1,0:T(2,128)(2,1)S(1)}, u32[]{:S(2)}, u32[]{:S(2)}) collective-permute-start(bf16[2,2048]{1,0:T(2,128)(2,1)S(1)} %get-tuple-element.151), channel_id=1, source_target_pairs={{0,4},{4,8},{8,12},{12,16},{16,20},{20,24},{24,28},{28,32},{32,36}... | collective-permute-start | bytes 24584 | tf_op jit(solution)/shard_map/ppermute | solution.py:84
  15.8 9.1 %copy-start = (bf16[256,2048]{1,0:T(8,128)(2,1)S(1)}, bf16[256,2048]{1,0:T(8,128)(2,1)}, u32[]{:S(2)}) copy-start(bf16[256,2048]{1,0:T(8,128)(2,1)} %param.15) | copy-start | bytes 3145732
  15.9 11.1 %copy-start.1 = (bf16[256,2048]{1,0:T(8,128)(2,1)S(1)}, bf16[256,2048]{1,0:T(8,128)(2,1)}, u32[]{:S(2)}) copy-start(bf16[256,2048]{1,0:T(8,128)(2,1)} %param.23) | copy-start | bytes 3145732
  15.9 15.6 %copy-start.6 = (f32[16,2048]{1,0:T(8,128)S(1)}, f32[16,2048]{1,0:T(8,128)}, u32[]{:S(2)}) copy-start(f32[16,2048]{1,0:T(8,128)} %param.26) | copy-start | bytes 393220
  15.9 15.6 %copy-start.7 = (f32[16,2048]{1,0:T(8,128)S(1)}, f32[16,2048]{1,0:T(8,128)}, u32[]{:S(2)}) copy-start(f32[16,2048]{1,0:T(8,128)} %param.25) | copy-start | bytes 393220
  15.9 16.4 %copy-start.8 = (f32[3,3,2048]{2,1,0:T(4,128)S(1)}, f32[3,3,2048]{2,1,0:T(4,128)}, u32[]{:S(2)}) copy-start(f32[3,3,2048]{2,1,0:T(4,128)} %param.24) | copy-start | bytes 221188
  21.0 14.1 %collective-permute-start = (bf16[127,2048]{1,0:T(8,128)(2,1)S(1)}, bf16[127,2048]{1,0:T(8,128)(2,1)S(1)}, u32[]{:S(2)}, u32[]{:S(2)}) collective-permute-start(bf16[127,2048]{1,0:T(8,128)(2,1)S(1)} %slice.731), channel_id=1, source_target_pairs={{0,4},{4,8},{8,12},{12,16},{16,20},{20,24},{24,28},{28,32},{32,36}... | collective-permute-start | bytes 1560584 | tf_op jit(solution)/shard_map/ppermute | solution.py:84
  25.0 8.1 %collective-permute-start.3 = (bf16[2,2048]{1,0:T(2,128)(2,1)S(1)}, bf16[2,2048]{1,0:T(2,128)(2,1)S(1)}, u32[]{:S(2)}, u32[]{:S(2)}) collective-permute-start(bf16[2,2048]{1,0:T(2,128)(2,1)S(1)} %slice.582), channel_id=1, source_target_pairs={{0,4},{4,8},{8,12},{12,16},{16,20},{20,24},{24,28},{28,32},{32,36}... | collective-permute-start | bytes 24584 | tf_op jit(solution)/shard_map/ppermute | solution.py:84
  27.5 59.0 %collective-permute-start.5 = (bf16[2,2048]{1,0:T(2,128)(2,1)}, bf16[2,2048]{1,0:T(2,128)(2,1)}, u32[]{:S(2)}, u32[]{:S(2)}) collective-permute-start(bf16[2,2048]{1,0:T(2,128)(2,1)} %slice.595), channel_id=1, source_target_pairs={{0,4},{4,8},{8,12},{12,16},{16,20},{20,24},{24,28},{28,32},{32,36}... | collective-permute-start | bytes 24584 | tf_op jit(solution)/shard_map/ppermute | solution.py:84
  36.9 41.9 %copy-start.48 = (f32[2048]{0:T(1024)S(1)}, f32[2048]{0:T(1024)}, u32[]{:S(2)}) copy-start(f32[2048]{0:T(1024)} %param.21) | copy-start | bytes 24580
  80.3 6.3 %collective-permute-start.6 = (bf16[2,2048]{1,0:T(2,128)(2,1)S(1)}, bf16[2,2048]{1,0:T(2,128)(2,1)S(1)}, u32[]{:S(2)}, u32[]{:S(2)}) collective-permute-start(bf16[2,2048]{1,0:T(2,128)(2,1)S(1)} %slice.739), channel_id=1, source_target_pairs={{0,4},{4,8},{8,12},{12,16},{16,20},{20,24},{24,28},{28,32},{32,36}... | collective-permute-start | bytes 24584 | tf_op jit(solution)/shard_map/ppermute | solution.py:84
  86.6 0.6 copy-start.49
  89.6 1.4 copy-start.52
  109.9 3.5 %copy-start.4 = (f32[4,16,2048]{2,1,0:T(8,128)S(1)}, f32[4,16,2048]{2,1,0:T(8,128)}, u32[]{:S(2)}) copy-start(f32[4,16,2048]{2,1,0:T(8,128)} %custom-call.1) | copy-start | bytes 1572868
  113.4 9.2 %copy-start.3 = (f32[16,2048]{0,1:T(8,128)S(1)}, f32[16,2048]{0,1:T(8,128)}, u32[]{:S(2)}) copy-start(f32[16,2048]{0,1:T(8,128)} %copy.40) | copy-start | bytes 393220
  115.9 130.8 %collective-permute-start.4 = (bf16[2,2048]{1,0:T(2,128)(2,1)}, bf16[2,2048]{1,0:T(2,128)(2,1)}, u32[]{:S(2)}, u32[]{:S(2)}) collective-permute-start(bf16[2,2048]{1,0:T(2,128)(2,1)} %slice.588), channel_id=1, source_target_pairs={{0,4},{4,8},{8,12},{12,16},{16,20},{20,24},{24,28},{28,32},{32,36}... | collective-permute-start | bytes 24584 | tf_op jit(solution)/shard_map/ppermute | solution.py:84
  162.4 31.5 %copy-start.5 = (f32[16,2048]{1,0:T(8,128)S(1)}, f32[16,2048]{1,0:T(8,128)}, u32[]{:S(2)}) copy-start(f32[16,2048]{1,0:T(8,128)} %get-tuple-element.154) | copy-start | bytes 393220
  193.9 4.0 %copy-start.50 = (f32[4]{0:T(128)S(1)}, f32[4]{0:T(128)}, u32[]{:S(2)}) copy-start(f32[4]{0:T(128)} %convert_multiply_fusion.1) | copy-start | bytes 52
  198.0 3.1 %copy-start.51 = (f32[64]{0:T(128)S(1)}, f32[64]{0:T(128)}, u32[]{:S(2)}) copy-start(f32[64]{0:T(128)} %broadcast_add_fusion) | copy-start | bytes 772
  225.5 4.0 %copy-start.9 = (f32[2048]{0:T(1024)S(1)}, f32[2048]{0:T(1024)}, u32[]{:S(2)}) copy-start(f32[2048]{0:T(1024)} %get-tuple-element.95) | copy-start | bytes 24580
  225.5 4.0 %copy-start.10 = (f32[2048]{0:T(1024)S(1)}, f32[2048]{0:T(1024)}, u32[]{:S(2)}) copy-start(f32[2048]{0:T(1024)} %get-tuple-element.96) | copy-start | bytes 24580
  225.5 4.0 %copy-start.11 = (f32[2048]{0:T(1024)S(1)}, f32[2048]{0:T(1024)}, u32[]{:S(2)}) copy-start(f32[2048]{0:T(1024)} %get-tuple-element.97) | copy-start | bytes 24580
  225.5 4.0 %copy-start.12 = (f32[2048]{0:T(1024)S(1)}, f32[2048]{0:T(1024)}, u32[]{:S(2)}) copy-start(f32[2048]{0:T(1024)} %get-tuple-element.98) | copy-start | bytes 24580
  225.5 4.0 %copy-start.13 = (f32[2048]{0:T(1024)S(1)}, f32[2048]{0:T(1024)}, u32[]{:S(2)}) copy-start(f32[2048]{0:T(1024)} %get-tuple-element.99) | copy-start | bytes 24580
  225.5 4.0 %copy-start.14 = (f32[2048]{0:T(1024)S(1)}, f32[2048]{0:T(1024)}, u32[]{:S(2)}) copy-start(f32[2048]{0:T(1024)} %get-tuple-element.100) | copy-start | bytes 24580
  225.6 4.0 %copy-start.15 = (f32[2048]{0:T(1024)S(1)}, f32[2048]{0:T(1024)}, u32[]{:S(2)}) copy-start(f32[2048]{0:T(1024)} %get-tuple-element.101) | copy-start | bytes 24580
  225.6 4.0 %copy-start.16 = (f32[2048]{0:T(1024)S(1)}, f32[2048]{0:T(1024)}, u32[]{:S(2)}) copy-start(f32[2048]{0:T(1024)} %get-tuple-element.102) | copy-start | bytes 24580
  225.6 4.0 %copy-start.17 = (f32[2048]{0:T(1024)S(1)}, f32[2048]{0:T(1024)}, u32[]{:S(2)}) copy-start(f32[2048]{0:T(1024)} %get-tuple-element.103) | copy-start | bytes 24580
  225.6 4.0 %copy-start.18 = (f32[2048]{0:T(1024)S(1)}, f32[2048]{0:T(1024)}, u32[]{:S(2)}) copy-start(f32[2048]{0:T(1024)} %get-tuple-element.104) | copy-start | bytes 24580
  225.6 4.0 %copy-start.19 = (f32[2048]{0:T(1024)S(1)}, f32[2048]{0:T(1024)}, u32[]{:S(2)}) copy-start(f32[2048]{0:T(1024)} %get-tuple-element.105) | copy-start | bytes 24580
  225.6 4.0 %copy-start.20 = (f32[2048]{0:T(1024)S(1)}, f32[2048]{0:T(1024)}, u32[]{:S(2)}) copy-start(f32[2048]{0:T(1024)} %get-tuple-element.106) | copy-start | bytes 24580
  225.6 4.0 %copy-start.21 = (f32[2048]{0:T(1024)S(1)}, f32[2048]{0:T(1024)}, u32[]{:S(2)}) copy-start(f32[2048]{0:T(1024)} %get-tuple-element.107) | copy-start | bytes 24580
  225.6 4.0 %copy-start.22 = (f32[2048]{0:T(1024)S(1)}, f32[2048]{0:T(1024)}, u32[]{:S(2)}) copy-start(f32[2048]{0:T(1024)} %get-tuple-element.108) | copy-start | bytes 24580
  225.6 4.0 %copy-start.23 = (f32[2048]{0:T(1024)S(1)}, f32[2048]{0:T(1024)}, u32[]{:S(2)}) copy-start(f32[2048]{0:T(1024)} %get-tuple-element.109) | copy-start | bytes 24580
  225.6 4.0 %copy-start.24 = (f32[2048]{0:T(1024)S(1)}, f32[2048]{0:T(1024)}, u32[]{:S(2)}) copy-start(f32[2048]{0:T(1024)} %get-tuple-element.110) | copy-start | bytes 24580
  225.7 4.0 %copy-start.25 = (f32[2048]{0:T(1024)S(1)}, f32[2048]{0:T(1024)}, u32[]{:S(2)}) copy-start(f32[2048]{0:T(1024)} %get-tuple-element.111) | copy-start | bytes 24580
  225.7 4.0 %copy-start.26 = (f32[2048]{0:T(1024)S(1)}, f32[2048]{0:T(1024)}, u32[]{:S(2)}) copy-start(f32[2048]{0:T(1024)} %get-tuple-element.112) | copy-start | bytes 24580
  225.7 4.0 %copy-start.27 = (f32[2048]{0:T(1024)S(1)}, f32[2048]{0:T(1024)}, u32[]{:S(2)}) copy-start(f32[2048]{0:T(1024)} %get-tuple-element.113) | copy-start | bytes 24580
  225.7 4.0 %copy-start.28 = (f32[2048]{0:T(1024)S(1)}, f32[2048]{0:T(1024)}, u32[]{:S(2)}) copy-start(f32[2048]{0:T(1024)} %get-tuple-element.114) | copy-start | bytes 24580
  225.7 4.0 %copy-start.29 = (f32[2048]{0:T(1024)S(1)}, f32[2048]{0:T(1024)}, u32[]{:S(2)}) copy-start(f32[2048]{0:T(1024)} %get-tuple-element.115) | copy-start | bytes 24580
  225.7 4.0 %copy-start.30 = (f32[2048]{0:T(1024)S(1)}, f32[2048]{0:T(1024)}, u32[]{:S(2)}) copy-start(f32[2048]{0:T(1024)} %get-tuple-element.116) | copy-start | bytes 24580
  225.7 4.0 %copy-start.31 = (f32[2048]{0:T(1024)S(1)}, f32[2048]{0:T(1024)}, u32[]{:S(2)}) copy-start(f32[2048]{0:T(1024)} %get-tuple-element.117) | copy-start | bytes 24580
  225.7 4.0 %copy-start.32 = (f32[2048]{0:T(1024)S(1)}, f32[2048]{0:T(1024)}, u32[]{:S(2)}) copy-start(f32[2048]{0:T(1024)} %get-tuple-element.118) | copy-start | bytes 24580
  225.7 4.0 %copy-start.33 = (f32[2048]{0:T(1024)S(1)}, f32[2048]{0:T(1024)}, u32[]{:S(2)}) copy-start(f32[2048]{0:T(1024)} %get-tuple-element.119) | copy-start | bytes 24580
  225.7 4.0 %copy-start.34 = (f32[2048]{0:T(1024)S(1)}, f32[2048]{0:T(1024)}, u32[]{:S(2)}) copy-start(f32[2048]{0:T(1024)} %get-tuple-element.120) | copy-start | bytes 24580
  225.8 4.0 %copy-start.35 = (f32[2048]{0:T(1024)S(1)}, f32[2048]{0:T(1024)}, u32[]{:S(2)}) copy-start(f32[2048]{0:T(1024)} %get-tuple-element.121) | copy-start | bytes 24580
  225.8 4.0 %copy-start.36 = (f32[2048]{0:T(1024)S(1)}, f32[2048]{0:T(1024)}, u32[]{:S(2)}) copy-start(f32[2048]{0:T(1024)} %get-tuple-element.122) | copy-start | bytes 24580
  225.8 4.0 %copy-start.37 = (f32[2048]{0:T(1024)S(1)}, f32[2048]{0:T(1024)}, u32[]{:S(2)}) copy-start(f32[2048]{0:T(1024)} %get-tuple-element.123) | copy-start | bytes 24580
  225.8 4.0 %copy-start.38 = (f32[2048]{0:T(1024)S(1)}, f32[2048]{0:T(1024)}, u32[]{:S(2)}) copy-start(f32[2048]{0:T(1024)} %get-tuple-element.124) | copy-start | bytes 24580
  225.8 4.0 %copy-start.39 = (f32[2048]{0:T(1024)S(1)}, f32[2048]{0:T(1024)}, u32[]{:S(2)}) copy-start(f32[2048]{0:T(1024)} %get-tuple-element.125) | copy-start | bytes 24580
  225.8 4.0 %copy-start.40 = (f32[2048]{0:T(1024)S(1)}, f32[2048]{0:T(1024)}, u32[]{:S(2)}) copy-start(f32[2048]{0:T(1024)} %get-tuple-element.126) | copy-start | bytes 24580
  225.8 4.0 %copy-start.41 = (f32[2048]{0:T(1024)S(1)}, f32[2048]{0:T(1024)}, u32[]{:S(2)}) copy-start(f32[2048]{0:T(1024)} %get-tuple-element.127) | copy-start | bytes 24580
  225.8 4.0 %copy-start.42 = (f32[2048]{0:T(1024)S(1)}, f32[2048]{0:T(1024)}, u32[]{:S(2)}) copy-start(f32[2048]{0:T(1024)} %get-tuple-element.128) | copy-start | bytes 24580
  225.8 4.0 %copy-start.43 = (f32[2048]{0:T(1024)S(1)}, f32[2048]{0:T(1024)}, u32[]{:S(2)}) copy-start(f32[2048]{0:T(1024)} %get-tuple-element.129) | copy-start | bytes 24580
  225.8 4.0 %copy-start.44 = (f32[2048]{0:T(1024)S(1)}, f32[2048]{0:T(1024)}, u32[]{:S(2)}) copy-start(f32[2048]{0:T(1024)} %get-tuple-element.130) | copy-start | bytes 24580
  225.8 4.0 %copy-start.45 = (f32[2048]{0:T(1024)S(1)}, f32[2048]{0:T(1024)}, u32[]{:S(2)}) copy-start(f32[2048]{0:T(1024)} %get-tuple-element.74) | copy-start | bytes 24580
  225.9 4.0 %copy-start.46 = (f32[2048]{0:T(1024)S(1)}, f32[2048]{0:T(1024)}, u32[]{:S(2)}) copy-start(f32[2048]{0:T(1024)} %get-tuple-element.75) | copy-start | bytes 24580
  225.9 4.0 %copy-start.47 = (f32[2048]{0:T(1024)S(1)}, f32[2048]{0:T(1024)}, u32[]{:S(2)}) copy-start(f32[2048]{0:T(1024)} %get-tuple-element.76) | copy-start | bytes 24580
  229.8 16.9 %copy-start.2 = (bf16[256,2048]{1,0:T(8,128)(2,1)S(1)}, bf16[256,2048]{1,0:T(8,128)(2,1)}, u32[]{:S(2)}) copy-start(bf16[256,2048]{1,0:T(8,128)(2,1)} %param.22) | copy-start | bytes 3145732
Sparse Core Ops, SparseCore 0:
  114.6 79.1 all-gather.2
where the time goes:
time: 260 us; the launch traced here: 256 us
  local copies, waits for them, and re-layouts  59.2 us (23%)
  other arithmetic  53.7 us (21%)
  matrix products  43.2 us (17%)
  Pallas kernels  32.4 us (12%)
  starting transfers between devices  23.7 us (9%)
  waiting for transfers between devices  20.6 us (8%)
  between operations  15 us (6%)
  blocking collectives  8.47 us (3%)
    slice x4, local copies, waits for them, and re-layouts, body(): inner = inner + impulse[offset] * padded[:, start:start + block_rows]  37.9 us
    pallas_call x1, Pallas kernels, medium_call(): pl.pallas_call(medium_kernel, grid=grid, in_specs=[pl.BlockSpec((span, bl...  32.4 us
    dot_general x1, matrix products, body(): jnp.einsum('bmc,msc->bsc', states, from_start, precision=lax.Precision.HI...  24.4 us
    ppermute x7, starting transfers between devices, passed_along(): lax.ppermute(value, axis, [(source, source + steps) for source in range(f...  23.6 us
    all_gather x1, waiting for transfers between devices, body(): lax.all_gather(final_state[None].astype(jnp.bfloat16), 'ctx', axis=0, til...  20.6 us
    dot_general x1, matrix products, body(): jnp.einsum('bsc,msc->bmc', blocks.astype(jnp.float32), to_end, precision=...  18.8 us
    add x1, other arithmetic, body(): inner + outer  16.8 us
    reduce_sum x1, other arithmetic, body(): jnp.sum(mode_weight[:, None, :] * jnp.exp(-rates_wide * positions[None, :...  12.7 us
  transfers between devices with their start and end apart: 8, of which 1 were waited for; matrix products, arithmetic and copies ran while one was open for 49% of the time, Pallas kernels for 13%

commit v1 on v0

--- a/solution.py
+++ b/solution.py
@@ -76,6 +76,125 @@
     )(ext, taps, skip, gate_feat)
 
 D = 8192
+
+
+LANE = 128
+GROUP = 4
+MODES_HALF = 8
+
+
+def _rows_to_f32(p_ref, pf_ref):
+    pf_ref[...] = p_ref[...].astype(jnp.float32)
+
+
+def modal_end_kernel(p_ref, e_ref, out_ref, pf_ref):
+    rows = p_ref.shape[0]
+    _rows_to_f32(p_ref, pf_ref)
+    lanes = [pl.ds(g * LANE, LANE) for g in range(GROUP)]
+    e_lo = [e_ref[0:8, ln] for ln in lanes]
+    e_hi = [e_ref[8:16, ln] for ln in lanes]
+
+    def step(i, carry):
+        lo, hi = carry
+        row = pl.multiple_of(i * 8, 8)
+        blocks = [pf_ref[pl.ds(row, 8), ln] for ln in lanes]
+        for j in range(8):
+            new_lo, new_hi = [], []
+            for g in range(GROUP):
+                pb = jnp.broadcast_to(blocks[g][j : j + 1], (8, LANE))
+                new_lo.append(e_lo[g] * lo[g] + pb)
+                new_hi.append(e_hi[g] * hi[g] + pb)
+            lo, hi = new_lo, new_hi
+        return lo, hi
+
+    zero = [jnp.zeros((8, LANE), jnp.float32) for _ in range(GROUP)]
+    lo, hi = lax.fori_loop(0, rows // 8, step, (zero, list(zero)))
+    for g, ln in enumerate(lanes):
+        out_ref[0:8, ln] = lo[g]
+        out_ref[8:16, ln] = hi[g]
+
+
+def modal_end_call(product, decay):
+    rows, width = product.shape
+    block = LANE * GROUP
+    return pl.pallas_call(
+        modal_end_kernel,
+        grid=(width // block,),
+        in_specs=[
+            pl.BlockSpec((rows, block), lambda i: (0, i)),
+            pl.BlockSpec((16, block), lambda i: (0, i)),
+        ],
+        out_specs=pl.BlockSpec((16, block), lambda i: (0, i)),
+        out_shape=jax.ShapeDtypeStruct((16, width), jnp.float32),
+        scratch_shapes=[pltpu.VMEM((rows, block), jnp.float32)],
+    )(product, decay)
+
+
+def modal_out_kernel(p_ref, e_ref, w_ref, s_ref, skip_ref, gate_ref, out_ref, pf_ref, z_ref):
+    rows = p_ref.shape[0]
+    _rows_to_f32(p_ref, pf_ref)
+    lanes = [pl.ds(g * LANE, LANE) for g in range(GROUP)]
+    e_lo = [e_ref[0:8, ln] for ln in lanes]
+    e_hi = [e_ref[8:16, ln] for ln in lanes]
+    w_lo = [w_ref[0:8, ln] for ln in lanes]
+    w_hi = [w_ref[8:16, ln] for ln in lanes]
+
+    def step(i, carry):
+        lo, hi = carry
+        row = pl.multiple_of(i * 8, 8)
+        blocks = [pf_ref[pl.ds(row, 8), ln] for ln in lanes]
+        for j in range(8):
+            new_lo, new_hi = [], []
+            for g in range(GROUP):
+                pb = jnp.broadcast_to(blocks[g][j : j + 1], (8, LANE))
+                a = e_lo[g] * lo[g] + pb
+                b = e_hi[g] * hi[g] + pb
+                z_ref[g, pl.ds(pl.multiple_of(i * 64 + 8 * j, 8), 8), :] = w_lo[g] * a + w_hi[g] * b
+                new_lo.append(a)
+                new_hi.append(b)
+            lo, hi = new_lo, new_hi
+        return lo, hi
+
+    init_lo = [s_ref[0:8, ln] for ln in lanes]
+    init_hi = [s_ref[8:16, ln] for ln in lanes]
+    lax.fori_loop(0, rows // 8, step, (init_lo, init_hi))
+
+    def reduce(i, carry):
+        row = pl.multiple_of(i * 8, 8)
+        for g, ln in enumerate(lanes):
+            total = z_ref[g, pl.ds(i * 64, 8, stride=8), :]
+            for j in range(1, 8):
+                total = total + z_ref[g, pl.ds(i * 64 + j, 8, stride=8), :]
+            own = pf_ref[pl.ds(row, 8), ln]
+            skip = jnp.broadcast_to(skip_ref[:, ln], (8, LANE))
+            conv = total + skip * own
+            out_ref[pl.ds(row, 8), ln] = (gate_ref[pl.ds(row, 8), ln] * conv).astype(out_ref.dtype)
+        return carry
+
+    lax.fori_loop(0, rows // 8, reduce, 0)
+
+
+def modal_out_call(product, decay, weight, start, skip, gate_feat):
+    rows, width = product.shape
+    block = LANE * GROUP
+    return pl.pallas_call(
+        modal_out_kernel,
+        grid=(width // block,),
+        in_specs=[
+            pl.BlockSpec((rows, block), lambda i: (0, i)),
+            pl.BlockSpec((16, block), lambda i: (0, i)),
+            pl.BlockSpec((16, block), lambda i: (0, i)),
+            pl.BlockSpec((16, block), lambda i: (0, i)),
+            pl.BlockSpec((1, block), lambda i: (0, i)),
+            pl.BlockSpec((rows, block), lambda i: (0, i)),
+        ],
+        out_specs=pl.BlockSpec((rows, block), lambda i: (0, i)),
+        out_shape=jax.ShapeDtypeStruct((rows, width), jnp.bfloat16),
+        scratch_shapes=[
+            pltpu.VMEM((rows, block), jnp.float32),
+            pltpu.VMEM((GROUP, rows * 8, LANE), jnp.float32),
+        ],
+    )(product, decay, weight, start, skip, gate_feat)
 
 
 def passed_along(value, axis, steps):
@@ -143,31 +262,9 @@
     key_feat_long = short_filter(jnp.concatenate([rim_key_long, key_long], 0), short_long[1])
     value_feat_long = short_filter(jnp.concatenate([rim_normed, normed], 0), short_long[2])
     product_long = (key_feat_long * value_feat_long).astype(jnp.bfloat16)
-    block_rows = 64
-    block_count = row_count // block_rows
-    positions = jnp.arange(block_rows).astype(jnp.float32)
     mode_weight = residues * jnp.sqrt(-jnp.expm1(-2.0 * decay_rates))
-    rates_wide = decay_rates[:, None, :]
-    to_end = jnp.exp(-rates_wide * (block_rows - 1.0 - positions)[None, :, None])
-    from_start = mode_weight[:, None, :] * jnp.exp(-rates_wide * (positions + 1.0)[None, :, None])
-    impulse = jnp.sum(
-        mode_weight[:, None, :] * jnp.exp(-rates_wide * positions[None, :, None]), axis=0
-    )
-    blocks = product_long.reshape(block_count, block_rows, width_local)
-    padded = jnp.pad(blocks, ((0, 0), (block_rows - 1, 0), (0, 0)))
-    inner = jnp.zeros(blocks.shape, jnp.float32)
-    for offset in range(block_rows):
-        start = block_rows - 1 - offset
-        inner = inner + impulse[offset] * padded[:, start : start + block_rows]
-    ends = jnp.einsum(
-        "bsc,msc->bmc", blocks.astype(jnp.float32), to_end, precision=lax.Precision.HIGHEST
-    )
-    block_decay = jnp.exp(-decay_rates * block_rows)
-
-    def advance(state, end):
-        return (block_decay * state + end, state)
-
-    final_state, starts = lax.scan(advance, jnp.zeros(decay_rates.shape, jnp.float32), ends)
+    step_decay = jnp.exp(-decay_rates)
+    final_state = modal_end_call(product_long, step_decay)
     position = lax.axis_index("ctx")
     piece = lax.all_gather(
         final_state[None].astype(jnp.bfloat16), "ctx", axis=0, tiled=True
@@ -179,15 +276,10 @@
         jnp.exp(-decay_rates[None] * row_count * jnp.maximum(gaps, 0.0)[:, None, None]),
         0.0,
     )
-    incoming = jnp.zeros_like(final_state) + jnp.sum(factors * piece, axis=0)
-    lead = jnp.exp(
-        -decay_rates[None]
-        * (block_rows * jnp.arange(block_count).astype(jnp.float32))[:, None, None]
-    )
-    states = starts + lead * incoming[None]
-    outer = jnp.einsum("bmc,msc->bsc", states, from_start, precision=lax.Precision.HIGHEST)
-    conv_long = (inner + outer).reshape(row_count, width_local) + skip_long * product_long
-    mixed_long = (gate_feat_long * conv_long).astype(jnp.bfloat16)
+    incoming = jnp.sum(factors * piece, axis=0)
+    mixed_long = modal_out_call(
+        product_long, step_decay, mode_weight, incoming, skip_long[None, :], gate_feat_long
+    )
     return (mixed_medium, mixed_long)
 
 

time: 260 us -> 200 us (0.77)
  local copies, waits for them, and re-layouts: 59.2 us -> 2.9 us
  waiting for transfers between devices: 20.6 us -> 75.2 us
  matrix products: 43.2 us -> 0 us
  other arithmetic: 53.7 us -> 22.6 us
  Pallas kernels: 32.4 us -> 47.5 us
    all_gather x1, waiting for transfers between devices: 20.6 us -> 70.7 us  [body(): lax.all_gather(final_state[None].astype(jnp.bfloat16), 'ctx', axis=0, til...]
    dot_general x2 -> x0, matrix products: 43.2 us -> none  [the longest x1 24.4 us: body(): jnp.einsum('bmc,msc->bsc', states, from_start, precision=lax.Precision.HI...]
    slice x4 -> x0, local copies, waits for them, and re-layouts: 37.9 us -> none  [body(): inner = inner + impulse[offset] * padded[:, start:start + block_rows]]
    add x7 -> x0, other arithmetic: 17.8 us -> none  [the longest x1 16.8 us: body(): inner + outer]
    pallas_call x0 -> x2, Pallas kernels: none -> 15.2 us  [the longest x1 10.5 us: modal_out_call(): pl.pallas_call(modal_out_kernel, grid=(width // block,), in_specs=[pl.Blo...]
    reduce_sum x2 -> x1, other arithmetic: 16.7 us -> 4.59 us  [body(): incoming = jnp.sum(factors * piece, axis=0)]
    ppermute x7, waiting for transfers between devices: 0.02 us -> 4.49 us  [passed_along(): lax.ppermute(value, axis, [(source, source + steps) for source in range(f...]
    unnamed x107 -> x14, local copies, waits for them, and re-layouts: 4.32 us -> 0.04 us
  transfers between devices with their start and end apart: 8 -> 8, of which waited for: 1 -> 3; matrix products, arithmetic and copies ran while one was open for 49% -> 8% of each run, Pallas kernels for 13% -> 16%
where the time goes in v1:
time: 200 us; the launch traced here: 196 us
  waiting for transfers between devices  75.2 us (38%)
  Pallas kernels  47.5 us (24%)
  starting transfers between devices  25.3 us (13%)
  other arithmetic  22.6 us (11%)
  between operations  14.3 us (7%)
  blocking collectives  8.5 us (4%)
  local copies, waits for them, and re-layouts  2.9 us (1%)
    all_gather x1, waiting for transfers between devices, body(): lax.all_gather(final_state[None].astype(jnp.bfloat16), 'ctx', axis=0, til...  70.7 us
    pallas_call x1, Pallas kernels, medium_call(): pl.pallas_call(medium_kernel, grid=grid, in_specs=[pl.BlockSpec((span, bl...  32.4 us
    ppermute x7, starting transfers between devices, passed_along(): lax.ppermute(value, axis, [(source, source + steps) for source in range(f...  25.2 us
    pallas_call x1, Pallas kernels, modal_out_call(): pl.pallas_call(modal_out_kernel, grid=(width // block,), in_specs=[pl.Blo...  10.5 us
    psum x1, blocking collectives, body(): total_squares = lax.psum(squares, 'ch')  8.5 us
    pallas_call x1, Pallas kernels, modal_end_call(): pl.pallas_call(modal_end_kernel, grid=(width // block,), in_specs=[pl.Blo...  4.71 us
    convert_element_type x1, other arithmetic, body(): late_product = (short_filter(key_medium, short_medium[1]) * short_filter(...  4.69 us
    reduce_sum x1, other arithmetic, body(): incoming = jnp.sum(factors * piece, axis=0)  4.59 us
  transfers between devices with their start and end apart: 8, of which 3 were waited for; matrix products, arithmetic and copies ran while one was open for 8% of the time, Pallas kernels for 16%

profile of v1, /device:TPU:25, one launch (start us, length us, event | category | flops | bytes accessed | tf_op | source)
XLA Modules:
  0.0 196.3 jit_solution(1206363736055422828)
XLA Ops:
  7.2 0.0 all-gather.3.cloned.1.call-start
  7.2 0.8 fusion.6
  8.0 4.1 %collective-permute-start.2 = (bf16[2,2048]{1,0:T(2,128)(2,1)S(1)}, bf16[2,2048]{1,0:T(2,128)(2,1)S(1)}, u32[]{:S(2)}, u32[]{:S(2)}) collective-permute-start(bf16[2,2048]{1,0:T(2,128)(2,1)S(1)} %get-tuple-element.9), channel_id=1, source_target_pairs={{0,4},{4,8},{8,12},{12,16},{16,20},{20,24},{24,28},{28,32},{32,36}... | collective-permute-start | bytes 24584 | tf_op jit(solution)/shard_map/ppermute | solution.py:203
  12.1 0.8 fusion.5
  12.9 1.9 collective-permute-start.1
  14.8 1.0 fusion.8
  15.9 0.0 copy-start
  15.9 0.0 copy-start.1
  15.9 0.0 copy-start.3
  15.9 0.0 copy-start.4
  15.9 4.7 %multiply_convert_fusion.2 = bf16[254,2048]{1,0:T(8,128)(2,1)S(1)} fusion(bf16[256,2048]{1,0:T(8,128)(2,1)} %param.15, f32[2048]{0:T(1024)S(1)} %bitcast.24, f32[2048]{0:T(1024)S(1)} %bitcast.26, f32[2048]{0:T(1024)S(1)} %bitcast.28, bf16[256,2048]{1,0:T(8,128)(2,1)} %param.14, f32[2048]{0:T(1024)S(1)} %bitcast.30, f32[2048]{0:T(1024)S(1)} %bitcast.32, ...), kind=kLoop, calls=%fused_computation.6 | loop fusion | flops 9363456 | bytes 7331840 | tf_op jit(solution)/shard_map/convert_element_type | solution.py:239
  20.6 0.1 slice.222
  20.8 3.9 %collective-permute-start = (bf16[127,2048]{1,0:T(8,128)(2,1)S(1)}, bf16[127,2048]{1,0:T(8,128)(2,1)S(1)}, u32[]{:S(2)}, u32[]{:S(2)}) collective-permute-start(bf16[127,2048]{1,0:T(8,128)(2,1)S(1)} %slice.222), channel_id=1, source_target_pairs={{0,4},{4,8},{8,12},{12,16},{16,20},{20,24},{24,28},{28,32},{32,36}... | collective-permute-start | bytes 1560584 | tf_op jit(solution)/shard_map/ppermute | solution.py:203
  24.7 0.0 copy-done
  24.7 1.9 collective-permute-start.3
  26.7 0.0 copy-done.1
  26.7 3.9 %collective-permute-start.4 = (bf16[2,2048]{1,0:T(2,128)(2,1)S(1)}, bf16[2,2048]{1,0:T(2,128)(2,1)S(1)}, u32[]{:S(2)}, u32[]{:S(2)}) collective-permute-start(bf16[2,2048]{1,0:T(2,128)(2,1)S(1)} %slice.206), channel_id=1, source_target_pairs={{0,4},{4,8},{8,12},{12,16},{16,20},{20,24},{24,28},{28,32},{32,36}... | collective-permute-start | bytes 24584 | tf_op jit(solution)/shard_map/ppermute | solution.py:203
  30.6 0.0 copy-done.3
  30.6 0.0 copy-done.4
  30.6 0.8 negate_multiply_fusion
  31.5 0.0 collective-permute-done.2
  31.5 0.0 collective-permute-done.1
  31.5 0.1 multiply_convert_fusion.3
  31.6 0.0 collective-permute-done.3
  31.6 2.0 %multiply_add_fusion.1.gate_ref = f32[256,2048]{1,0:T(8,128)} fusion(bf16[256,2048]{1,0:T(8,128)(2,1)S(1)} %copy-done, bf16[2,2048]{1,0:T(2,128)(2,1)S(1)} %collective-permute-done.3, f32[2048]{0:T(1024)S(1)} %bitcast.40, f32[2048]{0:T(1024)S(1)} %bitcast.41, f32[2048]{0:T(1024)S(1)} %bitcast.39), kind=kLoop, calls=%fused_computation.5 | loop fusion | flops 7340032 | bytes 3178496 | tf_op jit(solution)/shard_map/add | solution.py:207
  33.6 0.0 collective-permute-done
  33.6 1.8 pad_maximum_fusion.ext_ref
  35.4 0.0 copy-start.6
  35.4 32.4 %shard_map.140 = (bf16[256,2048]{1,0:T(8,128)(2,1)}, f32[256,128]{1,0:T(8,128)}) custom-call(bf16[384,2048]{1,0:T(8,128)(2,1)} %pad_maximum_fusion.ext_ref, f32[128,2048]{1,0:T(8,128)} %f_ref.1, f32[1,2048]{1,0:T(1,128)} %bitcast.48, f32[256,2048]{1,0:T(8,128)} %multiply_add_fusion.1.gate_ref), custom_call_target="tpu_custom_call" | custom-call | tf_op jit(solution)/shard_map/pallas_call | solution.py:56
  67.8 0.0 copy-start.5
  67.8 1.0 reduce_sum.18
  68.8 8.5 %psum.7 = f32[256]{0:T(256)S(1)} all-reduce(f32[256]{0:T(256)S(1)} %reduce_sum.18), channel_id=1, replica_groups=mesh['ctx'=64,'ch'=4] {'ch'}, use_global_device_ids=true, to_apply=%region_1.0 | all-reduce | flops 256 | bytes 2048 | tf_op jit(solution)/shard_map/psum | solution.py:255
  77.3 0.0 copy-done.6
  77.3 1.5 multiply_convert_fusion.1
  78.8 5.7 %collective-permute-start.5 = (bf16[2,2048]{1,0:T(2,128)(2,1)S(1)}, bf16[2,2048]{1,0:T(2,128)(2,1)S(1)}, u32[]{:S(2)}, u32[]{:S(2)}) collective-permute-start(bf16[2,2048]{1,0:T(2,128)(2,1)S(1)} %slice.227), channel_id=1, source_target_pairs={{0,4},{4,8},{8,12},{12,16},{16,20},{20,24},{24,28},{28,32},{32,36}... | collective-permute-start | bytes 24584 | tf_op jit(solution)/shard_map/ppermute | solution.py:203
  84.6 0.0 copy-done.5
  84.6 0.1 fusion.7
  84.6 0.0 collective-permute-done.4
  84.6 1.2 collective-permute-done.5
  85.8 0.0 copy-start.2
  85.8 2.5 %multiply_convert_fusion.p_ref = bf16[256,2048]{1,0:T(8,128)(2,1)} fusion(bf16[256,2048]{1,0:T(8,128)(2,1)S(1)} %multiply_convert_fusion.1, bf16[256,2048]{1,0:T(8,128)(2,1)S(1)} %copy-done.1, bf16[2,2048]{1,0:T(2,128)(2,1)S(1)} %collective-permute-done.5, bf16[2,2048]{1,0:T(2,128)(2,1)S(1)} %collective-permute-done.4, f32[2048]{0:T(1024)S(1)} %bitcast.42, ...), kind=kLoop, calls=%fused_computation.3 | loop fusion | flops 15728640 | bytes 3211264 | tf_op jit(solution)/shard_map/convert_element_type | solution.py:264
  88.3 4.7 %shard_map.141 = f32[16,2048]{1,0:T(8,128)} custom-call(bf16[256,2048]{1,0:T(8,128)(2,1)} %multiply_convert_fusion.p_ref, f32[16,2048]{1,0:T(8,128)} %get-tuple-element.12.e_ref), custom_call_target="tpu_custom_call" | custom-call | tf_op jit(solution)/shard_map/pallas_call | solution.py:120
  93.0 1.5 convert_element_type.133
  94.5 0.0 all-gather.3.cloned.1.call-update
  94.6 0.0 copy-done.2
  94.6 3.7 %collective-permute-start.6 = (bf16[2,2048]{1,0:T(2,128)(2,1)S(1)}, bf16[2,2048]{1,0:T(2,128)(2,1)S(1)}, u32[]{:S(2)}, u32[]{:S(2)}) collective-permute-start(bf16[2,2048]{1,0:T(2,128)(2,1)S(1)} %slice.218), channel_id=1, source_target_pairs={{0,4},{4,8},{8,12},{12,16},{16,20},{20,24},{24,28},{28,32},{32,36}... | collective-permute-start | bytes 24584 | tf_op jit(solution)/shard_map/ppermute | solution.py:203
  98.4 3.3 %collective-permute-done.6 = bf16[2,2048]{1,0:T(2,128)(2,1)S(1)} collective-permute-done((bf16[2,2048]{1,0:T(2,128)(2,1)S(1)}, bf16[2,2048]{1,0:T(2,128)(2,1)S(1)}, u32[]{:S(2)}, u32[]{:S(2)}) %collective-permute-start.6) | collective-permute-done | bytes 8224 | tf_op jit(solution)/shard_map/ppermute | solution.py:203
  101.7 2.0 %multiply_add_fusion.gate_ref = f32[256,2048]{1,0:T(8,128)} fusion(bf16[256,2048]{1,0:T(8,128)(2,1)S(1)} %copy-done.2, bf16[2,2048]{1,0:T(2,128)(2,1)S(1)} %collective-permute-done.6, f32[2048]{0:T(1024)S(1)} %bitcast.37, f32[2048]{0:T(1024)S(1)} %bitcast.38, f32[2048]{0:T(1024)S(1)} %bitcast.36), kind=kLoop, calls=%fused_computation.2 | loop fusion | flops 7340032 | bytes 3178496 | tf_op jit(solution)/shard_map/add | solution.py:207
  103.7 70.7 %all-gather.3.cloned.1.call-done = bf16[1024,2048]{1,0:T(8,128)(2,1)} async-done(((bf16[16,2048]{1,0:T(8,128)(2,1)}), bf16[1024,2048]{1,0:T(8,128)(2,1)}) %all-gather.3.cloned.1.call-update) | async-done | bytes 4194320 | tf_op jit(solution)/shard_map/all_gather | solution.py:269
  174.4 4.6 %fusion.s_ref = f32[16,2048]{1,0:T(8,128)} fusion(bf16[64,16,2048]{2,1,0:T(8,128)(2,1)} %bitcast.23, f32[64]{0:T(128)S(1)} %convert_maximum_fusion, f32[16,2048]{1,0:T(8,128)S(1)} %get-tuple-element.10, pred[64]{0:T(512)(128)(4,1)S(1)} %convert_compare_fusion), kind=kLoop, calls=%fused_computation.1 | loop fusion | flops 10452992 | bytes 4456768 | tf_op jit(solution)/shard_map/reduce_sum | solution.py:279
  179.0 10.5 %shard_map.142 = bf16[256,2048]{1,0:T(8,128)(2,1)} custom-call(bf16[256,2048]{1,0:T(8,128)(2,1)} %multiply_convert_fusion.p_ref, f32[16,2048]{1,0:T(8,128)} %get-tuple-element.12.e_ref, f32[16,2048]{1,0:T(8,128)} %get-tuple-element.11.w_ref, f32[16,2048]{1,0:T(8,128)} %fusion.s_ref, f32[1,2048]{1,0:T(1,128)} %bitcast.49, f32[256,2048]{1,0:T(8,128)} %multiply_add_fusion.gate_ref), custom_call_target="tpu_custom_call" | custom-call | tf_op jit(solution)/shard_map/pallas_call | solution.py:180
  (8 shorter events, 0.1 us)
Async XLA Ops:
  7.2 167.3 %all-gather.3.cloned.1.call-start = ((), (), s32[]{:S(2)}) async-start(), calls=%async_computation | async-start | bytes 4259840 | tf_op jit(solution)/shard_map/all_gather | solution.py:269
  8.0 23.5 %collective-permute-start.2 = (bf16[2,2048]{1,0:T(2,128)(2,1)S(1)}, bf16[2,2048]{1,0:T(2,128)(2,1)S(1)}, u32[]{:S(2)}, u32[]{:S(2)}) collective-permute-start(bf16[2,2048]{1,0:T(2,128)(2,1)S(1)} %get-tuple-element.9), channel_id=1, source_target_pairs={{0,4},{4,8},{8,12},{12,16},{16,20},{20,24},{24,28},{28,32},{32,36}... | collective-permute-start | bytes 24584 | tf_op jit(solution)/shard_map/ppermute | solution.py:203
  12.9 18.6 %collective-permute-start.1 = (bf16[2,2048]{1,0:T(2,128)(2,1)S(1)}, bf16[2,2048]{1,0:T(2,128)(2,1)S(1)}, u32[]{:S(2)}, u32[]{:S(2)}) collective-permute-start(bf16[2,2048]{1,0:T(2,128)(2,1)S(1)} %get-tuple-element.7), channel_id=1, source_target_pairs={{0,4},{4,8},{8,12},{12,16},{16,20},{20,24},{24,28},{28,32},{32,36}... | collective-permute-start | bytes 24584 | tf_op jit(solution)/shard_map/ppermute | solution.py:203
  15.9 8.8 %copy-start = (bf16[256,2048]{1,0:T(8,128)(2,1)S(1)}, bf16[256,2048]{1,0:T(8,128)(2,1)}, u32[]{:S(2)}) copy-start(bf16[256,2048]{1,0:T(8,128)(2,1)} %param.13) | copy-start | bytes 3145732
  15.9 10.8 %copy-start.1 = (bf16[256,2048]{1,0:T(8,128)(2,1)S(1)}, bf16[256,2048]{1,0:T(8,128)(2,1)}, u32[]{:S(2)}) copy-start(bf16[256,2048]{1,0:T(8,128)(2,1)} %param.21) | copy-start | bytes 3145732
  15.9 14.7 %copy-start.3 = (f32[16,2048]{1,0:T(8,128)S(1)}, f32[16,2048]{1,0:T(8,128)}, u32[]{:S(2)}) copy-start(f32[16,2048]{1,0:T(8,128)} %param.23) | copy-start | bytes 393220
  15.9 14.7 %copy-start.4 = (f32[16,2048]{1,0:T(8,128)S(1)}, f32[16,2048]{1,0:T(8,128)}, u32[]{:S(2)}) copy-start(f32[16,2048]{1,0:T(8,128)} %param.24) | copy-start | bytes 393220
  20.8 12.8 %collective-permute-start = (bf16[127,2048]{1,0:T(8,128)(2,1)S(1)}, bf16[127,2048]{1,0:T(8,128)(2,1)S(1)}, u32[]{:S(2)}, u32[]{:S(2)}) collective-permute-start(bf16[127,2048]{1,0:T(8,128)(2,1)S(1)} %slice.222), channel_id=1, source_target_pairs={{0,4},{4,8},{8,12},{12,16},{16,20},{20,24},{24,28},{28,32},{32,36}... | collective-permute-start | bytes 1560584 | tf_op jit(solution)/shard_map/ppermute | solution.py:203
  24.7 6.8 %collective-permute-start.3 = (bf16[2,2048]{1,0:T(2,128)(2,1)S(1)}, bf16[2,2048]{1,0:T(2,128)(2,1)S(1)}, u32[]{:S(2)}, u32[]{:S(2)}) collective-permute-start(bf16[2,2048]{1,0:T(2,128)(2,1)S(1)} %slice.200), channel_id=1, source_target_pairs={{0,4},{4,8},{8,12},{12,16},{16,20},{20,24},{24,28},{28,32},{32,36}... | collective-permute-start | bytes 24584 | tf_op jit(solution)/shard_map/ppermute | solution.py:203
  26.7 57.9 %collective-permute-start.4 = (bf16[2,2048]{1,0:T(2,128)(2,1)S(1)}, bf16[2,2048]{1,0:T(2,128)(2,1)S(1)}, u32[]{:S(2)}, u32[]{:S(2)}) collective-permute-start(bf16[2,2048]{1,0:T(2,128)(2,1)S(1)} %slice.206), channel_id=1, source_target_pairs={{0,4},{4,8},{8,12},{12,16},{16,20},{20,24},{24,28},{28,32},{32,36}... | collective-permute-start | bytes 24584 | tf_op jit(solution)/shard_map/ppermute | solution.py:203
  35.4 41.9 %copy-start.6 = (f32[2048]{0:T(1024)S(1)}, f32[2048]{0:T(1024)}, u32[]{:S(2)}) copy-start(f32[2048]{0:T(1024)} %param.19) | copy-start | bytes 24580
  67.8 16.8 %copy-start.5 = (f32[3,3,2048]{2,1,0:T(4,128)S(1)}, f32[3,3,2048]{2,1,0:T(4,128)}, u32[]{:S(2)}) copy-start(f32[3,3,2048]{2,1,0:T(4,128)} %param.22) | copy-start | bytes 221188
  78.8 7.0 %collective-permute-start.5 = (bf16[2,2048]{1,0:T(2,128)(2,1)S(1)}, bf16[2,2048]{1,0:T(2,128)(2,1)S(1)}, u32[]{:S(2)}, u32[]{:S(2)}) collective-permute-start(bf16[2,2048]{1,0:T(2,128)(2,1)S(1)} %slice.227), channel_id=1, source_target_pairs={{0,4},{4,8},{8,12},{12,16},{16,20},{20,24},{24,28},{28,32},{32,36}... | collective-permute-start | bytes 24584 | tf_op jit(solution)/shard_map/ppermute | solution.py:203
  85.8 8.8 %copy-start.2 = (bf16[256,2048]{1,0:T(8,128)(2,1)S(1)}, bf16[256,2048]{1,0:T(8,128)(2,1)}, u32[]{:S(2)}) copy-start(bf16[256,2048]{1,0:T(8,128)(2,1)} %param.20) | copy-start | bytes 3145732
  94.6 7.1 %collective-permute-start.6 = (bf16[2,2048]{1,0:T(2,128)(2,1)S(1)}, bf16[2,2048]{1,0:T(2,128)(2,1)S(1)}, u32[]{:S(2)}, u32[]{:S(2)}) collective-permute-start(bf16[2,2048]{1,0:T(2,128)(2,1)S(1)} %slice.218), channel_id=1, source_target_pairs={{0,4},{4,8},{8,12},{12,16},{16,20},{20,24},{24,28},{28,32},{32,36}... | collective-permute-start | bytes 24584 | tf_op jit(solution)/shard_map/ppermute | solution.py:203
Sparse Core Ops, SparseCore 0:
  94.7 79.6 all-gather.2

commit v2 on v1

--- a/solution.py
+++ b/solution.py
@@ -252,7 +252,12 @@
         extended, filter_medium, skip_medium[None, :], gate_feat
     )
     squares = jnp.sum(partial_squares, axis=1)
-    total_squares = lax.psum(squares, "ch")
+    ring = lax.axis_size("ch")
+    total_squares = squares
+    for shift in range(1, ring):
+        total_squares = total_squares + lax.ppermute(
+            squares, "ch", [(source, (source + shift) % ring) for source in range(ring)]
+        )
     inverse = lax.rsqrt(total_squares / D + 1e-06)
     normed = (mixed_medium * norm_gain * inverse[:, None]).astype(jnp.bfloat16)
     rim_gate_long, rim_key_long, rim_normed = passed_along(
@@ -265,18 +270,12 @@
     mode_weight = residues * jnp.sqrt(-jnp.expm1(-2.0 * decay_rates))
     step_decay = jnp.exp(-decay_rates)
     final_state = modal_end_call(product_long, step_decay)
-    position = lax.axis_index("ctx")
-    piece = lax.all_gather(
-        final_state[None].astype(jnp.bfloat16), "ctx", axis=0, tiled=True
-    ).astype(jnp.float32)
-    count = piece.shape[0]
-    gaps = (position - 1 - jnp.arange(count, dtype=jnp.int32)).astype(jnp.float32)
-    factors = jnp.where(
-        gaps[:, None, None] >= 0.0,
-        jnp.exp(-decay_rates[None] * row_count * jnp.maximum(gaps, 0.0)[:, None, None]),
-        0.0,
-    )
-    incoming = jnp.sum(factors * piece, axis=0)
+    incoming = passed_along(final_state, "ctx", 1)
+    span = 1
+    while span < lax.axis_size("ctx"):
+        earlier = passed_along(incoming, "ctx", span)
+        incoming = incoming + jnp.exp(-decay_rates * (row_count * span)) * earlier
+        span *= 2
     mixed_long = modal_out_call(
         product_long, step_decay, mode_weight, incoming, skip_long[None, :], gate_feat_long
     )

time: 200 us -> 165 us (0.82)
  the two profiles are of different devices: /device:TPU:25 before, /device:TPU:16 now
where the time goes in v2:
time: 165 us
  waiting for transfers between devices  58.8 us (36%)
  Pallas kernels  47.7 us (29%)
  starting transfers between devices  37 us (22%)
  other arithmetic  17.3 us (10%)
  local copies, waits for them, and re-layouts  2.9 us (2%)
    ppermute x14, waiting for transfers between devices, passed_along(): lax.ppermute(value, axis, [(source, source + steps) for source in range(f...  57.3 us
    pallas_call x1, Pallas kernels, medium_call(): pl.pallas_call(medium_kernel, grid=grid, in_specs=[pl.BlockSpec((span, bl...  32.4 us
    ppermute x14, starting transfers between devices, passed_along(): lax.ppermute(value, axis, [(source, source + steps) for source in range(f...  31.2 us
    pallas_call x1, Pallas kernels, modal_out_call(): pl.pallas_call(modal_out_kernel, grid=(width // block,), in_specs=[pl.Blo...  10.5 us
    ppermute x3, starting transfers between devices, body(): lax.ppermute(squares, 'ch', [(source, (source + shift) % ring) for source...  5.73 us
    pallas_call x1, Pallas kernels, modal_end_call(): pl.pallas_call(modal_end_kernel, grid=(width // block,), in_specs=[pl.Blo...  4.8 us
    convert_element_type x1, other arithmetic, body(): late_product = (short_filter(key_medium, short_medium[1]) * short_filter(...  4.77 us
    add x2, other arithmetic, short_filter(): weights[0] * extended[2:] + weights[1] * extended[1:-1]  4.04 us
  transfers between devices with their start and end apart: 17, of which 12 were waited for; matrix products, arithmetic and copies ran while one was open for 10% of the time, Pallas kernels for 20%

profile of v2, /device:TPU:16, one launch (start us, length us, event | category | flops | bytes accessed | tf_op | source)
XLA Modules:
  0.0 164.5 jit_solution(3256616453202247969)
XLA Ops:
  0.6 0.8 fusion.4
  1.4 1.9 %collective-permute-start.1 = (bf16[2,2048]{1,0:T(2,128)(2,1)S(1)}, bf16[2,2048]{1,0:T(2,128)(2,1)S(1)}, u32[]{:S(2)}, u32[]{:S(2)}) collective-permute-start(bf16[2,2048]{1,0:T(2,128)(2,1)S(1)} %get-tuple-element.7), channel_id=1, source_target_pairs={{0,4},{4,8},{8,12},{12,16},{16,20},{20,24},{24,28},{28,32},{32,36}... | collective-permute-start | bytes 24584 | tf_op jit(solution)/shard_map/ppermute | solution.py:203
  3.4 0.8 fusion.5
  4.2 3.9 %collective-permute-start.2 = (bf16[2,2048]{1,0:T(2,128)(2,1)S(1)}, bf16[2,2048]{1,0:T(2,128)(2,1)S(1)}, u32[]{:S(2)}, u32[]{:S(2)}) collective-permute-start(bf16[2,2048]{1,0:T(2,128)(2,1)S(1)} %get-tuple-element.9), channel_id=1, source_target_pairs={{0,4},{4,8},{8,12},{12,16},{16,20},{20,24},{24,28},{28,32},{32,36}... | collective-permute-start | bytes 24584 | tf_op jit(solution)/shard_map/ppermute | solution.py:203
  8.1 1.0 fusion.7
  9.1 0.0 copy-start.1
  9.1 0.0 copy-start.2
  9.2 4.8 %multiply_convert_fusion.2 = bf16[254,2048]{1,0:T(8,128)(2,1)S(1)} fusion(bf16[256,2048]{1,0:T(8,128)(2,1)} %param.15, f32[2048]{0:T(1024)S(1)} %bitcast.21, f32[2048]{0:T(1024)S(1)} %bitcast.23, f32[2048]{0:T(1024)S(1)} %bitcast.25, bf16[256,2048]{1,0:T(8,128)(2,1)} %param.14, f32[2048]{0:T(1024)S(1)} %bitcast.27, f32[2048]{0:T(1024)S(1)} %bitcast.29, ...), kind=kLoop, calls=%fused_computation.4 | loop fusion | flops 9363456 | bytes 7331840 | tf_op jit(solution)/shard_map/convert_element_type | solution.py:239
  13.9 0.1 slice.222
  14.1 1.9 %collective-permute-start = (bf16[127,2048]{1,0:T(8,128)(2,1)S(1)}, bf16[127,2048]{1,0:T(8,128)(2,1)S(1)}, u32[]{:S(2)}, u32[]{:S(2)}) collective-permute-start(bf16[127,2048]{1,0:T(8,128)(2,1)S(1)} %slice.222), channel_id=1, source_target_pairs={{0,4},{4,8},{8,12},{12,16},{16,20},{20,24},{24,28},{28,32},{32,36}... | collective-permute-start | bytes 1560584 | tf_op jit(solution)/shard_map/ppermute | solution.py:203
  16.0 0.0 copy-done.1
  16.0 3.9 %collective-permute-start.3 = (bf16[2,2048]{1,0:T(2,128)(2,1)S(1)}, bf16[2,2048]{1,0:T(2,128)(2,1)S(1)}, u32[]{:S(2)}, u32[]{:S(2)}) collective-permute-start(bf16[2,2048]{1,0:T(2,128)(2,1)S(1)} %slice.200), channel_id=1, source_target_pairs={{0,4},{4,8},{8,12},{12,16},{16,20},{20,24},{24,28},{28,32},{32,36}... | collective-permute-start | bytes 24584 | tf_op jit(solution)/shard_map/ppermute | solution.py:203
  20.0 0.0 copy-done.2
  20.0 1.9 %collective-permute-start.4 = (bf16[2,2048]{1,0:T(2,128)(2,1)S(1)}, bf16[2,2048]{1,0:T(2,128)(2,1)S(1)}, u32[]{:S(2)}, u32[]{:S(2)}) collective-permute-start(bf16[2,2048]{1,0:T(2,128)(2,1)S(1)} %slice.206), channel_id=1, source_target_pairs={{0,4},{4,8},{8,12},{12,16},{16,20},{20,24},{24,28},{28,32},{32,36}... | collective-permute-start | bytes 24584 | tf_op jit(solution)/shard_map/ppermute | solution.py:203
  21.9 0.0 collective-permute-done.1
  21.9 0.0 collective-permute-done.2
  22.0 0.1 multiply_convert_fusion.3
  22.0 4.7 %collective-permute-done.3 = bf16[2,2048]{1,0:T(2,128)(2,1)S(1)} collective-permute-done((bf16[2,2048]{1,0:T(2,128)(2,1)S(1)}, bf16[2,2048]{1,0:T(2,128)(2,1)S(1)}, u32[]{:S(2)}, u32[]{:S(2)}) %collective-permute-start.3) | collective-permute-done | bytes 8224 | tf_op jit(solution)/shard_map/ppermute | solution.py:203
  26.8 2.0 %multiply_add_fusion.1.gate_ref = f32[256,2048]{1,0:T(8,128)} fusion(bf16[256,2048]{1,0:T(8,128)(2,1)S(1)} %copy-done.1, bf16[2,2048]{1,0:T(2,128)(2,1)S(1)} %collective-permute-done.3, f32[2048]{0:T(1024)S(1)} %bitcast.37, f32[2048]{0:T(1024)S(1)} %bitcast.38, f32[2048]{0:T(1024)S(1)} %bitcast.36), kind=kLoop, calls=%fused_computation.3 | loop fusion | flops 7340032 | bytes 3178496 | tf_op jit(solution)/shard_map/add | solution.py:207
  28.8 0.0 collective-permute-done
  28.8 1.8 %pad_maximum_fusion.ext_ref = bf16[384,2048]{1,0:T(8,128)(2,1)} fusion(bf16[254,2048]{1,0:T(8,128)(2,1)S(1)} %multiply_convert_fusion.2, bf16[2,2048]{1,0:T(2,128)(2,1)S(1)} %multiply_convert_fusion.3, bf16[127,2048]{1,0:T(8,128)(2,1)S(1)} %collective-permute-done, bf16[384]{0:T(512)(128)(2,1)S(1)} %pad.8.clone), kind=kLoop, calls=%fused_computation.5 | loop fusion | flops 6291456 | bytes 3142400 | tf_op jit(solution)/shard_map/concatenate | solution.py:250
  30.5 0.0 copy-start
  30.5 0.0 copy-start.6
  30.5 32.4 %shard_map.140 = (bf16[256,2048]{1,0:T(8,128)(2,1)}, f32[256,128]{1,0:T(8,128)}) custom-call(bf16[384,2048]{1,0:T(8,128)(2,1)} %pad_maximum_fusion.ext_ref, f32[128,2048]{1,0:T(8,128)} %f_ref.1, f32[1,2048]{1,0:T(1,128)} %bitcast.45, f32[256,2048]{1,0:T(8,128)} %multiply_add_fusion.1.gate_ref), custom_call_target="tpu_custom_call" | custom-call | tf_op jit(solution)/shard_map/pallas_call | solution.py:56
  62.9 1.0 reduce_sum.9
  64.0 1.6 collective-permute-start.5
  65.6 2.7 %collective-permute-start.6 = (f32[256]{0:T(256)S(1)}, f32[256]{0:T(256)S(1)}, u32[]{:S(2)}, u32[]{:S(2)}) collective-permute-start(f32[256]{0:T(256)S(1)} %reduce_sum.9), channel_id=1, source_target_pairs={{0,2},{1,3},{2,0},{3,1},{4,6},{5,7},{6,4},{7,5},{8,10},{9,11},{10,... | collective-permute-start | bytes 3080 | tf_op jit(solution)/shard_map/ppermute | solution.py:258
  68.3 1.4 collective-permute-start.7
  69.7 0.0 copy-done
  69.7 0.7 negate_exponential_fusion.e_ref
  70.4 0.0 collective-permute-done.5
  70.4 0.2 collective-permute-done.6
  70.6 1.2 collective-permute-done.7
  71.9 0.0 copy-done.6
  71.9 1.5 multiply_convert_fusion.1
  73.4 1.9 %collective-permute-start.8 = (bf16[2,2048]{1,0:T(2,128)(2,1)S(1)}, bf16[2,2048]{1,0:T(2,128)(2,1)S(1)}, u32[]{:S(2)}, u32[]{:S(2)}) collective-permute-start(bf16[2,2048]{1,0:T(2,128)(2,1)S(1)} %slice.227), channel_id=1, source_target_pairs={{0,4},{4,8},{8,12},{12,16},{16,20},{20,24},{24,28},{28,32},{32,36}... | collective-permute-start | bytes 24584 | tf_op jit(solution)/shard_map/ppermute | solution.py:203
  75.3 0.0 copy-done.5
  75.3 0.1 fusion.6
  75.4 0.0 collective-permute-done.4
  75.4 5.1 %collective-permute-done.8 = bf16[2,2048]{1,0:T(2,128)(2,1)S(1)} collective-permute-done((bf16[2,2048]{1,0:T(2,128)(2,1)S(1)}, bf16[2,2048]{1,0:T(2,128)(2,1)S(1)}, u32[]{:S(2)}, u32[]{:S(2)}) %collective-permute-start.8) | collective-permute-done | bytes 8224 | tf_op jit(solution)/shard_map/ppermute | solution.py:203
  80.5 2.5 %multiply_convert_fusion.p_ref = bf16[256,2048]{1,0:T(8,128)(2,1)} fusion(bf16[256,2048]{1,0:T(8,128)(2,1)S(1)} %multiply_convert_fusion.1, bf16[256,2048]{1,0:T(8,128)(2,1)S(1)} %copy-done.2, bf16[2,2048]{1,0:T(2,128)(2,1)S(1)} %collective-permute-done.8, bf16[2,2048]{1,0:T(2,128)(2,1)S(1)} %collective-permute-done.4, f32[2048]{0:T(1024)S(1)} %bitcast.39, ...), kind=kLoop, calls=%fused_computation.1 | loop fusion | flops 15728640 | bytes 3211264 | tf_op jit(solution)/shard_map/convert_element_type | solution.py:269
  83.0 4.8 %shard_map.141 = f32[16,2048]{1,0:T(8,128)} custom-call(bf16[256,2048]{1,0:T(8,128)(2,1)} %multiply_convert_fusion.p_ref, f32[16,2048]{1,0:T(8,128)} %negate_exponential_fusion.e_ref), custom_call_target="tpu_custom_call" | custom-call | tf_op jit(solution)/shard_map/pallas_call | solution.py:120
  87.8 1.9 %collective-permute-start.9 = (f32[16,2048]{1,0:T(8,128)}, f32[16,2048]{1,0:T(8,128)S(1)}, u32[]{:S(2)}, u32[]{:S(2)}) collective-permute-start(f32[16,2048]{1,0:T(8,128)} %shard_map.141), channel_id=1, source_target_pairs={{0,4},{4,8},{8,12},{12,16},{16,20},{20,24},{24,28},{28,32},{32,36}... | collective-permute-start | bytes 393224 | tf_op jit(solution)/shard_map/ppermute | solution.py:203
  89.7 6.7 %collective-permute-done.9 = f32[16,2048]{1,0:T(8,128)S(1)} collective-permute-done((f32[16,2048]{1,0:T(8,128)}, f32[16,2048]{1,0:T(8,128)S(1)}, u32[]{:S(2)}, u32[]{:S(2)}) %collective-permute-start.9) | collective-permute-done | bytes 131104 | tf_op jit(solution)/shard_map/ppermute | solution.py:203
  96.4 1.9 %collective-permute-start.10 = (f32[16,2048]{1,0:T(8,128)S(1)}, f32[16,2048]{1,0:T(8,128)S(1)}, u32[]{:S(2)}, u32[]{:S(2)}) collective-permute-start(f32[16,2048]{1,0:T(8,128)S(1)} %collective-permute-done.9), channel_id=1, source_target_pairs={{0,4},{4,8},{8,12},{12,16},{16,20},{20,24},{24,28},{28,32},{32,36}... | collective-permute-start | bytes 393224 | tf_op jit(solution)/shard_map/ppermute | solution.py:203
  98.3 6.5 %collective-permute-done.10 = f32[16,2048]{1,0:T(8,128)S(1)} collective-permute-done((f32[16,2048]{1,0:T(8,128)S(1)}, f32[16,2048]{1,0:T(8,128)S(1)}, u32[]{:S(2)}, u32[]{:S(2)}) %collective-permute-start.10) | collective-permute-done | bytes 131104 | tf_op jit(solution)/shard_map/ppermute | solution.py:203
  104.8 1.9 %collective-permute-start.11 = (f32[16,2048]{1,0:T(8,128)S(1)}, f32[16,2048]{1,0:T(8,128)S(1)}, u32[]{:S(2)}, u32[]{:S(2)}) collective-permute-start(f32[16,2048]{1,0:T(8,128)S(1)} %multiply_add_fusion.7), channel_id=1, source_target_pairs={{0,8},{4,12},{8,16},{12,20},{16,24},{20,28},{24,32},{28,36},{32,40... | collective-permute-start | bytes 393224 | tf_op jit(solution)/shard_map/ppermute | solution.py:203
  106.7 7.9 %collective-permute-done.11 = f32[16,2048]{1,0:T(8,128)S(1)} collective-permute-done((f32[16,2048]{1,0:T(8,128)S(1)}, f32[16,2048]{1,0:T(8,128)S(1)}, u32[]{:S(2)}, u32[]{:S(2)}) %collective-permute-start.11) | collective-permute-done | bytes 131104 | tf_op jit(solution)/shard_map/ppermute | solution.py:203
  114.6 1.9 %collective-permute-start.12 = (f32[16,2048]{1,0:T(8,128)S(1)}, f32[16,2048]{1,0:T(8,128)S(1)}, u32[]{:S(2)}, u32[]{:S(2)}) collective-permute-start(f32[16,2048]{1,0:T(8,128)S(1)} %multiply_add_fusion.6), channel_id=1, source_target_pairs={{0,16},{4,20},{8,24},{12,28},{16,32},{20,36},{24,40},{28,44},{32,4... | collective-permute-start | bytes 393224 | tf_op jit(solution)/shard_map/ppermute | solution.py:203
  116.5 8.7 %collective-permute-done.12 = f32[16,2048]{1,0:T(8,128)S(1)} collective-permute-done((f32[16,2048]{1,0:T(8,128)S(1)}, f32[16,2048]{1,0:T(8,128)S(1)}, u32[]{:S(2)}, u32[]{:S(2)}) %collective-permute-start.12) | collective-permute-done | bytes 131104 | tf_op jit(solution)/shard_map/ppermute | solution.py:203
  125.3 0.0 copy-start.4
  125.3 2.1 %collective-permute-start.13 = (f32[16,2048]{1,0:T(8,128)S(1)}, f32[16,2048]{1,0:T(8,128)S(1)}, u32[]{:S(2)}, u32[]{:S(2)}) collective-permute-start(f32[16,2048]{1,0:T(8,128)S(1)} %multiply_add_fusion.5), channel_id=1, source_target_pairs={{0,32},{4,36},{8,40},{12,44},{16,48},{20,52},{24,56},{28,60},{32,6... | collective-permute-start | bytes 393224 | tf_op jit(solution)/shard_map/ppermute | solution.py:203
  127.3 10.6 %collective-permute-done.13 = f32[16,2048]{1,0:T(8,128)S(1)} collective-permute-done((f32[16,2048]{1,0:T(8,128)S(1)}, f32[16,2048]{1,0:T(8,128)S(1)}, u32[]{:S(2)}, u32[]{:S(2)}) %collective-permute-start.13) | collective-permute-done | bytes 131104 | tf_op jit(solution)/shard_map/ppermute | solution.py:203
  138.0 2.8 %collective-permute-start.14 = (f32[16,2048]{1,0:T(8,128)S(1)}, f32[16,2048]{1,0:T(8,128)S(1)}, u32[]{:S(2)}, u32[]{:S(2)}) collective-permute-start(f32[16,2048]{1,0:T(8,128)S(1)} %multiply_add_fusion.4), channel_id=1, source_target_pairs={{0,64},{4,68},{8,72},{12,76},{16,80},{20,84},{24,88},{28,92},{32,9... | collective-permute-start | bytes 393224 | tf_op jit(solution)/shard_map/ppermute | solution.py:203
  140.8 0.0 copy-done.3
  140.8 1.9 %collective-permute-start.16 = (bf16[2,2048]{1,0:T(2,128)(2,1)S(1)}, bf16[2,2048]{1,0:T(2,128)(2,1)S(1)}, u32[]{:S(2)}, u32[]{:S(2)}) collective-permute-start(bf16[2,2048]{1,0:T(2,128)(2,1)S(1)} %slice.218), channel_id=1, source_target_pairs={{0,4},{4,8},{8,12},{12,16},{16,20},{20,24},{24,28},{28,32},{32,36}... | collective-permute-start | bytes 24584 | tf_op jit(solution)/shard_map/ppermute | solution.py:203
  142.7 2.1 %collective-permute-done.14 = f32[16,2048]{1,0:T(8,128)S(1)} collective-permute-done((f32[16,2048]{1,0:T(8,128)S(1)}, f32[16,2048]{1,0:T(8,128)S(1)}, u32[]{:S(2)}, u32[]{:S(2)}) %collective-permute-start.14) | collective-permute-done | bytes 131104 | tf_op jit(solution)/shard_map/ppermute | solution.py:203
  144.9 1.3 collective-permute-start.15
  146.2 1.7 %collective-permute-done.16 = bf16[2,2048]{1,0:T(2,128)(2,1)S(1)} collective-permute-done((bf16[2,2048]{1,0:T(2,128)(2,1)S(1)}, bf16[2,2048]{1,0:T(2,128)(2,1)S(1)}, u32[]{:S(2)}, u32[]{:S(2)}) %collective-permute-start.16) | collective-permute-done | bytes 8224 | tf_op jit(solution)/shard_map/ppermute | solution.py:203
  147.9 2.0 %multiply_add_fusion.gate_ref = f32[256,2048]{1,0:T(8,128)} fusion(bf16[256,2048]{1,0:T(8,128)(2,1)S(1)} %copy-done.3, bf16[2,2048]{1,0:T(2,128)(2,1)S(1)} %collective-permute-done.16, f32[2048]{0:T(1024)S(1)} %bitcast.34, f32[2048]{0:T(1024)S(1)} %bitcast.35, f32[2048]{0:T(1024)S(1)} %bitcast.33), kind=kLoop, calls=%fused_computation | loop fusion | flops 7340032 | bytes 3178496 | tf_op jit(solution)/shard_map/add | solution.py:207
  149.9 3.4 %collective-permute-done.15 = f32[16,2048]{1,0:T(8,128)S(1)} collective-permute-done((f32[16,2048]{1,0:T(8,128)S(1)}, f32[16,2048]{1,0:T(8,128)S(1)}, u32[]{:S(2)}, u32[]{:S(2)}) %collective-permute-start.15) | collective-permute-done | bytes 131104 | tf_op jit(solution)/shard_map/ppermute | solution.py:203
  153.3 0.0 copy-done.4
  153.3 0.8 multiply_add_fusion.2
  154.1 10.5 %shard_map.142 = bf16[256,2048]{1,0:T(8,128)(2,1)} custom-call(bf16[256,2048]{1,0:T(8,128)(2,1)} %multiply_convert_fusion.p_ref, f32[16,2048]{1,0:T(8,128)} %negate_exponential_fusion.e_ref, f32[16,2048]{1,0:T(8,128)} %get-tuple-element.11.w_ref, f32[16,2048]{1,0:T(8,128)} %get-tuple-element.10.s_ref, f32[1,2048]{1,0:T(1,128)} %bitcast.46, ...), custom_call_target="tpu_custom_call" | custom-call | tf_op jit(solution)/shard_map/pallas_call | solution.py:180
  (13 shorter events, 0.2 us)
Async XLA Ops:
  1.4 20.5 %collective-permute-start.1 = (bf16[2,2048]{1,0:T(2,128)(2,1)S(1)}, bf16[2,2048]{1,0:T(2,128)(2,1)S(1)}, u32[]{:S(2)}, u32[]{:S(2)}) collective-permute-start(bf16[2,2048]{1,0:T(2,128)(2,1)S(1)} %get-tuple-element.7), channel_id=1, source_target_pairs={{0,4},{4,8},{8,12},{12,16},{16,20},{20,24},{24,28},{28,32},{32,36}... | collective-permute-start | bytes 24584 | tf_op jit(solution)/shard_map/ppermute | solution.py:203
  4.2 17.8 %collective-permute-start.2 = (bf16[2,2048]{1,0:T(2,128)(2,1)S(1)}, bf16[2,2048]{1,0:T(2,128)(2,1)S(1)}, u32[]{:S(2)}, u32[]{:S(2)}) collective-permute-start(bf16[2,2048]{1,0:T(2,128)(2,1)S(1)} %get-tuple-element.9), channel_id=1, source_target_pairs={{0,4},{4,8},{8,12},{12,16},{16,20},{20,24},{24,28},{28,32},{32,36}... | collective-permute-start | bytes 24584 | tf_op jit(solution)/shard_map/ppermute | solution.py:203
  9.1 6.9 %copy-start.1 = (bf16[256,2048]{1,0:T(8,128)(2,1)S(1)}, bf16[256,2048]{1,0:T(8,128)(2,1)}, u32[]{:S(2)}) copy-start(bf16[256,2048]{1,0:T(8,128)(2,1)} %param.13) | copy-start | bytes 3145732
  9.1 10.8 %copy-start.2 = (bf16[256,2048]{1,0:T(8,128)(2,1)S(1)}, bf16[256,2048]{1,0:T(8,128)(2,1)}, u32[]{:S(2)}) copy-start(bf16[256,2048]{1,0:T(8,128)(2,1)} %param.21) | copy-start | bytes 3145732
  14.1 14.7 %collective-permute-start = (bf16[127,2048]{1,0:T(8,128)(2,1)S(1)}, bf16[127,2048]{1,0:T(8,128)(2,1)S(1)}, u32[]{:S(2)}, u32[]{:S(2)}) collective-permute-start(bf16[127,2048]{1,0:T(8,128)(2,1)S(1)} %slice.222), channel_id=1, source_target_pairs={{0,4},{4,8},{8,12},{12,16},{16,20},{20,24},{24,28},{28,32},{32,36}... | collective-permute-start | bytes 1560584 | tf_op jit(solution)/shard_map/ppermute | solution.py:203
  16.0 10.7 %collective-permute-start.3 = (bf16[2,2048]{1,0:T(2,128)(2,1)S(1)}, bf16[2,2048]{1,0:T(2,128)(2,1)S(1)}, u32[]{:S(2)}, u32[]{:S(2)}) collective-permute-start(bf16[2,2048]{1,0:T(2,128)(2,1)S(1)} %slice.200), channel_id=1, source_target_pairs={{0,4},{4,8},{8,12},{12,16},{16,20},{20,24},{24,28},{28,32},{32,36}... | collective-permute-start | bytes 24584 | tf_op jit(solution)/shard_map/ppermute | solution.py:203
  20.0 55.4 %collective-permute-start.4 = (bf16[2,2048]{1,0:T(2,128)(2,1)S(1)}, bf16[2,2048]{1,0:T(2,128)(2,1)S(1)}, u32[]{:S(2)}, u32[]{:S(2)}) collective-permute-start(bf16[2,2048]{1,0:T(2,128)(2,1)S(1)} %slice.206), channel_id=1, source_target_pairs={{0,4},{4,8},{8,12},{12,16},{16,20},{20,24},{24,28},{28,32},{32,36}... | collective-permute-start | bytes 24584 | tf_op jit(solution)/shard_map/ppermute | solution.py:203
  30.5 39.2 %copy-start = (f32[16,2048]{1,0:T(8,128)S(1)}, f32[16,2048]{1,0:T(8,128)}, u32[]{:S(2)}) copy-start(f32[16,2048]{1,0:T(8,128)} %param.23) | copy-start | bytes 393220
  30.5 41.3 %copy-start.6 = (f32[2048]{0:T(1024)S(1)}, f32[2048]{0:T(1024)}, u32[]{:S(2)}) copy-start(f32[2048]{0:T(1024)} %param.19) | copy-start | bytes 24580
  62.9 12.4 %copy-start.5 = (f32[3,3,2048]{2,1,0:T(4,128)S(1)}, f32[3,3,2048]{2,1,0:T(4,128)}, u32[]{:S(2)}) copy-start(f32[3,3,2048]{2,1,0:T(4,128)} %param.22) | copy-start | bytes 221188
  64.0 6.4 %collective-permute-start.5 = (f32[256]{0:T(256)S(1)}, f32[256]{0:T(256)S(1)}, u32[]{:S(2)}, u32[]{:S(2)}) collective-permute-start(f32[256]{0:T(256)S(1)} %reduce_sum.9), channel_id=1, source_target_pairs={{0,1},{1,2},{2,3},{3,0},{4,5},{5,6},{6,7},{7,4},{8,9},{9,10},{10,1... | collective-permute-start | bytes 3080 | tf_op jit(solution)/shard_map/ppermute | solution.py:258
  65.6 5.1 %collective-permute-start.6 = (f32[256]{0:T(256)S(1)}, f32[256]{0:T(256)S(1)}, u32[]{:S(2)}, u32[]{:S(2)}) collective-permute-start(f32[256]{0:T(256)S(1)} %reduce_sum.9), channel_id=1, source_target_pairs={{0,2},{1,3},{2,0},{3,1},{4,6},{5,7},{6,4},{7,5},{8,10},{9,11},{10,... | collective-permute-start | bytes 3080 | tf_op jit(solution)/shard_map/ppermute | solution.py:258
  68.3 3.6 %collective-permute-start.7 = (f32[256]{0:T(256)S(1)}, f32[256]{0:T(256)S(1)}, u32[]{:S(2)}, u32[]{:S(2)}) collective-permute-start(f32[256]{0:T(256)S(1)} %reduce_sum.9), channel_id=1, source_target_pairs={{0,3},{1,0},{2,1},{3,2},{4,7},{5,4},{6,5},{7,6},{8,11},{9,8},{10,9... | collective-permute-start | bytes 3080 | tf_op jit(solution)/shard_map/ppermute | solution.py:258
  73.4 7.1 %collective-permute-start.8 = (bf16[2,2048]{1,0:T(2,128)(2,1)S(1)}, bf16[2,2048]{1,0:T(2,128)(2,1)S(1)}, u32[]{:S(2)}, u32[]{:S(2)}) collective-permute-start(bf16[2,2048]{1,0:T(2,128)(2,1)S(1)} %slice.227), channel_id=1, source_target_pairs={{0,4},{4,8},{8,12},{12,16},{16,20},{20,24},{24,28},{28,32},{32,36}... | collective-permute-start | bytes 24584 | tf_op jit(solution)/shard_map/ppermute | solution.py:203
  83.0 57.8 %copy-start.3 = (bf16[256,2048]{1,0:T(8,128)(2,1)S(1)}, bf16[256,2048]{1,0:T(8,128)(2,1)}, u32[]{:S(2)}) copy-start(bf16[256,2048]{1,0:T(8,128)(2,1)} %param.20) | copy-start | bytes 3145732
  87.8 8.6 %collective-permute-start.9 = (f32[16,2048]{1,0:T(8,128)}, f32[16,2048]{1,0:T(8,128)S(1)}, u32[]{:S(2)}, u32[]{:S(2)}) collective-permute-start(f32[16,2048]{1,0:T(8,128)} %shard_map.141), channel_id=1, source_target_pairs={{0,4},{4,8},{8,12},{12,16},{16,20},{20,24},{24,28},{28,32},{32,36}... | collective-permute-start | bytes 393224 | tf_op jit(solution)/shard_map/ppermute | solution.py:203
  96.4 8.4 %collective-permute-start.10 = (f32[16,2048]{1,0:T(8,128)S(1)}, f32[16,2048]{1,0:T(8,128)S(1)}, u32[]{:S(2)}, u32[]{:S(2)}) collective-permute-start(f32[16,2048]{1,0:T(8,128)S(1)} %collective-permute-done.9), channel_id=1, source_target_pairs={{0,4},{4,8},{8,12},{12,16},{16,20},{20,24},{24,28},{28,32},{32,36}... | collective-permute-start | bytes 393224 | tf_op jit(solution)/shard_map/ppermute | solution.py:203
  104.8 9.8 %collective-permute-start.11 = (f32[16,2048]{1,0:T(8,128)S(1)}, f32[16,2048]{1,0:T(8,128)S(1)}, u32[]{:S(2)}, u32[]{:S(2)}) collective-permute-start(f32[16,2048]{1,0:T(8,128)S(1)} %multiply_add_fusion.7), channel_id=1, source_target_pairs={{0,8},{4,12},{8,16},{12,20},{16,24},{20,28},{24,32},{28,36},{32,40... | collective-permute-start | bytes 393224 | tf_op jit(solution)/shard_map/ppermute | solution.py:203
  114.6 10.6 %collective-permute-start.12 = (f32[16,2048]{1,0:T(8,128)S(1)}, f32[16,2048]{1,0:T(8,128)S(1)}, u32[]{:S(2)}, u32[]{:S(2)}) collective-permute-start(f32[16,2048]{1,0:T(8,128)S(1)} %multiply_add_fusion.6), channel_id=1, source_target_pairs={{0,16},{4,20},{8,24},{12,28},{16,32},{20,36},{24,40},{28,44},{32,4... | collective-permute-start | bytes 393224 | tf_op jit(solution)/shard_map/ppermute | solution.py:203
  125.3 28.0 %copy-start.4 = (f32[16,2048]{1,0:T(8,128)S(1)}, f32[16,2048]{1,0:T(8,128)}, u32[]{:S(2)}) copy-start(f32[16,2048]{1,0:T(8,128)} %param.24) | copy-start | bytes 393220
  125.3 12.7 %collective-permute-start.13 = (f32[16,2048]{1,0:T(8,128)S(1)}, f32[16,2048]{1,0:T(8,128)S(1)}, u32[]{:S(2)}, u32[]{:S(2)}) collective-permute-start(f32[16,2048]{1,0:T(8,128)S(1)} %multiply_add_fusion.5), channel_id=1, source_target_pairs={{0,32},{4,36},{8,40},{12,44},{16,48},{20,52},{24,56},{28,60},{32,6... | collective-permute-start | bytes 393224 | tf_op jit(solution)/shard_map/ppermute | solution.py:203
  138.0 6.9 %collective-permute-start.14 = (f32[16,2048]{1,0:T(8,128)S(1)}, f32[16,2048]{1,0:T(8,128)S(1)}, u32[]{:S(2)}, u32[]{:S(2)}) collective-permute-start(f32[16,2048]{1,0:T(8,128)S(1)} %multiply_add_fusion.4), channel_id=1, source_target_pairs={{0,64},{4,68},{8,72},{12,76},{16,80},{20,84},{24,88},{28,92},{32,9... | collective-permute-start | bytes 393224 | tf_op jit(solution)/shard_map/ppermute | solution.py:203
  140.8 7.1 %collective-permute-start.16 = (bf16[2,2048]{1,0:T(2,128)(2,1)S(1)}, bf16[2,2048]{1,0:T(2,128)(2,1)S(1)}, u32[]{:S(2)}, u32[]{:S(2)}) collective-permute-start(bf16[2,2048]{1,0:T(2,128)(2,1)S(1)} %slice.218), channel_id=1, source_target_pairs={{0,4},{4,8},{8,12},{12,16},{16,20},{20,24},{24,28},{28,32},{32,36}... | collective-permute-start | bytes 24584 | tf_op jit(solution)/shard_map/ppermute | solution.py:203
  144.9 8.4 %collective-permute-start.15 = (f32[16,2048]{1,0:T(8,128)S(1)}, f32[16,2048]{1,0:T(8,128)S(1)}, u32[]{:S(2)}, u32[]{:S(2)}) collective-permute-start(f32[16,2048]{1,0:T(8,128)S(1)} %multiply_add_fusion.3), channel_id=1, source_target_pairs={{0,128},{4,132},{8,136},{12,140},{16,144},{20,148},{24,152},{28,15... | collective-permute-start | bytes 393224 | tf_op jit(solution)/shard_map/ppermute | solution.py:203

commit v3 on v2

--- a/solution.py
+++ b/solution.py
@@ -1,3 +1,4 @@
+import functools
 import jax
 import jax.numpy as jnp
 from jax import lax
@@ -195,6 +196,67 @@
             pltpu.VMEM((GROUP, rows * 8, LANE), jnp.float32),
         ],
     )(product, decay, weight, start, skip, gate_feat)
+
+
+def scan_kernel(count, rows, f_ref, r_ref, out_ref, send_ref, recv_ref, send_sem, recv_sem):
+    me = lax.axis_index("ctx")
+    plan = [(1, False)]
+    span = 1
+    while span < count:
+        plan.append((span, True))
+        span *= 2
+    out_ref[...] = jnp.zeros_like(out_ref)
+    for k, (shift, combine) in enumerate(plan):
+        if k == 0:
+            source = f_ref
+        else:
+            send_ref[k] = out_ref[...]
+            source = send_ref.at[k]
+        copy = pltpu.make_async_remote_copy(
+            src_ref=source,
+            dst_ref=recv_ref.at[k],
+            send_sem=send_sem.at[k],
+            recv_sem=recv_sem.at[k],
+            device_id={"ctx": me + shift},
+            device_id_type=pl.DeviceIdType.MESH,
+        )
+
+        @pl.when(me + shift < count)
+        def _():
+            copy.start()
+
+        @pl.when(me >= shift)
+        def _():
+            copy.wait_recv()
+            if combine:
+                factor = jnp.exp(r_ref[...] * (-1.0 * rows * shift))
+                out_ref[...] = out_ref[...] + factor * recv_ref[k]
+            else:
+                out_ref[...] = recv_ref[k]
+
+        @pl.when(me + shift < count)
+        def _():
+            copy.wait_send()
+
+
+def scan_call(final_state, decay_rates, count, rows):
+    steps = 1
+    while (1 << (steps - 1)) < count:
+        steps += 1
+    shape = final_state.shape
+    return pl.pallas_call(
+        functools.partial(scan_kernel, count, rows),
+        in_specs=[pl.BlockSpec(memory_space=pltpu.VMEM)] * 2,
+        out_specs=pl.BlockSpec(memory_space=pltpu.VMEM),
+        out_shape=jax.ShapeDtypeStruct(shape, jnp.float32),
+        scratch_shapes=[
+            pltpu.VMEM((steps,) + shape, jnp.float32),
+            pltpu.VMEM((steps,) + shape, jnp.float32),
+            pltpu.SemaphoreType.DMA((steps,)),
+            pltpu.SemaphoreType.DMA((steps,)),
+        ],
+        compiler_params=pltpu.CompilerParams(has_side_effects=True),
+    )(final_state, decay_rates)
 
 
 def passed_along(value, axis, steps):
@@ -270,12 +332,7 @@
     mode_weight = residues * jnp.sqrt(-jnp.expm1(-2.0 * decay_rates))
     step_decay = jnp.exp(-decay_rates)
     final_state = modal_end_call(product_long, step_decay)
-    incoming = passed_along(final_state, "ctx", 1)
-    span = 1
-    while span < lax.axis_size("ctx"):
-        earlier = passed_along(incoming, "ctx", span)
-        incoming = incoming + jnp.exp(-decay_rates * (row_count * span)) * earlier
-        span *= 2
+    incoming = scan_call(final_state, decay_rates, lax.axis_size("ctx"), row_count)
     mixed_long = modal_out_call(
         product_long, step_decay, mode_weight, incoming, skip_long[None, :], gate_feat_long
     )

time: 165 us -> 146 us (0.88)
  the two profiles are of different devices: /device:TPU:16 before, /device:TPU:24 now
where the time goes in v3:
time: 146 us
  Pallas kernels  94.9 us (65%)
  starting transfers between devices  25.2 us (17%)
  other arithmetic  16.4 us (11%)
  waiting for transfers between devices  5.19 us (4%)
  local copies, waits for them, and re-layouts  2.9 us (2%)
    pallas_call x1, Pallas kernels, scan_call(): pl.pallas_call(functools.partial(scan_kernel, count, rows), in_specs=[pl....  47.3 us
    pallas_call x1, Pallas kernels, medium_call(): pl.pallas_call(medium_kernel, grid=grid, in_specs=[pl.BlockSpec((span, bl...  32.4 us
    ppermute x7, starting transfers between devices, passed_along(): lax.ppermute(value, axis, [(source, source + steps) for source in range(f...  19.5 us
    pallas_call x1, Pallas kernels, modal_out_call(): pl.pallas_call(modal_out_kernel, grid=(width // block,), in_specs=[pl.Blo...  10.5 us
    ppermute x3, starting transfers between devices, body(): lax.ppermute(squares, 'ch', [(source, (source + shift) % ring) for source...  5.73 us
    convert_element_type x1, other arithmetic, body(): late_product = (short_filter(key_medium, short_medium[1]) * short_filter(...  4.77 us
    pallas_call x1, Pallas kernels, modal_end_call(): pl.pallas_call(modal_end_kernel, grid=(width // block,), in_specs=[pl.Blo...  4.71 us
    add x2, other arithmetic, short_filter(): weights[0] * extended[2:] + weights[1] * extended[1:-1]  4.06 us
  transfers between devices with their start and end apart: 10, of which 3 were waited for; matrix products, arithmetic and copies ran while one was open for 11% of the time, Pallas kernels for 22%

profile of v3, /device:TPU:24, one launch (start us, length us, event | category | flops | bytes accessed | tf_op | source)
XLA Modules:
  0.0 145.6 jit_solution(13438686473522512813)
XLA Ops:
  0.6 0.8 fusion.4
  1.4 1.9 %collective-permute-start.1 = (bf16[2,2048]{1,0:T(2,128)(2,1)S(1)}, bf16[2,2048]{1,0:T(2,128)(2,1)S(1)}, u32[]{:S(2)}, u32[]{:S(2)}) collective-permute-start(bf16[2,2048]{1,0:T(2,128)(2,1)S(1)} %get-tuple-element.7), channel_id=1, source_target_pairs={{0,4},{4,8},{8,12},{12,16},{16,20},{20,24},{24,28},{28,32},{32,36}... | collective-permute-start | bytes 24584 | tf_op jit(solution)/shard_map/ppermute | solution.py:265
  3.4 0.8 fusion.5
  4.2 3.9 %collective-permute-start.2 = (bf16[2,2048]{1,0:T(2,128)(2,1)S(1)}, bf16[2,2048]{1,0:T(2,128)(2,1)S(1)}, u32[]{:S(2)}, u32[]{:S(2)}) collective-permute-start(bf16[2,2048]{1,0:T(2,128)(2,1)S(1)} %get-tuple-element.9), channel_id=1, source_target_pairs={{0,4},{4,8},{8,12},{12,16},{16,20},{20,24},{24,28},{28,32},{32,36}... | collective-permute-start | bytes 24584 | tf_op jit(solution)/shard_map/ppermute | solution.py:265
  8.1 1.0 fusion.7
  9.1 0.0 copy-start
  9.1 0.0 copy-start.2
  9.2 0.0 copy-start.3
  9.2 0.0 copy-start.4
  9.2 0.0 copy-start.1
  9.2 4.8 %multiply_convert_fusion.2 = bf16[254,2048]{1,0:T(8,128)(2,1)S(1)} fusion(bf16[256,2048]{1,0:T(8,128)(2,1)} %param.15, f32[2048]{0:T(1024)S(1)} %bitcast.21, f32[2048]{0:T(1024)S(1)} %bitcast.23, f32[2048]{0:T(1024)S(1)} %bitcast.25, bf16[256,2048]{1,0:T(8,128)(2,1)} %param.14, f32[2048]{0:T(1024)S(1)} %bitcast.27, f32[2048]{0:T(1024)S(1)} %bitcast.29, ...), kind=kLoop, calls=%fused_computation.4 | loop fusion | flops 9363456 | bytes 7331840 | tf_op jit(solution)/shard_map/convert_element_type | solution.py:301
  14.0 0.1 slice.222
  14.1 1.9 %collective-permute-start = (bf16[127,2048]{1,0:T(8,128)(2,1)S(1)}, bf16[127,2048]{1,0:T(8,128)(2,1)S(1)}, u32[]{:S(2)}, u32[]{:S(2)}) collective-permute-start(bf16[127,2048]{1,0:T(8,128)(2,1)S(1)} %slice.222), channel_id=1, source_target_pairs={{0,4},{4,8},{8,12},{12,16},{16,20},{20,24},{24,28},{28,32},{32,36}... | collective-permute-start | bytes 1560584 | tf_op jit(solution)/shard_map/ppermute | solution.py:265
  16.0 0.0 copy-done
  16.1 3.9 %collective-permute-start.3 = (bf16[2,2048]{1,0:T(2,128)(2,1)S(1)}, bf16[2,2048]{1,0:T(2,128)(2,1)S(1)}, u32[]{:S(2)}, u32[]{:S(2)}) collective-permute-start(bf16[2,2048]{1,0:T(2,128)(2,1)S(1)} %slice.200), channel_id=1, source_target_pairs={{0,4},{4,8},{8,12},{12,16},{16,20},{20,24},{24,28},{28,32},{32,36}... | collective-permute-start | bytes 24584 | tf_op jit(solution)/shard_map/ppermute | solution.py:265
  20.0 0.0 copy-done.2
  20.0 1.9 %collective-permute-start.4 = (bf16[2,2048]{1,0:T(2,128)(2,1)S(1)}, bf16[2,2048]{1,0:T(2,128)(2,1)S(1)}, u32[]{:S(2)}, u32[]{:S(2)}) collective-permute-start(bf16[2,2048]{1,0:T(2,128)(2,1)S(1)} %slice.206), channel_id=1, source_target_pairs={{0,4},{4,8},{8,12},{12,16},{16,20},{20,24},{24,28},{28,32},{32,36}... | collective-permute-start | bytes 24584 | tf_op jit(solution)/shard_map/ppermute | solution.py:265
  22.0 0.0 copy-done.3
  22.0 0.0 copy-done.4
  22.0 0.8 sqrt_multiply_fusion
  22.8 0.0 copy-done.1
  22.8 0.0 collective-permute-done.1
  22.8 3.9 %collective-permute-start.9 = (bf16[2,2048]{1,0:T(2,128)(2,1)S(1)}, bf16[2,2048]{1,0:T(2,128)(2,1)S(1)}, u32[]{:S(2)}, u32[]{:S(2)}) collective-permute-start(bf16[2,2048]{1,0:T(2,128)(2,1)S(1)} %slice.218), channel_id=1, source_target_pairs={{0,4},{4,8},{8,12},{12,16},{16,20},{20,24},{24,28},{28,32},{32,36}... | collective-permute-start | bytes 24584 | tf_op jit(solution)/shard_map/ppermute | solution.py:265
  26.8 0.0 collective-permute-done.2
  26.8 0.1 multiply_convert_fusion.3
  26.8 0.0 collective-permute-done.3
  26.9 2.0 %multiply_add_fusion.1.gate_ref = f32[256,2048]{1,0:T(8,128)} fusion(bf16[256,2048]{1,0:T(8,128)(2,1)S(1)} %copy-done, bf16[2,2048]{1,0:T(2,128)(2,1)S(1)} %collective-permute-done.3, f32[2048]{0:T(1024)S(1)} %bitcast.34, f32[2048]{0:T(1024)S(1)} %bitcast.35, f32[2048]{0:T(1024)S(1)} %bitcast.33), kind=kLoop, calls=%fused_computation.3 | loop fusion | flops 7340032 | bytes 3178496 | tf_op jit(solution)/shard_map/add | solution.py:269
  28.9 0.0 collective-permute-done
  28.9 1.8 %pad_maximum_fusion.ext_ref = bf16[384,2048]{1,0:T(8,128)(2,1)} fusion(bf16[254,2048]{1,0:T(8,128)(2,1)S(1)} %multiply_convert_fusion.2, bf16[2,2048]{1,0:T(2,128)(2,1)S(1)} %multiply_convert_fusion.3, bf16[127,2048]{1,0:T(8,128)(2,1)S(1)} %collective-permute-done, bf16[384]{0:T(512)(128)(2,1)S(1)} %pad.8.clone), kind=kLoop, calls=%fused_computation.5 | loop fusion | flops 6291456 | bytes 3142400 | tf_op jit(solution)/shard_map/concatenate | solution.py:312
  30.7 0.0 copy-start.5
  30.7 0.0 copy-start.6
  30.7 32.4 %shard_map.140 = (bf16[256,2048]{1,0:T(8,128)(2,1)}, f32[256,128]{1,0:T(8,128)}) custom-call(bf16[384,2048]{1,0:T(8,128)(2,1)} %pad_maximum_fusion.ext_ref, f32[128,2048]{1,0:T(8,128)} %f_ref.1, f32[1,2048]{1,0:T(1,128)} %bitcast.45, f32[256,2048]{1,0:T(8,128)} %multiply_add_fusion.1.gate_ref), custom_call_target="tpu_custom_call" | custom-call | tf_op jit(solution)/shard_map/pallas_call | solution.py:57
  63.1 1.0 reduce_sum.9
  64.1 1.6 %collective-permute-start.5 = (f32[256]{0:T(256)S(1)}, f32[256]{0:T(256)S(1)}, u32[]{:S(2)}, u32[]{:S(2)}) collective-permute-start(f32[256]{0:T(256)S(1)} %reduce_sum.9), channel_id=1, source_target_pairs={{0,1},{1,2},{2,3},{3,0},{4,5},{5,6},{6,7},{7,4},{8,9},{9,10},{10,1... | collective-permute-start | bytes 3080 | tf_op jit(solution)/shard_map/ppermute | solution.py:320
  65.6 2.7 %collective-permute-start.6 = (f32[256]{0:T(256)S(1)}, f32[256]{0:T(256)S(1)}, u32[]{:S(2)}, u32[]{:S(2)}) collective-permute-start(f32[256]{0:T(256)S(1)} %reduce_sum.9), channel_id=1, source_target_pairs={{0,2},{1,3},{2,0},{3,1},{4,6},{5,7},{6,4},{7,5},{8,10},{9,11},{10,... | collective-permute-start | bytes 3080 | tf_op jit(solution)/shard_map/ppermute | solution.py:320
  68.4 1.4 collective-permute-start.7
  69.8 0.0 copy-done.5
  69.8 0.1 fusion.6
  69.9 0.0 collective-permute-done.5
  69.9 0.8 collective-permute-done.6
  70.7 1.2 collective-permute-done.7
  72.0 0.0 copy-done.6
  72.0 1.5 %multiply_convert_fusion.1 = bf16[256,2048]{1,0:T(8,128)(2,1)S(1)} fusion(bf16[256,2048]{1,0:T(8,128)(2,1)} %get-tuple-element.2, f32[256]{0:T(256)S(1)} %add_rsqrt_fusion, f32[2048]{0:T(1024)S(1)} %copy-done.6), kind=kLoop, calls=%fused_computation.2 | loop fusion | flops 2097152 | bytes 2106368 | tf_op jit(solution)/shard_map/convert_element_type | solution.py:324
  73.5 1.9 %collective-permute-start.8 = (bf16[2,2048]{1,0:T(2,128)(2,1)S(1)}, bf16[2,2048]{1,0:T(2,128)(2,1)S(1)}, u32[]{:S(2)}, u32[]{:S(2)}) collective-permute-start(bf16[2,2048]{1,0:T(2,128)(2,1)S(1)} %slice.227), channel_id=1, source_target_pairs={{0,4},{4,8},{8,12},{12,16},{16,20},{20,24},{24,28},{28,32},{32,36}... | collective-permute-start | bytes 24584 | tf_op jit(solution)/shard_map/ppermute | solution.py:265
  75.4 0.0 collective-permute-done.9
  75.4 2.0 %multiply_add_fusion.gate_ref = f32[256,2048]{1,0:T(8,128)} fusion(bf16[256,2048]{1,0:T(8,128)(2,1)S(1)} %copy-done.1, bf16[2,2048]{1,0:T(2,128)(2,1)S(1)} %collective-permute-done.9, f32[2048]{0:T(1024)S(1)} %bitcast.43, f32[2048]{0:T(1024)S(1)} %bitcast.44, f32[2048]{0:T(1024)S(1)} %bitcast.42), kind=kLoop, calls=%fused_computation | loop fusion | flops 7340032 | bytes 3178496 | tf_op jit(solution)/shard_map/add | solution.py:269
  77.4 0.0 collective-permute-done.4
  77.4 3.1 %collective-permute-done.8 = bf16[2,2048]{1,0:T(2,128)(2,1)S(1)} collective-permute-done((bf16[2,2048]{1,0:T(2,128)(2,1)S(1)}, bf16[2,2048]{1,0:T(2,128)(2,1)S(1)}, u32[]{:S(2)}, u32[]{:S(2)}) %collective-permute-start.8) | collective-permute-done | bytes 8224 | tf_op jit(solution)/shard_map/ppermute | solution.py:265
  80.6 2.5 %multiply_convert_fusion.p_ref = bf16[256,2048]{1,0:T(8,128)(2,1)} fusion(bf16[256,2048]{1,0:T(8,128)(2,1)S(1)} %multiply_convert_fusion.1, bf16[256,2048]{1,0:T(8,128)(2,1)S(1)} %copy-done.2, bf16[2,2048]{1,0:T(2,128)(2,1)S(1)} %collective-permute-done.8, bf16[2,2048]{1,0:T(2,128)(2,1)S(1)} %collective-permute-done.4, f32[2048]{0:T(1024)S(1)} %bitcast.36, ...), kind=kLoop, calls=%fused_computation.1 | loop fusion | flops 15728640 | bytes 3211264 | tf_op jit(solution)/shard_map/convert_element_type | solution.py:331
  83.0 4.7 %shard_map.141.f_ref = f32[16,2048]{1,0:T(8,128)} custom-call(bf16[256,2048]{1,0:T(8,128)(2,1)} %multiply_convert_fusion.p_ref, f32[16,2048]{1,0:T(8,128)} %get-tuple-element.11.e_ref), custom_call_target="tpu_custom_call" | custom-call | tf_op jit(solution)/shard_map/pallas_call | solution.py:121
  87.7 47.3 %shard_map.142.s_ref = f32[16,2048]{1,0:T(8,128)} custom-call(f32[16,2048]{1,0:T(8,128)} %shard_map.141.f_ref, f32[16,2048]{1,0:T(8,128)} %r_ref.1), custom_call_target="tpu_custom_call" | custom-call | tf_op jit(solution)/shard_map/pallas_call | solution.py:247
  135.1 10.5 %shard_map.143 = bf16[256,2048]{1,0:T(8,128)(2,1)} custom-call(bf16[256,2048]{1,0:T(8,128)(2,1)} %multiply_convert_fusion.p_ref, f32[16,2048]{1,0:T(8,128)} %get-tuple-element.11.e_ref, f32[16,2048]{1,0:T(8,128)} %get-tuple-element.10.w_ref, f32[16,2048]{1,0:T(8,128)} %shard_map.142.s_ref, f32[1,2048]{1,0:T(1,128)} %bitcast.46, ...), custom_call_target="tpu_custom_call" | custom-call | tf_op jit(solution)/shard_map/pallas_call | solution.py:181
  (6 shorter events, 0.1 us)
Async XLA Ops:
  1.4 21.4 %collective-permute-start.1 = (bf16[2,2048]{1,0:T(2,128)(2,1)S(1)}, bf16[2,2048]{1,0:T(2,128)(2,1)S(1)}, u32[]{:S(2)}, u32[]{:S(2)}) collective-permute-start(bf16[2,2048]{1,0:T(2,128)(2,1)S(1)} %get-tuple-element.7), channel_id=1, source_target_pairs={{0,4},{4,8},{8,12},{12,16},{16,20},{20,24},{24,28},{28,32},{32,36}... | collective-permute-start | bytes 24584 | tf_op jit(solution)/shard_map/ppermute | solution.py:265
  4.2 22.6 %collective-permute-start.2 = (bf16[2,2048]{1,0:T(2,128)(2,1)S(1)}, bf16[2,2048]{1,0:T(2,128)(2,1)S(1)}, u32[]{:S(2)}, u32[]{:S(2)}) collective-permute-start(bf16[2,2048]{1,0:T(2,128)(2,1)S(1)} %get-tuple-element.9), channel_id=1, source_target_pairs={{0,4},{4,8},{8,12},{12,16},{16,20},{20,24},{24,28},{28,32},{32,36}... | collective-permute-start | bytes 24584 | tf_op jit(solution)/shard_map/ppermute | solution.py:265
  9.1 6.9 %copy-start = (bf16[256,2048]{1,0:T(8,128)(2,1)S(1)}, bf16[256,2048]{1,0:T(8,128)(2,1)}, u32[]{:S(2)}) copy-start(bf16[256,2048]{1,0:T(8,128)(2,1)} %param.13) | copy-start | bytes 3145732
  9.1 10.9 %copy-start.2 = (bf16[256,2048]{1,0:T(8,128)(2,1)S(1)}, bf16[256,2048]{1,0:T(8,128)(2,1)}, u32[]{:S(2)}) copy-start(bf16[256,2048]{1,0:T(8,128)(2,1)} %param.21) | copy-start | bytes 3145732
  9.2 12.8 %copy-start.3 = (f32[16,2048]{1,0:T(8,128)S(1)}, f32[16,2048]{1,0:T(8,128)}, u32[]{:S(2)}) copy-start(f32[16,2048]{1,0:T(8,128)} %r_ref.1) | copy-start | bytes 393220
  9.2 12.8 %copy-start.4 = (f32[16,2048]{1,0:T(8,128)S(1)}, f32[16,2048]{1,0:T(8,128)}, u32[]{:S(2)}) copy-start(f32[16,2048]{1,0:T(8,128)} %param.24) | copy-start | bytes 393220
  9.2 13.6 %copy-start.1 = (bf16[256,2048]{1,0:T(8,128)(2,1)S(1)}, bf16[256,2048]{1,0:T(8,128)(2,1)}, u32[]{:S(2)}) copy-start(bf16[256,2048]{1,0:T(8,128)(2,1)} %param.20) | copy-start | bytes 3145732
  14.1 14.8 %collective-permute-start = (bf16[127,2048]{1,0:T(8,128)(2,1)S(1)}, bf16[127,2048]{1,0:T(8,128)(2,1)S(1)}, u32[]{:S(2)}, u32[]{:S(2)}) collective-permute-start(bf16[127,2048]{1,0:T(8,128)(2,1)S(1)} %slice.222), channel_id=1, source_target_pairs={{0,4},{4,8},{8,12},{12,16},{16,20},{20,24},{24,28},{28,32},{32,36}... | collective-permute-start | bytes 1560584 | tf_op jit(solution)/shard_map/ppermute | solution.py:265
  16.1 10.8 %collective-permute-start.3 = (bf16[2,2048]{1,0:T(2,128)(2,1)S(1)}, bf16[2,2048]{1,0:T(2,128)(2,1)S(1)}, u32[]{:S(2)}, u32[]{:S(2)}) collective-permute-start(bf16[2,2048]{1,0:T(2,128)(2,1)S(1)} %slice.200), channel_id=1, source_target_pairs={{0,4},{4,8},{8,12},{12,16},{16,20},{20,24},{24,28},{28,32},{32,36}... | collective-permute-start | bytes 24584 | tf_op jit(solution)/shard_map/ppermute | solution.py:265
  20.0 57.4 %collective-permute-start.4 = (bf16[2,2048]{1,0:T(2,128)(2,1)S(1)}, bf16[2,2048]{1,0:T(2,128)(2,1)S(1)}, u32[]{:S(2)}, u32[]{:S(2)}) collective-permute-start(bf16[2,2048]{1,0:T(2,128)(2,1)S(1)} %slice.206), channel_id=1, source_target_pairs={{0,4},{4,8},{8,12},{12,16},{16,20},{20,24},{24,28},{28,32},{32,36}... | collective-permute-start | bytes 24584 | tf_op jit(solution)/shard_map/ppermute | solution.py:265
  22.8 52.6 %collective-permute-start.9 = (bf16[2,2048]{1,0:T(2,128)(2,1)S(1)}, bf16[2,2048]{1,0:T(2,128)(2,1)S(1)}, u32[]{:S(2)}, u32[]{:S(2)}) collective-permute-start(bf16[2,2048]{1,0:T(2,128)(2,1)S(1)} %slice.218), channel_id=1, source_target_pairs={{0,4},{4,8},{8,12},{12,16},{16,20},{20,24},{24,28},{28,32},{32,36}... | collective-permute-start | bytes 24584 | tf_op jit(solution)/shard_map/ppermute | solution.py:265
  30.7 39.2 %copy-start.5 = (f32[3,3,2048]{2,1,0:T(4,128)S(1)}, f32[3,3,2048]{2,1,0:T(4,128)}, u32[]{:S(2)}) copy-start(f32[3,3,2048]{2,1,0:T(4,128)} %param.22) | copy-start | bytes 221188
  30.7 41.3 %copy-start.6 = (f32[2048]{0:T(1024)S(1)}, f32[2048]{0:T(1024)}, u32[]{:S(2)}) copy-start(f32[2048]{0:T(1024)} %param.19) | copy-start | bytes 24580
  64.1 5.8 %collective-permute-start.5 = (f32[256]{0:T(256)S(1)}, f32[256]{0:T(256)S(1)}, u32[]{:S(2)}, u32[]{:S(2)}) collective-permute-start(f32[256]{0:T(256)S(1)} %reduce_sum.9), channel_id=1, source_target_pairs={{0,1},{1,2},{2,3},{3,0},{4,5},{5,6},{6,7},{7,4},{8,9},{9,10},{10,1... | collective-permute-start | bytes 3080 | tf_op jit(solution)/shard_map/ppermute | solution.py:320
  65.6 5.1 %collective-permute-start.6 = (f32[256]{0:T(256)S(1)}, f32[256]{0:T(256)S(1)}, u32[]{:S(2)}, u32[]{:S(2)}) collective-permute-start(f32[256]{0:T(256)S(1)} %reduce_sum.9), channel_id=1, source_target_pairs={{0,2},{1,3},{2,0},{3,1},{4,6},{5,7},{6,4},{7,5},{8,10},{9,11},{10,... | collective-permute-start | bytes 3080 | tf_op jit(solution)/shard_map/ppermute | solution.py:320
  68.4 3.6 %collective-permute-start.7 = (f32[256]{0:T(256)S(1)}, f32[256]{0:T(256)S(1)}, u32[]{:S(2)}, u32[]{:S(2)}) collective-permute-start(f32[256]{0:T(256)S(1)} %reduce_sum.9), channel_id=1, source_target_pairs={{0,3},{1,0},{2,1},{3,2},{4,7},{5,4},{6,5},{7,6},{8,11},{9,8},{10,9... | collective-permute-start | bytes 3080 | tf_op jit(solution)/shard_map/ppermute | solution.py:320
  73.5 7.1 %collective-permute-start.8 = (bf16[2,2048]{1,0:T(2,128)(2,1)S(1)}, bf16[2,2048]{1,0:T(2,128)(2,1)S(1)}, u32[]{:S(2)}, u32[]{:S(2)}) collective-permute-start(bf16[2,2048]{1,0:T(2,128)(2,1)S(1)} %slice.227), channel_id=1, source_target_pairs={{0,4},{4,8},{8,12},{12,16},{16,20},{20,24},{24,28},{28,32},{32,36}... | collective-permute-start | bytes 24584 | tf_op jit(solution)/shard_map/ppermute | solution.py:265

commit v4 on v2

--- a/solution.py
+++ b/solution.py
@@ -1,3 +1,4 @@
+import functools
 import jax
 import jax.numpy as jnp
 from jax import lax
@@ -195,6 +196,71 @@
             pltpu.VMEM((GROUP, rows * 8, LANE), jnp.float32),
         ],
     )(product, decay, weight, start, skip, gate_feat)
+
+
+def scan_kernel(count, rows, f_ref, r_ref, out_ref, send_ref, recv_ref, send_sem, recv_sem):
+    me = lax.axis_index("ctx")
+    plan = []
+    span = 1
+    while span * 4 < count:
+        plan.append([(span * i, span * i) for i in range(1, 4)])
+        span *= 4
+    plan.append([(1 + span * i, span * i) for i in range(count // span)])
+    out_ref[...] = f_ref[...]
+    for k, sends in enumerate(plan):
+        send_ref[k] = out_ref[...]
+        last = k == len(plan) - 1
+        if last:
+            out_ref[...] = jnp.zeros_like(out_ref)
+        copies = []
+        for i, (shift, power) in enumerate(sends):
+            copy = pltpu.make_async_remote_copy(
+                src_ref=send_ref.at[k],
+                dst_ref=recv_ref.at[k, i],
+                send_sem=send_sem.at[k, i],
+                recv_sem=recv_sem.at[k, i],
+                device_id={"ctx": me + shift},
+                device_id_type=pl.DeviceIdType.MESH,
+            )
+            copies.append((shift, power, copy))
+
+            @pl.when(me + shift < count)
+            def _():
+                copy.start()
+
+        for i, (shift, power, copy) in enumerate(copies):
+
+            @pl.when(me >= shift)
+            def _():
+                copy.wait_recv()
+                if power == 0:
+                    out_ref[...] = out_ref[...] + recv_ref[k, i]
+                else:
+                    factor = jnp.exp(r_ref[...] * (-1.0 * rows * power))
+                    out_ref[...] = out_ref[...] + factor * recv_ref[k, i]
+
+        for shift, power, copy in copies:
+
+            @pl.when(me + shift < count)
+            def _():
+                copy.wait_send()
+
+
+def scan_call(final_state, decay_rates, count, rows):
+    shape = final_state.shape
+    return pl.pallas_call(
+        functools.partial(scan_kernel, count, rows),
+        in_specs=[pl.BlockSpec(memory_space=pltpu.VMEM)] * 2,
+        out_specs=pl.BlockSpec(memory_space=pltpu.VMEM),
+        out_shape=jax.ShapeDtypeStruct(shape, jnp.float32),
+        scratch_shapes=[
+            pltpu.VMEM((3,) + shape, jnp.float32),
+            pltpu.VMEM((3, 4) + shape, jnp.float32),
+            pltpu.SemaphoreType.DMA((3, 4)),
+            pltpu.SemaphoreType.DMA((3, 4)),
+        ],
+        compiler_params=pltpu.CompilerParams(has_side_effects=True),
+    )(final_state, decay_rates)
 
 
 def passed_along(value, axis, steps):
@@ -270,12 +336,7 @@
     mode_weight = residues * jnp.sqrt(-jnp.expm1(-2.0 * decay_rates))
     step_decay = jnp.exp(-decay_rates)
     final_state = modal_end_call(product_long, step_decay)
-    incoming = passed_along(final_state, "ctx", 1)
-    span = 1
-    while span < lax.axis_size("ctx"):
-        earlier = passed_along(incoming, "ctx", span)
-        incoming = incoming + jnp.exp(-decay_rates * (row_count * span)) * earlier
-        span *= 2
+    incoming = scan_call(final_state, decay_rates, lax.axis_size("ctx"), row_count)
     mixed_long = modal_out_call(
         product_long, step_decay, mode_weight, incoming, skip_long[None, :], gate_feat_long
     )

time: 165 us -> 144 us (0.87)
  the two profiles are of different devices: /device:TPU:16 before, /device:TPU:25 now
where the time goes in v4:
time: 144 us; the launch traced here: 142 us
  Pallas kernels  91.1 us (63%)
  starting transfers between devices  29.2 us (20%)
  other arithmetic  16.4 us (11%)
  local copies, waits for them, and re-layouts  2.9 us (2%)
  waiting for transfers between devices  1.51 us (1%)
    pallas_call x1, Pallas kernels, scan_call(): pl.pallas_call(functools.partial(scan_kernel, count, rows), in_specs=[pl....  43.5 us
    pallas_call x1, Pallas kernels, medium_call(): pl.pallas_call(medium_kernel, grid=grid, in_specs=[pl.BlockSpec((span, bl...  32.4 us
    ppermute x7, starting transfers between devices, passed_along(): lax.ppermute(value, axis, [(source, source + steps) for source in range(f...  24.3 us
    pallas_call x1, Pallas kernels, modal_out_call(): pl.pallas_call(modal_out_kernel, grid=(width // block,), in_specs=[pl.Blo...  10.5 us
    ppermute x3, starting transfers between devices, body(): lax.ppermute(squares, 'ch', [(source, (source + shift) % ring) for source...  4.89 us
    convert_element_type x1, other arithmetic, body(): late_product = (short_filter(key_medium, short_medium[1]) * short_filter(...  4.77 us
    pallas_call x1, Pallas kernels, modal_end_call(): pl.pallas_call(modal_end_kernel, grid=(width // block,), in_specs=[pl.Blo...  4.71 us
    add x2, other arithmetic, short_filter(): weights[0] * extended[2:] + weights[1] * extended[1:-1]  4.06 us
  transfers between devices with their start and end apart: 10, of which 2 were waited for; matrix products, arithmetic and copies ran while one was open for 11% of the time, Pallas kernels for 23%

profile of v4, /device:TPU:25, one launch (start us, length us, event | category | flops | bytes accessed | tf_op | source)
XLA Modules:
  0.0 142.1 jit_solution(4633665420158412450)
XLA Ops:
  0.6 0.8 fusion.4
  1.4 4.1 %collective-permute-start.1 = (bf16[2,2048]{1,0:T(2,128)(2,1)S(1)}, bf16[2,2048]{1,0:T(2,128)(2,1)S(1)}, u32[]{:S(2)}, u32[]{:S(2)}) collective-permute-start(bf16[2,2048]{1,0:T(2,128)(2,1)S(1)} %get-tuple-element.7), channel_id=1, source_target_pairs={{0,4},{4,8},{8,12},{12,16},{16,20},{20,24},{24,28},{28,32},{32,36}... | collective-permute-start | bytes 24584 | tf_op jit(solution)/shard_map/ppermute | solution.py:269
  5.5 0.8 fusion.5
  6.3 1.9 %collective-permute-start.2 = (bf16[2,2048]{1,0:T(2,128)(2,1)S(1)}, bf16[2,2048]{1,0:T(2,128)(2,1)S(1)}, u32[]{:S(2)}, u32[]{:S(2)}) collective-permute-start(bf16[2,2048]{1,0:T(2,128)(2,1)S(1)} %get-tuple-element.9), channel_id=1, source_target_pairs={{0,4},{4,8},{8,12},{12,16},{16,20},{20,24},{24,28},{28,32},{32,36}... | collective-permute-start | bytes 24584 | tf_op jit(solution)/shard_map/ppermute | solution.py:269
  8.3 1.0 fusion.7
  9.3 0.0 copy-start
  9.3 0.0 copy-start.2
  9.3 0.0 copy-start.3
  9.3 0.0 copy-start.4
  9.4 0.0 copy-start.1
  9.4 4.8 %multiply_convert_fusion.2 = bf16[254,2048]{1,0:T(8,128)(2,1)S(1)} fusion(bf16[256,2048]{1,0:T(8,128)(2,1)} %param.15, f32[2048]{0:T(1024)S(1)} %bitcast.21, f32[2048]{0:T(1024)S(1)} %bitcast.23, f32[2048]{0:T(1024)S(1)} %bitcast.25, bf16[256,2048]{1,0:T(8,128)(2,1)} %param.14, f32[2048]{0:T(1024)S(1)} %bitcast.27, f32[2048]{0:T(1024)S(1)} %bitcast.29, ...), kind=kLoop, calls=%fused_computation.4 | loop fusion | flops 9363456 | bytes 7331840 | tf_op jit(solution)/shard_map/convert_element_type | solution.py:305
  14.1 0.1 slice.222
  14.3 3.9 %collective-permute-start = (bf16[127,2048]{1,0:T(8,128)(2,1)S(1)}, bf16[127,2048]{1,0:T(8,128)(2,1)S(1)}, u32[]{:S(2)}, u32[]{:S(2)}) collective-permute-start(bf16[127,2048]{1,0:T(8,128)(2,1)S(1)} %slice.222), channel_id=1, source_target_pairs={{0,4},{4,8},{8,12},{12,16},{16,20},{20,24},{24,28},{28,32},{32,36}... | collective-permute-start | bytes 1560584 | tf_op jit(solution)/shard_map/ppermute | solution.py:269
  18.2 0.0 copy-done
  18.3 1.9 %collective-permute-start.3 = (bf16[2,2048]{1,0:T(2,128)(2,1)S(1)}, bf16[2,2048]{1,0:T(2,128)(2,1)S(1)}, u32[]{:S(2)}, u32[]{:S(2)}) collective-permute-start(bf16[2,2048]{1,0:T(2,128)(2,1)S(1)} %slice.200), channel_id=1, source_target_pairs={{0,4},{4,8},{8,12},{12,16},{16,20},{20,24},{24,28},{28,32},{32,36}... | collective-permute-start | bytes 24584 | tf_op jit(solution)/shard_map/ppermute | solution.py:269
  20.2 0.0 copy-done.2
  20.2 3.9 %collective-permute-start.4 = (bf16[2,2048]{1,0:T(2,128)(2,1)S(1)}, bf16[2,2048]{1,0:T(2,128)(2,1)S(1)}, u32[]{:S(2)}, u32[]{:S(2)}) collective-permute-start(bf16[2,2048]{1,0:T(2,128)(2,1)S(1)} %slice.206), channel_id=1, source_target_pairs={{0,4},{4,8},{8,12},{12,16},{16,20},{20,24},{24,28},{28,32},{32,36}... | collective-permute-start | bytes 24584 | tf_op jit(solution)/shard_map/ppermute | solution.py:269
  24.1 0.0 copy-done.3
  24.2 0.0 copy-done.4
  24.2 0.8 sqrt_multiply_fusion
  25.0 0.0 copy-done.1
  25.0 0.0 collective-permute-done.1
  25.0 1.9 %collective-permute-start.9 = (bf16[2,2048]{1,0:T(2,128)(2,1)S(1)}, bf16[2,2048]{1,0:T(2,128)(2,1)S(1)}, u32[]{:S(2)}, u32[]{:S(2)}) collective-permute-start(bf16[2,2048]{1,0:T(2,128)(2,1)S(1)} %slice.218), channel_id=1, source_target_pairs={{0,4},{4,8},{8,12},{12,16},{16,20},{20,24},{24,28},{28,32},{32,36}... | collective-permute-start | bytes 24584 | tf_op jit(solution)/shard_map/ppermute | solution.py:269
  26.9 0.0 collective-permute-done.2
  26.9 0.1 multiply_convert_fusion.3
  27.0 0.0 collective-permute-done.3
  27.0 2.0 %multiply_add_fusion.1.gate_ref = f32[256,2048]{1,0:T(8,128)} fusion(bf16[256,2048]{1,0:T(8,128)(2,1)S(1)} %copy-done, bf16[2,2048]{1,0:T(2,128)(2,1)S(1)} %collective-permute-done.3, f32[2048]{0:T(1024)S(1)} %bitcast.34, f32[2048]{0:T(1024)S(1)} %bitcast.35, f32[2048]{0:T(1024)S(1)} %bitcast.33), kind=kLoop, calls=%fused_computation.3 | loop fusion | flops 7340032 | bytes 3178496 | tf_op jit(solution)/shard_map/add | solution.py:273
  29.1 0.0 collective-permute-done
  29.1 1.8 %pad_maximum_fusion.ext_ref = bf16[384,2048]{1,0:T(8,128)(2,1)} fusion(bf16[254,2048]{1,0:T(8,128)(2,1)S(1)} %multiply_convert_fusion.2, bf16[2,2048]{1,0:T(2,128)(2,1)S(1)} %multiply_convert_fusion.3, bf16[127,2048]{1,0:T(8,128)(2,1)S(1)} %collective-permute-done, bf16[384]{0:T(512)(128)(2,1)S(1)} %pad.8.clone), kind=kLoop, calls=%fused_computation.5 | loop fusion | flops 6291456 | bytes 3142400 | tf_op jit(solution)/shard_map/concatenate | solution.py:316
  30.8 0.0 copy-start.5
  30.8 0.0 copy-start.6
  30.8 32.4 %shard_map.140 = (bf16[256,2048]{1,0:T(8,128)(2,1)}, f32[256,128]{1,0:T(8,128)}) custom-call(bf16[384,2048]{1,0:T(8,128)(2,1)} %pad_maximum_fusion.ext_ref, f32[128,2048]{1,0:T(8,128)} %f_ref.1, f32[1,2048]{1,0:T(1,128)} %bitcast.45, f32[256,2048]{1,0:T(8,128)} %multiply_add_fusion.1.gate_ref), custom_call_target="tpu_custom_call" | custom-call | tf_op jit(solution)/shard_map/pallas_call | solution.py:57
  63.2 1.0 reduce_sum.9
  64.3 1.3 collective-permute-start.5
  65.5 2.5 %collective-permute-start.6 = (f32[256]{0:T(256)S(1)}, f32[256]{0:T(256)S(1)}, u32[]{:S(2)}, u32[]{:S(2)}) collective-permute-start(f32[256]{0:T(256)S(1)} %reduce_sum.9), channel_id=1, source_target_pairs={{0,2},{1,3},{2,0},{3,1},{4,6},{5,7},{6,4},{7,5},{8,10},{9,11},{10,... | collective-permute-start | bytes 3080 | tf_op jit(solution)/shard_map/ppermute | solution.py:324
  68.0 1.2 collective-permute-start.7
  69.1 0.0 copy-done.5
  69.1 0.1 fusion.6
  69.2 0.0 collective-permute-done.5
  69.2 0.3 collective-permute-done.6
  69.5 1.2 collective-permute-done.7
  70.7 0.0 copy-done.6
  70.7 1.5 %multiply_convert_fusion.1 = bf16[256,2048]{1,0:T(8,128)(2,1)S(1)} fusion(bf16[256,2048]{1,0:T(8,128)(2,1)} %get-tuple-element.2, f32[256]{0:T(256)S(1)} %add_rsqrt_fusion, f32[2048]{0:T(1024)S(1)} %copy-done.6), kind=kLoop, calls=%fused_computation.2 | loop fusion | flops 2097152 | bytes 2106368 | tf_op jit(solution)/shard_map/convert_element_type | solution.py:328
  72.2 6.6 %collective-permute-start.8 = (bf16[2,2048]{1,0:T(2,128)(2,1)S(1)}, bf16[2,2048]{1,0:T(2,128)(2,1)S(1)}, u32[]{:S(2)}, u32[]{:S(2)}) collective-permute-start(bf16[2,2048]{1,0:T(2,128)(2,1)S(1)} %slice.227), channel_id=1, source_target_pairs={{0,4},{4,8},{8,12},{12,16},{16,20},{20,24},{24,28},{28,32},{32,36}... | collective-permute-start | bytes 24584 | tf_op jit(solution)/shard_map/ppermute | solution.py:269
  78.8 0.0 collective-permute-done.9
  78.8 2.0 %multiply_add_fusion.gate_ref = f32[256,2048]{1,0:T(8,128)} fusion(bf16[256,2048]{1,0:T(8,128)(2,1)S(1)} %copy-done.1, bf16[2,2048]{1,0:T(2,128)(2,1)S(1)} %collective-permute-done.9, f32[2048]{0:T(1024)S(1)} %bitcast.43, f32[2048]{0:T(1024)S(1)} %bitcast.44, f32[2048]{0:T(1024)S(1)} %bitcast.42), kind=kLoop, calls=%fused_computation | loop fusion | flops 7340032 | bytes 3178496 | tf_op jit(solution)/shard_map/add | solution.py:273
  80.8 0.0 collective-permute-done.4
  80.8 0.0 collective-permute-done.8
  80.8 2.5 %multiply_convert_fusion.p_ref = bf16[256,2048]{1,0:T(8,128)(2,1)} fusion(bf16[256,2048]{1,0:T(8,128)(2,1)S(1)} %multiply_convert_fusion.1, bf16[256,2048]{1,0:T(8,128)(2,1)S(1)} %copy-done.2, bf16[2,2048]{1,0:T(2,128)(2,1)S(1)} %collective-permute-done.8, bf16[2,2048]{1,0:T(2,128)(2,1)S(1)} %collective-permute-done.4, f32[2048]{0:T(1024)S(1)} %bitcast.36, ...), kind=kLoop, calls=%fused_computation.1 | loop fusion | flops 15728640 | bytes 3211264 | tf_op jit(solution)/shard_map/convert_element_type | solution.py:335
  83.3 4.7 %shard_map.141.f_ref = f32[16,2048]{1,0:T(8,128)} custom-call(bf16[256,2048]{1,0:T(8,128)(2,1)} %multiply_convert_fusion.p_ref, f32[16,2048]{1,0:T(8,128)} %get-tuple-element.11.e_ref), custom_call_target="tpu_custom_call" | custom-call | tf_op jit(solution)/shard_map/pallas_call | solution.py:121
  88.0 43.5 %shard_map.142.s_ref = f32[16,2048]{1,0:T(8,128)} custom-call(f32[16,2048]{1,0:T(8,128)} %shard_map.141.f_ref, f32[16,2048]{1,0:T(8,128)} %r_ref.1), custom_call_target="tpu_custom_call" | custom-call | tf_op jit(solution)/shard_map/pallas_call | solution.py:251
  131.6 10.5 %shard_map.143 = bf16[256,2048]{1,0:T(8,128)(2,1)} custom-call(bf16[256,2048]{1,0:T(8,128)(2,1)} %multiply_convert_fusion.p_ref, f32[16,2048]{1,0:T(8,128)} %get-tuple-element.11.e_ref, f32[16,2048]{1,0:T(8,128)} %get-tuple-element.10.w_ref, f32[16,2048]{1,0:T(8,128)} %shard_map.142.s_ref, f32[1,2048]{1,0:T(1,128)} %bitcast.46, ...), custom_call_target="tpu_custom_call" | custom-call | tf_op jit(solution)/shard_map/pallas_call | solution.py:181
  (6 shorter events, 0.1 us)
Async XLA Ops:
  1.4 23.6 %collective-permute-start.1 = (bf16[2,2048]{1,0:T(2,128)(2,1)S(1)}, bf16[2,2048]{1,0:T(2,128)(2,1)S(1)}, u32[]{:S(2)}, u32[]{:S(2)}) collective-permute-start(bf16[2,2048]{1,0:T(2,128)(2,1)S(1)} %get-tuple-element.7), channel_id=1, source_target_pairs={{0,4},{4,8},{8,12},{12,16},{16,20},{20,24},{24,28},{28,32},{32,36}... | collective-permute-start | bytes 24584 | tf_op jit(solution)/shard_map/ppermute | solution.py:269
  6.3 20.6 %collective-permute-start.2 = (bf16[2,2048]{1,0:T(2,128)(2,1)S(1)}, bf16[2,2048]{1,0:T(2,128)(2,1)S(1)}, u32[]{:S(2)}, u32[]{:S(2)}) collective-permute-start(bf16[2,2048]{1,0:T(2,128)(2,1)S(1)} %get-tuple-element.9), channel_id=1, source_target_pairs={{0,4},{4,8},{8,12},{12,16},{16,20},{20,24},{24,28},{28,32},{32,36}... | collective-permute-start | bytes 24584 | tf_op jit(solution)/shard_map/ppermute | solution.py:269
  9.3 8.9 %copy-start = (bf16[256,2048]{1,0:T(8,128)(2,1)S(1)}, bf16[256,2048]{1,0:T(8,128)(2,1)}, u32[]{:S(2)}) copy-start(bf16[256,2048]{1,0:T(8,128)(2,1)} %param.13) | copy-start | bytes 3145732
  9.3 10.9 %copy-start.2 = (bf16[256,2048]{1,0:T(8,128)(2,1)S(1)}, bf16[256,2048]{1,0:T(8,128)(2,1)}, u32[]{:S(2)}) copy-start(bf16[256,2048]{1,0:T(8,128)(2,1)} %param.21) | copy-start | bytes 3145732
  9.3 14.8 %copy-start.3 = (f32[16,2048]{1,0:T(8,128)S(1)}, f32[16,2048]{1,0:T(8,128)}, u32[]{:S(2)}) copy-start(f32[16,2048]{1,0:T(8,128)} %r_ref.1) | copy-start | bytes 393220
  9.3 14.8 %copy-start.4 = (f32[16,2048]{1,0:T(8,128)S(1)}, f32[16,2048]{1,0:T(8,128)}, u32[]{:S(2)}) copy-start(f32[16,2048]{1,0:T(8,128)} %param.24) | copy-start | bytes 393220
  9.4 15.6 %copy-start.1 = (bf16[256,2048]{1,0:T(8,128)(2,1)S(1)}, bf16[256,2048]{1,0:T(8,128)(2,1)}, u32[]{:S(2)}) copy-start(bf16[256,2048]{1,0:T(8,128)(2,1)} %param.20) | copy-start | bytes 3145732
  14.3 14.8 %collective-permute-start = (bf16[127,2048]{1,0:T(8,128)(2,1)S(1)}, bf16[127,2048]{1,0:T(8,128)(2,1)S(1)}, u32[]{:S(2)}, u32[]{:S(2)}) collective-permute-start(bf16[127,2048]{1,0:T(8,128)(2,1)S(1)} %slice.222), channel_id=1, source_target_pairs={{0,4},{4,8},{8,12},{12,16},{16,20},{20,24},{24,28},{28,32},{32,36}... | collective-permute-start | bytes 1560584 | tf_op jit(solution)/shard_map/ppermute | solution.py:269
  18.3 8.8 %collective-permute-start.3 = (bf16[2,2048]{1,0:T(2,128)(2,1)S(1)}, bf16[2,2048]{1,0:T(2,128)(2,1)S(1)}, u32[]{:S(2)}, u32[]{:S(2)}) collective-permute-start(bf16[2,2048]{1,0:T(2,128)(2,1)S(1)} %slice.200), channel_id=1, source_target_pairs={{0,4},{4,8},{8,12},{12,16},{16,20},{20,24},{24,28},{28,32},{32,36}... | collective-permute-start | bytes 24584 | tf_op jit(solution)/shard_map/ppermute | solution.py:269
  20.2 60.6 %collective-permute-start.4 = (bf16[2,2048]{1,0:T(2,128)(2,1)S(1)}, bf16[2,2048]{1,0:T(2,128)(2,1)S(1)}, u32[]{:S(2)}, u32[]{:S(2)}) collective-permute-start(bf16[2,2048]{1,0:T(2,128)(2,1)S(1)} %slice.206), channel_id=1, source_target_pairs={{0,4},{4,8},{8,12},{12,16},{16,20},{20,24},{24,28},{28,32},{32,36}... | collective-permute-start | bytes 24584 | tf_op jit(solution)/shard_map/ppermute | solution.py:269
  25.0 53.8 %collective-permute-start.9 = (bf16[2,2048]{1,0:T(2,128)(2,1)S(1)}, bf16[2,2048]{1,0:T(2,128)(2,1)S(1)}, u32[]{:S(2)}, u32[]{:S(2)}) collective-permute-start(bf16[2,2048]{1,0:T(2,128)(2,1)S(1)} %slice.218), channel_id=1, source_target_pairs={{0,4},{4,8},{8,12},{12,16},{16,20},{20,24},{24,28},{28,32},{32,36}... | collective-permute-start | bytes 24584 | tf_op jit(solution)/shard_map/ppermute | solution.py:269
  30.8 38.3 %copy-start.5 = (f32[3,3,2048]{2,1,0:T(4,128)S(1)}, f32[3,3,2048]{2,1,0:T(4,128)}, u32[]{:S(2)}) copy-start(f32[3,3,2048]{2,1,0:T(4,128)} %param.22) | copy-start | bytes 221188
  30.8 39.9 %copy-start.6 = (f32[2048]{0:T(1024)S(1)}, f32[2048]{0:T(1024)}, u32[]{:S(2)}) copy-start(f32[2048]{0:T(1024)} %param.19) | copy-start | bytes 24580
  64.3 5.0 %collective-permute-start.5 = (f32[256]{0:T(256)S(1)}, f32[256]{0:T(256)S(1)}, u32[]{:S(2)}, u32[]{:S(2)}) collective-permute-start(f32[256]{0:T(256)S(1)} %reduce_sum.9), channel_id=1, source_target_pairs={{0,1},{1,2},{2,3},{3,0},{4,5},{5,6},{6,7},{7,4},{8,9},{9,10},{10,1... | collective-permute-start | bytes 3080 | tf_op jit(solution)/shard_map/ppermute | solution.py:324
  65.5 3.9 %collective-permute-start.6 = (f32[256]{0:T(256)S(1)}, f32[256]{0:T(256)S(1)}, u32[]{:S(2)}, u32[]{:S(2)}) collective-permute-start(f32[256]{0:T(256)S(1)} %reduce_sum.9), channel_id=1, source_target_pairs={{0,2},{1,3},{2,0},{3,1},{4,6},{5,7},{6,4},{7,5},{8,10},{9,11},{10,... | collective-permute-start | bytes 3080 | tf_op jit(solution)/shard_map/ppermute | solution.py:324
  68.0 2.7 %collective-permute-start.7 = (f32[256]{0:T(256)S(1)}, f32[256]{0:T(256)S(1)}, u32[]{:S(2)}, u32[]{:S(2)}) collective-permute-start(f32[256]{0:T(256)S(1)} %reduce_sum.9), channel_id=1, source_target_pairs={{0,3},{1,0},{2,1},{3,2},{4,7},{5,4},{6,5},{7,6},{8,11},{9,8},{10,9... | collective-permute-start | bytes 3080 | tf_op jit(solution)/shard_map/ppermute | solution.py:324
  72.2 8.6 %collective-permute-start.8 = (bf16[2,2048]{1,0:T(2,128)(2,1)S(1)}, bf16[2,2048]{1,0:T(2,128)(2,1)S(1)}, u32[]{:S(2)}, u32[]{:S(2)}) collective-permute-start(bf16[2,2048]{1,0:T(2,128)(2,1)S(1)} %slice.227), channel_id=1, source_target_pairs={{0,4},{4,8},{8,12},{12,16},{16,20},{20,24},{24,28},{28,32},{32,36}... | collective-permute-start | bytes 24584 | tf_op jit(solution)/shard_map/ppermute | solution.py:269

commit v5 on v4

--- a/solution.py
+++ b/solution.py
@@ -206,6 +206,22 @@
         plan.append([(span * i, span * i) for i in range(1, 4)])
         span *= 4
     plan.append([(1 + span * i, span * i) for i in range(count // span)])
+    barrier = pltpu.get_barrier_semaphore()
+    partners = sorted({shift for sends in plan for shift, _ in sends})
+    for shift in partners:
+        for other in (me + shift, me - shift):
+
+            @pl.when(jnp.logical_and(other >= 0, other < count))
+            def _():
+                pl.semaphore_signal(
+                    barrier, 1, device_id={"ctx": other}, device_id_type=pl.DeviceIdType.MESH
+                )
+
+    peers = 0
+    for shift in partners:
+        peers = peers + (1 - (me + shift) // count) + (me - shift + count) // count
+    pl.semaphore_wait(barrier, peers)
+
     out_ref[...] = f_ref[...]
     for k, sends in enumerate(plan):
         send_ref[k] = out_ref[...]
@@ -259,7 +275,7 @@
             pltpu.SemaphoreType.DMA((3, 4)),
             pltpu.SemaphoreType.DMA((3, 4)),
         ],
-        compiler_params=pltpu.CompilerParams(has_side_effects=True),
+        compiler_params=pltpu.CompilerParams(collective_id=0, has_side_effects=True),
     )(final_state, decay_rates)
 
 

time: 144 us -> 134 us (0.931); the launches traced: 142 us -> 134 us
  Pallas kernels: 91.1 us -> 82.8 us
    pallas_call x1, Pallas kernels: 43.5 us -> 35.2 us  [scan_call(): pl.pallas_call(functools.partial(scan_kernel, count, rows), in_specs=[pl....]
  transfers between devices with their start and end apart: 10 -> 10, of which waited for: 2 -> 2; matrix products, arithmetic and copies ran while one was open for 11% -> 12% of each run, Pallas kernels for 23% -> 24%
where the time goes in v5:
time: 134 us
  Pallas kernels  82.8 us (62%)
  starting transfers between devices  29.2 us (22%)
  other arithmetic  16.4 us (12%)
  local copies, waits for them, and re-layouts  2.9 us (2%)
  waiting for transfers between devices  1.51 us (1%)
    pallas_call x1, Pallas kernels, scan_call(): pl.pallas_call(functools.partial(scan_kernel, count, rows), in_specs=[pl....  35.2 us
    pallas_call x1, Pallas kernels, medium_call(): pl.pallas_call(medium_kernel, grid=grid, in_specs=[pl.BlockSpec((span, bl...  32.4 us
    ppermute x7, starting transfers between devices, passed_along(): lax.ppermute(value, axis, [(source, source + steps) for source in range(f...  24.3 us
    pallas_call x1, Pallas kernels, modal_out_call(): pl.pallas_call(modal_out_kernel, grid=(width // block,), in_specs=[pl.Blo...  10.5 us
    ppermute x3, starting transfers between devices, body(): lax.ppermute(squares, 'ch', [(source, (source + shift) % ring) for source...  4.89 us
    convert_element_type x1, other arithmetic, body(): late_product = (short_filter(key_medium, short_medium[1]) * short_filter(...  4.77 us
    pallas_call x1, Pallas kernels, modal_end_call(): pl.pallas_call(modal_end_kernel, grid=(width // block,), in_specs=[pl.Blo...  4.71 us
    add x2, other arithmetic, short_filter(): weights[0] * extended[2:] + weights[1] * extended[1:-1]  4.06 us
  transfers between devices with their start and end apart: 10, of which 2 were waited for; matrix products, arithmetic and copies ran while one was open for 12% of the time, Pallas kernels for 24%

profile of v5, /device:TPU:25, one launch (start us, length us, event | category | flops | bytes accessed | tf_op | source)
XLA Modules:
  0.0 133.7 jit_solution(17529673795789429757)
XLA Ops:
  0.6 0.8 fusion.4
  1.4 4.1 %collective-permute-start.1 = (bf16[2,2048]{1,0:T(2,128)(2,1)S(1)}, bf16[2,2048]{1,0:T(2,128)(2,1)S(1)}, u32[]{:S(2)}, u32[]{:S(2)}) collective-permute-start(bf16[2,2048]{1,0:T(2,128)(2,1)S(1)} %get-tuple-element.7), channel_id=1, source_target_pairs={{0,4},{4,8},{8,12},{12,16},{16,20},{20,24},{24,28},{28,32},{32,36}... | collective-permute-start | bytes 24584 | tf_op jit(solution)/shard_map/ppermute | solution.py:285
  5.5 0.8 fusion.5
  6.3 1.9 %collective-permute-start.2 = (bf16[2,2048]{1,0:T(2,128)(2,1)S(1)}, bf16[2,2048]{1,0:T(2,128)(2,1)S(1)}, u32[]{:S(2)}, u32[]{:S(2)}) collective-permute-start(bf16[2,2048]{1,0:T(2,128)(2,1)S(1)} %get-tuple-element.9), channel_id=1, source_target_pairs={{0,4},{4,8},{8,12},{12,16},{16,20},{20,24},{24,28},{28,32},{32,36}... | collective-permute-start | bytes 24584 | tf_op jit(solution)/shard_map/ppermute | solution.py:285
  8.3 1.0 fusion.7
  9.3 0.0 copy-start
  9.3 0.0 copy-start.2
  9.3 0.0 copy-start.3
  9.3 0.0 copy-start.4
  9.4 0.0 copy-start.1
  9.4 4.8 %multiply_convert_fusion.2 = bf16[254,2048]{1,0:T(8,128)(2,1)S(1)} fusion(bf16[256,2048]{1,0:T(8,128)(2,1)} %param.15, f32[2048]{0:T(1024)S(1)} %bitcast.21, f32[2048]{0:T(1024)S(1)} %bitcast.23, f32[2048]{0:T(1024)S(1)} %bitcast.25, bf16[256,2048]{1,0:T(8,128)(2,1)} %param.14, f32[2048]{0:T(1024)S(1)} %bitcast.27, f32[2048]{0:T(1024)S(1)} %bitcast.29, ...), kind=kLoop, calls=%fused_computation.4 | loop fusion | flops 9363456 | bytes 7331840 | tf_op jit(solution)/shard_map/convert_element_type | solution.py:321
  14.1 0.1 slice.222
  14.3 3.9 %collective-permute-start = (bf16[127,2048]{1,0:T(8,128)(2,1)S(1)}, bf16[127,2048]{1,0:T(8,128)(2,1)S(1)}, u32[]{:S(2)}, u32[]{:S(2)}) collective-permute-start(bf16[127,2048]{1,0:T(8,128)(2,1)S(1)} %slice.222), channel_id=1, source_target_pairs={{0,4},{4,8},{8,12},{12,16},{16,20},{20,24},{24,28},{28,32},{32,36}... | collective-permute-start | bytes 1560584 | tf_op jit(solution)/shard_map/ppermute | solution.py:285
  18.2 0.0 copy-done
  18.3 1.9 %collective-permute-start.3 = (bf16[2,2048]{1,0:T(2,128)(2,1)S(1)}, bf16[2,2048]{1,0:T(2,128)(2,1)S(1)}, u32[]{:S(2)}, u32[]{:S(2)}) collective-permute-start(bf16[2,2048]{1,0:T(2,128)(2,1)S(1)} %slice.200), channel_id=1, source_target_pairs={{0,4},{4,8},{8,12},{12,16},{16,20},{20,24},{24,28},{28,32},{32,36}... | collective-permute-start | bytes 24584 | tf_op jit(solution)/shard_map/ppermute | solution.py:285
  20.2 0.0 copy-done.2
  20.2 3.9 %collective-permute-start.4 = (bf16[2,2048]{1,0:T(2,128)(2,1)S(1)}, bf16[2,2048]{1,0:T(2,128)(2,1)S(1)}, u32[]{:S(2)}, u32[]{:S(2)}) collective-permute-start(bf16[2,2048]{1,0:T(2,128)(2,1)S(1)} %slice.206), channel_id=1, source_target_pairs={{0,4},{4,8},{8,12},{12,16},{16,20},{20,24},{24,28},{28,32},{32,36}... | collective-permute-start | bytes 24584 | tf_op jit(solution)/shard_map/ppermute | solution.py:285
  24.1 0.0 copy-done.3
  24.2 0.0 copy-done.4
  24.2 0.8 sqrt_multiply_fusion
  25.0 0.0 copy-done.1
  25.0 0.0 collective-permute-done.1
  25.0 1.9 %collective-permute-start.9 = (bf16[2,2048]{1,0:T(2,128)(2,1)S(1)}, bf16[2,2048]{1,0:T(2,128)(2,1)S(1)}, u32[]{:S(2)}, u32[]{:S(2)}) collective-permute-start(bf16[2,2048]{1,0:T(2,128)(2,1)S(1)} %slice.218), channel_id=1, source_target_pairs={{0,4},{4,8},{8,12},{12,16},{16,20},{20,24},{24,28},{28,32},{32,36}... | collective-permute-start | bytes 24584 | tf_op jit(solution)/shard_map/ppermute | solution.py:285
  26.9 0.0 collective-permute-done.2
  26.9 0.1 multiply_convert_fusion.3
  27.0 0.0 collective-permute-done.3
  27.0 2.0 %multiply_add_fusion.1.gate_ref = f32[256,2048]{1,0:T(8,128)} fusion(bf16[256,2048]{1,0:T(8,128)(2,1)S(1)} %copy-done, bf16[2,2048]{1,0:T(2,128)(2,1)S(1)} %collective-permute-done.3, f32[2048]{0:T(1024)S(1)} %bitcast.34, f32[2048]{0:T(1024)S(1)} %bitcast.35, f32[2048]{0:T(1024)S(1)} %bitcast.33), kind=kLoop, calls=%fused_computation.3 | loop fusion | flops 7340032 | bytes 3178496 | tf_op jit(solution)/shard_map/add | solution.py:289
  29.1 0.0 collective-permute-done
  29.1 1.8 %pad_maximum_fusion.ext_ref = bf16[384,2048]{1,0:T(8,128)(2,1)} fusion(bf16[254,2048]{1,0:T(8,128)(2,1)S(1)} %multiply_convert_fusion.2, bf16[2,2048]{1,0:T(2,128)(2,1)S(1)} %multiply_convert_fusion.3, bf16[127,2048]{1,0:T(8,128)(2,1)S(1)} %collective-permute-done, bf16[384]{0:T(512)(128)(2,1)S(1)} %pad.8.clone), kind=kLoop, calls=%fused_computation.5 | loop fusion | flops 6291456 | bytes 3142400 | tf_op jit(solution)/shard_map/concatenate | solution.py:332
  30.8 0.0 copy-start.5
  30.8 0.0 copy-start.6
  30.8 32.4 %shard_map.140 = (bf16[256,2048]{1,0:T(8,128)(2,1)}, f32[256,128]{1,0:T(8,128)}) custom-call(bf16[384,2048]{1,0:T(8,128)(2,1)} %pad_maximum_fusion.ext_ref, f32[128,2048]{1,0:T(8,128)} %f_ref.1, f32[1,2048]{1,0:T(1,128)} %bitcast.45, f32[256,2048]{1,0:T(8,128)} %multiply_add_fusion.1.gate_ref), custom_call_target="tpu_custom_call" | custom-call | tf_op jit(solution)/shard_map/pallas_call | solution.py:57
  63.2 1.0 reduce_sum.9
  64.3 1.3 collective-permute-start.5
  65.5 2.5 %collective-permute-start.6 = (f32[256]{0:T(256)S(1)}, f32[256]{0:T(256)S(1)}, u32[]{:S(2)}, u32[]{:S(2)}) collective-permute-start(f32[256]{0:T(256)S(1)} %reduce_sum.9), channel_id=1, source_target_pairs={{0,2},{1,3},{2,0},{3,1},{4,6},{5,7},{6,4},{7,5},{8,10},{9,11},{10,... | collective-permute-start | bytes 3080 | tf_op jit(solution)/shard_map/ppermute | solution.py:340
  68.0 1.2 collective-permute-start.7
  69.1 0.0 copy-done.5
  69.1 0.1 fusion.6
  69.2 0.0 collective-permute-done.5
  69.2 0.3 collective-permute-done.6
  69.5 1.2 collective-permute-done.7
  70.7 0.0 copy-done.6
  70.7 1.5 %multiply_convert_fusion.1 = bf16[256,2048]{1,0:T(8,128)(2,1)S(1)} fusion(bf16[256,2048]{1,0:T(8,128)(2,1)} %get-tuple-element.2, f32[256]{0:T(256)S(1)} %add_rsqrt_fusion, f32[2048]{0:T(1024)S(1)} %copy-done.6), kind=kLoop, calls=%fused_computation.2 | loop fusion | flops 2097152 | bytes 2106368 | tf_op jit(solution)/shard_map/convert_element_type | solution.py:344
  72.2 6.6 %collective-permute-start.8 = (bf16[2,2048]{1,0:T(2,128)(2,1)S(1)}, bf16[2,2048]{1,0:T(2,128)(2,1)S(1)}, u32[]{:S(2)}, u32[]{:S(2)}) collective-permute-start(bf16[2,2048]{1,0:T(2,128)(2,1)S(1)} %slice.227), channel_id=1, source_target_pairs={{0,4},{4,8},{8,12},{12,16},{16,20},{20,24},{24,28},{28,32},{32,36}... | collective-permute-start | bytes 24584 | tf_op jit(solution)/shard_map/ppermute | solution.py:285
  78.8 0.0 collective-permute-done.9
  78.8 2.0 %multiply_add_fusion.gate_ref = f32[256,2048]{1,0:T(8,128)} fusion(bf16[256,2048]{1,0:T(8,128)(2,1)S(1)} %copy-done.1, bf16[2,2048]{1,0:T(2,128)(2,1)S(1)} %collective-permute-done.9, f32[2048]{0:T(1024)S(1)} %bitcast.43, f32[2048]{0:T(1024)S(1)} %bitcast.44, f32[2048]{0:T(1024)S(1)} %bitcast.42), kind=kLoop, calls=%fused_computation | loop fusion | flops 7340032 | bytes 3178496 | tf_op jit(solution)/shard_map/add | solution.py:289
  80.8 0.0 collective-permute-done.4
  80.8 0.0 collective-permute-done.8
  80.8 2.5 %multiply_convert_fusion.p_ref = bf16[256,2048]{1,0:T(8,128)(2,1)} fusion(bf16[256,2048]{1,0:T(8,128)(2,1)S(1)} %multiply_convert_fusion.1, bf16[256,2048]{1,0:T(8,128)(2,1)S(1)} %copy-done.2, bf16[2,2048]{1,0:T(2,128)(2,1)S(1)} %collective-permute-done.8, bf16[2,2048]{1,0:T(2,128)(2,1)S(1)} %collective-permute-done.4, f32[2048]{0:T(1024)S(1)} %bitcast.36, ...), kind=kLoop, calls=%fused_computation.1 | loop fusion | flops 15728640 | bytes 3211264 | tf_op jit(solution)/shard_map/convert_element_type | solution.py:351
  83.3 4.7 %shard_map.141.f_ref = f32[16,2048]{1,0:T(8,128)} custom-call(bf16[256,2048]{1,0:T(8,128)(2,1)} %multiply_convert_fusion.p_ref, f32[16,2048]{1,0:T(8,128)} %get-tuple-element.11.e_ref), custom_call_target="tpu_custom_call" | custom-call | tf_op jit(solution)/shard_map/pallas_call | solution.py:121
  88.0 35.2 %shard_map.142.s_ref = f32[16,2048]{1,0:T(8,128)} custom-call(f32[16,2048]{1,0:T(8,128)} %shard_map.141.f_ref, f32[16,2048]{1,0:T(8,128)} %r_ref.1), custom_call_target="tpu_custom_call" | custom-call | tf_op jit(solution)/shard_map/pallas_call | solution.py:267
  123.3 10.5 %shard_map.143 = bf16[256,2048]{1,0:T(8,128)(2,1)} custom-call(bf16[256,2048]{1,0:T(8,128)(2,1)} %multiply_convert_fusion.p_ref, f32[16,2048]{1,0:T(8,128)} %get-tuple-element.11.e_ref, f32[16,2048]{1,0:T(8,128)} %get-tuple-element.10.w_ref, f32[16,2048]{1,0:T(8,128)} %shard_map.142.s_ref, f32[1,2048]{1,0:T(1,128)} %bitcast.46, ...), custom_call_target="tpu_custom_call" | custom-call | tf_op jit(solution)/shard_map/pallas_call | solution.py:181
  (6 shorter events, 0.1 us)
Async XLA Ops:
  1.4 23.6 %collective-permute-start.1 = (bf16[2,2048]{1,0:T(2,128)(2,1)S(1)}, bf16[2,2048]{1,0:T(2,128)(2,1)S(1)}, u32[]{:S(2)}, u32[]{:S(2)}) collective-permute-start(bf16[2,2048]{1,0:T(2,128)(2,1)S(1)} %get-tuple-element.7), channel_id=1, source_target_pairs={{0,4},{4,8},{8,12},{12,16},{16,20},{20,24},{24,28},{28,32},{32,36}... | collective-permute-start | bytes 24584 | tf_op jit(solution)/shard_map/ppermute | solution.py:285
  6.3 20.6 %collective-permute-start.2 = (bf16[2,2048]{1,0:T(2,128)(2,1)S(1)}, bf16[2,2048]{1,0:T(2,128)(2,1)S(1)}, u32[]{:S(2)}, u32[]{:S(2)}) collective-permute-start(bf16[2,2048]{1,0:T(2,128)(2,1)S(1)} %get-tuple-element.9), channel_id=1, source_target_pairs={{0,4},{4,8},{8,12},{12,16},{16,20},{20,24},{24,28},{28,32},{32,36}... | collective-permute-start | bytes 24584 | tf_op jit(solution)/shard_map/ppermute | solution.py:285
  9.3 8.9 %copy-start = (bf16[256,2048]{1,0:T(8,128)(2,1)S(1)}, bf16[256,2048]{1,0:T(8,128)(2,1)}, u32[]{:S(2)}) copy-start(bf16[256,2048]{1,0:T(8,128)(2,1)} %param.13) | copy-start | bytes 3145732
  9.3 10.9 %copy-start.2 = (bf16[256,2048]{1,0:T(8,128)(2,1)S(1)}, bf16[256,2048]{1,0:T(8,128)(2,1)}, u32[]{:S(2)}) copy-start(bf16[256,2048]{1,0:T(8,128)(2,1)} %param.21) | copy-start | bytes 3145732
  9.3 14.8 %copy-start.3 = (f32[16,2048]{1,0:T(8,128)S(1)}, f32[16,2048]{1,0:T(8,128)}, u32[]{:S(2)}) copy-start(f32[16,2048]{1,0:T(8,128)} %r_ref.1) | copy-start | bytes 393220
  9.3 14.8 %copy-start.4 = (f32[16,2048]{1,0:T(8,128)S(1)}, f32[16,2048]{1,0:T(8,128)}, u32[]{:S(2)}) copy-start(f32[16,2048]{1,0:T(8,128)} %param.24) | copy-start | bytes 393220
  9.4 15.6 %copy-start.1 = (bf16[256,2048]{1,0:T(8,128)(2,1)S(1)}, bf16[256,2048]{1,0:T(8,128)(2,1)}, u32[]{:S(2)}) copy-start(bf16[256,2048]{1,0:T(8,128)(2,1)} %param.20) | copy-start | bytes 3145732
  14.3 14.8 %collective-permute-start = (bf16[127,2048]{1,0:T(8,128)(2,1)S(1)}, bf16[127,2048]{1,0:T(8,128)(2,1)S(1)}, u32[]{:S(2)}, u32[]{:S(2)}) collective-permute-start(bf16[127,2048]{1,0:T(8,128)(2,1)S(1)} %slice.222), channel_id=1, source_target_pairs={{0,4},{4,8},{8,12},{12,16},{16,20},{20,24},{24,28},{28,32},{32,36}... | collective-permute-start | bytes 1560584 | tf_op jit(solution)/shard_map/ppermute | solution.py:285
  18.3 8.8 %collective-permute-start.3 = (bf16[2,2048]{1,0:T(2,128)(2,1)S(1)}, bf16[2,2048]{1,0:T(2,128)(2,1)S(1)}, u32[]{:S(2)}, u32[]{:S(2)}) collective-permute-start(bf16[2,2048]{1,0:T(2,128)(2,1)S(1)} %slice.200), channel_id=1, source_target_pairs={{0,4},{4,8},{8,12},{12,16},{16,20},{20,24},{24,28},{28,32},{32,36}... | collective-permute-start | bytes 24584 | tf_op jit(solution)/shard_map/ppermute | solution.py:285
  20.2 60.6 %collective-permute-start.4 = (bf16[2,2048]{1,0:T(2,128)(2,1)S(1)}, bf16[2,2048]{1,0:T(2,128)(2,1)S(1)}, u32[]{:S(2)}, u32[]{:S(2)}) collective-permute-start(bf16[2,2048]{1,0:T(2,128)(2,1)S(1)} %slice.206), channel_id=1, source_target_pairs={{0,4},{4,8},{8,12},{12,16},{16,20},{20,24},{24,28},{28,32},{32,36}... | collective-permute-start | bytes 24584 | tf_op jit(solution)/shard_map/ppermute | solution.py:285
  25.0 53.8 %collective-permute-start.9 = (bf16[2,2048]{1,0:T(2,128)(2,1)S(1)}, bf16[2,2048]{1,0:T(2,128)(2,1)S(1)}, u32[]{:S(2)}, u32[]{:S(2)}) collective-permute-start(bf16[2,2048]{1,0:T(2,128)(2,1)S(1)} %slice.218), channel_id=1, source_target_pairs={{0,4},{4,8},{8,12},{12,16},{16,20},{20,24},{24,28},{28,32},{32,36}... | collective-permute-start | bytes 24584 | tf_op jit(solution)/shard_map/ppermute | solution.py:285
  30.8 38.3 %copy-start.5 = (f32[3,3,2048]{2,1,0:T(4,128)S(1)}, f32[3,3,2048]{2,1,0:T(4,128)}, u32[]{:S(2)}) copy-start(f32[3,3,2048]{2,1,0:T(4,128)} %param.22) | copy-start | bytes 221188
  30.8 39.9 %copy-start.6 = (f32[2048]{0:T(1024)S(1)}, f32[2048]{0:T(1024)}, u32[]{:S(2)}) copy-start(f32[2048]{0:T(1024)} %param.19) | copy-start | bytes 24580
  64.3 5.0 %collective-permute-start.5 = (f32[256]{0:T(256)S(1)}, f32[256]{0:T(256)S(1)}, u32[]{:S(2)}, u32[]{:S(2)}) collective-permute-start(f32[256]{0:T(256)S(1)} %reduce_sum.9), channel_id=1, source_target_pairs={{0,1},{1,2},{2,3},{3,0},{4,5},{5,6},{6,7},{7,4},{8,9},{9,10},{10,1... | collective-permute-start | bytes 3080 | tf_op jit(solution)/shard_map/ppermute | solution.py:340
  65.5 3.9 %collective-permute-start.6 = (f32[256]{0:T(256)S(1)}, f32[256]{0:T(256)S(1)}, u32[]{:S(2)}, u32[]{:S(2)}) collective-permute-start(f32[256]{0:T(256)S(1)} %reduce_sum.9), channel_id=1, source_target_pairs={{0,2},{1,3},{2,0},{3,1},{4,6},{5,7},{6,4},{7,5},{8,10},{9,11},{10,... | collective-permute-start | bytes 3080 | tf_op jit(solution)/shard_map/ppermute | solution.py:340
  68.0 2.7 %collective-permute-start.7 = (f32[256]{0:T(256)S(1)}, f32[256]{0:T(256)S(1)}, u32[]{:S(2)}, u32[]{:S(2)}) collective-permute-start(f32[256]{0:T(256)S(1)} %reduce_sum.9), channel_id=1, source_target_pairs={{0,3},{1,0},{2,1},{3,2},{4,7},{5,4},{6,5},{7,6},{8,11},{9,8},{10,9... | collective-permute-start | bytes 3080 | tf_op jit(solution)/shard_map/ppermute | solution.py:340
  72.2 8.6 %collective-permute-start.8 = (bf16[2,2048]{1,0:T(2,128)(2,1)S(1)}, bf16[2,2048]{1,0:T(2,128)(2,1)S(1)}, u32[]{:S(2)}, u32[]{:S(2)}) collective-permute-start(bf16[2,2048]{1,0:T(2,128)(2,1)S(1)} %slice.227), channel_id=1, source_target_pairs={{0,4},{4,8},{8,12},{12,16},{16,20},{20,24},{24,28},{28,32},{32,36}... | collective-permute-start | bytes 24584 | tf_op jit(solution)/shard_map/ppermute | solution.py:285

commit v6 on v5

--- a/solution.py
+++ b/solution.py
@@ -319,10 +319,25 @@
     late_product = (
         short_filter(key_medium, short_medium[1]) * short_filter(value_medium, short_medium[2])
     ).astype(jnp.bfloat16)
-    rim_gate, rim_key, rim_value, rim_product = passed_along(
-        (gate_medium[-2:], key_medium[-2:], value_medium[-2:], late_product[-(tap_count - 1) :]),
+    halo = tap_count - 1
+    rims = passed_along(
+        jnp.concatenate(
+            [
+                late_product[-halo:],
+                gate_medium[-2:],
+                key_medium[-2:],
+                value_medium[-2:],
+                gate_long[-2:],
+                key_long[-2:],
+            ],
+            0,
+        ),
         "ctx",
         1,
+    )
+    rim_product = rims[:halo]
+    rim_gate, rim_key, rim_value, rim_gate_long, rim_key_long = (
+        rims[halo + 2 * i : halo + 2 * i + 2] for i in range(5)
     )
     head_key = short_filter(jnp.concatenate([rim_key, key_medium[:2]], 0), short_medium[1])
     head_value = short_filter(jnp.concatenate([rim_value, value_medium[:2]], 0), short_medium[2])
@@ -342,9 +357,7 @@
         )
     inverse = lax.rsqrt(total_squares / D + 1e-06)
     normed = (mixed_medium * norm_gain * inverse[:, None]).astype(jnp.bfloat16)
-    rim_gate_long, rim_key_long, rim_normed = passed_along(
-        (gate_long[-2:], key_long[-2:], normed[-2:]), "ctx", 1
-    )
+    rim_normed = passed_along(normed[-2:], "ctx", 1)
     gate_feat_long = short_filter(jnp.concatenate([rim_gate_long, gate_long], 0), short_long[0])
     key_feat_long = short_filter(jnp.concatenate([rim_key_long, key_long], 0), short_long[1])
     value_feat_long = short_filter(jnp.concatenate([rim_normed, normed], 0), short_long[2])

time: 134 us -> 139 us (1.037); the launches traced: 134 us -> 137 us
  starting transfers between devices: 29.2 us -> 15.2 us
  waiting for transfers between devices: 1.51 us -> 8.01 us
  Pallas kernels: 82.8 us -> 87.8 us
  local copies, waits for them, and re-layouts: 2.9 us -> 7.44 us
    ppermute x7 -> x2, starting transfers between devices: 24.3 us -> 10.3 us  [passed_along(): lax.ppermute(value, axis, [(source, source + steps) for source in range(f...]
    ppermute x7 -> x2, waiting for transfers between devices: 0.02 us -> 6.81 us  [passed_along(): lax.ppermute(value, axis, [(source, source + steps) for source in range(f...]
    pallas_call x1, Pallas kernels: 35.2 us -> 40.2 us  [scan_call(): pl.pallas_call(functools.partial(scan_kernel, count, rows), in_specs=[pl....]
    concatenate x0 -> x1, local copies, waits for them, and re-layouts: none -> 1.9 us  [body(): jnp.concatenate([late_product[-halo:], gate_medium[-2:], key_medium[-2:],...]
  transfers between devices with their start and end apart: 10 -> 5, of which waited for: 2 -> 4; matrix products, arithmetic and copies ran while one was open for 12% -> 2% of each run, Pallas kernels for 24% -> 0%
where the time goes in v6:
time: 139 us; the launch traced here: 137 us
  Pallas kernels  87.8 us (63%)
  other arithmetic  17.4 us (13%)
  starting transfers between devices  15.2 us (11%)
  waiting for transfers between devices  8.01 us (6%)
  local copies, waits for them, and re-layouts  7.44 us (5%)
    pallas_call x1, Pallas kernels, scan_call(): pl.pallas_call(functools.partial(scan_kernel, count, rows), in_specs=[pl....  40.2 us
    pallas_call x1, Pallas kernels, medium_call(): pl.pallas_call(medium_kernel, grid=grid, in_specs=[pl.BlockSpec((span, bl...  32.4 us
    pallas_call x1, Pallas kernels, modal_out_call(): pl.pallas_call(modal_out_kernel, grid=(width // block,), in_specs=[pl.Blo...  10.5 us
    ppermute x2, starting transfers between devices, passed_along(): lax.ppermute(value, axis, [(source, source + steps) for source in range(f...  10.3 us
    ppermute x2, waiting for transfers between devices, passed_along(): lax.ppermute(value, axis, [(source, source + steps) for source in range(f...  6.81 us
    ppermute x3, starting transfers between devices, body(): lax.ppermute(squares, 'ch', [(source, (source + shift) % ring) for source...  4.89 us
    convert_element_type x1, other arithmetic, body(): late_product = (short_filter(key_medium, short_medium[1]) * short_filter(...  4.77 us
    pallas_call x1, Pallas kernels, modal_end_call(): pl.pallas_call(modal_end_kernel, grid=(width // block,), in_specs=[pl.Blo...  4.71 us
  transfers between devices with their start and end apart: 5, of which 4 were waited for; matrix products, arithmetic and copies ran while one was open for 2% of the time, Pallas kernels for 0%

profile of v6, /device:TPU:25, one launch (start us, length us, event | category | flops | bytes accessed | tf_op | source)
XLA Modules:
  0.0 136.7 jit_solution(3062297421921485881)
XLA Ops:
  0.6 1.0 fusion.8
  1.7 1.4 %fusion.4 = (bf16[2,2048]{1,0:T(2,128)(2,1)}, bf16[2,2048]{1,0:T(2,128)(2,1)}, bf16[2,2048]{1,0:T(2,128)(2,1)}, bf16[2,2048]{1,0:T(2,128)(2,1)}) fusion(bf16[256,2048]{1,0:T(8,128)(2,1)} %param.14, bf16[256,2048]{1,0:T(8,128)(2,1)} %param.15), kind=kLoop, calls=%fused_computation.28 | loop fusion | bytes 65536 | tf_op jit(solution)/shard_map/slice | solution.py:342
  3.1 0.0 copy-start
  3.1 4.8 %multiply_convert_fusion.2 = bf16[254,2048]{1,0:T(8,128)(2,1)S(1)} fusion(bf16[256,2048]{1,0:T(8,128)(2,1)} %param.15, f32[2048]{0:T(1024)S(1)} %bitcast.21, f32[2048]{0:T(1024)S(1)} %bitcast.23, f32[2048]{0:T(1024)S(1)} %bitcast.25, bf16[256,2048]{1,0:T(8,128)(2,1)} %param.14, f32[2048]{0:T(1024)S(1)} %bitcast.27, f32[2048]{0:T(1024)S(1)} %bitcast.29, ...), kind=kLoop, calls=%fused_computation.4 | loop fusion | flops 9363456 | bytes 7331840 | tf_op jit(solution)/shard_map/convert_element_type | solution.py:321
  7.9 0.0 copy-start.3
  7.9 0.0 copy-start.4
  7.9 0.1 slice.246
  8.0 0.0 copy-done
  8.1 1.4 %slice.213 = bf16[2,2048]{1,0:T(2,128)(2,1)} slice(bf16[256,2048]{1,0:T(8,128)(2,1)} %param.20), slice={[254:256], [0:2048]} | slice | bytes 16384 | tf_op jit(solution)/shard_map/slice | solution.py:330
  9.5 1.4 slice.214
  10.8 1.9 %concatenate.24 = bf16[137,2048]{1,0:T(8,128)(2,1)S(1)} concatenate(bf16[127,2048]{1,0:T(8,128)(2,1)S(1)} %slice.246, bf16[2,2048]{1,0:T(2,128)(2,1)S(1)} %slice.210, bf16[2,2048]{1,0:T(2,128)(2,1)} %get-tuple-element.7, bf16[2,2048]{1,0:T(2,128)(2,1)} %get-tuple-element.35, bf16[2,2048]{1,0:T(2,128)(2,1)} %slice.213, bf16[2,2048]{1,0:T(2,128)(2,1)} %slice.214), dimensions={0} | concatenate | bytes 1122304 | tf_op jit(solution)/shard_map/concatenate | solution.py:324
  12.7 4.1 %collective-permute-start = (bf16[137,2048]{1,0:T(8,128)(2,1)S(1)}, bf16[137,2048]{1,0:T(8,128)(2,1)S(1)}, u32[]{:S(2)}, u32[]{:S(2)}) collective-permute-start(bf16[137,2048]{1,0:T(8,128)(2,1)S(1)} %concatenate.24), channel_id=1, source_target_pairs={{0,4},{4,8},{8,12},{12,16},{16,20},{20,24},{24,28},{28,32},{32,36}... | collective-permute-start | bytes 1683464 | tf_op jit(solution)/shard_map/ppermute | solution.py:285
  16.8 0.0 copy-done.3
  16.9 0.0 copy-done.4
  16.9 0.8 sqrt_multiply_fusion
  17.7 6.0 %collective-permute-done = bf16[137,2048]{1,0:T(8,128)(2,1)S(1)} collective-permute-done((bf16[137,2048]{1,0:T(8,128)(2,1)S(1)}, bf16[137,2048]{1,0:T(8,128)(2,1)S(1)}, u32[]{:S(2)}, u32[]{:S(2)}) %collective-permute-start) | collective-permute-done | bytes 561184 | tf_op jit(solution)/shard_map/ppermute | solution.py:285
  23.7 0.9 multiply_convert_fusion.3
  24.6 1.8 %pad_maximum_fusion.ext_ref = bf16[384,2048]{1,0:T(8,128)(2,1)} fusion(bf16[254,2048]{1,0:T(8,128)(2,1)S(1)} %multiply_convert_fusion.2, bf16[2,2048]{1,0:T(2,128)(2,1)S(1)} %multiply_convert_fusion.3, bf16[127,2048]{1,0:T(8,128)(2,1)S(1)} %slice.247, bf16[384]{0:T(512)(128)(2,1)S(1)} %pad.8.clone), kind=kLoop, calls=%fused_computation.5 | loop fusion | flops 6291456 | bytes 3142400 | tf_op jit(solution)/shard_map/concatenate | solution.py:347
  26.4 2.0 %multiply_add_fusion.1.gate_ref = f32[256,2048]{1,0:T(8,128)} fusion(bf16[256,2048]{1,0:T(8,128)(2,1)S(1)} %copy-done, bf16[2,2048]{1,0:T(2,128)(2,1)S(1)} %get-tuple-element.12, f32[2048]{0:T(1024)S(1)} %bitcast.34, f32[2048]{0:T(1024)S(1)} %bitcast.35, f32[2048]{0:T(1024)S(1)} %bitcast.33), kind=kLoop, calls=%fused_computation.3 | loop fusion | flops 7340032 | bytes 3178496 | tf_op jit(solution)/shard_map/add | solution.py:289
  28.4 0.0 copy-start.5
  28.4 0.0 copy-start.6
  28.4 32.4 %shard_map.140 = (bf16[256,2048]{1,0:T(8,128)(2,1)}, f32[256,128]{1,0:T(8,128)}) custom-call(bf16[384,2048]{1,0:T(8,128)(2,1)} %pad_maximum_fusion.ext_ref, f32[128,2048]{1,0:T(8,128)} %f_ref.1, f32[1,2048]{1,0:T(1,128)} %bitcast.45, f32[256,2048]{1,0:T(8,128)} %multiply_add_fusion.1.gate_ref), custom_call_target="tpu_custom_call" | custom-call | tf_op jit(solution)/shard_map/pallas_call | solution.py:57
  60.8 0.0 copy-start.1
  60.8 1.1 reduce_sum.9
  61.9 1.3 collective-permute-start.1
  63.2 2.5 %collective-permute-start.2 = (f32[256]{0:T(256)S(1)}, f32[256]{0:T(256)S(1)}, u32[]{:S(2)}, u32[]{:S(2)}) collective-permute-start(f32[256]{0:T(256)S(1)} %reduce_sum.9), channel_id=1, source_target_pairs={{0,2},{1,3},{2,0},{3,1},{4,6},{5,7},{6,4},{7,5},{8,10},{9,11},{10,... | collective-permute-start | bytes 3080 | tf_op jit(solution)/shard_map/ppermute | solution.py:355
  65.7 1.2 collective-permute-start.3
  66.8 0.0 copy-done.5
  66.8 0.1 fusion.7
  66.9 0.0 collective-permute-done.1
  66.9 0.3 collective-permute-done.2
  67.1 0.9 collective-permute-done.3
  68.1 0.0 copy-done.6
  68.1 1.5 %multiply_convert_fusion.1 = bf16[256,2048]{1,0:T(8,128)(2,1)S(1)} fusion(bf16[256,2048]{1,0:T(8,128)(2,1)} %get-tuple-element.2, f32[256]{0:T(256)S(1)} %add_rsqrt_fusion, f32[2048]{0:T(1024)S(1)} %copy-done.6), kind=kLoop, calls=%fused_computation.2 | loop fusion | flops 2097152 | bytes 2106368 | tf_op jit(solution)/shard_map/convert_element_type | solution.py:359
  69.6 0.0 copy-start.2
  69.6 6.2 %collective-permute-start.4 = (bf16[2,2048]{1,0:T(2,128)(2,1)S(1)}, bf16[2,2048]{1,0:T(2,128)(2,1)S(1)}, u32[]{:S(2)}, u32[]{:S(2)}) collective-permute-start(bf16[2,2048]{1,0:T(2,128)(2,1)S(1)} %slice.256), channel_id=1, source_target_pairs={{0,4},{4,8},{8,12},{12,16},{16,20},{20,24},{24,28},{28,32},{32,36}... | collective-permute-start | bytes 24584 | tf_op jit(solution)/shard_map/ppermute | solution.py:285
  75.9 0.0 copy-done.1
  75.9 2.0 %multiply_add_fusion.gate_ref = f32[256,2048]{1,0:T(8,128)} fusion(bf16[256,2048]{1,0:T(8,128)(2,1)S(1)} %copy-done.1, bf16[2,2048]{1,0:T(2,128)(2,1)S(1)} %get-tuple-element.10, f32[2048]{0:T(1024)S(1)} %bitcast.43, f32[2048]{0:T(1024)S(1)} %bitcast.44, f32[2048]{0:T(1024)S(1)} %bitcast.42), kind=kLoop, calls=%fused_computation | loop fusion | flops 7340032 | bytes 3178496 | tf_op jit(solution)/shard_map/add | solution.py:289
  77.9 0.8 collective-permute-done.4
  78.7 0.0 copy-done.2
  78.7 2.5 %multiply_convert_fusion.p_ref = bf16[256,2048]{1,0:T(8,128)(2,1)} fusion(bf16[256,2048]{1,0:T(8,128)(2,1)S(1)} %multiply_convert_fusion.1, bf16[256,2048]{1,0:T(8,128)(2,1)S(1)} %copy-done.2, bf16[2,2048]{1,0:T(2,128)(2,1)S(1)} %collective-permute-done.4, bf16[2,2048]{1,0:T(2,128)(2,1)S(1)} %get-tuple-element.11, f32[2048]{0:T(1024)S(1)} %bitcast.36, ...), kind=kLoop, calls=%fused_computation.1 | loop fusion | flops 15728640 | bytes 3211264 | tf_op jit(solution)/shard_map/convert_element_type | solution.py:364
  81.3 4.7 %shard_map.141.f_ref = f32[16,2048]{1,0:T(8,128)} custom-call(bf16[256,2048]{1,0:T(8,128)(2,1)} %multiply_convert_fusion.p_ref, f32[16,2048]{1,0:T(8,128)} %get-tuple-element.16.e_ref), custom_call_target="tpu_custom_call" | custom-call | tf_op jit(solution)/shard_map/pallas_call | solution.py:121
  86.0 40.2 %shard_map.142.s_ref = f32[16,2048]{1,0:T(8,128)} custom-call(f32[16,2048]{1,0:T(8,128)} %shard_map.141.f_ref, f32[16,2048]{1,0:T(8,128)} %r_ref.1), custom_call_target="tpu_custom_call" | custom-call | tf_op jit(solution)/shard_map/pallas_call | solution.py:267
  126.2 10.5 %shard_map.143 = bf16[256,2048]{1,0:T(8,128)(2,1)} custom-call(bf16[256,2048]{1,0:T(8,128)(2,1)} %multiply_convert_fusion.p_ref, f32[16,2048]{1,0:T(8,128)} %get-tuple-element.16.e_ref, f32[16,2048]{1,0:T(8,128)} %get-tuple-element.15.w_ref, f32[16,2048]{1,0:T(8,128)} %shard_map.142.s_ref, f32[1,2048]{1,0:T(1,128)} %bitcast.46, ...), custom_call_target="tpu_custom_call" | custom-call | tf_op jit(solution)/shard_map/pallas_call | solution.py:181
  (6 shorter events, 0.1 us)
Async XLA Ops:
  3.1 4.9 %copy-start = (bf16[256,2048]{1,0:T(8,128)(2,1)S(1)}, bf16[256,2048]{1,0:T(8,128)(2,1)}, u32[]{:S(2)}) copy-start(bf16[256,2048]{1,0:T(8,128)(2,1)} %param.13) | copy-start | bytes 3145732
  7.9 9.0 %copy-start.3 = (f32[16,2048]{1,0:T(8,128)S(1)}, f32[16,2048]{1,0:T(8,128)}, u32[]{:S(2)}) copy-start(f32[16,2048]{1,0:T(8,128)} %r_ref.1) | copy-start | bytes 393220
  7.9 9.0 %copy-start.4 = (f32[16,2048]{1,0:T(8,128)S(1)}, f32[16,2048]{1,0:T(8,128)}, u32[]{:S(2)}) copy-start(f32[16,2048]{1,0:T(8,128)} %param.24) | copy-start | bytes 393220
  12.7 10.9 %collective-permute-start = (bf16[137,2048]{1,0:T(8,128)(2,1)S(1)}, bf16[137,2048]{1,0:T(8,128)(2,1)S(1)}, u32[]{:S(2)}, u32[]{:S(2)}) collective-permute-start(bf16[137,2048]{1,0:T(8,128)(2,1)S(1)} %concatenate.24), channel_id=1, source_target_pairs={{0,4},{4,8},{8,12},{12,16},{16,20},{20,24},{24,28},{28,32},{32,36}... | collective-permute-start | bytes 1683464 | tf_op jit(solution)/shard_map/ppermute | solution.py:285
  28.4 38.4 %copy-start.5 = (f32[3,3,2048]{2,1,0:T(4,128)S(1)}, f32[3,3,2048]{2,1,0:T(4,128)}, u32[]{:S(2)}) copy-start(f32[3,3,2048]{2,1,0:T(4,128)} %param.22) | copy-start | bytes 221188
  28.4 39.7 %copy-start.6 = (f32[2048]{0:T(1024)S(1)}, f32[2048]{0:T(1024)}, u32[]{:S(2)}) copy-start(f32[2048]{0:T(1024)} %param.19) | copy-start | bytes 24580
  60.8 15.1 %copy-start.1 = (bf16[256,2048]{1,0:T(8,128)(2,1)S(1)}, bf16[256,2048]{1,0:T(8,128)(2,1)}, u32[]{:S(2)}) copy-start(bf16[256,2048]{1,0:T(8,128)(2,1)} %param.20) | copy-start | bytes 3145732
  61.9 5.0 %collective-permute-start.1 = (f32[256]{0:T(256)S(1)}, f32[256]{0:T(256)S(1)}, u32[]{:S(2)}, u32[]{:S(2)}) collective-permute-start(f32[256]{0:T(256)S(1)} %reduce_sum.9), channel_id=1, source_target_pairs={{0,1},{1,2},{2,3},{3,0},{4,5},{5,6},{6,7},{7,4},{8,9},{9,10},{10,1... | collective-permute-start | bytes 3080 | tf_op jit(solution)/shard_map/ppermute | solution.py:355
  63.2 3.9 %collective-permute-start.2 = (f32[256]{0:T(256)S(1)}, f32[256]{0:T(256)S(1)}, u32[]{:S(2)}, u32[]{:S(2)}) collective-permute-start(f32[256]{0:T(256)S(1)} %reduce_sum.9), channel_id=1, source_target_pairs={{0,2},{1,3},{2,0},{3,1},{4,6},{5,7},{6,4},{7,5},{8,10},{9,11},{10,... | collective-permute-start | bytes 3080 | tf_op jit(solution)/shard_map/ppermute | solution.py:355
  65.7 2.4 %collective-permute-start.3 = (f32[256]{0:T(256)S(1)}, f32[256]{0:T(256)S(1)}, u32[]{:S(2)}, u32[]{:S(2)}) collective-permute-start(f32[256]{0:T(256)S(1)} %reduce_sum.9), channel_id=1, source_target_pairs={{0,3},{1,0},{2,1},{3,2},{4,7},{5,4},{6,5},{7,6},{8,11},{9,8},{10,9... | collective-permute-start | bytes 3080 | tf_op jit(solution)/shard_map/ppermute | solution.py:355
  69.6 9.1 %copy-start.2 = (bf16[256,2048]{1,0:T(8,128)(2,1)S(1)}, bf16[256,2048]{1,0:T(8,128)(2,1)}, u32[]{:S(2)}) copy-start(bf16[256,2048]{1,0:T(8,128)(2,1)} %param.21) | copy-start | bytes 3145732
  69.6 9.1 %collective-permute-start.4 = (bf16[2,2048]{1,0:T(2,128)(2,1)S(1)}, bf16[2,2048]{1,0:T(2,128)(2,1)S(1)}, u32[]{:S(2)}, u32[]{:S(2)}) collective-permute-start(bf16[2,2048]{1,0:T(2,128)(2,1)S(1)} %slice.256), channel_id=1, source_target_pairs={{0,4},{4,8},{8,12},{12,16},{16,20},{20,24},{24,28},{28,32},{32,36}... | collective-permute-start | bytes 24584 | tf_op jit(solution)/shard_map/ppermute | solution.py:285

commit v7 on v6

--- a/solution.py
+++ b/solution.py
@@ -224,7 +224,7 @@
 
     out_ref[...] = f_ref[...]
     for k, sends in enumerate(plan):
-        send_ref[k] = out_ref[...]
+        send_ref[k] = out_ref[...].astype(send_ref.dtype)
         last = k == len(plan) - 1
         if last:
             out_ref[...] = jnp.zeros_like(out_ref)
@@ -250,10 +250,10 @@
             def _():
                 copy.wait_recv()
                 if power == 0:
-                    out_ref[...] = out_ref[...] + recv_ref[k, i]
+                    out_ref[...] = out_ref[...] + recv_ref[k, i].astype(jnp.float32)
                 else:
                     factor = jnp.exp(r_ref[...] * (-1.0 * rows * power))
-                    out_ref[...] = out_ref[...] + factor * recv_ref[k, i]
+                    out_ref[...] = out_ref[...] + factor * recv_ref[k, i].astype(jnp.float32)
 
         for shift, power, copy in copies:
 
@@ -270,8 +270,8 @@
         out_specs=pl.BlockSpec(memory_space=pltpu.VMEM),
         out_shape=jax.ShapeDtypeStruct(shape, jnp.float32),
         scratch_shapes=[
-            pltpu.VMEM((3,) + shape, jnp.float32),
-            pltpu.VMEM((3, 4) + shape, jnp.float32),
+            pltpu.VMEM((3,) + shape, jnp.bfloat16),
+            pltpu.VMEM((3, 4) + shape, jnp.bfloat16),
             pltpu.SemaphoreType.DMA((3, 4)),
             pltpu.SemaphoreType.DMA((3, 4)),
         ],

time: 139 us -> 126 us (0.906); the launches traced: 137 us -> 125 us
  Pallas kernels: 87.8 us -> 76.3 us
    pallas_call x1, Pallas kernels: 40.2 us -> 28.8 us  [scan_call(): pl.pallas_call(functools.partial(scan_kernel, count, rows), in_specs=[pl....]
where the time goes in v7:
time: 126 us; the launch traced here: 125 us
  Pallas kernels  76.3 us (61%)
  other arithmetic  17.4 us (14%)
  starting transfers between devices  15.2 us (12%)
  waiting for transfers between devices  8.01 us (6%)
  local copies, waits for them, and re-layouts  7.44 us (6%)
    pallas_call x1, Pallas kernels, medium_call(): pl.pallas_call(medium_kernel, grid=grid, in_specs=[pl.BlockSpec((span, bl...  32.4 us
    pallas_call x1, Pallas kernels, scan_call(): pl.pallas_call(functools.partial(scan_kernel, count, rows), in_specs=[pl....  28.8 us
    pallas_call x1, Pallas kernels, modal_out_call(): pl.pallas_call(modal_out_kernel, grid=(width // block,), in_specs=[pl.Blo...  10.5 us
    ppermute x2, starting transfers between devices, passed_along(): lax.ppermute(value, axis, [(source, source + steps) for source in range(f...  10.3 us
    ppermute x2, waiting for transfers between devices, passed_along(): lax.ppermute(value, axis, [(source, source + steps) for source in range(f...  6.81 us
    ppermute x3, starting transfers between devices, body(): lax.ppermute(squares, 'ch', [(source, (source + shift) % ring) for source...  4.89 us
    convert_element_type x1, other arithmetic, body(): late_product = (short_filter(key_medium, short_medium[1]) * short_filter(...  4.77 us
    pallas_call x1, Pallas kernels, modal_end_call(): pl.pallas_call(modal_end_kernel, grid=(width // block,), in_specs=[pl.Blo...  4.71 us
  transfers between devices with their start and end apart: 5, of which 4 were waited for; matrix products, arithmetic and copies ran while one was open for 2% of the time, Pallas kernels for 0%

profile of v7, /device:TPU:25, one launch (start us, length us, event | category | flops | bytes accessed | tf_op | source)
XLA Modules:
  0.0 125.2 jit_solution(12209926541572311550)
XLA Ops:
  0.6 1.0 fusion.8
  1.7 1.4 %fusion.4 = (bf16[2,2048]{1,0:T(2,128)(2,1)}, bf16[2,2048]{1,0:T(2,128)(2,1)}, bf16[2,2048]{1,0:T(2,128)(2,1)}, bf16[2,2048]{1,0:T(2,128)(2,1)}) fusion(bf16[256,2048]{1,0:T(8,128)(2,1)} %param.14, bf16[256,2048]{1,0:T(8,128)(2,1)} %param.15), kind=kLoop, calls=%fused_computation.28 | loop fusion | bytes 65536 | tf_op jit(solution)/shard_map/slice | solution.py:342
  3.1 0.0 copy-start
  3.1 4.8 %multiply_convert_fusion.2 = bf16[254,2048]{1,0:T(8,128)(2,1)S(1)} fusion(bf16[256,2048]{1,0:T(8,128)(2,1)} %param.15, f32[2048]{0:T(1024)S(1)} %bitcast.21, f32[2048]{0:T(1024)S(1)} %bitcast.23, f32[2048]{0:T(1024)S(1)} %bitcast.25, bf16[256,2048]{1,0:T(8,128)(2,1)} %param.14, f32[2048]{0:T(1024)S(1)} %bitcast.27, f32[2048]{0:T(1024)S(1)} %bitcast.29, ...), kind=kLoop, calls=%fused_computation.4 | loop fusion | flops 9363456 | bytes 7331840 | tf_op jit(solution)/shard_map/convert_element_type | solution.py:321
  7.9 0.0 copy-start.3
  7.9 0.0 copy-start.4
  7.9 0.1 slice.246
  8.0 0.0 copy-done
  8.1 1.4 %slice.213 = bf16[2,2048]{1,0:T(2,128)(2,1)} slice(bf16[256,2048]{1,0:T(8,128)(2,1)} %param.20), slice={[254:256], [0:2048]} | slice | bytes 16384 | tf_op jit(solution)/shard_map/slice | solution.py:330
  9.5 1.4 %slice.214 = bf16[2,2048]{1,0:T(2,128)(2,1)} slice(bf16[256,2048]{1,0:T(8,128)(2,1)} %param.21), slice={[254:256], [0:2048]} | slice | bytes 16384 | tf_op jit(solution)/shard_map/slice | solution.py:331
  10.8 1.9 %concatenate.24 = bf16[137,2048]{1,0:T(8,128)(2,1)S(1)} concatenate(bf16[127,2048]{1,0:T(8,128)(2,1)S(1)} %slice.246, bf16[2,2048]{1,0:T(2,128)(2,1)S(1)} %slice.210, bf16[2,2048]{1,0:T(2,128)(2,1)} %get-tuple-element.7, bf16[2,2048]{1,0:T(2,128)(2,1)} %get-tuple-element.35, bf16[2,2048]{1,0:T(2,128)(2,1)} %slice.213, bf16[2,2048]{1,0:T(2,128)(2,1)} %slice.214), dimensions={0} | concatenate | bytes 1122304 | tf_op jit(solution)/shard_map/concatenate | solution.py:324
  12.7 4.1 %collective-permute-start = (bf16[137,2048]{1,0:T(8,128)(2,1)S(1)}, bf16[137,2048]{1,0:T(8,128)(2,1)S(1)}, u32[]{:S(2)}, u32[]{:S(2)}) collective-permute-start(bf16[137,2048]{1,0:T(8,128)(2,1)S(1)} %concatenate.24), channel_id=1, source_target_pairs={{0,4},{4,8},{8,12},{12,16},{16,20},{20,24},{24,28},{28,32},{32,36}... | collective-permute-start | bytes 1683464 | tf_op jit(solution)/shard_map/ppermute | solution.py:285
  16.8 0.0 copy-done.3
  16.9 0.0 copy-done.4
  16.9 0.8 sqrt_multiply_fusion
  17.7 6.0 %collective-permute-done = bf16[137,2048]{1,0:T(8,128)(2,1)S(1)} collective-permute-done((bf16[137,2048]{1,0:T(8,128)(2,1)S(1)}, bf16[137,2048]{1,0:T(8,128)(2,1)S(1)}, u32[]{:S(2)}, u32[]{:S(2)}) %collective-permute-start) | collective-permute-done | bytes 561184 | tf_op jit(solution)/shard_map/ppermute | solution.py:285
  23.7 0.9 multiply_convert_fusion.3
  24.6 1.8 %pad_maximum_fusion.ext_ref = bf16[384,2048]{1,0:T(8,128)(2,1)} fusion(bf16[254,2048]{1,0:T(8,128)(2,1)S(1)} %multiply_convert_fusion.2, bf16[2,2048]{1,0:T(2,128)(2,1)S(1)} %multiply_convert_fusion.3, bf16[127,2048]{1,0:T(8,128)(2,1)S(1)} %slice.247, bf16[384]{0:T(512)(128)(2,1)S(1)} %pad.8.clone), kind=kLoop, calls=%fused_computation.5 | loop fusion | flops 6291456 | bytes 3142400 | tf_op jit(solution)/shard_map/concatenate | solution.py:347
  26.4 2.0 %multiply_add_fusion.1.gate_ref = f32[256,2048]{1,0:T(8,128)} fusion(bf16[256,2048]{1,0:T(8,128)(2,1)S(1)} %copy-done, bf16[2,2048]{1,0:T(2,128)(2,1)S(1)} %get-tuple-element.12, f32[2048]{0:T(1024)S(1)} %bitcast.34, f32[2048]{0:T(1024)S(1)} %bitcast.35, f32[2048]{0:T(1024)S(1)} %bitcast.33), kind=kLoop, calls=%fused_computation.3 | loop fusion | flops 7340032 | bytes 3178496 | tf_op jit(solution)/shard_map/add | solution.py:289
  28.4 0.0 copy-start.5
  28.4 0.0 copy-start.6
  28.4 32.4 %shard_map.140 = (bf16[256,2048]{1,0:T(8,128)(2,1)}, f32[256,128]{1,0:T(8,128)}) custom-call(bf16[384,2048]{1,0:T(8,128)(2,1)} %pad_maximum_fusion.ext_ref, f32[128,2048]{1,0:T(8,128)} %f_ref.1, f32[1,2048]{1,0:T(1,128)} %bitcast.45, f32[256,2048]{1,0:T(8,128)} %multiply_add_fusion.1.gate_ref), custom_call_target="tpu_custom_call" | custom-call | tf_op jit(solution)/shard_map/pallas_call | solution.py:57
  60.8 0.0 copy-start.1
  60.8 1.1 reduce_sum.9
  61.9 1.3 %collective-permute-start.1 = (f32[256]{0:T(256)S(1)}, f32[256]{0:T(256)S(1)}, u32[]{:S(2)}, u32[]{:S(2)}) collective-permute-start(f32[256]{0:T(256)S(1)} %reduce_sum.9), channel_id=1, source_target_pairs={{0,1},{1,2},{2,3},{3,0},{4,5},{5,6},{6,7},{7,4},{8,9},{9,10},{10,1... | collective-permute-start | bytes 3080 | tf_op jit(solution)/shard_map/ppermute | solution.py:355
  63.2 2.5 %collective-permute-start.2 = (f32[256]{0:T(256)S(1)}, f32[256]{0:T(256)S(1)}, u32[]{:S(2)}, u32[]{:S(2)}) collective-permute-start(f32[256]{0:T(256)S(1)} %reduce_sum.9), channel_id=1, source_target_pairs={{0,2},{1,3},{2,0},{3,1},{4,6},{5,7},{6,4},{7,5},{8,10},{9,11},{10,... | collective-permute-start | bytes 3080 | tf_op jit(solution)/shard_map/ppermute | solution.py:355
  65.7 1.2 collective-permute-start.3
  66.8 0.0 copy-done.5
  66.8 0.1 fusion.7
  66.9 0.0 collective-permute-done.1
  66.9 0.3 collective-permute-done.2
  67.1 0.9 collective-permute-done.3
  68.1 0.0 copy-done.6
  68.1 1.5 %multiply_convert_fusion.1 = bf16[256,2048]{1,0:T(8,128)(2,1)S(1)} fusion(bf16[256,2048]{1,0:T(8,128)(2,1)} %get-tuple-element.2, f32[256]{0:T(256)S(1)} %add_rsqrt_fusion, f32[2048]{0:T(1024)S(1)} %copy-done.6), kind=kLoop, calls=%fused_computation.2 | loop fusion | flops 2097152 | bytes 2106368 | tf_op jit(solution)/shard_map/convert_element_type | solution.py:359
  69.6 0.0 copy-start.2
  69.6 6.2 %collective-permute-start.4 = (bf16[2,2048]{1,0:T(2,128)(2,1)S(1)}, bf16[2,2048]{1,0:T(2,128)(2,1)S(1)}, u32[]{:S(2)}, u32[]{:S(2)}) collective-permute-start(bf16[2,2048]{1,0:T(2,128)(2,1)S(1)} %slice.256), channel_id=1, source_target_pairs={{0,4},{4,8},{8,12},{12,16},{16,20},{20,24},{24,28},{28,32},{32,36}... | collective-permute-start | bytes 24584 | tf_op jit(solution)/shard_map/ppermute | solution.py:285
  75.9 0.0 copy-done.1
  75.9 2.0 %multiply_add_fusion.gate_ref = f32[256,2048]{1,0:T(8,128)} fusion(bf16[256,2048]{1,0:T(8,128)(2,1)S(1)} %copy-done.1, bf16[2,2048]{1,0:T(2,128)(2,1)S(1)} %get-tuple-element.10, f32[2048]{0:T(1024)S(1)} %bitcast.43, f32[2048]{0:T(1024)S(1)} %bitcast.44, f32[2048]{0:T(1024)S(1)} %bitcast.42), kind=kLoop, calls=%fused_computation | loop fusion | flops 7340032 | bytes 3178496 | tf_op jit(solution)/shard_map/add | solution.py:289
  77.9 0.8 collective-permute-done.4
  78.7 0.0 copy-done.2
  78.7 2.5 %multiply_convert_fusion.p_ref = bf16[256,2048]{1,0:T(8,128)(2,1)} fusion(bf16[256,2048]{1,0:T(8,128)(2,1)S(1)} %multiply_convert_fusion.1, bf16[256,2048]{1,0:T(8,128)(2,1)S(1)} %copy-done.2, bf16[2,2048]{1,0:T(2,128)(2,1)S(1)} %collective-permute-done.4, bf16[2,2048]{1,0:T(2,128)(2,1)S(1)} %get-tuple-element.11, f32[2048]{0:T(1024)S(1)} %bitcast.36, ...), kind=kLoop, calls=%fused_computation.1 | loop fusion | flops 15728640 | bytes 3211264 | tf_op jit(solution)/shard_map/convert_element_type | solution.py:364
  81.3 4.7 %shard_map.141.f_ref = f32[16,2048]{1,0:T(8,128)} custom-call(bf16[256,2048]{1,0:T(8,128)(2,1)} %multiply_convert_fusion.p_ref, f32[16,2048]{1,0:T(8,128)} %get-tuple-element.16.e_ref), custom_call_target="tpu_custom_call" | custom-call | tf_op jit(solution)/shard_map/pallas_call | solution.py:121
  86.0 28.8 %shard_map.142.s_ref = f32[16,2048]{1,0:T(8,128)} custom-call(f32[16,2048]{1,0:T(8,128)} %shard_map.141.f_ref, f32[16,2048]{1,0:T(8,128)} %r_ref.1), custom_call_target="tpu_custom_call" | custom-call | tf_op jit(solution)/shard_map/pallas_call | solution.py:267
  114.7 10.5 %shard_map.143 = bf16[256,2048]{1,0:T(8,128)(2,1)} custom-call(bf16[256,2048]{1,0:T(8,128)(2,1)} %multiply_convert_fusion.p_ref, f32[16,2048]{1,0:T(8,128)} %get-tuple-element.16.e_ref, f32[16,2048]{1,0:T(8,128)} %get-tuple-element.15.w_ref, f32[16,2048]{1,0:T(8,128)} %shard_map.142.s_ref, f32[1,2048]{1,0:T(1,128)} %bitcast.46, ...), custom_call_target="tpu_custom_call" | custom-call | tf_op jit(solution)/shard_map/pallas_call | solution.py:181
  (6 shorter events, 0.1 us)
Async XLA Ops:
  3.1 4.9 %copy-start = (bf16[256,2048]{1,0:T(8,128)(2,1)S(1)}, bf16[256,2048]{1,0:T(8,128)(2,1)}, u32[]{:S(2)}) copy-start(bf16[256,2048]{1,0:T(8,128)(2,1)} %param.13) | copy-start | bytes 3145732
  7.9 9.0 %copy-start.3 = (f32[16,2048]{1,0:T(8,128)S(1)}, f32[16,2048]{1,0:T(8,128)}, u32[]{:S(2)}) copy-start(f32[16,2048]{1,0:T(8,128)} %r_ref.1) | copy-start | bytes 393220
  7.9 9.0 %copy-start.4 = (f32[16,2048]{1,0:T(8,128)S(1)}, f32[16,2048]{1,0:T(8,128)}, u32[]{:S(2)}) copy-start(f32[16,2048]{1,0:T(8,128)} %param.24) | copy-start | bytes 393220
  12.7 10.9 %collective-permute-start = (bf16[137,2048]{1,0:T(8,128)(2,1)S(1)}, bf16[137,2048]{1,0:T(8,128)(2,1)S(1)}, u32[]{:S(2)}, u32[]{:S(2)}) collective-permute-start(bf16[137,2048]{1,0:T(8,128)(2,1)S(1)} %concatenate.24), channel_id=1, source_target_pairs={{0,4},{4,8},{8,12},{12,16},{16,20},{20,24},{24,28},{28,32},{32,36}... | collective-permute-start | bytes 1683464 | tf_op jit(solution)/shard_map/ppermute | solution.py:285
  28.4 38.4 %copy-start.5 = (f32[3,3,2048]{2,1,0:T(4,128)S(1)}, f32[3,3,2048]{2,1,0:T(4,128)}, u32[]{:S(2)}) copy-start(f32[3,3,2048]{2,1,0:T(4,128)} %param.22) | copy-start | bytes 221188
  28.4 39.7 %copy-start.6 = (f32[2048]{0:T(1024)S(1)}, f32[2048]{0:T(1024)}, u32[]{:S(2)}) copy-start(f32[2048]{0:T(1024)} %param.19) | copy-start | bytes 24580
  60.8 15.1 %copy-start.1 = (bf16[256,2048]{1,0:T(8,128)(2,1)S(1)}, bf16[256,2048]{1,0:T(8,128)(2,1)}, u32[]{:S(2)}) copy-start(bf16[256,2048]{1,0:T(8,128)(2,1)} %param.20) | copy-start | bytes 3145732
  61.9 5.0 %collective-permute-start.1 = (f32[256]{0:T(256)S(1)}, f32[256]{0:T(256)S(1)}, u32[]{:S(2)}, u32[]{:S(2)}) collective-permute-start(f32[256]{0:T(256)S(1)} %reduce_sum.9), channel_id=1, source_target_pairs={{0,1},{1,2},{2,3},{3,0},{4,5},{5,6},{6,7},{7,4},{8,9},{9,10},{10,1... | collective-permute-start | bytes 3080 | tf_op jit(solution)/shard_map/ppermute | solution.py:355
  63.2 3.9 %collective-permute-start.2 = (f32[256]{0:T(256)S(1)}, f32[256]{0:T(256)S(1)}, u32[]{:S(2)}, u32[]{:S(2)}) collective-permute-start(f32[256]{0:T(256)S(1)} %reduce_sum.9), channel_id=1, source_target_pairs={{0,2},{1,3},{2,0},{3,1},{4,6},{5,7},{6,4},{7,5},{8,10},{9,11},{10,... | collective-permute-start | bytes 3080 | tf_op jit(solution)/shard_map/ppermute | solution.py:355
  65.7 2.4 %collective-permute-start.3 = (f32[256]{0:T(256)S(1)}, f32[256]{0:T(256)S(1)}, u32[]{:S(2)}, u32[]{:S(2)}) collective-permute-start(f32[256]{0:T(256)S(1)} %reduce_sum.9), channel_id=1, source_target_pairs={{0,3},{1,0},{2,1},{3,2},{4,7},{5,4},{6,5},{7,6},{8,11},{9,8},{10,9... | collective-permute-start | bytes 3080 | tf_op jit(solution)/shard_map/ppermute | solution.py:355
  69.6 9.1 %copy-start.2 = (bf16[256,2048]{1,0:T(8,128)(2,1)S(1)}, bf16[256,2048]{1,0:T(8,128)(2,1)}, u32[]{:S(2)}) copy-start(bf16[256,2048]{1,0:T(8,128)(2,1)} %param.21) | copy-start | bytes 3145732
  69.6 9.1 %collective-permute-start.4 = (bf16[2,2048]{1,0:T(2,128)(2,1)S(1)}, bf16[2,2048]{1,0:T(2,128)(2,1)S(1)}, u32[]{:S(2)}, u32[]{:S(2)}) collective-permute-start(bf16[2,2048]{1,0:T(2,128)(2,1)S(1)} %slice.256), channel_id=1, source_target_pairs={{0,4},{4,8},{8,12},{12,16},{16,20},{20,24},{24,28},{28,32},{32,36}... | collective-permute-start | bytes 24584 | tf_op jit(solution)/shard_map/ppermute | solution.py:285

commit v8 on v7

--- a/solution.py
+++ b/solution.py
@@ -198,8 +198,12 @@
     )(product, decay, weight, start, skip, gate_feat)
 
 
+PIECES = 4
+
+
 def scan_kernel(count, rows, f_ref, r_ref, out_ref, send_ref, recv_ref, send_sem, recv_sem):
     me = lax.axis_index("ctx")
+    piece = out_ref.shape[1] // PIECES
     plan = []
     span = 1
     while span * 4 < count:
@@ -230,36 +234,44 @@
             out_ref[...] = jnp.zeros_like(out_ref)
         copies = []
         for i, (shift, power) in enumerate(sends):
-            copy = pltpu.make_async_remote_copy(
-                src_ref=send_ref.at[k],
-                dst_ref=recv_ref.at[k, i],
-                send_sem=send_sem.at[k, i],
-                recv_sem=recv_sem.at[k, i],
-                device_id={"ctx": me + shift},
-                device_id_type=pl.DeviceIdType.MESH,
-            )
-            copies.append((shift, power, copy))
+            parts = []
+            for c in range(PIECES):
+                lanes = pl.ds(c * piece, piece)
+                parts.append(
+                    pltpu.make_async_remote_copy(
+                        src_ref=send_ref.at[k, :, lanes],
+                        dst_ref=recv_ref.at[k, i, :, lanes],
+                        send_sem=send_sem.at[k, i, c],
+                        recv_sem=recv_sem.at[k, i, c],
+                        device_id={"ctx": me + shift},
+                        device_id_type=pl.DeviceIdType.MESH,
+                    )
+                )
+            copies.append((shift, power, parts))
 
             @pl.when(me + shift < count)
             def _():
-                copy.start()
-
-        for i, (shift, power, copy) in enumerate(copies):
+                for part in parts:
+                    part.start()
+
+        for i, (shift, power, parts) in enumerate(copies):
 
             @pl.when(me >= shift)
             def _():
-                copy.wait_recv()
+                for part in parts:
+                    part.wait_recv()
                 if power == 0:
                     out_ref[...] = out_ref[...] + recv_ref[k, i].astype(jnp.float32)
                 else:
                     factor = jnp.exp(r_ref[...] * (-1.0 * rows * power))
                     out_ref[...] = out_ref[...] + factor * recv_ref[k, i].astype(jnp.float32)
 
-        for shift, power, copy in copies:
+        for shift, power, parts in copies:
 
             @pl.when(me + shift < count)
             def _():
-                copy.wait_send()
+                for part in parts:
+                    part.wait_send()
 
 
 def scan_call(final_state, decay_rates, count, rows):
@@ -272,8 +284,8 @@
         scratch_shapes=[
             pltpu.VMEM((3,) + shape, jnp.bfloat16),
             pltpu.VMEM((3, 4) + shape, jnp.bfloat16),
-            pltpu.SemaphoreType.DMA((3, 4)),
-            pltpu.SemaphoreType.DMA((3, 4)),
+            pltpu.SemaphoreType.DMA((3, 4, PIECES)),
+            pltpu.SemaphoreType.DMA((3, 4, PIECES)),
         ],
         compiler_params=pltpu.CompilerParams(collective_id=0, has_side_effects=True),
     )(final_state, decay_rates)

time: 126 us -> 127 us (level)
  no operation moved by 1% of the time
where the time goes in v8:
time: 127 us; the launch traced here: 126 us
  Pallas kernels  77.2 us (61%)
  other arithmetic  17.4 us (14%)
  starting transfers between devices  15.2 us (12%)
  waiting for transfers between devices  8.01 us (6%)
  local copies, waits for them, and re-layouts  7.44 us (6%)
    pallas_call x1, Pallas kernels, medium_call(): pl.pallas_call(medium_kernel, grid=grid, in_specs=[pl.BlockSpec((span, bl...  32.4 us
    pallas_call x1, Pallas kernels, scan_call(): pl.pallas_call(functools.partial(scan_kernel, count, rows), in_specs=[pl....  29.6 us
    pallas_call x1, Pallas kernels, modal_out_call(): pl.pallas_call(modal_out_kernel, grid=(width // block,), in_specs=[pl.Blo...  10.5 us
    ppermute x2, starting transfers between devices, passed_along(): lax.ppermute(value, axis, [(source, source + steps) for source in range(f...  10.3 us
    ppermute x2, waiting for transfers between devices, passed_along(): lax.ppermute(value, axis, [(source, source + steps) for source in range(f...  6.81 us
    ppermute x3, starting transfers between devices, body(): lax.ppermute(squares, 'ch', [(source, (source + shift) % ring) for source...  4.89 us
    convert_element_type x1, other arithmetic, body(): late_product = (short_filter(key_medium, short_medium[1]) * short_filter(...  4.77 us
    pallas_call x1, Pallas kernels, modal_end_call(): pl.pallas_call(modal_end_kernel, grid=(width // block,), in_specs=[pl.Blo...  4.71 us
  transfers between devices with their start and end apart: 5, of which 4 were waited for; matrix products, arithmetic and copies ran while one was open for 2% of the time, Pallas kernels for 0%

profile of v8, /device:TPU:25, one launch (start us, length us, event | category | flops | bytes accessed | tf_op | source)
XLA Modules:
  0.0 126.0 jit_solution(14640855585859450188)
XLA Ops:
  0.6 1.0 fusion.8
  1.7 1.4 %fusion.4 = (bf16[2,2048]{1,0:T(2,128)(2,1)}, bf16[2,2048]{1,0:T(2,128)(2,1)}, bf16[2,2048]{1,0:T(2,128)(2,1)}, bf16[2,2048]{1,0:T(2,128)(2,1)}) fusion(bf16[256,2048]{1,0:T(8,128)(2,1)} %param.14, bf16[256,2048]{1,0:T(8,128)(2,1)} %param.15), kind=kLoop, calls=%fused_computation.28 | loop fusion | bytes 65536 | tf_op jit(solution)/shard_map/slice | solution.py:354
  3.1 0.0 copy-start
  3.1 4.8 %multiply_convert_fusion.2 = bf16[254,2048]{1,0:T(8,128)(2,1)S(1)} fusion(bf16[256,2048]{1,0:T(8,128)(2,1)} %param.15, f32[2048]{0:T(1024)S(1)} %bitcast.21, f32[2048]{0:T(1024)S(1)} %bitcast.23, f32[2048]{0:T(1024)S(1)} %bitcast.25, bf16[256,2048]{1,0:T(8,128)(2,1)} %param.14, f32[2048]{0:T(1024)S(1)} %bitcast.27, f32[2048]{0:T(1024)S(1)} %bitcast.29, ...), kind=kLoop, calls=%fused_computation.4 | loop fusion | flops 9363456 | bytes 7331840 | tf_op jit(solution)/shard_map/convert_element_type | solution.py:333
  7.9 0.0 copy-start.3
  7.9 0.0 copy-start.4
  7.9 0.1 slice.246
  8.0 0.0 copy-done
  8.1 1.4 %slice.213 = bf16[2,2048]{1,0:T(2,128)(2,1)} slice(bf16[256,2048]{1,0:T(8,128)(2,1)} %param.20), slice={[254:256], [0:2048]} | slice | bytes 16384 | tf_op jit(solution)/shard_map/slice | solution.py:342
  9.5 1.4 %slice.214 = bf16[2,2048]{1,0:T(2,128)(2,1)} slice(bf16[256,2048]{1,0:T(8,128)(2,1)} %param.21), slice={[254:256], [0:2048]} | slice | bytes 16384 | tf_op jit(solution)/shard_map/slice | solution.py:343
  10.8 1.9 %concatenate.24 = bf16[137,2048]{1,0:T(8,128)(2,1)S(1)} concatenate(bf16[127,2048]{1,0:T(8,128)(2,1)S(1)} %slice.246, bf16[2,2048]{1,0:T(2,128)(2,1)S(1)} %slice.210, bf16[2,2048]{1,0:T(2,128)(2,1)} %get-tuple-element.7, bf16[2,2048]{1,0:T(2,128)(2,1)} %get-tuple-element.35, bf16[2,2048]{1,0:T(2,128)(2,1)} %slice.213, bf16[2,2048]{1,0:T(2,128)(2,1)} %slice.214), dimensions={0} | concatenate | bytes 1122304 | tf_op jit(solution)/shard_map/concatenate | solution.py:336
  12.7 4.1 %collective-permute-start = (bf16[137,2048]{1,0:T(8,128)(2,1)S(1)}, bf16[137,2048]{1,0:T(8,128)(2,1)S(1)}, u32[]{:S(2)}, u32[]{:S(2)}) collective-permute-start(bf16[137,2048]{1,0:T(8,128)(2,1)S(1)} %concatenate.24), channel_id=1, source_target_pairs={{0,4},{4,8},{8,12},{12,16},{16,20},{20,24},{24,28},{28,32},{32,36}... | collective-permute-start | bytes 1683464 | tf_op jit(solution)/shard_map/ppermute | solution.py:297
  16.8 0.0 copy-done.3
  16.9 0.0 copy-done.4
  16.9 0.8 sqrt_multiply_fusion
  17.7 6.0 %collective-permute-done = bf16[137,2048]{1,0:T(8,128)(2,1)S(1)} collective-permute-done((bf16[137,2048]{1,0:T(8,128)(2,1)S(1)}, bf16[137,2048]{1,0:T(8,128)(2,1)S(1)}, u32[]{:S(2)}, u32[]{:S(2)}) %collective-permute-start) | collective-permute-done | bytes 561184 | tf_op jit(solution)/shard_map/ppermute | solution.py:297
  23.7 0.9 multiply_convert_fusion.3
  24.6 1.8 %pad_maximum_fusion.ext_ref = bf16[384,2048]{1,0:T(8,128)(2,1)} fusion(bf16[254,2048]{1,0:T(8,128)(2,1)S(1)} %multiply_convert_fusion.2, bf16[2,2048]{1,0:T(2,128)(2,1)S(1)} %multiply_convert_fusion.3, bf16[127,2048]{1,0:T(8,128)(2,1)S(1)} %slice.247, bf16[384]{0:T(512)(128)(2,1)S(1)} %pad.8.clone), kind=kLoop, calls=%fused_computation.5 | loop fusion | flops 6291456 | bytes 3142400 | tf_op jit(solution)/shard_map/concatenate | solution.py:359
  26.4 2.0 %multiply_add_fusion.1.gate_ref = f32[256,2048]{1,0:T(8,128)} fusion(bf16[256,2048]{1,0:T(8,128)(2,1)S(1)} %copy-done, bf16[2,2048]{1,0:T(2,128)(2,1)S(1)} %get-tuple-element.12, f32[2048]{0:T(1024)S(1)} %bitcast.34, f32[2048]{0:T(1024)S(1)} %bitcast.35, f32[2048]{0:T(1024)S(1)} %bitcast.33), kind=kLoop, calls=%fused_computation.3 | loop fusion | flops 7340032 | bytes 3178496 | tf_op jit(solution)/shard_map/add | solution.py:301
  28.4 0.0 copy-start.5
  28.4 0.0 copy-start.6
  28.4 32.4 %shard_map.140 = (bf16[256,2048]{1,0:T(8,128)(2,1)}, f32[256,128]{1,0:T(8,128)}) custom-call(bf16[384,2048]{1,0:T(8,128)(2,1)} %pad_maximum_fusion.ext_ref, f32[128,2048]{1,0:T(8,128)} %f_ref.1, f32[1,2048]{1,0:T(1,128)} %bitcast.45, f32[256,2048]{1,0:T(8,128)} %multiply_add_fusion.1.gate_ref), custom_call_target="tpu_custom_call" | custom-call | tf_op jit(solution)/shard_map/pallas_call | solution.py:57
  60.8 0.0 copy-start.1
  60.8 1.1 reduce_sum.9
  61.9 1.3 %collective-permute-start.1 = (f32[256]{0:T(256)S(1)}, f32[256]{0:T(256)S(1)}, u32[]{:S(2)}, u32[]{:S(2)}) collective-permute-start(f32[256]{0:T(256)S(1)} %reduce_sum.9), channel_id=1, source_target_pairs={{0,1},{1,2},{2,3},{3,0},{4,5},{5,6},{6,7},{7,4},{8,9},{9,10},{10,1... | collective-permute-start | bytes 3080 | tf_op jit(solution)/shard_map/ppermute | solution.py:367
  63.2 2.5 %collective-permute-start.2 = (f32[256]{0:T(256)S(1)}, f32[256]{0:T(256)S(1)}, u32[]{:S(2)}, u32[]{:S(2)}) collective-permute-start(f32[256]{0:T(256)S(1)} %reduce_sum.9), channel_id=1, source_target_pairs={{0,2},{1,3},{2,0},{3,1},{4,6},{5,7},{6,4},{7,5},{8,10},{9,11},{10,... | collective-permute-start | bytes 3080 | tf_op jit(solution)/shard_map/ppermute | solution.py:367
  65.7 1.2 collective-permute-start.3
  66.8 0.0 copy-done.5
  66.8 0.1 fusion.7
  66.9 0.0 collective-permute-done.1
  66.9 0.3 collective-permute-done.2
  67.1 0.9 collective-permute-done.3
  68.1 0.0 copy-done.6
  68.1 1.5 %multiply_convert_fusion.1 = bf16[256,2048]{1,0:T(8,128)(2,1)S(1)} fusion(bf16[256,2048]{1,0:T(8,128)(2,1)} %get-tuple-element.2, f32[256]{0:T(256)S(1)} %add_rsqrt_fusion, f32[2048]{0:T(1024)S(1)} %copy-done.6), kind=kLoop, calls=%fused_computation.2 | loop fusion | flops 2097152 | bytes 2106368 | tf_op jit(solution)/shard_map/convert_element_type | solution.py:371
  69.6 0.0 copy-start.2
  69.6 6.2 %collective-permute-start.4 = (bf16[2,2048]{1,0:T(2,128)(2,1)S(1)}, bf16[2,2048]{1,0:T(2,128)(2,1)S(1)}, u32[]{:S(2)}, u32[]{:S(2)}) collective-permute-start(bf16[2,2048]{1,0:T(2,128)(2,1)S(1)} %slice.256), channel_id=1, source_target_pairs={{0,4},{4,8},{8,12},{12,16},{16,20},{20,24},{24,28},{28,32},{32,36}... | collective-permute-start | bytes 24584 | tf_op jit(solution)/shard_map/ppermute | solution.py:297
  75.9 0.0 copy-done.1
  75.9 2.0 %multiply_add_fusion.gate_ref = f32[256,2048]{1,0:T(8,128)} fusion(bf16[256,2048]{1,0:T(8,128)(2,1)S(1)} %copy-done.1, bf16[2,2048]{1,0:T(2,128)(2,1)S(1)} %get-tuple-element.10, f32[2048]{0:T(1024)S(1)} %bitcast.43, f32[2048]{0:T(1024)S(1)} %bitcast.44, f32[2048]{0:T(1024)S(1)} %bitcast.42), kind=kLoop, calls=%fused_computation | loop fusion | flops 7340032 | bytes 3178496 | tf_op jit(solution)/shard_map/add | solution.py:301
  77.9 0.8 collective-permute-done.4
  78.7 0.0 copy-done.2
  78.7 2.5 %multiply_convert_fusion.p_ref = bf16[256,2048]{1,0:T(8,128)(2,1)} fusion(bf16[256,2048]{1,0:T(8,128)(2,1)S(1)} %multiply_convert_fusion.1, bf16[256,2048]{1,0:T(8,128)(2,1)S(1)} %copy-done.2, bf16[2,2048]{1,0:T(2,128)(2,1)S(1)} %collective-permute-done.4, bf16[2,2048]{1,0:T(2,128)(2,1)S(1)} %get-tuple-element.11, f32[2048]{0:T(1024)S(1)} %bitcast.36, ...), kind=kLoop, calls=%fused_computation.1 | loop fusion | flops 15728640 | bytes 3211264 | tf_op jit(solution)/shard_map/convert_element_type | solution.py:376
  81.3 4.7 %shard_map.141.f_ref = f32[16,2048]{1,0:T(8,128)} custom-call(bf16[256,2048]{1,0:T(8,128)(2,1)} %multiply_convert_fusion.p_ref, f32[16,2048]{1,0:T(8,128)} %get-tuple-element.16.e_ref), custom_call_target="tpu_custom_call" | custom-call | tf_op jit(solution)/shard_map/pallas_call | solution.py:121
  86.0 29.6 %shard_map.142.s_ref = f32[16,2048]{1,0:T(8,128)} custom-call(f32[16,2048]{1,0:T(8,128)} %shard_map.141.f_ref, f32[16,2048]{1,0:T(8,128)} %r_ref.1), custom_call_target="tpu_custom_call" | custom-call | tf_op jit(solution)/shard_map/pallas_call | solution.py:279
  115.6 10.5 %shard_map.143 = bf16[256,2048]{1,0:T(8,128)(2,1)} custom-call(bf16[256,2048]{1,0:T(8,128)(2,1)} %multiply_convert_fusion.p_ref, f32[16,2048]{1,0:T(8,128)} %get-tuple-element.16.e_ref, f32[16,2048]{1,0:T(8,128)} %get-tuple-element.15.w_ref, f32[16,2048]{1,0:T(8,128)} %shard_map.142.s_ref, f32[1,2048]{1,0:T(1,128)} %bitcast.46, ...), custom_call_target="tpu_custom_call" | custom-call | tf_op jit(solution)/shard_map/pallas_call | solution.py:181
  (6 shorter events, 0.1 us)
Async XLA Ops:
  3.1 4.9 %copy-start = (bf16[256,2048]{1,0:T(8,128)(2,1)S(1)}, bf16[256,2048]{1,0:T(8,128)(2,1)}, u32[]{:S(2)}) copy-start(bf16[256,2048]{1,0:T(8,128)(2,1)} %param.13) | copy-start | bytes 3145732
  7.9 9.0 %copy-start.3 = (f32[16,2048]{1,0:T(8,128)S(1)}, f32[16,2048]{1,0:T(8,128)}, u32[]{:S(2)}) copy-start(f32[16,2048]{1,0:T(8,128)} %r_ref.1) | copy-start | bytes 393220
  7.9 9.0 %copy-start.4 = (f32[16,2048]{1,0:T(8,128)S(1)}, f32[16,2048]{1,0:T(8,128)}, u32[]{:S(2)}) copy-start(f32[16,2048]{1,0:T(8,128)} %param.24) | copy-start | bytes 393220
  12.7 10.9 %collective-permute-start = (bf16[137,2048]{1,0:T(8,128)(2,1)S(1)}, bf16[137,2048]{1,0:T(8,128)(2,1)S(1)}, u32[]{:S(2)}, u32[]{:S(2)}) collective-permute-start(bf16[137,2048]{1,0:T(8,128)(2,1)S(1)} %concatenate.24), channel_id=1, source_target_pairs={{0,4},{4,8},{8,12},{12,16},{16,20},{20,24},{24,28},{28,32},{32,36}... | collective-permute-start | bytes 1683464 | tf_op jit(solution)/shard_map/ppermute | solution.py:297
  28.4 38.4 %copy-start.5 = (f32[3,3,2048]{2,1,0:T(4,128)S(1)}, f32[3,3,2048]{2,1,0:T(4,128)}, u32[]{:S(2)}) copy-start(f32[3,3,2048]{2,1,0:T(4,128)} %param.22) | copy-start | bytes 221188
  28.4 39.7 %copy-start.6 = (f32[2048]{0:T(1024)S(1)}, f32[2048]{0:T(1024)}, u32[]{:S(2)}) copy-start(f32[2048]{0:T(1024)} %param.19) | copy-start | bytes 24580
  60.8 15.1 %copy-start.1 = (bf16[256,2048]{1,0:T(8,128)(2,1)S(1)}, bf16[256,2048]{1,0:T(8,128)(2,1)}, u32[]{:S(2)}) copy-start(bf16[256,2048]{1,0:T(8,128)(2,1)} %param.20) | copy-start | bytes 3145732
  61.9 5.0 %collective-permute-start.1 = (f32[256]{0:T(256)S(1)}, f32[256]{0:T(256)S(1)}, u32[]{:S(2)}, u32[]{:S(2)}) collective-permute-start(f32[256]{0:T(256)S(1)} %reduce_sum.9), channel_id=1, source_target_pairs={{0,1},{1,2},{2,3},{3,0},{4,5},{5,6},{6,7},{7,4},{8,9},{9,10},{10,1... | collective-permute-start | bytes 3080 | tf_op jit(solution)/shard_map/ppermute | solution.py:367
  63.2 3.9 %collective-permute-start.2 = (f32[256]{0:T(256)S(1)}, f32[256]{0:T(256)S(1)}, u32[]{:S(2)}, u32[]{:S(2)}) collective-permute-start(f32[256]{0:T(256)S(1)} %reduce_sum.9), channel_id=1, source_target_pairs={{0,2},{1,3},{2,0},{3,1},{4,6},{5,7},{6,4},{7,5},{8,10},{9,11},{10,... | collective-permute-start | bytes 3080 | tf_op jit(solution)/shard_map/ppermute | solution.py:367
  65.7 2.4 %collective-permute-start.3 = (f32[256]{0:T(256)S(1)}, f32[256]{0:T(256)S(1)}, u32[]{:S(2)}, u32[]{:S(2)}) collective-permute-start(f32[256]{0:T(256)S(1)} %reduce_sum.9), channel_id=1, source_target_pairs={{0,3},{1,0},{2,1},{3,2},{4,7},{5,4},{6,5},{7,6},{8,11},{9,8},{10,9... | collective-permute-start | bytes 3080 | tf_op jit(solution)/shard_map/ppermute | solution.py:367
  69.6 9.1 %copy-start.2 = (bf16[256,2048]{1,0:T(8,128)(2,1)S(1)}, bf16[256,2048]{1,0:T(8,128)(2,1)}, u32[]{:S(2)}) copy-start(bf16[256,2048]{1,0:T(8,128)(2,1)} %param.21) | copy-start | bytes 3145732
  69.6 9.1 %collective-permute-start.4 = (bf16[2,2048]{1,0:T(2,128)(2,1)S(1)}, bf16[2,2048]{1,0:T(2,128)(2,1)S(1)}, u32[]{:S(2)}, u32[]{:S(2)}) collective-permute-start(bf16[2,2048]{1,0:T(2,128)(2,1)S(1)} %slice.256), channel_id=1, source_target_pairs={{0,4},{4,8},{8,12},{12,16},{16,20},{20,24},{24,28},{28,32},{32,36}... | collective-permute-start | bytes 24584 | tf_op jit(solution)/shard_map/ppermute | solution.py:297

commit v9 on v7

--- a/solution.py
+++ b/solution.py
@@ -200,12 +200,11 @@
 
 def scan_kernel(count, rows, f_ref, r_ref, out_ref, send_ref, recv_ref, send_sem, recv_sem):
     me = lax.axis_index("ctx")
-    plan = []
+    plan = [[(1, 0)]]
     span = 1
-    while span * 4 < count:
-        plan.append([(span * i, span * i) for i in range(1, 4)])
-        span *= 4
-    plan.append([(1 + span * i, span * i) for i in range(count // span)])
+    while span < count:
+        plan.append([(span, span)])
+        span *= 2
     barrier = pltpu.get_barrier_semaphore()
     partners = sorted({shift for sends in plan for shift, _ in sends})
     for shift in partners:
@@ -225,8 +224,7 @@
     out_ref[...] = f_ref[...]
     for k, sends in enumerate(plan):
         send_ref[k] = out_ref[...].astype(send_ref.dtype)
-        last = k == len(plan) - 1
-        if last:
+        if k == 0:
             out_ref[...] = jnp.zeros_like(out_ref)
         copies = []
         for i, (shift, power) in enumerate(sends):
@@ -264,16 +262,19 @@
 
 def scan_call(final_state, decay_rates, count, rows):
     shape = final_state.shape
+    rounds = 1
+    while (1 << (rounds - 1)) < count:
+        rounds += 1
     return pl.pallas_call(
         functools.partial(scan_kernel, count, rows),
         in_specs=[pl.BlockSpec(memory_space=pltpu.VMEM)] * 2,
         out_specs=pl.BlockSpec(memory_space=pltpu.VMEM),
         out_shape=jax.ShapeDtypeStruct(shape, jnp.float32),
         scratch_shapes=[
-            pltpu.VMEM((3,) + shape, jnp.bfloat16),
-            pltpu.VMEM((3, 4) + shape, jnp.bfloat16),
-            pltpu.SemaphoreType.DMA((3, 4)),
-            pltpu.SemaphoreType.DMA((3, 4)),
+            pltpu.VMEM((rounds,) + shape, jnp.bfloat16),
+            pltpu.VMEM((rounds, 1) + shape, jnp.bfloat16),
+            pltpu.SemaphoreType.DMA((rounds, 1)),
+            pltpu.SemaphoreType.DMA((rounds, 1)),
         ],
         compiler_params=pltpu.CompilerParams(collective_id=0, has_side_effects=True),
     )(final_state, decay_rates)

time: 126 us -> 131 us (1.040)
  the two profiles are of different devices: /device:TPU:25 before, /device:TPU:24 now
where the time goes in v9:
time: 131 us
  Pallas kernels  78 us (60%)
  other arithmetic  17.4 us (13%)
  waiting for transfers between devices  17.4 us (13%)
  starting transfers between devices  9.7 us (7%)
  local copies, waits for them, and re-layouts  7.44 us (6%)
    pallas_call x1, Pallas kernels, medium_call(): pl.pallas_call(medium_kernel, grid=grid, in_specs=[pl.BlockSpec((span, bl...  32.4 us
    pallas_call x1, Pallas kernels, scan_call(): pl.pallas_call(functools.partial(scan_kernel, count, rows), in_specs=[pl....  30.4 us
    ppermute x2, waiting for transfers between devices, passed_along(): lax.ppermute(value, axis, [(source, source + steps) for source in range(f...  15.3 us
    pallas_call x1, Pallas kernels, modal_out_call(): pl.pallas_call(modal_out_kernel, grid=(width // block,), in_specs=[pl.Blo...  10.5 us
    ppermute x3, starting transfers between devices, body(): lax.ppermute(squares, 'ch', [(source, (source + shift) % ring) for source...  5.73 us
    convert_element_type x1, other arithmetic, body(): late_product = (short_filter(key_medium, short_medium[1]) * short_filter(...  4.77 us
    pallas_call x1, Pallas kernels, modal_end_call(): pl.pallas_call(modal_end_kernel, grid=(width // block,), in_specs=[pl.Blo...  4.71 us
    add x2, other arithmetic, short_filter(): weights[0] * extended[2:] + weights[1] * extended[1:-1]  4.05 us
  transfers between devices with their start and end apart: 5, of which 4 were waited for; matrix products, arithmetic and copies ran while one was open for 2% of the time, Pallas kernels for 0%

profile of v9, /device:TPU:24, one launch (start us, length us, event | category | flops | bytes accessed | tf_op | source)
XLA Modules:
  0.0 130.7 jit_solution(4812806750649733587)
XLA Ops:
  0.6 1.0 fusion.8
  1.7 1.4 %fusion.4 = (bf16[2,2048]{1,0:T(2,128)(2,1)}, bf16[2,2048]{1,0:T(2,128)(2,1)}, bf16[2,2048]{1,0:T(2,128)(2,1)}, bf16[2,2048]{1,0:T(2,128)(2,1)}) fusion(bf16[256,2048]{1,0:T(8,128)(2,1)} %param.14, bf16[256,2048]{1,0:T(8,128)(2,1)} %param.15), kind=kLoop, calls=%fused_computation.28 | loop fusion | bytes 65536 | tf_op jit(solution)/shard_map/slice | solution.py:343
  3.1 0.0 copy-start
  3.1 4.8 %multiply_convert_fusion.2 = bf16[254,2048]{1,0:T(8,128)(2,1)S(1)} fusion(bf16[256,2048]{1,0:T(8,128)(2,1)} %param.15, f32[2048]{0:T(1024)S(1)} %bitcast.21, f32[2048]{0:T(1024)S(1)} %bitcast.23, f32[2048]{0:T(1024)S(1)} %bitcast.25, bf16[256,2048]{1,0:T(8,128)(2,1)} %param.14, f32[2048]{0:T(1024)S(1)} %bitcast.27, f32[2048]{0:T(1024)S(1)} %bitcast.29, ...), kind=kLoop, calls=%fused_computation.4 | loop fusion | flops 9363456 | bytes 7331840 | tf_op jit(solution)/shard_map/convert_element_type | solution.py:322
  7.9 0.0 copy-start.3
  7.9 0.0 copy-start.4
  7.9 0.1 slice.246
  8.0 0.0 copy-done
  8.1 1.4 %slice.213 = bf16[2,2048]{1,0:T(2,128)(2,1)} slice(bf16[256,2048]{1,0:T(8,128)(2,1)} %param.20), slice={[254:256], [0:2048]} | slice | bytes 16384 | tf_op jit(solution)/shard_map/slice | solution.py:331
  9.5 1.4 %slice.214 = bf16[2,2048]{1,0:T(2,128)(2,1)} slice(bf16[256,2048]{1,0:T(8,128)(2,1)} %param.21), slice={[254:256], [0:2048]} | slice | bytes 16384 | tf_op jit(solution)/shard_map/slice | solution.py:332
  10.8 1.9 %concatenate.24 = bf16[137,2048]{1,0:T(8,128)(2,1)S(1)} concatenate(bf16[127,2048]{1,0:T(8,128)(2,1)S(1)} %slice.246, bf16[2,2048]{1,0:T(2,128)(2,1)S(1)} %slice.210, bf16[2,2048]{1,0:T(2,128)(2,1)} %get-tuple-element.7, bf16[2,2048]{1,0:T(2,128)(2,1)} %get-tuple-element.35, bf16[2,2048]{1,0:T(2,128)(2,1)} %slice.213, bf16[2,2048]{1,0:T(2,128)(2,1)} %slice.214), dimensions={0} | concatenate | bytes 1122304 | tf_op jit(solution)/shard_map/concatenate | solution.py:325
  12.7 1.9 %collective-permute-start = (bf16[137,2048]{1,0:T(8,128)(2,1)S(1)}, bf16[137,2048]{1,0:T(8,128)(2,1)S(1)}, u32[]{:S(2)}, u32[]{:S(2)}) collective-permute-start(bf16[137,2048]{1,0:T(8,128)(2,1)S(1)} %concatenate.24), channel_id=1, source_target_pairs={{0,4},{4,8},{8,12},{12,16},{16,20},{20,24},{24,28},{28,32},{32,36}... | collective-permute-start | bytes 1683464 | tf_op jit(solution)/shard_map/ppermute | solution.py:286
  14.7 0.0 copy-done.3
  14.7 0.0 copy-done.4
  14.7 0.8 sqrt_multiply_fusion
  15.5 12.2 %collective-permute-done = bf16[137,2048]{1,0:T(8,128)(2,1)S(1)} collective-permute-done((bf16[137,2048]{1,0:T(8,128)(2,1)S(1)}, bf16[137,2048]{1,0:T(8,128)(2,1)S(1)}, u32[]{:S(2)}, u32[]{:S(2)}) %collective-permute-start) | collective-permute-done | bytes 561184 | tf_op jit(solution)/shard_map/ppermute | solution.py:286
  27.7 0.9 multiply_convert_fusion.3
  28.6 1.8 %pad_maximum_fusion.ext_ref = bf16[384,2048]{1,0:T(8,128)(2,1)} fusion(bf16[254,2048]{1,0:T(8,128)(2,1)S(1)} %multiply_convert_fusion.2, bf16[2,2048]{1,0:T(2,128)(2,1)S(1)} %multiply_convert_fusion.3, bf16[127,2048]{1,0:T(8,128)(2,1)S(1)} %slice.247, bf16[384]{0:T(512)(128)(2,1)S(1)} %pad.8.clone), kind=kLoop, calls=%fused_computation.5 | loop fusion | flops 6291456 | bytes 3142400 | tf_op jit(solution)/shard_map/concatenate | solution.py:348
  30.4 2.0 %multiply_add_fusion.1.gate_ref = f32[256,2048]{1,0:T(8,128)} fusion(bf16[256,2048]{1,0:T(8,128)(2,1)S(1)} %copy-done, bf16[2,2048]{1,0:T(2,128)(2,1)S(1)} %get-tuple-element.12, f32[2048]{0:T(1024)S(1)} %bitcast.34, f32[2048]{0:T(1024)S(1)} %bitcast.35, f32[2048]{0:T(1024)S(1)} %bitcast.33), kind=kLoop, calls=%fused_computation.3 | loop fusion | flops 7340032 | bytes 3178496 | tf_op jit(solution)/shard_map/add | solution.py:290
  32.4 0.0 copy-start.5
  32.4 0.0 copy-start.6
  32.4 32.4 %shard_map.140 = (bf16[256,2048]{1,0:T(8,128)(2,1)}, f32[256,128]{1,0:T(8,128)}) custom-call(bf16[384,2048]{1,0:T(8,128)(2,1)} %pad_maximum_fusion.ext_ref, f32[128,2048]{1,0:T(8,128)} %f_ref.1, f32[1,2048]{1,0:T(1,128)} %bitcast.45, f32[256,2048]{1,0:T(8,128)} %multiply_add_fusion.1.gate_ref), custom_call_target="tpu_custom_call" | custom-call | tf_op jit(solution)/shard_map/pallas_call | solution.py:57
  64.8 0.0 copy-start.1
  64.8 1.1 reduce_sum.9
  65.9 1.6 %collective-permute-start.1 = (f32[256]{0:T(256)S(1)}, f32[256]{0:T(256)S(1)}, u32[]{:S(2)}, u32[]{:S(2)}) collective-permute-start(f32[256]{0:T(256)S(1)} %reduce_sum.9), channel_id=1, source_target_pairs={{0,1},{1,2},{2,3},{3,0},{4,5},{5,6},{6,7},{7,4},{8,9},{9,10},{10,1... | collective-permute-start | bytes 3080 | tf_op jit(solution)/shard_map/ppermute | solution.py:356
  67.5 2.7 %collective-permute-start.2 = (f32[256]{0:T(256)S(1)}, f32[256]{0:T(256)S(1)}, u32[]{:S(2)}, u32[]{:S(2)}) collective-permute-start(f32[256]{0:T(256)S(1)} %reduce_sum.9), channel_id=1, source_target_pairs={{0,2},{1,3},{2,0},{3,1},{4,6},{5,7},{6,4},{7,5},{8,10},{9,11},{10,... | collective-permute-start | bytes 3080 | tf_op jit(solution)/shard_map/ppermute | solution.py:356
  70.2 1.4 %collective-permute-start.3 = (f32[256]{0:T(256)S(1)}, f32[256]{0:T(256)S(1)}, u32[]{:S(2)}, u32[]{:S(2)}) collective-permute-start(f32[256]{0:T(256)S(1)} %reduce_sum.9), channel_id=1, source_target_pairs={{0,3},{1,0},{2,1},{3,2},{4,7},{5,4},{6,5},{7,6},{8,11},{9,8},{10,9... | collective-permute-start | bytes 3080 | tf_op jit(solution)/shard_map/ppermute | solution.py:356
  71.7 0.0 copy-done.5
  71.7 0.1 fusion.7
  71.7 0.0 collective-permute-done.1
  71.7 0.8 collective-permute-done.2
  72.6 1.2 collective-permute-done.3
  73.8 0.0 copy-done.6
  73.8 1.5 %multiply_convert_fusion.1 = bf16[256,2048]{1,0:T(8,128)(2,1)S(1)} fusion(bf16[256,2048]{1,0:T(8,128)(2,1)} %get-tuple-element.2, f32[256]{0:T(256)S(1)} %add_rsqrt_fusion, f32[2048]{0:T(1024)S(1)} %copy-done.6), kind=kLoop, calls=%fused_computation.2 | loop fusion | flops 2097152 | bytes 2106368 | tf_op jit(solution)/shard_map/convert_element_type | solution.py:360
  75.3 0.0 copy-start.2
  75.4 2.1 %collective-permute-start.4 = (bf16[2,2048]{1,0:T(2,128)(2,1)S(1)}, bf16[2,2048]{1,0:T(2,128)(2,1)S(1)}, u32[]{:S(2)}, u32[]{:S(2)}) collective-permute-start(bf16[2,2048]{1,0:T(2,128)(2,1)S(1)} %slice.256), channel_id=1, source_target_pairs={{0,4},{4,8},{8,12},{12,16},{16,20},{20,24},{24,28},{28,32},{32,36}... | collective-permute-start | bytes 24584 | tf_op jit(solution)/shard_map/ppermute | solution.py:286
  77.4 0.0 copy-done.1
  77.4 2.0 %multiply_add_fusion.gate_ref = f32[256,2048]{1,0:T(8,128)} fusion(bf16[256,2048]{1,0:T(8,128)(2,1)S(1)} %copy-done.1, bf16[2,2048]{1,0:T(2,128)(2,1)S(1)} %get-tuple-element.10, f32[2048]{0:T(1024)S(1)} %bitcast.43, f32[2048]{0:T(1024)S(1)} %bitcast.44, f32[2048]{0:T(1024)S(1)} %bitcast.42), kind=kLoop, calls=%fused_computation | loop fusion | flops 7340032 | bytes 3178496 | tf_op jit(solution)/shard_map/add | solution.py:290
  79.5 3.1 %collective-permute-done.4 = bf16[2,2048]{1,0:T(2,128)(2,1)S(1)} collective-permute-done((bf16[2,2048]{1,0:T(2,128)(2,1)S(1)}, bf16[2,2048]{1,0:T(2,128)(2,1)S(1)}, u32[]{:S(2)}, u32[]{:S(2)}) %collective-permute-start.4) | collective-permute-done | bytes 8224 | tf_op jit(solution)/shard_map/ppermute | solution.py:286
  82.6 0.0 copy-done.2
  82.6 2.5 %multiply_convert_fusion.p_ref = bf16[256,2048]{1,0:T(8,128)(2,1)} fusion(bf16[256,2048]{1,0:T(8,128)(2,1)S(1)} %multiply_convert_fusion.1, bf16[256,2048]{1,0:T(8,128)(2,1)S(1)} %copy-done.2, bf16[2,2048]{1,0:T(2,128)(2,1)S(1)} %collective-permute-done.4, bf16[2,2048]{1,0:T(2,128)(2,1)S(1)} %get-tuple-element.11, f32[2048]{0:T(1024)S(1)} %bitcast.36, ...), kind=kLoop, calls=%fused_computation.1 | loop fusion | flops 15728640 | bytes 3211264 | tf_op jit(solution)/shard_map/convert_element_type | solution.py:365
  85.1 4.7 %shard_map.141.f_ref = f32[16,2048]{1,0:T(8,128)} custom-call(bf16[256,2048]{1,0:T(8,128)(2,1)} %multiply_convert_fusion.p_ref, f32[16,2048]{1,0:T(8,128)} %get-tuple-element.16.e_ref), custom_call_target="tpu_custom_call" | custom-call | tf_op jit(solution)/shard_map/pallas_call | solution.py:121
  89.8 30.4 %shard_map.142.s_ref = f32[16,2048]{1,0:T(8,128)} custom-call(f32[16,2048]{1,0:T(8,128)} %shard_map.141.f_ref, f32[16,2048]{1,0:T(8,128)} %r_ref.1), custom_call_target="tpu_custom_call" | custom-call | tf_op jit(solution)/shard_map/pallas_call | solution.py:268
  120.2 10.5 %shard_map.143 = bf16[256,2048]{1,0:T(8,128)(2,1)} custom-call(bf16[256,2048]{1,0:T(8,128)(2,1)} %multiply_convert_fusion.p_ref, f32[16,2048]{1,0:T(8,128)} %get-tuple-element.16.e_ref, f32[16,2048]{1,0:T(8,128)} %get-tuple-element.15.w_ref, f32[16,2048]{1,0:T(8,128)} %shard_map.142.s_ref, f32[1,2048]{1,0:T(1,128)} %bitcast.46, ...), custom_call_target="tpu_custom_call" | custom-call | tf_op jit(solution)/shard_map/pallas_call | solution.py:181
  (6 shorter events, 0.1 us)
Async XLA Ops:
  3.1 4.9 %copy-start = (bf16[256,2048]{1,0:T(8,128)(2,1)S(1)}, bf16[256,2048]{1,0:T(8,128)(2,1)}, u32[]{:S(2)}) copy-start(bf16[256,2048]{1,0:T(8,128)(2,1)} %param.13) | copy-start | bytes 3145732
  7.9 6.8 %copy-start.3 = (f32[16,2048]{1,0:T(8,128)S(1)}, f32[16,2048]{1,0:T(8,128)}, u32[]{:S(2)}) copy-start(f32[16,2048]{1,0:T(8,128)} %r_ref.1) | copy-start | bytes 393220
  7.9 6.8 %copy-start.4 = (f32[16,2048]{1,0:T(8,128)S(1)}, f32[16,2048]{1,0:T(8,128)}, u32[]{:S(2)}) copy-start(f32[16,2048]{1,0:T(8,128)} %param.24) | copy-start | bytes 393220
  12.7 14.9 %collective-permute-start = (bf16[137,2048]{1,0:T(8,128)(2,1)S(1)}, bf16[137,2048]{1,0:T(8,128)(2,1)S(1)}, u32[]{:S(2)}, u32[]{:S(2)}) collective-permute-start(bf16[137,2048]{1,0:T(8,128)(2,1)S(1)} %concatenate.24), channel_id=1, source_target_pairs={{0,4},{4,8},{8,12},{12,16},{16,20},{20,24},{24,28},{28,32},{32,36}... | collective-permute-start | bytes 1683464 | tf_op jit(solution)/shard_map/ppermute | solution.py:286
  32.4 39.3 %copy-start.5 = (f32[3,3,2048]{2,1,0:T(4,128)S(1)}, f32[3,3,2048]{2,1,0:T(4,128)}, u32[]{:S(2)}) copy-start(f32[3,3,2048]{2,1,0:T(4,128)} %param.22) | copy-start | bytes 221188
  32.4 41.4 %copy-start.6 = (f32[2048]{0:T(1024)S(1)}, f32[2048]{0:T(1024)}, u32[]{:S(2)}) copy-start(f32[2048]{0:T(1024)} %param.19) | copy-start | bytes 24580
  64.8 12.6 %copy-start.1 = (bf16[256,2048]{1,0:T(8,128)(2,1)S(1)}, bf16[256,2048]{1,0:T(8,128)(2,1)}, u32[]{:S(2)}) copy-start(bf16[256,2048]{1,0:T(8,128)(2,1)} %param.20) | copy-start | bytes 3145732
  65.9 5.8 %collective-permute-start.1 = (f32[256]{0:T(256)S(1)}, f32[256]{0:T(256)S(1)}, u32[]{:S(2)}, u32[]{:S(2)}) collective-permute-start(f32[256]{0:T(256)S(1)} %reduce_sum.9), channel_id=1, source_target_pairs={{0,1},{1,2},{2,3},{3,0},{4,5},{5,6},{6,7},{7,4},{8,9},{9,10},{10,1... | collective-permute-start | bytes 3080 | tf_op jit(solution)/shard_map/ppermute | solution.py:356
  67.5 5.1 %collective-permute-start.2 = (f32[256]{0:T(256)S(1)}, f32[256]{0:T(256)S(1)}, u32[]{:S(2)}, u32[]{:S(2)}) collective-permute-start(f32[256]{0:T(256)S(1)} %reduce_sum.9), channel_id=1, source_target_pairs={{0,2},{1,3},{2,0},{3,1},{4,6},{5,7},{6,4},{7,5},{8,10},{9,11},{10,... | collective-permute-start | bytes 3080 | tf_op jit(solution)/shard_map/ppermute | solution.py:356
  70.2 3.6 %collective-permute-start.3 = (f32[256]{0:T(256)S(1)}, f32[256]{0:T(256)S(1)}, u32[]{:S(2)}, u32[]{:S(2)}) collective-permute-start(f32[256]{0:T(256)S(1)} %reduce_sum.9), channel_id=1, source_target_pairs={{0,3},{1,0},{2,1},{3,2},{4,7},{5,4},{6,5},{7,6},{8,11},{9,8},{10,9... | collective-permute-start | bytes 3080 | tf_op jit(solution)/shard_map/ppermute | solution.py:356
  75.3 7.2 %copy-start.2 = (bf16[256,2048]{1,0:T(8,128)(2,1)S(1)}, bf16[256,2048]{1,0:T(8,128)(2,1)}, u32[]{:S(2)}) copy-start(bf16[256,2048]{1,0:T(8,128)(2,1)} %param.21) | copy-start | bytes 3145732
  75.4 7.2 %collective-permute-start.4 = (bf16[2,2048]{1,0:T(2,128)(2,1)S(1)}, bf16[2,2048]{1,0:T(2,128)(2,1)S(1)}, u32[]{:S(2)}, u32[]{:S(2)}) collective-permute-start(bf16[2,2048]{1,0:T(2,128)(2,1)S(1)} %slice.256), channel_id=1, source_target_pairs={{0,4},{4,8},{8,12},{12,16},{16,20},{20,24},{24,28},{28,32},{32,36}... | collective-permute-start | bytes 24584 | tf_op jit(solution)/shard_map/ppermute | solution.py:286

commit v10 on v5

--- a/solution.py
+++ b/solution.py
@@ -224,7 +224,7 @@
 
     out_ref[...] = f_ref[...]
     for k, sends in enumerate(plan):
-        send_ref[k] = out_ref[...]
+        send_ref[k] = out_ref[...].astype(send_ref.dtype)
         last = k == len(plan) - 1
         if last:
             out_ref[...] = jnp.zeros_like(out_ref)
@@ -250,10 +250,10 @@
             def _():
                 copy.wait_recv()
                 if power == 0:
-                    out_ref[...] = out_ref[...] + recv_ref[k, i]
+                    out_ref[...] = out_ref[...] + recv_ref[k, i].astype(jnp.float32)
                 else:
                     factor = jnp.exp(r_ref[...] * (-1.0 * rows * power))
-                    out_ref[...] = out_ref[...] + factor * recv_ref[k, i]
+                    out_ref[...] = out_ref[...] + factor * recv_ref[k, i].astype(jnp.float32)
 
         for shift, power, copy in copies:
 
@@ -270,8 +270,8 @@
         out_specs=pl.BlockSpec(memory_space=pltpu.VMEM),
         out_shape=jax.ShapeDtypeStruct(shape, jnp.float32),
         scratch_shapes=[
-            pltpu.VMEM((3,) + shape, jnp.float32),
-            pltpu.VMEM((3, 4) + shape, jnp.float32),
+            pltpu.VMEM((3,) + shape, jnp.bfloat16),
+            pltpu.VMEM((3, 4) + shape, jnp.bfloat16),
             pltpu.SemaphoreType.DMA((3, 4)),
             pltpu.SemaphoreType.DMA((3, 4)),
         ],

time: 134 us -> 123 us (0.918)
  Pallas kernels: 82.8 us -> 71.6 us
    pallas_call x1, Pallas kernels: 35.2 us -> 24 us  [scan_call(): pl.pallas_call(functools.partial(scan_kernel, count, rows), in_specs=[pl....]
  transfers between devices with their start and end apart: 10 -> 10, of which waited for: 2 -> 2; matrix products, arithmetic and copies ran while one was open for 12% -> 13% of each run, Pallas kernels for 24% -> 26%
where the time goes in v10:
time: 123 us
  Pallas kernels  71.6 us (58%)
  starting transfers between devices  29.2 us (24%)
  other arithmetic  16.4 us (13%)
  local copies, waits for them, and re-layouts  2.9 us (2%)
  waiting for transfers between devices  1.51 us (1%)
    pallas_call x1, Pallas kernels, medium_call(): pl.pallas_call(medium_kernel, grid=grid, in_specs=[pl.BlockSpec((span, bl...  32.4 us
    ppermute x7, starting transfers between devices, passed_along(): lax.ppermute(value, axis, [(source, source + steps) for source in range(f...  24.3 us
    pallas_call x1, Pallas kernels, scan_call(): pl.pallas_call(functools.partial(scan_kernel, count, rows), in_specs=[pl....  24 us
    pallas_call x1, Pallas kernels, modal_out_call(): pl.pallas_call(modal_out_kernel, grid=(width // block,), in_specs=[pl.Blo...  10.5 us
    ppermute x3, starting transfers between devices, body(): lax.ppermute(squares, 'ch', [(source, (source + shift) % ring) for source...  4.89 us
    convert_element_type x1, other arithmetic, body(): late_product = (short_filter(key_medium, short_medium[1]) * short_filter(...  4.77 us
    pallas_call x1, Pallas kernels, modal_end_call(): pl.pallas_call(modal_end_kernel, grid=(width // block,), in_specs=[pl.Blo...  4.71 us
    add x2, other arithmetic, short_filter(): weights[0] * extended[2:] + weights[1] * extended[1:-1]  4.06 us
  transfers between devices with their start and end apart: 10, of which 2 were waited for; matrix products, arithmetic and copies ran while one was open for 13% of the time, Pallas kernels for 26%

profile of v10, /device:TPU:25, one launch (start us, length us, event | category | flops | bytes accessed | tf_op | source)
XLA Modules:
  0.0 122.6 jit_solution(8550237220298663707)
XLA Ops:
  0.6 0.8 fusion.4
  1.4 4.1 %collective-permute-start.1 = (bf16[2,2048]{1,0:T(2,128)(2,1)S(1)}, bf16[2,2048]{1,0:T(2,128)(2,1)S(1)}, u32[]{:S(2)}, u32[]{:S(2)}) collective-permute-start(bf16[2,2048]{1,0:T(2,128)(2,1)S(1)} %get-tuple-element.7), channel_id=1, source_target_pairs={{0,4},{4,8},{8,12},{12,16},{16,20},{20,24},{24,28},{28,32},{32,36}... | collective-permute-start | bytes 24584 | tf_op jit(solution)/shard_map/ppermute | solution.py:285
  5.5 0.8 fusion.5
  6.3 1.9 %collective-permute-start.2 = (bf16[2,2048]{1,0:T(2,128)(2,1)S(1)}, bf16[2,2048]{1,0:T(2,128)(2,1)S(1)}, u32[]{:S(2)}, u32[]{:S(2)}) collective-permute-start(bf16[2,2048]{1,0:T(2,128)(2,1)S(1)} %get-tuple-element.9), channel_id=1, source_target_pairs={{0,4},{4,8},{8,12},{12,16},{16,20},{20,24},{24,28},{28,32},{32,36}... | collective-permute-start | bytes 24584 | tf_op jit(solution)/shard_map/ppermute | solution.py:285
  8.3 1.0 fusion.7
  9.3 0.0 copy-start
  9.3 0.0 copy-start.2
  9.3 0.0 copy-start.3
  9.3 0.0 copy-start.4
  9.4 0.0 copy-start.1
  9.4 4.8 %multiply_convert_fusion.2 = bf16[254,2048]{1,0:T(8,128)(2,1)S(1)} fusion(bf16[256,2048]{1,0:T(8,128)(2,1)} %param.15, f32[2048]{0:T(1024)S(1)} %bitcast.21, f32[2048]{0:T(1024)S(1)} %bitcast.23, f32[2048]{0:T(1024)S(1)} %bitcast.25, bf16[256,2048]{1,0:T(8,128)(2,1)} %param.14, f32[2048]{0:T(1024)S(1)} %bitcast.27, f32[2048]{0:T(1024)S(1)} %bitcast.29, ...), kind=kLoop, calls=%fused_computation.4 | loop fusion | flops 9363456 | bytes 7331840 | tf_op jit(solution)/shard_map/convert_element_type | solution.py:321
  14.1 0.1 slice.222
  14.3 3.9 %collective-permute-start = (bf16[127,2048]{1,0:T(8,128)(2,1)S(1)}, bf16[127,2048]{1,0:T(8,128)(2,1)S(1)}, u32[]{:S(2)}, u32[]{:S(2)}) collective-permute-start(bf16[127,2048]{1,0:T(8,128)(2,1)S(1)} %slice.222), channel_id=1, source_target_pairs={{0,4},{4,8},{8,12},{12,16},{16,20},{20,24},{24,28},{28,32},{32,36}... | collective-permute-start | bytes 1560584 | tf_op jit(solution)/shard_map/ppermute | solution.py:285
  18.2 0.0 copy-done
  18.3 1.9 %collective-permute-start.3 = (bf16[2,2048]{1,0:T(2,128)(2,1)S(1)}, bf16[2,2048]{1,0:T(2,128)(2,1)S(1)}, u32[]{:S(2)}, u32[]{:S(2)}) collective-permute-start(bf16[2,2048]{1,0:T(2,128)(2,1)S(1)} %slice.200), channel_id=1, source_target_pairs={{0,4},{4,8},{8,12},{12,16},{16,20},{20,24},{24,28},{28,32},{32,36}... | collective-permute-start | bytes 24584 | tf_op jit(solution)/shard_map/ppermute | solution.py:285
  20.2 0.0 copy-done.2
  20.2 3.9 %collective-permute-start.4 = (bf16[2,2048]{1,0:T(2,128)(2,1)S(1)}, bf16[2,2048]{1,0:T(2,128)(2,1)S(1)}, u32[]{:S(2)}, u32[]{:S(2)}) collective-permute-start(bf16[2,2048]{1,0:T(2,128)(2,1)S(1)} %slice.206), channel_id=1, source_target_pairs={{0,4},{4,8},{8,12},{12,16},{16,20},{20,24},{24,28},{28,32},{32,36}... | collective-permute-start | bytes 24584 | tf_op jit(solution)/shard_map/ppermute | solution.py:285
  24.1 0.0 copy-done.3
  24.2 0.0 copy-done.4
  24.2 0.8 sqrt_multiply_fusion
  25.0 0.0 copy-done.1
  25.0 0.0 collective-permute-done.1
  25.0 1.9 %collective-permute-start.9 = (bf16[2,2048]{1,0:T(2,128)(2,1)S(1)}, bf16[2,2048]{1,0:T(2,128)(2,1)S(1)}, u32[]{:S(2)}, u32[]{:S(2)}) collective-permute-start(bf16[2,2048]{1,0:T(2,128)(2,1)S(1)} %slice.218), channel_id=1, source_target_pairs={{0,4},{4,8},{8,12},{12,16},{16,20},{20,24},{24,28},{28,32},{32,36}... | collective-permute-start | bytes 24584 | tf_op jit(solution)/shard_map/ppermute | solution.py:285
  26.9 0.0 collective-permute-done.2
  26.9 0.1 multiply_convert_fusion.3
  27.0 0.0 collective-permute-done.3
  27.0 2.0 %multiply_add_fusion.1.gate_ref = f32[256,2048]{1,0:T(8,128)} fusion(bf16[256,2048]{1,0:T(8,128)(2,1)S(1)} %copy-done, bf16[2,2048]{1,0:T(2,128)(2,1)S(1)} %collective-permute-done.3, f32[2048]{0:T(1024)S(1)} %bitcast.34, f32[2048]{0:T(1024)S(1)} %bitcast.35, f32[2048]{0:T(1024)S(1)} %bitcast.33), kind=kLoop, calls=%fused_computation.3 | loop fusion | flops 7340032 | bytes 3178496 | tf_op jit(solution)/shard_map/add | solution.py:289
  29.1 0.0 collective-permute-done
  29.1 1.8 %pad_maximum_fusion.ext_ref = bf16[384,2048]{1,0:T(8,128)(2,1)} fusion(bf16[254,2048]{1,0:T(8,128)(2,1)S(1)} %multiply_convert_fusion.2, bf16[2,2048]{1,0:T(2,128)(2,1)S(1)} %multiply_convert_fusion.3, bf16[127,2048]{1,0:T(8,128)(2,1)S(1)} %collective-permute-done, bf16[384]{0:T(512)(128)(2,1)S(1)} %pad.8.clone), kind=kLoop, calls=%fused_computation.5 | loop fusion | flops 6291456 | bytes 3142400 | tf_op jit(solution)/shard_map/concatenate | solution.py:332
  30.8 0.0 copy-start.5
  30.8 0.0 copy-start.6
  30.8 32.4 %shard_map.140 = (bf16[256,2048]{1,0:T(8,128)(2,1)}, f32[256,128]{1,0:T(8,128)}) custom-call(bf16[384,2048]{1,0:T(8,128)(2,1)} %pad_maximum_fusion.ext_ref, f32[128,2048]{1,0:T(8,128)} %f_ref.1, f32[1,2048]{1,0:T(1,128)} %bitcast.45, f32[256,2048]{1,0:T(8,128)} %multiply_add_fusion.1.gate_ref), custom_call_target="tpu_custom_call" | custom-call | tf_op jit(solution)/shard_map/pallas_call | solution.py:57
  63.2 1.0 reduce_sum.9
  64.3 1.3 %collective-permute-start.5 = (f32[256]{0:T(256)S(1)}, f32[256]{0:T(256)S(1)}, u32[]{:S(2)}, u32[]{:S(2)}) collective-permute-start(f32[256]{0:T(256)S(1)} %reduce_sum.9), channel_id=1, source_target_pairs={{0,1},{1,2},{2,3},{3,0},{4,5},{5,6},{6,7},{7,4},{8,9},{9,10},{10,1... | collective-permute-start | bytes 3080 | tf_op jit(solution)/shard_map/ppermute | solution.py:340
  65.5 2.5 %collective-permute-start.6 = (f32[256]{0:T(256)S(1)}, f32[256]{0:T(256)S(1)}, u32[]{:S(2)}, u32[]{:S(2)}) collective-permute-start(f32[256]{0:T(256)S(1)} %reduce_sum.9), channel_id=1, source_target_pairs={{0,2},{1,3},{2,0},{3,1},{4,6},{5,7},{6,4},{7,5},{8,10},{9,11},{10,... | collective-permute-start | bytes 3080 | tf_op jit(solution)/shard_map/ppermute | solution.py:340
  68.0 1.2 collective-permute-start.7
  69.1 0.0 copy-done.5
  69.1 0.1 fusion.6
  69.2 0.0 collective-permute-done.5
  69.2 0.3 collective-permute-done.6
  69.5 1.2 %collective-permute-done.7 = f32[256]{0:T(256)S(1)} collective-permute-done((f32[256]{0:T(256)S(1)}, f32[256]{0:T(256)S(1)}, u32[]{:S(2)}, u32[]{:S(2)}) %collective-permute-start.7) | collective-permute-done | bytes 1056 | tf_op jit(solution)/shard_map/ppermute | solution.py:340
  70.7 0.0 copy-done.6
  70.7 1.5 %multiply_convert_fusion.1 = bf16[256,2048]{1,0:T(8,128)(2,1)S(1)} fusion(bf16[256,2048]{1,0:T(8,128)(2,1)} %get-tuple-element.2, f32[256]{0:T(256)S(1)} %add_rsqrt_fusion, f32[2048]{0:T(1024)S(1)} %copy-done.6), kind=kLoop, calls=%fused_computation.2 | loop fusion | flops 2097152 | bytes 2106368 | tf_op jit(solution)/shard_map/convert_element_type | solution.py:344
  72.2 6.6 %collective-permute-start.8 = (bf16[2,2048]{1,0:T(2,128)(2,1)S(1)}, bf16[2,2048]{1,0:T(2,128)(2,1)S(1)}, u32[]{:S(2)}, u32[]{:S(2)}) collective-permute-start(bf16[2,2048]{1,0:T(2,128)(2,1)S(1)} %slice.227), channel_id=1, source_target_pairs={{0,4},{4,8},{8,12},{12,16},{16,20},{20,24},{24,28},{28,32},{32,36}... | collective-permute-start | bytes 24584 | tf_op jit(solution)/shard_map/ppermute | solution.py:285
  78.8 0.0 collective-permute-done.9
  78.8 2.0 %multiply_add_fusion.gate_ref = f32[256,2048]{1,0:T(8,128)} fusion(bf16[256,2048]{1,0:T(8,128)(2,1)S(1)} %copy-done.1, bf16[2,2048]{1,0:T(2,128)(2,1)S(1)} %collective-permute-done.9, f32[2048]{0:T(1024)S(1)} %bitcast.43, f32[2048]{0:T(1024)S(1)} %bitcast.44, f32[2048]{0:T(1024)S(1)} %bitcast.42), kind=kLoop, calls=%fused_computation | loop fusion | flops 7340032 | bytes 3178496 | tf_op jit(solution)/shard_map/add | solution.py:289
  80.8 0.0 collective-permute-done.4
  80.8 0.0 collective-permute-done.8
  80.8 2.5 %multiply_convert_fusion.p_ref = bf16[256,2048]{1,0:T(8,128)(2,1)} fusion(bf16[256,2048]{1,0:T(8,128)(2,1)S(1)} %multiply_convert_fusion.1, bf16[256,2048]{1,0:T(8,128)(2,1)S(1)} %copy-done.2, bf16[2,2048]{1,0:T(2,128)(2,1)S(1)} %collective-permute-done.8, bf16[2,2048]{1,0:T(2,128)(2,1)S(1)} %collective-permute-done.4, f32[2048]{0:T(1024)S(1)} %bitcast.36, ...), kind=kLoop, calls=%fused_computation.1 | loop fusion | flops 15728640 | bytes 3211264 | tf_op jit(solution)/shard_map/convert_element_type | solution.py:351
  83.3 4.7 %shard_map.141.f_ref = f32[16,2048]{1,0:T(8,128)} custom-call(bf16[256,2048]{1,0:T(8,128)(2,1)} %multiply_convert_fusion.p_ref, f32[16,2048]{1,0:T(8,128)} %get-tuple-element.11.e_ref), custom_call_target="tpu_custom_call" | custom-call | tf_op jit(solution)/shard_map/pallas_call | solution.py:121
  88.0 24.0 %shard_map.142.s_ref = f32[16,2048]{1,0:T(8,128)} custom-call(f32[16,2048]{1,0:T(8,128)} %shard_map.141.f_ref, f32[16,2048]{1,0:T(8,128)} %r_ref.1), custom_call_target="tpu_custom_call" | custom-call | tf_op jit(solution)/shard_map/pallas_call | solution.py:267
  112.1 10.5 %shard_map.143 = bf16[256,2048]{1,0:T(8,128)(2,1)} custom-call(bf16[256,2048]{1,0:T(8,128)(2,1)} %multiply_convert_fusion.p_ref, f32[16,2048]{1,0:T(8,128)} %get-tuple-element.11.e_ref, f32[16,2048]{1,0:T(8,128)} %get-tuple-element.10.w_ref, f32[16,2048]{1,0:T(8,128)} %shard_map.142.s_ref, f32[1,2048]{1,0:T(1,128)} %bitcast.46, ...), custom_call_target="tpu_custom_call" | custom-call | tf_op jit(solution)/shard_map/pallas_call | solution.py:181
  (6 shorter events, 0.1 us)
Async XLA Ops:
  1.4 23.6 %collective-permute-start.1 = (bf16[2,2048]{1,0:T(2,128)(2,1)S(1)}, bf16[2,2048]{1,0:T(2,128)(2,1)S(1)}, u32[]{:S(2)}, u32[]{:S(2)}) collective-permute-start(bf16[2,2048]{1,0:T(2,128)(2,1)S(1)} %get-tuple-element.7), channel_id=1, source_target_pairs={{0,4},{4,8},{8,12},{12,16},{16,20},{20,24},{24,28},{28,32},{32,36}... | collective-permute-start | bytes 24584 | tf_op jit(solution)/shard_map/ppermute | solution.py:285
  6.3 20.6 %collective-permute-start.2 = (bf16[2,2048]{1,0:T(2,128)(2,1)S(1)}, bf16[2,2048]{1,0:T(2,128)(2,1)S(1)}, u32[]{:S(2)}, u32[]{:S(2)}) collective-permute-start(bf16[2,2048]{1,0:T(2,128)(2,1)S(1)} %get-tuple-element.9), channel_id=1, source_target_pairs={{0,4},{4,8},{8,12},{12,16},{16,20},{20,24},{24,28},{28,32},{32,36}... | collective-permute-start | bytes 24584 | tf_op jit(solution)/shard_map/ppermute | solution.py:285
  9.3 8.9 %copy-start = (bf16[256,2048]{1,0:T(8,128)(2,1)S(1)}, bf16[256,2048]{1,0:T(8,128)(2,1)}, u32[]{:S(2)}) copy-start(bf16[256,2048]{1,0:T(8,128)(2,1)} %param.13) | copy-start | bytes 3145732
  9.3 10.9 %copy-start.2 = (bf16[256,2048]{1,0:T(8,128)(2,1)S(1)}, bf16[256,2048]{1,0:T(8,128)(2,1)}, u32[]{:S(2)}) copy-start(bf16[256,2048]{1,0:T(8,128)(2,1)} %param.21) | copy-start | bytes 3145732
  9.3 14.8 %copy-start.3 = (f32[16,2048]{1,0:T(8,128)S(1)}, f32[16,2048]{1,0:T(8,128)}, u32[]{:S(2)}) copy-start(f32[16,2048]{1,0:T(8,128)} %r_ref.1) | copy-start | bytes 393220
  9.3 14.8 %copy-start.4 = (f32[16,2048]{1,0:T(8,128)S(1)}, f32[16,2048]{1,0:T(8,128)}, u32[]{:S(2)}) copy-start(f32[16,2048]{1,0:T(8,128)} %param.24) | copy-start | bytes 393220
  9.4 15.6 %copy-start.1 = (bf16[256,2048]{1,0:T(8,128)(2,1)S(1)}, bf16[256,2048]{1,0:T(8,128)(2,1)}, u32[]{:S(2)}) copy-start(bf16[256,2048]{1,0:T(8,128)(2,1)} %param.20) | copy-start | bytes 3145732
  14.3 14.8 %collective-permute-start = (bf16[127,2048]{1,0:T(8,128)(2,1)S(1)}, bf16[127,2048]{1,0:T(8,128)(2,1)S(1)}, u32[]{:S(2)}, u32[]{:S(2)}) collective-permute-start(bf16[127,2048]{1,0:T(8,128)(2,1)S(1)} %slice.222), channel_id=1, source_target_pairs={{0,4},{4,8},{8,12},{12,16},{16,20},{20,24},{24,28},{28,32},{32,36}... | collective-permute-start | bytes 1560584 | tf_op jit(solution)/shard_map/ppermute | solution.py:285
  18.3 8.8 %collective-permute-start.3 = (bf16[2,2048]{1,0:T(2,128)(2,1)S(1)}, bf16[2,2048]{1,0:T(2,128)(2,1)S(1)}, u32[]{:S(2)}, u32[]{:S(2)}) collective-permute-start(bf16[2,2048]{1,0:T(2,128)(2,1)S(1)} %slice.200), channel_id=1, source_target_pairs={{0,4},{4,8},{8,12},{12,16},{16,20},{20,24},{24,28},{28,32},{32,36}... | collective-permute-start | bytes 24584 | tf_op jit(solution)/shard_map/ppermute | solution.py:285
  20.2 60.6 %collective-permute-start.4 = (bf16[2,2048]{1,0:T(2,128)(2,1)S(1)}, bf16[2,2048]{1,0:T(2,128)(2,1)S(1)}, u32[]{:S(2)}, u32[]{:S(2)}) collective-permute-start(bf16[2,2048]{1,0:T(2,128)(2,1)S(1)} %slice.206), channel_id=1, source_target_pairs={{0,4},{4,8},{8,12},{12,16},{16,20},{20,24},{24,28},{28,32},{32,36}... | collective-permute-start | bytes 24584 | tf_op jit(solution)/shard_map/ppermute | solution.py:285
  25.0 53.8 %collective-permute-start.9 = (bf16[2,2048]{1,0:T(2,128)(2,1)S(1)}, bf16[2,2048]{1,0:T(2,128)(2,1)S(1)}, u32[]{:S(2)}, u32[]{:S(2)}) collective-permute-start(bf16[2,2048]{1,0:T(2,128)(2,1)S(1)} %slice.218), channel_id=1, source_target_pairs={{0,4},{4,8},{8,12},{12,16},{16,20},{20,24},{24,28},{28,32},{32,36}... | collective-permute-start | bytes 24584 | tf_op jit(solution)/shard_map/ppermute | solution.py:285
  30.8 38.3 %copy-start.5 = (f32[3,3,2048]{2,1,0:T(4,128)S(1)}, f32[3,3,2048]{2,1,0:T(4,128)}, u32[]{:S(2)}) copy-start(f32[3,3,2048]{2,1,0:T(4,128)} %param.22) | copy-start | bytes 221188
  30.8 39.9 %copy-start.6 = (f32[2048]{0:T(1024)S(1)}, f32[2048]{0:T(1024)}, u32[]{:S(2)}) copy-start(f32[2048]{0:T(1024)} %param.19) | copy-start | bytes 24580
  64.3 5.0 %collective-permute-start.5 = (f32[256]{0:T(256)S(1)}, f32[256]{0:T(256)S(1)}, u32[]{:S(2)}, u32[]{:S(2)}) collective-permute-start(f32[256]{0:T(256)S(1)} %reduce_sum.9), channel_id=1, source_target_pairs={{0,1},{1,2},{2,3},{3,0},{4,5},{5,6},{6,7},{7,4},{8,9},{9,10},{10,1... | collective-permute-start | bytes 3080 | tf_op jit(solution)/shard_map/ppermute | solution.py:340
  65.5 3.9 %collective-permute-start.6 = (f32[256]{0:T(256)S(1)}, f32[256]{0:T(256)S(1)}, u32[]{:S(2)}, u32[]{:S(2)}) collective-permute-start(f32[256]{0:T(256)S(1)} %reduce_sum.9), channel_id=1, source_target_pairs={{0,2},{1,3},{2,0},{3,1},{4,6},{5,7},{6,4},{7,5},{8,10},{9,11},{10,... | collective-permute-start | bytes 3080 | tf_op jit(solution)/shard_map/ppermute | solution.py:340
  68.0 2.7 %collective-permute-start.7 = (f32[256]{0:T(256)S(1)}, f32[256]{0:T(256)S(1)}, u32[]{:S(2)}, u32[]{:S(2)}) collective-permute-start(f32[256]{0:T(256)S(1)} %reduce_sum.9), channel_id=1, source_target_pairs={{0,3},{1,0},{2,1},{3,2},{4,7},{5,4},{6,5},{7,6},{8,11},{9,8},{10,9... | collective-permute-start | bytes 3080 | tf_op jit(solution)/shard_map/ppermute | solution.py:340
  72.2 8.6 %collective-permute-start.8 = (bf16[2,2048]{1,0:T(2,128)(2,1)S(1)}, bf16[2,2048]{1,0:T(2,128)(2,1)S(1)}, u32[]{:S(2)}, u32[]{:S(2)}) collective-permute-start(bf16[2,2048]{1,0:T(2,128)(2,1)S(1)} %slice.227), channel_id=1, source_target_pairs={{0,4},{4,8},{8,12},{12,16},{16,20},{20,24},{24,28},{28,32},{32,36}... | collective-permute-start | bytes 24584 | tf_op jit(solution)/shard_map/ppermute | solution.py:285

commit v11 on v10

--- a/solution.py
+++ b/solution.py
@@ -277,6 +277,53 @@
         ],
         compiler_params=pltpu.CompilerParams(collective_id=0, has_side_effects=True),
     )(final_state, decay_rates)
+
+
+def channel_sum_kernel(count, x_ref, out_ref, recv_ref, send_sem, recv_sem):
+    me = lax.axis_index("ch")
+    barrier = pltpu.get_barrier_semaphore()
+    for shift in range(1, count):
+        pl.semaphore_signal(
+            barrier,
+            1,
+            device_id={"ch": (me + shift) % count},
+            device_id_type=pl.DeviceIdType.MESH,
+        )
+    pl.semaphore_wait(barrier, count - 1)
+    copies = []
+    for shift in range(1, count):
+        copy = pltpu.make_async_remote_copy(
+            src_ref=x_ref,
+            dst_ref=recv_ref.at[shift],
+            send_sem=send_sem.at[shift],
+            recv_sem=recv_sem.at[shift],
+            device_id={"ch": (me + shift) % count},
+            device_id_type=pl.DeviceIdType.MESH,
+        )
+        copy.start()
+        copies.append(copy)
+    total = x_ref[...]
+    for shift, copy in zip(range(1, count), copies):
+        copy.wait_recv()
+        total = total + recv_ref[shift]
+    out_ref[...] = total
+    for copy in copies:
+        copy.wait_send()
+
+
+def channel_sum_call(values, count):
+    return pl.pallas_call(
+        functools.partial(channel_sum_kernel, count),
+        in_specs=[pl.BlockSpec(memory_space=pltpu.VMEM)],
+        out_specs=pl.BlockSpec(memory_space=pltpu.VMEM),
+        out_shape=jax.ShapeDtypeStruct(values.shape, jnp.float32),
+        scratch_shapes=[
+            pltpu.VMEM((count,) + values.shape, jnp.float32),
+            pltpu.SemaphoreType.DMA((count,)),
+            pltpu.SemaphoreType.DMA((count,)),
+        ],
+        compiler_params=pltpu.CompilerParams(collective_id=1, has_side_effects=True),
+    )(values)
 
 
 def passed_along(value, axis, steps):
@@ -334,12 +381,9 @@
         extended, filter_medium, skip_medium[None, :], gate_feat
     )
     squares = jnp.sum(partial_squares, axis=1)
-    ring = lax.axis_size("ch")
-    total_squares = squares
-    for shift in range(1, ring):
-        total_squares = total_squares + lax.ppermute(
-            squares, "ch", [(source, (source + shift) % ring) for source in range(ring)]
-        )
+    total_squares = channel_sum_call(
+        squares.reshape(-1, 128), lax.axis_size("ch")
+    ).reshape(squares.shape)
     inverse = lax.rsqrt(total_squares / D + 1e-06)
     normed = (mixed_medium * norm_gain * inverse[:, None]).astype(jnp.bfloat16)
     rim_gate_long, rim_key_long, rim_normed = passed_along(

time: 123 us -> 130 us (1.057)
  Pallas kernels: 71.6 us -> 83.2 us
  starting transfers between devices: 29.2 us -> 24 us
  waiting for transfers between devices: 1.51 us -> 0.02 us
  other arithmetic: 16.4 us -> 17.8 us
    pallas_call x0 -> x1, Pallas kernels: none -> 5.95 us  [channel_sum_call(): pl.pallas_call(functools.partial(channel_sum_kernel, count), in_specs=[pl...]
    pallas_call x1, Pallas kernels: 32.4 us -> 38 us  [medium_call(): pl.pallas_call(medium_kernel, grid=grid, in_specs=[pl.BlockSpec((span, bl...]
    ppermute x3 -> x0, starting transfers between devices: 4.89 us -> none  [body(): lax.ppermute(squares, 'ch', [(source, (source + shift) % ring) for source...]
    ppermute x3 -> x0, waiting for transfers between devices: 1.49 us -> none  [body(): lax.ppermute(squares, 'ch', [(source, (source + shift) % ring) for source...]
  transfers between devices with their start and end apart: 10 -> 7, of which waited for: 2 -> 0; matrix products, arithmetic and copies ran while one was open for 13% -> 13% of each run, Pallas kernels for 26% -> 34%
where the time goes in v11:
time: 130 us; the launch traced here: 129 us
  Pallas kernels  83.2 us (64%)
  starting transfers between devices  24 us (18%)
  other arithmetic  17.8 us (14%)
  local copies, waits for them, and re-layouts  2.91 us (2%)
    pallas_call x1, Pallas kernels, medium_call(): pl.pallas_call(medium_kernel, grid=grid, in_specs=[pl.BlockSpec((span, bl...  38 us
    pallas_call x1, Pallas kernels, scan_call(): pl.pallas_call(functools.partial(scan_kernel, count, rows), in_specs=[pl....  24.2 us
    ppermute x7, starting transfers between devices, passed_along(): lax.ppermute(value, axis, [(source, source + steps) for source in range(f...  24 us
    pallas_call x1, Pallas kernels, modal_out_call(): pl.pallas_call(modal_out_kernel, grid=(width // block,), in_specs=[pl.Blo...  10.4 us
    pallas_call x1, Pallas kernels, channel_sum_call(): pl.pallas_call(functools.partial(channel_sum_kernel, count), in_specs=[pl...  5.95 us
    convert_element_type x1, other arithmetic, body(): late_product = (short_filter(key_medium, short_medium[1]) * short_filter(...  4.77 us
    pallas_call x1, Pallas kernels, modal_end_call(): pl.pallas_call(modal_end_kernel, grid=(width // block,), in_specs=[pl.Blo...  4.71 us
    add x2, other arithmetic, short_filter(): weights[0] * extended[2:] + weights[1] * extended[1:-1]  4.07 us
  transfers between devices with their start and end apart: 7, of which 0 were waited for; matrix products, arithmetic and copies ran while one was open for 13% of the time, Pallas kernels for 34%

profile of v11, /device:TPU:25, one launch (start us, length us, event | category | flops | bytes accessed | tf_op | source)
XLA Modules:
  0.0 128.8 jit_solution(15001383770458905590)
XLA Ops:
  0.6 0.8 fusion.4
  1.4 4.1 %collective-permute-start.1 = (bf16[2,2048]{1,0:T(2,128)(2,1)S(1)}, bf16[2,2048]{1,0:T(2,128)(2,1)S(1)}, u32[]{:S(2)}, u32[]{:S(2)}) collective-permute-start(bf16[2,2048]{1,0:T(2,128)(2,1)S(1)} %get-tuple-element.7), channel_id=1, source_target_pairs={{0,4},{4,8},{8,12},{12,16},{16,20},{20,24},{24,28},{28,32},{32,36}... | collective-permute-start | bytes 24584 | tf_op jit(solution)/shard_map/ppermute | solution.py:332
  5.5 0.8 fusion.5
  6.3 1.9 %collective-permute-start.2 = (bf16[2,2048]{1,0:T(2,128)(2,1)S(1)}, bf16[2,2048]{1,0:T(2,128)(2,1)S(1)}, u32[]{:S(2)}, u32[]{:S(2)}) collective-permute-start(bf16[2,2048]{1,0:T(2,128)(2,1)S(1)} %get-tuple-element.9), channel_id=1, source_target_pairs={{0,4},{4,8},{8,12},{12,16},{16,20},{20,24},{24,28},{28,32},{32,36}... | collective-permute-start | bytes 24584 | tf_op jit(solution)/shard_map/ppermute | solution.py:332
  8.3 1.0 fusion.7
  9.3 0.0 copy-start
  9.3 0.0 copy-start.2
  9.3 0.0 copy-start.3
  9.3 0.0 copy-start.4
  9.4 0.0 copy-start.5
  9.4 0.0 copy-start.1
  9.4 4.8 %multiply_convert_fusion.2 = bf16[254,2048]{1,0:T(8,128)(2,1)S(1)} fusion(bf16[256,2048]{1,0:T(8,128)(2,1)} %param.15, f32[2048]{0:T(1024)S(1)} %bitcast.24, f32[2048]{0:T(1024)S(1)} %bitcast.26, f32[2048]{0:T(1024)S(1)} %bitcast.28, bf16[256,2048]{1,0:T(8,128)(2,1)} %param.14, f32[2048]{0:T(1024)S(1)} %bitcast.30, f32[2048]{0:T(1024)S(1)} %bitcast.32, ...), kind=kLoop, calls=%fused_computation.4 | loop fusion | flops 9363456 | bytes 7331840 | tf_op jit(solution)/shard_map/convert_element_type | solution.py:368
  14.2 0.1 slice.222
  14.3 3.9 %collective-permute-start = (bf16[127,2048]{1,0:T(8,128)(2,1)S(1)}, bf16[127,2048]{1,0:T(8,128)(2,1)S(1)}, u32[]{:S(2)}, u32[]{:S(2)}) collective-permute-start(bf16[127,2048]{1,0:T(8,128)(2,1)S(1)} %slice.222), channel_id=1, source_target_pairs={{0,4},{4,8},{8,12},{12,16},{16,20},{20,24},{24,28},{28,32},{32,36}... | collective-permute-start | bytes 1560584 | tf_op jit(solution)/shard_map/ppermute | solution.py:332
  18.2 0.0 copy-done
  18.3 1.9 %collective-permute-start.3 = (bf16[2,2048]{1,0:T(2,128)(2,1)S(1)}, bf16[2,2048]{1,0:T(2,128)(2,1)S(1)}, u32[]{:S(2)}, u32[]{:S(2)}) collective-permute-start(bf16[2,2048]{1,0:T(2,128)(2,1)S(1)} %slice.200), channel_id=1, source_target_pairs={{0,4},{4,8},{8,12},{12,16},{16,20},{20,24},{24,28},{28,32},{32,36}... | collective-permute-start | bytes 24584 | tf_op jit(solution)/shard_map/ppermute | solution.py:332
  20.2 0.0 copy-done.2
  20.2 3.9 %collective-permute-start.4 = (bf16[2,2048]{1,0:T(2,128)(2,1)S(1)}, bf16[2,2048]{1,0:T(2,128)(2,1)S(1)}, u32[]{:S(2)}, u32[]{:S(2)}) collective-permute-start(bf16[2,2048]{1,0:T(2,128)(2,1)S(1)} %slice.206), channel_id=1, source_target_pairs={{0,4},{4,8},{8,12},{12,16},{16,20},{20,24},{24,28},{28,32},{32,36}... | collective-permute-start | bytes 24584 | tf_op jit(solution)/shard_map/ppermute | solution.py:332
  24.2 0.0 copy-done.3
  24.2 0.0 copy-done.4
  24.2 0.8 sqrt_multiply_fusion
  25.0 0.0 copy-done.5
  25.0 0.1 fusion.6
  25.0 0.0 copy-done.1
  25.1 0.0 collective-permute-done.1
  25.1 1.9 %collective-permute-start.6 = (bf16[2,2048]{1,0:T(2,128)(2,1)S(1)}, bf16[2,2048]{1,0:T(2,128)(2,1)S(1)}, u32[]{:S(2)}, u32[]{:S(2)}) collective-permute-start(bf16[2,2048]{1,0:T(2,128)(2,1)S(1)} %slice.218), channel_id=1, source_target_pairs={{0,4},{4,8},{8,12},{12,16},{16,20},{20,24},{24,28},{28,32},{32,36}... | collective-permute-start | bytes 24584 | tf_op jit(solution)/shard_map/ppermute | solution.py:332
  27.0 0.0 collective-permute-done.2
  27.0 0.1 multiply_convert_fusion.3
  27.1 0.0 collective-permute-done.3
  27.1 2.0 %multiply_add_fusion.1.gate_ref = f32[256,2048]{1,0:T(8,128)} fusion(bf16[256,2048]{1,0:T(8,128)(2,1)S(1)} %copy-done, bf16[2,2048]{1,0:T(2,128)(2,1)S(1)} %collective-permute-done.3, f32[2048]{0:T(1024)S(1)} %bitcast.46, f32[2048]{0:T(1024)S(1)} %bitcast.47, f32[2048]{0:T(1024)S(1)} %bitcast.45), kind=kLoop, calls=%fused_computation.3 | loop fusion | flops 7340032 | bytes 3178496 | tf_op jit(solution)/shard_map/add | solution.py:336
  29.1 0.0 collective-permute-done
  29.1 1.8 %pad_maximum_fusion.ext_ref = bf16[384,2048]{1,0:T(8,128)(2,1)} fusion(bf16[254,2048]{1,0:T(8,128)(2,1)S(1)} %multiply_convert_fusion.2, bf16[2,2048]{1,0:T(2,128)(2,1)S(1)} %multiply_convert_fusion.3, bf16[127,2048]{1,0:T(8,128)(2,1)S(1)} %collective-permute-done, bf16[384]{0:T(512)(128)(2,1)S(1)} %pad.8.clone), kind=kLoop, calls=%fused_computation.5 | loop fusion | flops 6291456 | bytes 3142400 | tf_op jit(solution)/shard_map/concatenate | solution.py:379
  30.9 0.0 copy-start.6
  30.9 38.0 %shard_map.140 = (bf16[256,2048]{1,0:T(8,128)(2,1)}, f32[256,128]{1,0:T(8,128)}) custom-call(bf16[384,2048]{1,0:T(8,128)(2,1)} %pad_maximum_fusion.ext_ref, f32[128,2048]{1,0:T(8,128)} %f_ref.1, f32[1,2048]{1,0:T(1,128)} %bitcast.48, f32[256,2048]{1,0:T(8,128)} %multiply_add_fusion.1.gate_ref), custom_call_target="tpu_custom_call" | custom-call | tf_op jit(solution)/shard_map/pallas_call | solution.py:57
  68.9 1.6 %reduce_sum.9 = f32[256]{0:T(256)} reduce(f32[256,128]{1,0:T(8,128)} %get-tuple-element.5, f32[]{:T(128)} %constant.2.clone.1), dimensions={1}, to_apply=%region_0.0 | reduce | flops 32512 | bytes 132100 | tf_op jit(solution)/shard_map/reduce_sum | solution.py:383
  70.5 6.0 %shard_map.141 = f32[2,128]{1,0:T(2,128)} custom-call(f32[2,128]{1,0:T(2,128)} %bitcast.50), custom_call_target="tpu_custom_call" | custom-call | tf_op jit(solution)/shard_map/pallas_call | solution.py:315
  76.5 0.7 rsqrt_bitcast_fusion
  77.2 0.0 copy-done.6
  77.2 1.5 %multiply_convert_fusion.1 = bf16[256,2048]{1,0:T(8,128)(2,1)S(1)} fusion(bf16[256,2048]{1,0:T(8,128)(2,1)} %get-tuple-element.2, f32[256]{0:T(256)S(1)} %rsqrt_bitcast_fusion, f32[2048]{0:T(1024)S(1)} %copy-done.6), kind=kLoop, calls=%fused_computation.2 | loop fusion | flops 2097152 | bytes 2106368 | tf_op jit(solution)/shard_map/convert_element_type | solution.py:388
  78.7 6.3 %collective-permute-start.5 = (bf16[2,2048]{1,0:T(2,128)(2,1)S(1)}, bf16[2,2048]{1,0:T(2,128)(2,1)S(1)}, u32[]{:S(2)}, u32[]{:S(2)}) collective-permute-start(bf16[2,2048]{1,0:T(2,128)(2,1)S(1)} %slice.227), channel_id=1, source_target_pairs={{0,4},{4,8},{8,12},{12,16},{16,20},{20,24},{24,28},{28,32},{32,36}... | collective-permute-start | bytes 24584 | tf_op jit(solution)/shard_map/ppermute | solution.py:332
  85.0 0.0 collective-permute-done.6
  85.0 2.0 %multiply_add_fusion.gate_ref = f32[256,2048]{1,0:T(8,128)} fusion(bf16[256,2048]{1,0:T(8,128)(2,1)S(1)} %copy-done.1, bf16[2,2048]{1,0:T(2,128)(2,1)S(1)} %collective-permute-done.6, f32[2048]{0:T(1024)S(1)} %bitcast.43, f32[2048]{0:T(1024)S(1)} %bitcast.44, f32[2048]{0:T(1024)S(1)} %bitcast.42), kind=kLoop, calls=%fused_computation | loop fusion | flops 7340032 | bytes 3178496 | tf_op jit(solution)/shard_map/add | solution.py:336
  87.0 0.0 collective-permute-done.4
  87.0 0.0 collective-permute-done.5
  87.0 2.5 %multiply_convert_fusion.p_ref = bf16[256,2048]{1,0:T(8,128)(2,1)} fusion(bf16[256,2048]{1,0:T(8,128)(2,1)S(1)} %multiply_convert_fusion.1, bf16[256,2048]{1,0:T(8,128)(2,1)S(1)} %copy-done.2, bf16[2,2048]{1,0:T(2,128)(2,1)S(1)} %collective-permute-done.5, bf16[2,2048]{1,0:T(2,128)(2,1)S(1)} %collective-permute-done.4, f32[2048]{0:T(1024)S(1)} %bitcast.36, ...), kind=kLoop, calls=%fused_computation.1 | loop fusion | flops 15728640 | bytes 3211264 | tf_op jit(solution)/shard_map/convert_element_type | solution.py:395
  89.5 4.7 %shard_map.142.f_ref = f32[16,2048]{1,0:T(8,128)} custom-call(bf16[256,2048]{1,0:T(8,128)(2,1)} %multiply_convert_fusion.p_ref, f32[16,2048]{1,0:T(8,128)} %get-tuple-element.11.e_ref), custom_call_target="tpu_custom_call" | custom-call | tf_op jit(solution)/shard_map/pallas_call | solution.py:121
  94.3 24.2 %shard_map.143.s_ref = f32[16,2048]{1,0:T(8,128)} custom-call(f32[16,2048]{1,0:T(8,128)} %shard_map.142.f_ref, f32[16,2048]{1,0:T(8,128)} %r_ref.1), custom_call_target="tpu_custom_call" | custom-call | tf_op jit(solution)/shard_map/pallas_call | solution.py:267
  118.4 10.4 %shard_map.144 = bf16[256,2048]{1,0:T(8,128)(2,1)} custom-call(bf16[256,2048]{1,0:T(8,128)(2,1)} %multiply_convert_fusion.p_ref, f32[16,2048]{1,0:T(8,128)} %get-tuple-element.11.e_ref, f32[16,2048]{1,0:T(8,128)} %get-tuple-element.10.w_ref, f32[16,2048]{1,0:T(8,128)} %shard_map.143.s_ref, f32[1,2048]{1,0:T(1,128)} %bitcast.49, ...), custom_call_target="tpu_custom_call" | custom-call | tf_op jit(solution)/shard_map/pallas_call | solution.py:181
  (5 shorter events, 0.1 us)
Async XLA Ops:
  1.4 23.6 %collective-permute-start.1 = (bf16[2,2048]{1,0:T(2,128)(2,1)S(1)}, bf16[2,2048]{1,0:T(2,128)(2,1)S(1)}, u32[]{:S(2)}, u32[]{:S(2)}) collective-permute-start(bf16[2,2048]{1,0:T(2,128)(2,1)S(1)} %get-tuple-element.7), channel_id=1, source_target_pairs={{0,4},{4,8},{8,12},{12,16},{16,20},{20,24},{24,28},{28,32},{32,36}... | collective-permute-start | bytes 24584 | tf_op jit(solution)/shard_map/ppermute | solution.py:332
  6.3 20.7 %collective-permute-start.2 = (bf16[2,2048]{1,0:T(2,128)(2,1)S(1)}, bf16[2,2048]{1,0:T(2,128)(2,1)S(1)}, u32[]{:S(2)}, u32[]{:S(2)}) collective-permute-start(bf16[2,2048]{1,0:T(2,128)(2,1)S(1)} %get-tuple-element.9), channel_id=1, source_target_pairs={{0,4},{4,8},{8,12},{12,16},{16,20},{20,24},{24,28},{28,32},{32,36}... | collective-permute-start | bytes 24584 | tf_op jit(solution)/shard_map/ppermute | solution.py:332
  9.3 8.9 %copy-start = (bf16[256,2048]{1,0:T(8,128)(2,1)S(1)}, bf16[256,2048]{1,0:T(8,128)(2,1)}, u32[]{:S(2)}) copy-start(bf16[256,2048]{1,0:T(8,128)(2,1)} %param.13) | copy-start | bytes 3145732
  9.3 10.9 %copy-start.2 = (bf16[256,2048]{1,0:T(8,128)(2,1)S(1)}, bf16[256,2048]{1,0:T(8,128)(2,1)}, u32[]{:S(2)}) copy-start(bf16[256,2048]{1,0:T(8,128)(2,1)} %param.21) | copy-start | bytes 3145732
  9.3 14.8 %copy-start.3 = (f32[16,2048]{1,0:T(8,128)S(1)}, f32[16,2048]{1,0:T(8,128)}, u32[]{:S(2)}) copy-start(f32[16,2048]{1,0:T(8,128)} %r_ref.1) | copy-start | bytes 393220
  9.3 14.8 %copy-start.4 = (f32[16,2048]{1,0:T(8,128)S(1)}, f32[16,2048]{1,0:T(8,128)}, u32[]{:S(2)}) copy-start(f32[16,2048]{1,0:T(8,128)} %param.24) | copy-start | bytes 393220
  9.4 15.6 %copy-start.5 = (f32[3,3,2048]{2,1,0:T(4,128)S(1)}, f32[3,3,2048]{2,1,0:T(4,128)}, u32[]{:S(2)}) copy-start(f32[3,3,2048]{2,1,0:T(4,128)} %param.22) | copy-start | bytes 221188
  9.4 15.7 %copy-start.1 = (bf16[256,2048]{1,0:T(8,128)(2,1)S(1)}, bf16[256,2048]{1,0:T(8,128)(2,1)}, u32[]{:S(2)}) copy-start(bf16[256,2048]{1,0:T(8,128)(2,1)} %param.20) | copy-start | bytes 3145732
  14.3 14.8 %collective-permute-start = (bf16[127,2048]{1,0:T(8,128)(2,1)S(1)}, bf16[127,2048]{1,0:T(8,128)(2,1)S(1)}, u32[]{:S(2)}, u32[]{:S(2)}) collective-permute-start(bf16[127,2048]{1,0:T(8,128)(2,1)S(1)} %slice.222), channel_id=1, source_target_pairs={{0,4},{4,8},{8,12},{12,16},{16,20},{20,24},{24,28},{28,32},{32,36}... | collective-permute-start | bytes 1560584 | tf_op jit(solution)/shard_map/ppermute | solution.py:332
  18.3 8.8 %collective-permute-start.3 = (bf16[2,2048]{1,0:T(2,128)(2,1)S(1)}, bf16[2,2048]{1,0:T(2,128)(2,1)S(1)}, u32[]{:S(2)}, u32[]{:S(2)}) collective-permute-start(bf16[2,2048]{1,0:T(2,128)(2,1)S(1)} %slice.200), channel_id=1, source_target_pairs={{0,4},{4,8},{8,12},{12,16},{16,20},{20,24},{24,28},{28,32},{32,36}... | collective-permute-start | bytes 24584 | tf_op jit(solution)/shard_map/ppermute | solution.py:332
  20.2 66.8 %collective-permute-start.4 = (bf16[2,2048]{1,0:T(2,128)(2,1)S(1)}, bf16[2,2048]{1,0:T(2,128)(2,1)S(1)}, u32[]{:S(2)}, u32[]{:S(2)}) collective-permute-start(bf16[2,2048]{1,0:T(2,128)(2,1)S(1)} %slice.206), channel_id=1, source_target_pairs={{0,4},{4,8},{8,12},{12,16},{16,20},{20,24},{24,28},{28,32},{32,36}... | collective-permute-start | bytes 24584 | tf_op jit(solution)/shard_map/ppermute | solution.py:332
  25.1 59.9 %collective-permute-start.6 = (bf16[2,2048]{1,0:T(2,128)(2,1)S(1)}, bf16[2,2048]{1,0:T(2,128)(2,1)S(1)}, u32[]{:S(2)}, u32[]{:S(2)}) collective-permute-start(bf16[2,2048]{1,0:T(2,128)(2,1)S(1)} %slice.218), channel_id=1, source_target_pairs={{0,4},{4,8},{8,12},{12,16},{16,20},{20,24},{24,28},{28,32},{32,36}... | collective-permute-start | bytes 24584 | tf_op jit(solution)/shard_map/ppermute | solution.py:332
  30.9 46.2 %copy-start.6 = (f32[2048]{0:T(1024)S(1)}, f32[2048]{0:T(1024)}, u32[]{:S(2)}) copy-start(f32[2048]{0:T(1024)} %param.19) | copy-start | bytes 24580
  78.7 8.3 %collective-permute-start.5 = (bf16[2,2048]{1,0:T(2,128)(2,1)S(1)}, bf16[2,2048]{1,0:T(2,128)(2,1)S(1)}, u32[]{:S(2)}, u32[]{:S(2)}) collective-permute-start(bf16[2,2048]{1,0:T(2,128)(2,1)S(1)} %slice.227), channel_id=1, source_target_pairs={{0,4},{4,8},{8,12},{12,16},{16,20},{20,24},{24,28},{28,32},{32,36}... | collective-permute-start | bytes 24584 | tf_op jit(solution)/shard_map/ppermute | solution.py:332

commit v12 on v10

--- a/solution.py
+++ b/solution.py
@@ -131,10 +131,22 @@
     )(product, decay)
 
 
-def modal_out_kernel(p_ref, e_ref, w_ref, s_ref, skip_ref, gate_ref, out_ref, pf_ref, z_ref):
+def modal_out_kernel(
+    p_ref, e_ref, w_ref, s_ref, skip_ref, raw_ref, rim_ref, tap_ref, out_ref, pf_ref, z_ref, gate_ref
+):
     rows = p_ref.shape[0]
     _rows_to_f32(p_ref, pf_ref)
     lanes = [pl.ds(g * LANE, LANE) for g in range(GROUP)]
+    for ln in lanes:
+        extended = jnp.concatenate(
+            [rim_ref[:, ln], raw_ref[:, ln].astype(jnp.float32)], 0
+        )
+        taps = tap_ref[:, ln]
+        gate_ref[:, ln] = (
+            taps[0:1] * extended[8 : rows + 8]
+            + taps[1:2] * extended[7 : rows + 7]
+            + taps[2:3] * extended[6 : rows + 6]
+        )
     e_lo = [e_ref[0:8, ln] for ln in lanes]
     e_hi = [e_ref[8:16, ln] for ln in lanes]
     w_lo = [w_ref[0:8, ln] for ln in lanes]
@@ -175,7 +187,7 @@
     lax.fori_loop(0, rows // 8, reduce, 0)
 
 
-def modal_out_call(product, decay, weight, start, skip, gate_feat):
+def modal_out_call(product, decay, weight, start, skip, gate, rim, taps):
     rows, width = product.shape
     block = LANE * GROUP
     return pl.pallas_call(
@@ -188,14 +200,17 @@
             pl.BlockSpec((16, block), lambda i: (0, i)),
             pl.BlockSpec((1, block), lambda i: (0, i)),
             pl.BlockSpec((rows, block), lambda i: (0, i)),
+            pl.BlockSpec((8, block), lambda i: (0, i)),
+            pl.BlockSpec((3, block), lambda i: (0, i)),
         ],
         out_specs=pl.BlockSpec((rows, block), lambda i: (0, i)),
         out_shape=jax.ShapeDtypeStruct((rows, width), jnp.bfloat16),
         scratch_shapes=[
             pltpu.VMEM((rows, block), jnp.float32),
             pltpu.VMEM((GROUP, rows * 8, LANE), jnp.float32),
-        ],
-    )(product, decay, weight, start, skip, gate_feat)
+            pltpu.VMEM((rows, block), jnp.float32),
+        ],
+    )(product, decay, weight, start, skip, gate, rim, taps)
 
 
 def scan_kernel(count, rows, f_ref, r_ref, out_ref, send_ref, recv_ref, send_sem, recv_sem):
@@ -345,7 +360,6 @@
     rim_gate_long, rim_key_long, rim_normed = passed_along(
         (gate_long[-2:], key_long[-2:], normed[-2:]), "ctx", 1
     )
-    gate_feat_long = short_filter(jnp.concatenate([rim_gate_long, gate_long], 0), short_long[0])
     key_feat_long = short_filter(jnp.concatenate([rim_key_long, key_long], 0), short_long[1])
     value_feat_long = short_filter(jnp.concatenate([rim_normed, normed], 0), short_long[2])
     product_long = (key_feat_long * value_feat_long).astype(jnp.bfloat16)
@@ -354,7 +368,14 @@
     final_state = modal_end_call(product_long, step_decay)
     incoming = scan_call(final_state, decay_rates, lax.axis_size("ctx"), row_count)
     mixed_long = modal_out_call(
-        product_long, step_decay, mode_weight, incoming, skip_long[None, :], gate_feat_long
+        product_long,
+        step_decay,
+        mode_weight,
+        incoming,
+        skip_long[None, :],
+        gate_long,
+        jnp.pad(rim_gate_long.astype(jnp.float32), ((6, 0), (0, 0))),
+        short_long[0],
     )
     return (mixed_medium, mixed_long)
 

time: 123 us -> 124 us (level)
  other arithmetic: 16.4 us -> 15 us
  local copies, waits for them, and re-layouts: 2.9 us -> 4.25 us
    add x2 -> x1, other arithmetic: 4.06 us -> 2.04 us  [short_filter(): weights[0] * extended[2:] + weights[1] * extended[1:-1]]
where the time goes in v12:
time: 124 us; the launch traced here: 123 us
  Pallas kernels  72.4 us (58%)
  starting transfers between devices  29.2 us (24%)
  other arithmetic  15 us (12%)
  local copies, waits for them, and re-layouts  4.25 us (3%)
    pallas_call x1, Pallas kernels, medium_call(): pl.pallas_call(medium_kernel, grid=grid, in_specs=[pl.BlockSpec((span, bl...  32.4 us
    pallas_call x1, Pallas kernels, scan_call(): pl.pallas_call(functools.partial(scan_kernel, count, rows), in_specs=[pl....  24.5 us
    ppermute x7, starting transfers between devices, passed_along(): lax.ppermute(value, axis, [(source, source + steps) for source in range(f...  24.3 us
    pallas_call x1, Pallas kernels, modal_out_call(): pl.pallas_call(modal_out_kernel, grid=(width // block,), in_specs=[pl.Blo...  10.8 us
    ppermute x3, starting transfers between devices, body(): lax.ppermute(squares, 'ch', [(source, (source + shift) % ring) for source...  4.89 us
    convert_element_type x1, other arithmetic, body(): late_product = (short_filter(key_medium, short_medium[1]) * short_filter(...  4.77 us
    pallas_call x1, Pallas kernels, modal_end_call(): pl.pallas_call(modal_end_kernel, grid=(width // block,), in_specs=[pl.Blo...  4.71 us
  transfers between devices with their start and end apart: 10, of which 2 were waited for; matrix products, arithmetic and copies ran while one was open for 13% of the time, Pallas kernels for 26%

profile of v12, /device:TPU:25, one launch (start us, length us, event | category | flops | bytes accessed | tf_op | source)
XLA Modules:
  0.0 122.8 jit_solution(333958132105953653)
XLA Ops:
  0.6 0.8 fusion.3
  1.4 4.1 %collective-permute-start.1 = (bf16[2,2048]{1,0:T(2,128)(2,1)S(1)}, bf16[2,2048]{1,0:T(2,128)(2,1)S(1)}, u32[]{:S(2)}, u32[]{:S(2)}) collective-permute-start(bf16[2,2048]{1,0:T(2,128)(2,1)S(1)} %get-tuple-element.7), channel_id=1, source_target_pairs={{0,4},{4,8},{8,12},{12,16},{16,20},{20,24},{24,28},{28,32},{32,36}... | collective-permute-start | bytes 24584 | tf_op jit(solution)/shard_map/ppermute | solution.py:300
  5.5 0.8 fusion.4
  6.3 1.9 %collective-permute-start.2 = (bf16[2,2048]{1,0:T(2,128)(2,1)S(1)}, bf16[2,2048]{1,0:T(2,128)(2,1)S(1)}, u32[]{:S(2)}, u32[]{:S(2)}) collective-permute-start(bf16[2,2048]{1,0:T(2,128)(2,1)S(1)} %get-tuple-element.9), channel_id=1, source_target_pairs={{0,4},{4,8},{8,12},{12,16},{16,20},{20,24},{24,28},{28,32},{32,36}... | collective-permute-start | bytes 24584 | tf_op jit(solution)/shard_map/ppermute | solution.py:300
  8.3 1.0 fusion.6
  9.3 0.0 copy-start
  9.3 0.0 copy-start.1
  9.3 0.0 copy-start.2
  9.3 0.0 copy-start.3
  9.4 0.0 copy-start.4
  9.4 4.8 %multiply_convert_fusion.2 = bf16[254,2048]{1,0:T(8,128)(2,1)S(1)} fusion(bf16[256,2048]{1,0:T(8,128)(2,1)} %param.15, f32[2048]{0:T(1024)S(1)} %bitcast.20, f32[2048]{0:T(1024)S(1)} %bitcast.22, f32[2048]{0:T(1024)S(1)} %bitcast.24, bf16[256,2048]{1,0:T(8,128)(2,1)} %param.14, f32[2048]{0:T(1024)S(1)} %bitcast.26, f32[2048]{0:T(1024)S(1)} %bitcast.28, ...), kind=kLoop, calls=%fused_computation.3 | loop fusion | flops 9363456 | bytes 7331840 | tf_op jit(solution)/shard_map/convert_element_type | solution.py:336
  14.1 0.1 slice.199
  14.3 3.9 %collective-permute-start = (bf16[127,2048]{1,0:T(8,128)(2,1)S(1)}, bf16[127,2048]{1,0:T(8,128)(2,1)S(1)}, u32[]{:S(2)}, u32[]{:S(2)}) collective-permute-start(bf16[127,2048]{1,0:T(8,128)(2,1)S(1)} %slice.199), channel_id=1, source_target_pairs={{0,4},{4,8},{8,12},{12,16},{16,20},{20,24},{24,28},{28,32},{32,36}... | collective-permute-start | bytes 1560584 | tf_op jit(solution)/shard_map/ppermute | solution.py:300
  18.2 0.0 copy-done
  18.2 1.9 %collective-permute-start.3 = (bf16[2,2048]{1,0:T(2,128)(2,1)S(1)}, bf16[2,2048]{1,0:T(2,128)(2,1)S(1)}, u32[]{:S(2)}, u32[]{:S(2)}) collective-permute-start(bf16[2,2048]{1,0:T(2,128)(2,1)S(1)} %slice.181), channel_id=1, source_target_pairs={{0,4},{4,8},{8,12},{12,16},{16,20},{20,24},{24,28},{28,32},{32,36}... | collective-permute-start | bytes 24584 | tf_op jit(solution)/shard_map/ppermute | solution.py:300
  20.2 0.0 copy-done.1
  20.2 3.9 %collective-permute-start.4 = (bf16[2,2048]{1,0:T(2,128)(2,1)S(1)}, bf16[2,2048]{1,0:T(2,128)(2,1)S(1)}, u32[]{:S(2)}, u32[]{:S(2)}) collective-permute-start(bf16[2,2048]{1,0:T(2,128)(2,1)S(1)} %slice.187), channel_id=1, source_target_pairs={{0,4},{4,8},{8,12},{12,16},{16,20},{20,24},{24,28},{28,32},{32,36}... | collective-permute-start | bytes 24584 | tf_op jit(solution)/shard_map/ppermute | solution.py:300
  24.1 0.0 copy-done.2
  24.2 0.0 copy-done.3
  24.2 0.8 sqrt_multiply_fusion
  25.0 0.0 copy-done.4
  25.0 0.8 slice.197
  25.8 0.0 collective-permute-done.1
  25.8 1.9 %collective-permute-start.9 = (bf16[2,2048]{1,0:T(2,128)(2,1)S(1)}, bf16[2,2048]{1,0:T(2,128)(2,1)S(1)}, u32[]{:S(2)}, u32[]{:S(2)}) collective-permute-start(bf16[2,2048]{1,0:T(2,128)(2,1)S(1)} %slice.197), channel_id=1, source_target_pairs={{0,4},{4,8},{8,12},{12,16},{16,20},{20,24},{24,28},{28,32},{32,36}... | collective-permute-start | bytes 24584 | tf_op jit(solution)/shard_map/ppermute | solution.py:300
  27.7 0.0 collective-permute-done.2
  27.7 0.1 multiply_convert_fusion.3
  27.8 0.0 collective-permute-done.3
  27.8 2.0 %multiply_add_fusion.gate_ref = f32[256,2048]{1,0:T(8,128)} fusion(bf16[256,2048]{1,0:T(8,128)(2,1)S(1)} %copy-done, bf16[2,2048]{1,0:T(2,128)(2,1)S(1)} %collective-permute-done.3, f32[2048]{0:T(1024)S(1)} %bitcast.39, f32[2048]{0:T(1024)S(1)} %bitcast.40, f32[2048]{0:T(1024)S(1)} %bitcast.38), kind=kLoop, calls=%fused_computation.2 | loop fusion | flops 7340032 | bytes 3178496 | tf_op jit(solution)/shard_map/add | solution.py:304
  29.9 0.0 collective-permute-done
  29.9 1.8 %pad_maximum_fusion.ext_ref = bf16[384,2048]{1,0:T(8,128)(2,1)} fusion(bf16[254,2048]{1,0:T(8,128)(2,1)S(1)} %multiply_convert_fusion.2, bf16[2,2048]{1,0:T(2,128)(2,1)S(1)} %multiply_convert_fusion.3, bf16[127,2048]{1,0:T(8,128)(2,1)S(1)} %collective-permute-done, bf16[384]{0:T(512)(128)(2,1)S(1)} %pad.14.clone), kind=kLoop, calls=%fused_computation.4 | loop fusion | flops 6291456 | bytes 3142400 | tf_op jit(solution)/shard_map/concatenate | solution.py:347
  31.6 0.0 copy-start.5
  31.6 32.4 %shard_map.140 = (bf16[256,2048]{1,0:T(8,128)(2,1)}, f32[256,128]{1,0:T(8,128)}) custom-call(bf16[384,2048]{1,0:T(8,128)(2,1)} %pad_maximum_fusion.ext_ref, f32[128,2048]{1,0:T(8,128)} %f_ref.1, f32[1,2048]{1,0:T(1,128)} %bitcast.41, f32[256,2048]{1,0:T(8,128)} %multiply_add_fusion.gate_ref), custom_call_target="tpu_custom_call" | custom-call | tf_op jit(solution)/shard_map/pallas_call | solution.py:57
  64.0 1.0 reduce_sum.9
  65.0 1.3 %collective-permute-start.5 = (f32[256]{0:T(256)S(1)}, f32[256]{0:T(256)S(1)}, u32[]{:S(2)}, u32[]{:S(2)}) collective-permute-start(f32[256]{0:T(256)S(1)} %reduce_sum.9), channel_id=1, source_target_pairs={{0,1},{1,2},{2,3},{3,0},{4,5},{5,6},{6,7},{7,4},{8,9},{9,10},{10,1... | collective-permute-start | bytes 3080 | tf_op jit(solution)/shard_map/ppermute | solution.py:355
  66.3 2.5 %collective-permute-start.6 = (f32[256]{0:T(256)S(1)}, f32[256]{0:T(256)S(1)}, u32[]{:S(2)}, u32[]{:S(2)}) collective-permute-start(f32[256]{0:T(256)S(1)} %reduce_sum.9), channel_id=1, source_target_pairs={{0,2},{1,3},{2,0},{3,1},{4,6},{5,7},{6,4},{7,5},{8,10},{9,11},{10,... | collective-permute-start | bytes 3080 | tf_op jit(solution)/shard_map/ppermute | solution.py:355
  68.7 1.2 collective-permute-start.7
  69.9 0.6 slice_bitcast_fusion.tap_ref
  70.5 0.0 collective-permute-done.5
  70.5 0.0 collective-permute-done.6
  70.5 0.9 collective-permute-done.7
  71.5 0.0 copy-done.5
  71.5 1.5 %multiply_convert_fusion.1 = bf16[256,2048]{1,0:T(8,128)(2,1)S(1)} fusion(bf16[256,2048]{1,0:T(8,128)(2,1)} %get-tuple-element.2, f32[256]{0:T(256)S(1)} %add_rsqrt_fusion, f32[2048]{0:T(1024)S(1)} %copy-done.5), kind=kLoop, calls=%fused_computation.1 | loop fusion | flops 2097152 | bytes 2106368 | tf_op jit(solution)/shard_map/convert_element_type | solution.py:359
  73.0 6.6 %collective-permute-start.8 = (bf16[2,2048]{1,0:T(2,128)(2,1)S(1)}, bf16[2,2048]{1,0:T(2,128)(2,1)S(1)}, u32[]{:S(2)}, u32[]{:S(2)}) collective-permute-start(bf16[2,2048]{1,0:T(2,128)(2,1)S(1)} %slice.204), channel_id=1, source_target_pairs={{0,4},{4,8},{8,12},{12,16},{16,20},{20,24},{24,28},{28,32},{32,36}... | collective-permute-start | bytes 24584 | tf_op jit(solution)/shard_map/ppermute | solution.py:300
  79.6 0.0 collective-permute-done.9
  79.6 0.6 pad_convert_fusion.rim_ref
  80.2 0.0 collective-permute-done.4
  80.2 0.1 collective-permute-done.8
  80.3 2.4 %multiply_convert_fusion.p_ref = bf16[256,2048]{1,0:T(8,128)(2,1)} fusion(bf16[256,2048]{1,0:T(8,128)(2,1)S(1)} %multiply_convert_fusion.1, bf16[256,2048]{1,0:T(8,128)(2,1)S(1)} %copy-done.1, bf16[2,2048]{1,0:T(2,128)(2,1)S(1)} %collective-permute-done.8, bf16[2,2048]{1,0:T(2,128)(2,1)S(1)} %collective-permute-done.4, f32[2048]{0:T(1024)S(1)} %bitcast.37, ...), kind=kLoop, calls=%fused_computation | loop fusion | flops 15728640 | bytes 3211264 | tf_op jit(solution)/shard_map/convert_element_type | solution.py:365
  82.8 4.7 %shard_map.141.f_ref = f32[16,2048]{1,0:T(8,128)} custom-call(bf16[256,2048]{1,0:T(8,128)(2,1)} %multiply_convert_fusion.p_ref, f32[16,2048]{1,0:T(8,128)} %get-tuple-element.11.e_ref), custom_call_target="tpu_custom_call" | custom-call | tf_op jit(solution)/shard_map/pallas_call | solution.py:121
  87.5 24.5 %shard_map.142.s_ref = f32[16,2048]{1,0:T(8,128)} custom-call(f32[16,2048]{1,0:T(8,128)} %shard_map.141.f_ref, f32[16,2048]{1,0:T(8,128)} %r_ref.1), custom_call_target="tpu_custom_call" | custom-call | tf_op jit(solution)/shard_map/pallas_call | solution.py:282
  112.0 10.8 %shard_map.143 = bf16[256,2048]{1,0:T(8,128)(2,1)} custom-call(bf16[256,2048]{1,0:T(8,128)(2,1)} %multiply_convert_fusion.p_ref, f32[16,2048]{1,0:T(8,128)} %get-tuple-element.11.e_ref, f32[16,2048]{1,0:T(8,128)} %get-tuple-element.10.w_ref, f32[16,2048]{1,0:T(8,128)} %shard_map.142.s_ref, f32[1,2048]{1,0:T(1,128)} %bitcast.42, bf16[256,2048]{1,0:T(8,128)(2,1)} %raw_ref.1, ...), custom_call_target="tpu_custom_call" | custom-call | tf_op jit(solution)/shard_map/pallas_call | solution.py:193
  (6 shorter events, 0.1 us)
Async XLA Ops:
  1.4 24.4 %collective-permute-start.1 = (bf16[2,2048]{1,0:T(2,128)(2,1)S(1)}, bf16[2,2048]{1,0:T(2,128)(2,1)S(1)}, u32[]{:S(2)}, u32[]{:S(2)}) collective-permute-start(bf16[2,2048]{1,0:T(2,128)(2,1)S(1)} %get-tuple-element.7), channel_id=1, source_target_pairs={{0,4},{4,8},{8,12},{12,16},{16,20},{20,24},{24,28},{28,32},{32,36}... | collective-permute-start | bytes 24584 | tf_op jit(solution)/shard_map/ppermute | solution.py:300
  6.3 21.4 %collective-permute-start.2 = (bf16[2,2048]{1,0:T(2,128)(2,1)S(1)}, bf16[2,2048]{1,0:T(2,128)(2,1)S(1)}, u32[]{:S(2)}, u32[]{:S(2)}) collective-permute-start(bf16[2,2048]{1,0:T(2,128)(2,1)S(1)} %get-tuple-element.9), channel_id=1, source_target_pairs={{0,4},{4,8},{8,12},{12,16},{16,20},{20,24},{24,28},{28,32},{32,36}... | collective-permute-start | bytes 24584 | tf_op jit(solution)/shard_map/ppermute | solution.py:300
  9.3 8.9 %copy-start = (bf16[256,2048]{1,0:T(8,128)(2,1)S(1)}, bf16[256,2048]{1,0:T(8,128)(2,1)}, u32[]{:S(2)}) copy-start(bf16[256,2048]{1,0:T(8,128)(2,1)} %param.13) | copy-start | bytes 3145732
  9.3 10.9 %copy-start.1 = (bf16[256,2048]{1,0:T(8,128)(2,1)S(1)}, bf16[256,2048]{1,0:T(8,128)(2,1)}, u32[]{:S(2)}) copy-start(bf16[256,2048]{1,0:T(8,128)(2,1)} %param.21) | copy-start | bytes 3145732
  9.3 14.8 %copy-start.2 = (f32[16,2048]{1,0:T(8,128)S(1)}, f32[16,2048]{1,0:T(8,128)}, u32[]{:S(2)}) copy-start(f32[16,2048]{1,0:T(8,128)} %r_ref.1) | copy-start | bytes 393220
  9.3 14.8 %copy-start.3 = (f32[16,2048]{1,0:T(8,128)S(1)}, f32[16,2048]{1,0:T(8,128)}, u32[]{:S(2)}) copy-start(f32[16,2048]{1,0:T(8,128)} %param.24) | copy-start | bytes 393220
  9.4 15.6 %copy-start.4 = (f32[3,3,2048]{2,1,0:T(4,128)S(1)}, f32[3,3,2048]{2,1,0:T(4,128)}, u32[]{:S(2)}) copy-start(f32[3,3,2048]{2,1,0:T(4,128)} %param.22) | copy-start | bytes 221188
  14.3 15.6 %collective-permute-start = (bf16[127,2048]{1,0:T(8,128)(2,1)S(1)}, bf16[127,2048]{1,0:T(8,128)(2,1)S(1)}, u32[]{:S(2)}, u32[]{:S(2)}) collective-permute-start(bf16[127,2048]{1,0:T(8,128)(2,1)S(1)} %slice.199), channel_id=1, source_target_pairs={{0,4},{4,8},{8,12},{12,16},{16,20},{20,24},{24,28},{28,32},{32,36}... | collective-permute-start | bytes 1560584 | tf_op jit(solution)/shard_map/ppermute | solution.py:300
  18.2 9.6 %collective-permute-start.3 = (bf16[2,2048]{1,0:T(2,128)(2,1)S(1)}, bf16[2,2048]{1,0:T(2,128)(2,1)S(1)}, u32[]{:S(2)}, u32[]{:S(2)}) collective-permute-start(bf16[2,2048]{1,0:T(2,128)(2,1)S(1)} %slice.181), channel_id=1, source_target_pairs={{0,4},{4,8},{8,12},{12,16},{16,20},{20,24},{24,28},{28,32},{32,36}... | collective-permute-start | bytes 24584 | tf_op jit(solution)/shard_map/ppermute | solution.py:300
  20.2 60.0 %collective-permute-start.4 = (bf16[2,2048]{1,0:T(2,128)(2,1)S(1)}, bf16[2,2048]{1,0:T(2,128)(2,1)S(1)}, u32[]{:S(2)}, u32[]{:S(2)}) collective-permute-start(bf16[2,2048]{1,0:T(2,128)(2,1)S(1)} %slice.187), channel_id=1, source_target_pairs={{0,4},{4,8},{8,12},{12,16},{16,20},{20,24},{24,28},{28,32},{32,36}... | collective-permute-start | bytes 24584 | tf_op jit(solution)/shard_map/ppermute | solution.py:300
  25.8 53.8 %collective-permute-start.9 = (bf16[2,2048]{1,0:T(2,128)(2,1)S(1)}, bf16[2,2048]{1,0:T(2,128)(2,1)S(1)}, u32[]{:S(2)}, u32[]{:S(2)}) collective-permute-start(bf16[2,2048]{1,0:T(2,128)(2,1)S(1)} %slice.197), channel_id=1, source_target_pairs={{0,4},{4,8},{8,12},{12,16},{16,20},{20,24},{24,28},{28,32},{32,36}... | collective-permute-start | bytes 24584 | tf_op jit(solution)/shard_map/ppermute | solution.py:300
  31.6 39.8 %copy-start.5 = (f32[2048]{0:T(1024)S(1)}, f32[2048]{0:T(1024)}, u32[]{:S(2)}) copy-start(f32[2048]{0:T(1024)} %param.19) | copy-start | bytes 24580
  65.0 5.5 %collective-permute-start.5 = (f32[256]{0:T(256)S(1)}, f32[256]{0:T(256)S(1)}, u32[]{:S(2)}, u32[]{:S(2)}) collective-permute-start(f32[256]{0:T(256)S(1)} %reduce_sum.9), channel_id=1, source_target_pairs={{0,1},{1,2},{2,3},{3,0},{4,5},{5,6},{6,7},{7,4},{8,9},{9,10},{10,1... | collective-permute-start | bytes 3080 | tf_op jit(solution)/shard_map/ppermute | solution.py:355
  66.3 4.2 %collective-permute-start.6 = (f32[256]{0:T(256)S(1)}, f32[256]{0:T(256)S(1)}, u32[]{:S(2)}, u32[]{:S(2)}) collective-permute-start(f32[256]{0:T(256)S(1)} %reduce_sum.9), channel_id=1, source_target_pairs={{0,2},{1,3},{2,0},{3,1},{4,6},{5,7},{6,4},{7,5},{8,10},{9,11},{10,... | collective-permute-start | bytes 3080 | tf_op jit(solution)/shard_map/ppermute | solution.py:355
  68.7 2.7 %collective-permute-start.7 = (f32[256]{0:T(256)S(1)}, f32[256]{0:T(256)S(1)}, u32[]{:S(2)}, u32[]{:S(2)}) collective-permute-start(f32[256]{0:T(256)S(1)} %reduce_sum.9), channel_id=1, source_target_pairs={{0,3},{1,0},{2,1},{3,2},{4,7},{5,4},{6,5},{7,6},{8,11},{9,8},{10,9... | collective-permute-start | bytes 3080 | tf_op jit(solution)/shard_map/ppermute | solution.py:355
  73.0 7.3 %collective-permute-start.8 = (bf16[2,2048]{1,0:T(2,128)(2,1)S(1)}, bf16[2,2048]{1,0:T(2,128)(2,1)S(1)}, u32[]{:S(2)}, u32[]{:S(2)}) collective-permute-start(bf16[2,2048]{1,0:T(2,128)(2,1)S(1)} %slice.204), channel_id=1, source_target_pairs={{0,4},{4,8},{8,12},{12,16},{16,20},{20,24},{24,28},{28,32},{32,36}... | collective-permute-start | bytes 24584 | tf_op jit(solution)/shard_map/ppermute | solution.py:300

commit v13 on v12

--- a/solution.py
+++ b/solution.py
@@ -11,7 +11,9 @@
 RB = 8
 
 
-def medium_kernel(ext_ref, f_ref, skip_ref, gate_ref, out_ref, ss_ref, q_ref):
+def medium_kernel(
+    ext_ref, f_ref, skip_ref, raw_ref, rim_ref, tap_ref, out_ref, ss_ref, q_ref, gate_ref
+):
     rows = out_ref.shape[0]
     width = out_ref.shape[1]
     span = ext_ref.shape[0]
@@ -25,6 +27,13 @@
         ext = ext_ref[:, lanes].astype(jnp.float32)
         for b in range(8):
             q_ref[b, 8:, :] = ext[8 - b : span - b]
+        extended = jnp.concatenate([rim_ref[:, lanes], raw_ref[:, lanes].astype(jnp.float32)], 0)
+        taps = tap_ref[:, lanes]
+        gate_ref[...] = (
+            taps[0:1] * extended[8 : rows + 8]
+            + taps[1:2] * extended[7 : rows + 7]
+            + taps[2:3] * extended[6 : rows + 6]
+        )
 
         def block(kb, carry):
             acc = [jnp.zeros((8, SUB), jnp.float32) for _ in range(RB)]
@@ -41,7 +50,7 @@
                 row = pl.multiple_of(kb * (8 * RB) + 8 * kk, 8)
                 own = q_ref[0, pl.ds(row + TAPS, 8), :]
                 conv = acc[kk] + skip * own
-                mixed = (gate_ref[pl.ds(row, 8), lanes] * conv).astype(jnp.bfloat16)
+                mixed = (gate_ref[pl.ds(row, 8), :] * conv).astype(jnp.bfloat16)
                 out_ref[pl.ds(row, 8), lanes] = mixed
                 m = mixed.astype(jnp.float32)
                 ss_ref[pl.ds(row, 8), :] += m * m
@@ -50,9 +59,9 @@
         lax.fori_loop(0, rows // (8 * RB), block, 0)
 
 
-def medium_call(ext, taps, skip, gate_feat, block=512, interpret=False):
+def medium_call(ext, taps, skip, gate, rim, gate_taps, block=512, interpret=False):
     span, width = ext.shape
-    rows = gate_feat.shape[0]
+    rows = gate.shape[0]
     grid = (width // block,)
     return pl.pallas_call(
         medium_kernel,
@@ -62,6 +71,8 @@
             pl.BlockSpec((TAPS, block), lambda i: (0, i)),
             pl.BlockSpec((1, block), lambda i: (0, i)),
             pl.BlockSpec((rows, block), lambda i: (0, i)),
+            pl.BlockSpec((8, block), lambda i: (0, i)),
+            pl.BlockSpec((3, block), lambda i: (0, i)),
         ],
         out_specs=[
             pl.BlockSpec((rows, block), lambda i: (0, i)),
@@ -71,10 +82,13 @@
             jax.ShapeDtypeStruct((rows, width), jnp.bfloat16),
             jax.ShapeDtypeStruct((rows, SUB), jnp.float32),
         ],
-        scratch_shapes=[pltpu.VMEM((8, span, SUB), jnp.float32)],
+        scratch_shapes=[
+            pltpu.VMEM((8, span, SUB), jnp.float32),
+            pltpu.VMEM((rows, SUB), jnp.float32),
+        ],
         compiler_params=pltpu.CompilerParams(dimension_semantics=("arbitrary",)),
         interpret=interpret,
-    )(ext, taps, skip, gate_feat)
+    )(ext, taps, skip, gate, rim, gate_taps)
 
 D = 8192
 
@@ -343,10 +357,14 @@
     head_value = short_filter(jnp.concatenate([rim_value, value_medium[:2]], 0), short_medium[2])
     head_product = (head_key * head_value).astype(jnp.bfloat16)
     product = jnp.concatenate([rim_product, head_product, late_product], 0)
-    gate_feat = short_filter(jnp.concatenate([rim_gate, gate_medium], 0), short_medium[0])
     extended = jnp.concatenate([jnp.zeros((1, width_local), jnp.bfloat16), product], 0)
     mixed_medium, partial_squares = medium_call(
-        extended, filter_medium, skip_medium[None, :], gate_feat
+        extended,
+        filter_medium,
+        skip_medium[None, :],
+        gate_medium,
+        jnp.pad(rim_gate.astype(jnp.float32), ((6, 0), (0, 0))),
+        short_medium[0],
     )
     squares = jnp.sum(partial_squares, axis=1)
     ring = lax.axis_size("ch")

time: 124 us -> 123 us (level)
  local copies, waits for them, and re-layouts: 4.25 us -> 6.31 us
  Pallas kernels: 72.4 us -> 71 us
    add x1 -> x0, other arithmetic: 2.04 us -> none  [short_filter(): weights[0] * extended[2:] + weights[1] * extended[1:-1]]
    squeeze x0 -> x1, local copies, waits for them, and re-layouts: none -> 1.38 us  [body(): short_medium[0]]
    pallas_call x1, Pallas kernels: 32.4 us -> 31.1 us  [medium_call(): pl.pallas_call(medium_kernel, grid=grid, in_specs=[pl.BlockSpec((span, bl...]
  transfers between devices with their start and end apart: 10 -> 10, of which waited for: 2 -> 2; matrix products, arithmetic and copies ran while one was open for 13% -> 14% of each run, Pallas kernels for 26% -> 25%
where the time goes in v13:
time: 123 us; the launch traced here: 122 us
  Pallas kernels  71 us (58%)
  starting transfers between devices  29.2 us (24%)
  other arithmetic  13.8 us (11%)
  local copies, waits for them, and re-layouts  6.31 us (5%)
    pallas_call x1, Pallas kernels, medium_call(): pl.pallas_call(medium_kernel, grid=grid, in_specs=[pl.BlockSpec((span, bl...  31.1 us
    pallas_call x1, Pallas kernels, scan_call(): pl.pallas_call(functools.partial(scan_kernel, count, rows), in_specs=[pl....  24.5 us
    ppermute x7, starting transfers between devices, passed_along(): lax.ppermute(value, axis, [(source, source + steps) for source in range(f...  24.3 us
    pallas_call x1, Pallas kernels, modal_out_call(): pl.pallas_call(modal_out_kernel, grid=(width // block,), in_specs=[pl.Blo...  10.8 us
    convert_element_type x1, other arithmetic, body(): late_product = (short_filter(key_medium, short_medium[1]) * short_filter(...  4.91 us
    ppermute x3, starting transfers between devices, body(): lax.ppermute(squares, 'ch', [(source, (source + shift) % ring) for source...  4.89 us
    pallas_call x1, Pallas kernels, modal_end_call(): pl.pallas_call(modal_end_kernel, grid=(width // block,), in_specs=[pl.Blo...  4.71 us
    convert_element_type x1, other arithmetic, body(): product_long = (key_feat_long * value_feat_long).astype(jnp.bfloat16)  2.46 us
  transfers between devices with their start and end apart: 10, of which 2 were waited for; matrix products, arithmetic and copies ran while one was open for 14% of the time, Pallas kernels for 25%

profile of v13, /device:TPU:25, one launch (start us, length us, event | category | flops | bytes accessed | tf_op | source)
XLA Modules:
  0.0 122.3 jit_solution(471264203523757984)
XLA Ops:
  0.6 0.8 fusion.2
  1.4 4.1 %collective-permute-start.1 = (bf16[2,2048]{1,0:T(2,128)(2,1)S(1)}, bf16[2,2048]{1,0:T(2,128)(2,1)S(1)}, u32[]{:S(2)}, u32[]{:S(2)}) collective-permute-start(bf16[2,2048]{1,0:T(2,128)(2,1)S(1)} %get-tuple-element.7), channel_id=1, source_target_pairs={{0,4},{4,8},{8,12},{12,16},{16,20},{20,24},{24,28},{28,32},{32,36}... | collective-permute-start | bytes 24584 | tf_op jit(solution)/shard_map/ppermute | solution.py:314
  5.5 0.8 fusion.3
  6.3 1.9 %collective-permute-start.2 = (bf16[2,2048]{1,0:T(2,128)(2,1)S(1)}, bf16[2,2048]{1,0:T(2,128)(2,1)S(1)}, u32[]{:S(2)}, u32[]{:S(2)}) collective-permute-start(bf16[2,2048]{1,0:T(2,128)(2,1)S(1)} %get-tuple-element.9), channel_id=1, source_target_pairs={{0,4},{4,8},{8,12},{12,16},{16,20},{20,24},{24,28},{28,32},{32,36}... | collective-permute-start | bytes 24584 | tf_op jit(solution)/shard_map/ppermute | solution.py:314
  8.3 1.0 fusion.5
  9.2 0.0 copy-start
  9.2 0.0 copy-start.3
  9.3 0.0 copy-start.1
  9.3 0.0 copy-start.2
  9.3 4.9 %multiply_convert_fusion.2 = bf16[254,2048]{1,0:T(8,128)(2,1)S(1)} fusion(bf16[256,2048]{1,0:T(8,128)(2,1)} %param.15, f32[2048]{0:T(1024)S(1)} %bitcast.29, f32[2048]{0:T(1024)S(1)} %bitcast.21, f32[2048]{0:T(1024)S(1)} %bitcast.23, bf16[256,2048]{1,0:T(8,128)(2,1)} %param.14, f32[2048]{0:T(1024)S(1)} %bitcast.25, f32[2048]{0:T(1024)S(1)} %bitcast.27, ...), kind=kLoop, calls=%fused_computation.2 | loop fusion | flops 9363456 | bytes 7331840 | tf_op jit(solution)/shard_map/convert_element_type | solution.py:350
  14.2 0.1 slice.176
  14.3 3.9 %collective-permute-start = (bf16[127,2048]{1,0:T(8,128)(2,1)S(1)}, bf16[127,2048]{1,0:T(8,128)(2,1)S(1)}, u32[]{:S(2)}, u32[]{:S(2)}) collective-permute-start(bf16[127,2048]{1,0:T(8,128)(2,1)S(1)} %slice.176), channel_id=1, source_target_pairs={{0,4},{4,8},{8,12},{12,16},{16,20},{20,24},{24,28},{28,32},{32,36}... | collective-permute-start | bytes 1560584 | tf_op jit(solution)/shard_map/ppermute | solution.py:314
  18.3 0.8 slice.160
  19.0 1.9 %collective-permute-start.3 = (bf16[2,2048]{1,0:T(2,128)(2,1)S(1)}, bf16[2,2048]{1,0:T(2,128)(2,1)S(1)}, u32[]{:S(2)}, u32[]{:S(2)}) collective-permute-start(bf16[2,2048]{1,0:T(2,128)(2,1)S(1)} %slice.160), channel_id=1, source_target_pairs={{0,4},{4,8},{8,12},{12,16},{16,20},{20,24},{24,28},{28,32},{32,36}... | collective-permute-start | bytes 24584 | tf_op jit(solution)/shard_map/ppermute | solution.py:314
  21.0 0.0 copy-done
  21.0 3.9 %collective-permute-start.4 = (bf16[2,2048]{1,0:T(2,128)(2,1)S(1)}, bf16[2,2048]{1,0:T(2,128)(2,1)S(1)}, u32[]{:S(2)}, u32[]{:S(2)}) collective-permute-start(bf16[2,2048]{1,0:T(2,128)(2,1)S(1)} %slice.164), channel_id=1, source_target_pairs={{0,4},{4,8},{8,12},{12,16},{16,20},{20,24},{24,28},{28,32},{32,36}... | collective-permute-start | bytes 24584 | tf_op jit(solution)/shard_map/ppermute | solution.py:314
  24.9 0.0 copy-done.3
  25.0 0.0 copy-done.1
  25.0 0.0 copy-done.2
  25.0 0.8 sqrt_multiply_fusion
  25.8 1.4 %slice_bitcast_fusion.1.tap_ref = f32[3,2048]{1,0:T(4,128)} fusion(f32[3,3,2048]{2,1,0:T(4,128)} %param.16), kind=kLoop, calls=%fused_computation.16 | loop fusion | bytes 49152 | tf_op jit(solution)/shard_map/squeeze | solution.py:367
  27.2 0.8 slice.174
  28.0 0.0 collective-permute-done.3
  28.0 1.9 %collective-permute-start.9 = (bf16[2,2048]{1,0:T(2,128)(2,1)S(1)}, bf16[2,2048]{1,0:T(2,128)(2,1)S(1)}, u32[]{:S(2)}, u32[]{:S(2)}) collective-permute-start(bf16[2,2048]{1,0:T(2,128)(2,1)S(1)} %slice.174), channel_id=1, source_target_pairs={{0,4},{4,8},{8,12},{12,16},{16,20},{20,24},{24,28},{28,32},{32,36}... | collective-permute-start | bytes 24584 | tf_op jit(solution)/shard_map/ppermute | solution.py:314
  29.9 0.6 pad_convert_fusion.1.rim_ref
  30.6 0.0 collective-permute-done.1
  30.6 0.0 collective-permute-done.2
  30.6 0.1 multiply_convert_fusion.3
  30.6 0.0 collective-permute-done
  30.6 1.8 %pad_maximum_fusion.ext_ref = bf16[384,2048]{1,0:T(8,128)(2,1)} fusion(bf16[254,2048]{1,0:T(8,128)(2,1)S(1)} %multiply_convert_fusion.2, bf16[2,2048]{1,0:T(2,128)(2,1)S(1)} %multiply_convert_fusion.3, bf16[127,2048]{1,0:T(8,128)(2,1)S(1)} %collective-permute-done, bf16[384]{0:T(512)(128)(2,1)S(1)} %pad.19.clone), kind=kLoop, calls=%fused_computation.3 | loop fusion | flops 6291456 | bytes 3142400 | tf_op jit(solution)/shard_map/concatenate | solution.py:360
  32.4 0.0 copy-start.4
  32.4 31.1 %shard_map.140 = (bf16[256,2048]{1,0:T(8,128)(2,1)}, f32[256,128]{1,0:T(8,128)}) custom-call(bf16[384,2048]{1,0:T(8,128)(2,1)} %pad_maximum_fusion.ext_ref, f32[128,2048]{1,0:T(8,128)} %f_ref.1, f32[1,2048]{1,0:T(1,128)} %bitcast.37, bf16[256,2048]{1,0:T(8,128)(2,1)} %raw_ref.2, f32[8,2048]{1,0:T(8,128)} %pad_convert_fusion.1.rim_ref, ...), custom_call_target="tpu_custom_call" | custom-call | tf_op jit(solution)/shard_map/pallas_call | solution.py:66
  63.5 1.0 reduce_sum.9
  64.5 1.3 %collective-permute-start.5 = (f32[256]{0:T(256)S(1)}, f32[256]{0:T(256)S(1)}, u32[]{:S(2)}, u32[]{:S(2)}) collective-permute-start(f32[256]{0:T(256)S(1)} %reduce_sum.9), channel_id=1, source_target_pairs={{0,1},{1,2},{2,3},{3,0},{4,5},{5,6},{6,7},{7,4},{8,9},{9,10},{10,1... | collective-permute-start | bytes 3080 | tf_op jit(solution)/shard_map/ppermute | solution.py:373
  65.8 2.5 %collective-permute-start.6 = (f32[256]{0:T(256)S(1)}, f32[256]{0:T(256)S(1)}, u32[]{:S(2)}, u32[]{:S(2)}) collective-permute-start(f32[256]{0:T(256)S(1)} %reduce_sum.9), channel_id=1, source_target_pairs={{0,2},{1,3},{2,0},{3,1},{4,6},{5,7},{6,4},{7,5},{8,10},{9,11},{10,... | collective-permute-start | bytes 3080 | tf_op jit(solution)/shard_map/ppermute | solution.py:373
  68.3 1.2 collective-permute-start.7
  69.4 0.6 slice_bitcast_fusion.tap_ref
  70.0 0.0 collective-permute-done.5
  70.0 0.0 collective-permute-done.6
  70.0 0.9 collective-permute-done.7
  71.0 0.0 copy-done.4
  71.0 1.5 %multiply_convert_fusion.1 = bf16[256,2048]{1,0:T(8,128)(2,1)S(1)} fusion(bf16[256,2048]{1,0:T(8,128)(2,1)} %get-tuple-element.2, f32[256]{0:T(256)S(1)} %add_rsqrt_fusion, f32[2048]{0:T(1024)S(1)} %copy-done.4), kind=kLoop, calls=%fused_computation.1 | loop fusion | flops 2097152 | bytes 2106368 | tf_op jit(solution)/shard_map/convert_element_type | solution.py:377
  72.5 6.6 %collective-permute-start.8 = (bf16[2,2048]{1,0:T(2,128)(2,1)S(1)}, bf16[2,2048]{1,0:T(2,128)(2,1)S(1)}, u32[]{:S(2)}, u32[]{:S(2)}) collective-permute-start(bf16[2,2048]{1,0:T(2,128)(2,1)S(1)} %slice.179), channel_id=1, source_target_pairs={{0,4},{4,8},{8,12},{12,16},{16,20},{20,24},{24,28},{28,32},{32,36}... | collective-permute-start | bytes 24584 | tf_op jit(solution)/shard_map/ppermute | solution.py:314
  79.1 0.0 collective-permute-done.9
  79.1 0.6 pad_convert_fusion.rim_ref
  79.7 0.0 collective-permute-done.4
  79.7 0.1 collective-permute-done.8
  79.8 2.5 %multiply_convert_fusion.p_ref = bf16[256,2048]{1,0:T(8,128)(2,1)} fusion(bf16[256,2048]{1,0:T(8,128)(2,1)S(1)} %multiply_convert_fusion.1, bf16[256,2048]{1,0:T(8,128)(2,1)S(1)} %copy-done, bf16[2,2048]{1,0:T(2,128)(2,1)S(1)} %collective-permute-done.8, bf16[2,2048]{1,0:T(2,128)(2,1)S(1)} %collective-permute-done.4, f32[2048]{0:T(1024)S(1)} %bitcast.36, ...), kind=kLoop, calls=%fused_computation | loop fusion | flops 15728640 | bytes 3211264 | tf_op jit(solution)/shard_map/convert_element_type | solution.py:383
  82.3 4.7 %shard_map.141.f_ref = f32[16,2048]{1,0:T(8,128)} custom-call(bf16[256,2048]{1,0:T(8,128)(2,1)} %multiply_convert_fusion.p_ref, f32[16,2048]{1,0:T(8,128)} %get-tuple-element.11.e_ref), custom_call_target="tpu_custom_call" | custom-call | tf_op jit(solution)/shard_map/pallas_call | solution.py:135
  87.0 24.5 %shard_map.142.s_ref = f32[16,2048]{1,0:T(8,128)} custom-call(f32[16,2048]{1,0:T(8,128)} %shard_map.141.f_ref, f32[16,2048]{1,0:T(8,128)} %r_ref.1), custom_call_target="tpu_custom_call" | custom-call | tf_op jit(solution)/shard_map/pallas_call | solution.py:296
  111.5 10.8 %shard_map.143 = bf16[256,2048]{1,0:T(8,128)(2,1)} custom-call(bf16[256,2048]{1,0:T(8,128)(2,1)} %multiply_convert_fusion.p_ref, f32[16,2048]{1,0:T(8,128)} %get-tuple-element.11.e_ref, f32[16,2048]{1,0:T(8,128)} %get-tuple-element.10.w_ref, f32[16,2048]{1,0:T(8,128)} %shard_map.142.s_ref, f32[1,2048]{1,0:T(1,128)} %bitcast.38, bf16[256,2048]{1,0:T(8,128)(2,1)} %raw_ref.3, ...), custom_call_target="tpu_custom_call" | custom-call | tf_op jit(solution)/shard_map/pallas_call | solution.py:207
  (5 shorter events, 0.1 us)
Async XLA Ops:
  1.4 29.1 %collective-permute-start.1 = (bf16[2,2048]{1,0:T(2,128)(2,1)S(1)}, bf16[2,2048]{1,0:T(2,128)(2,1)S(1)}, u32[]{:S(2)}, u32[]{:S(2)}) collective-permute-start(bf16[2,2048]{1,0:T(2,128)(2,1)S(1)} %get-tuple-element.7), channel_id=1, source_target_pairs={{0,4},{4,8},{8,12},{12,16},{16,20},{20,24},{24,28},{28,32},{32,36}... | collective-permute-start | bytes 24584 | tf_op jit(solution)/shard_map/ppermute | solution.py:314
  6.3 24.2 %collective-permute-start.2 = (bf16[2,2048]{1,0:T(2,128)(2,1)S(1)}, bf16[2,2048]{1,0:T(2,128)(2,1)S(1)}, u32[]{:S(2)}, u32[]{:S(2)}) collective-permute-start(bf16[2,2048]{1,0:T(2,128)(2,1)S(1)} %get-tuple-element.9), channel_id=1, source_target_pairs={{0,4},{4,8},{8,12},{12,16},{16,20},{20,24},{24,28},{28,32},{32,36}... | collective-permute-start | bytes 24584 | tf_op jit(solution)/shard_map/ppermute | solution.py:314
  9.2 11.7 %copy-start = (bf16[256,2048]{1,0:T(8,128)(2,1)S(1)}, bf16[256,2048]{1,0:T(8,128)(2,1)}, u32[]{:S(2)}) copy-start(bf16[256,2048]{1,0:T(8,128)(2,1)} %param.21) | copy-start | bytes 3145732
  9.2 15.7 %copy-start.3 = (f32[3,3,2048]{2,1,0:T(4,128)S(1)}, f32[3,3,2048]{2,1,0:T(4,128)}, u32[]{:S(2)}) copy-start(f32[3,3,2048]{2,1,0:T(4,128)} %param.22) | copy-start | bytes 221188
  9.3 15.7 %copy-start.1 = (f32[16,2048]{1,0:T(8,128)S(1)}, f32[16,2048]{1,0:T(8,128)}, u32[]{:S(2)}) copy-start(f32[16,2048]{1,0:T(8,128)} %r_ref.1) | copy-start | bytes 393220
  9.3 15.7 %copy-start.2 = (f32[16,2048]{1,0:T(8,128)S(1)}, f32[16,2048]{1,0:T(8,128)}, u32[]{:S(2)}) copy-start(f32[16,2048]{1,0:T(8,128)} %param.24) | copy-start | bytes 393220
  14.3 16.3 %collective-permute-start = (bf16[127,2048]{1,0:T(8,128)(2,1)S(1)}, bf16[127,2048]{1,0:T(8,128)(2,1)S(1)}, u32[]{:S(2)}, u32[]{:S(2)}) collective-permute-start(bf16[127,2048]{1,0:T(8,128)(2,1)S(1)} %slice.176), channel_id=1, source_target_pairs={{0,4},{4,8},{8,12},{12,16},{16,20},{20,24},{24,28},{28,32},{32,36}... | collective-permute-start | bytes 1560584 | tf_op jit(solution)/shard_map/ppermute | solution.py:314
  19.0 8.9 %collective-permute-start.3 = (bf16[2,2048]{1,0:T(2,128)(2,1)S(1)}, bf16[2,2048]{1,0:T(2,128)(2,1)S(1)}, u32[]{:S(2)}, u32[]{:S(2)}) collective-permute-start(bf16[2,2048]{1,0:T(2,128)(2,1)S(1)} %slice.160), channel_id=1, source_target_pairs={{0,4},{4,8},{8,12},{12,16},{16,20},{20,24},{24,28},{28,32},{32,36}... | collective-permute-start | bytes 24584 | tf_op jit(solution)/shard_map/ppermute | solution.py:314
  21.0 58.7 %collective-permute-start.4 = (bf16[2,2048]{1,0:T(2,128)(2,1)S(1)}, bf16[2,2048]{1,0:T(2,128)(2,1)S(1)}, u32[]{:S(2)}, u32[]{:S(2)}) collective-permute-start(bf16[2,2048]{1,0:T(2,128)(2,1)S(1)} %slice.164), channel_id=1, source_target_pairs={{0,4},{4,8},{8,12},{12,16},{16,20},{20,24},{24,28},{28,32},{32,36}... | collective-permute-start | bytes 24584 | tf_op jit(solution)/shard_map/ppermute | solution.py:314
  28.0 51.1 %collective-permute-start.9 = (bf16[2,2048]{1,0:T(2,128)(2,1)S(1)}, bf16[2,2048]{1,0:T(2,128)(2,1)S(1)}, u32[]{:S(2)}, u32[]{:S(2)}) collective-permute-start(bf16[2,2048]{1,0:T(2,128)(2,1)S(1)} %slice.174), channel_id=1, source_target_pairs={{0,4},{4,8},{8,12},{12,16},{16,20},{20,24},{24,28},{28,32},{32,36}... | collective-permute-start | bytes 24584 | tf_op jit(solution)/shard_map/ppermute | solution.py:314
  32.4 38.5 %copy-start.4 = (f32[2048]{0:T(1024)S(1)}, f32[2048]{0:T(1024)}, u32[]{:S(2)}) copy-start(f32[2048]{0:T(1024)} %param.19) | copy-start | bytes 24580
  64.5 5.5 %collective-permute-start.5 = (f32[256]{0:T(256)S(1)}, f32[256]{0:T(256)S(1)}, u32[]{:S(2)}, u32[]{:S(2)}) collective-permute-start(f32[256]{0:T(256)S(1)} %reduce_sum.9), channel_id=1, source_target_pairs={{0,1},{1,2},{2,3},{3,0},{4,5},{5,6},{6,7},{7,4},{8,9},{9,10},{10,1... | collective-permute-start | bytes 3080 | tf_op jit(solution)/shard_map/ppermute | solution.py:373
  65.8 4.2 %collective-permute-start.6 = (f32[256]{0:T(256)S(1)}, f32[256]{0:T(256)S(1)}, u32[]{:S(2)}, u32[]{:S(2)}) collective-permute-start(f32[256]{0:T(256)S(1)} %reduce_sum.9), channel_id=1, source_target_pairs={{0,2},{1,3},{2,0},{3,1},{4,6},{5,7},{6,4},{7,5},{8,10},{9,11},{10,... | collective-permute-start | bytes 3080 | tf_op jit(solution)/shard_map/ppermute | solution.py:373
  68.3 2.7 %collective-permute-start.7 = (f32[256]{0:T(256)S(1)}, f32[256]{0:T(256)S(1)}, u32[]{:S(2)}, u32[]{:S(2)}) collective-permute-start(f32[256]{0:T(256)S(1)} %reduce_sum.9), channel_id=1, source_target_pairs={{0,3},{1,0},{2,1},{3,2},{4,7},{5,4},{6,5},{7,6},{8,11},{9,8},{10,9... | collective-permute-start | bytes 3080 | tf_op jit(solution)/shard_map/ppermute | solution.py:373
  72.5 7.3 %collective-permute-start.8 = (bf16[2,2048]{1,0:T(2,128)(2,1)S(1)}, bf16[2,2048]{1,0:T(2,128)(2,1)S(1)}, u32[]{:S(2)}, u32[]{:S(2)}) collective-permute-start(bf16[2,2048]{1,0:T(2,128)(2,1)S(1)} %slice.179), channel_id=1, source_target_pairs={{0,4},{4,8},{8,12},{12,16},{16,20},{20,24},{24,28},{28,32},{32,36}... | collective-permute-start | bytes 24584 | tf_op jit(solution)/shard_map/ppermute | solution.py:314

commit v14 on v10

--- a/solution.py
+++ b/solution.py
@@ -80,7 +80,7 @@
 
 
 LANE = 128
-GROUP = 4
+GROUP = 8
 MODES_HALF = 8
 
 

time: 123 us -> 122 us (level)
  transfers between devices with their start and end apart: 10 -> 10, of which waited for: 2 -> 2; matrix products, arithmetic and copies ran while one was open for 13% -> 13% of each run, Pallas kernels for 26% -> 27%
where the time goes in v14:
time: 122 us
  Pallas kernels  70.6 us (58%)
  starting transfers between devices  29.2 us (24%)
  other arithmetic  16.4 us (13%)
  local copies, waits for them, and re-layouts  2.9 us (2%)
  waiting for transfers between devices  1.51 us (1%)
    pallas_call x1, Pallas kernels, medium_call(): pl.pallas_call(medium_kernel, grid=grid, in_specs=[pl.BlockSpec((span, bl...  32.4 us
    ppermute x7, starting transfers between devices, passed_along(): lax.ppermute(value, axis, [(source, source + steps) for source in range(f...  24.3 us
    pallas_call x1, Pallas kernels, scan_call(): pl.pallas_call(functools.partial(scan_kernel, count, rows), in_specs=[pl....  24 us
    pallas_call x1, Pallas kernels, modal_out_call(): pl.pallas_call(modal_out_kernel, grid=(width // block,), in_specs=[pl.Blo...  9.94 us
    ppermute x3, starting transfers between devices, body(): lax.ppermute(squares, 'ch', [(source, (source + shift) % ring) for source...  4.89 us
    convert_element_type x1, other arithmetic, body(): late_product = (short_filter(key_medium, short_medium[1]) * short_filter(...  4.77 us
    pallas_call x1, Pallas kernels, modal_end_call(): pl.pallas_call(modal_end_kernel, grid=(width // block,), in_specs=[pl.Blo...  4.26 us
    add x2, other arithmetic, short_filter(): weights[0] * extended[2:] + weights[1] * extended[1:-1]  4.06 us
  transfers between devices with their start and end apart: 10, of which 2 were waited for; matrix products, arithmetic and copies ran while one was open for 13% of the time, Pallas kernels for 27%

profile of v14, /device:TPU:25, one launch (start us, length us, event | category | flops | bytes accessed | tf_op | source)
XLA Modules:
  0.0 121.6 jit_solution(9215952172990690966)
XLA Ops:
  0.6 0.8 fusion.4
  1.4 4.1 %collective-permute-start.1 = (bf16[2,2048]{1,0:T(2,128)(2,1)S(1)}, bf16[2,2048]{1,0:T(2,128)(2,1)S(1)}, u32[]{:S(2)}, u32[]{:S(2)}) collective-permute-start(bf16[2,2048]{1,0:T(2,128)(2,1)S(1)} %get-tuple-element.7), channel_id=1, source_target_pairs={{0,4},{4,8},{8,12},{12,16},{16,20},{20,24},{24,28},{28,32},{32,36}... | collective-permute-start | bytes 24584 | tf_op jit(solution)/shard_map/ppermute | solution.py:285
  5.5 0.8 fusion.5
  6.3 1.9 %collective-permute-start.2 = (bf16[2,2048]{1,0:T(2,128)(2,1)S(1)}, bf16[2,2048]{1,0:T(2,128)(2,1)S(1)}, u32[]{:S(2)}, u32[]{:S(2)}) collective-permute-start(bf16[2,2048]{1,0:T(2,128)(2,1)S(1)} %get-tuple-element.9), channel_id=1, source_target_pairs={{0,4},{4,8},{8,12},{12,16},{16,20},{20,24},{24,28},{28,32},{32,36}... | collective-permute-start | bytes 24584 | tf_op jit(solution)/shard_map/ppermute | solution.py:285
  8.3 1.0 fusion.7
  9.3 0.0 copy-start
  9.3 0.0 copy-start.2
  9.3 0.0 copy-start.3
  9.3 0.0 copy-start.4
  9.4 0.0 copy-start.1
  9.4 4.8 %multiply_convert_fusion.2 = bf16[254,2048]{1,0:T(8,128)(2,1)S(1)} fusion(bf16[256,2048]{1,0:T(8,128)(2,1)} %param.15, f32[2048]{0:T(1024)S(1)} %bitcast.21, f32[2048]{0:T(1024)S(1)} %bitcast.23, f32[2048]{0:T(1024)S(1)} %bitcast.25, bf16[256,2048]{1,0:T(8,128)(2,1)} %param.14, f32[2048]{0:T(1024)S(1)} %bitcast.27, f32[2048]{0:T(1024)S(1)} %bitcast.29, ...), kind=kLoop, calls=%fused_computation.4 | loop fusion | flops 9363456 | bytes 7331840 | tf_op jit(solution)/shard_map/convert_element_type | solution.py:321
  14.1 0.1 slice.222
  14.3 3.9 %collective-permute-start = (bf16[127,2048]{1,0:T(8,128)(2,1)S(1)}, bf16[127,2048]{1,0:T(8,128)(2,1)S(1)}, u32[]{:S(2)}, u32[]{:S(2)}) collective-permute-start(bf16[127,2048]{1,0:T(8,128)(2,1)S(1)} %slice.222), channel_id=1, source_target_pairs={{0,4},{4,8},{8,12},{12,16},{16,20},{20,24},{24,28},{28,32},{32,36}... | collective-permute-start | bytes 1560584 | tf_op jit(solution)/shard_map/ppermute | solution.py:285
  18.2 0.0 copy-done
  18.3 1.9 %collective-permute-start.3 = (bf16[2,2048]{1,0:T(2,128)(2,1)S(1)}, bf16[2,2048]{1,0:T(2,128)(2,1)S(1)}, u32[]{:S(2)}, u32[]{:S(2)}) collective-permute-start(bf16[2,2048]{1,0:T(2,128)(2,1)S(1)} %slice.200), channel_id=1, source_target_pairs={{0,4},{4,8},{8,12},{12,16},{16,20},{20,24},{24,28},{28,32},{32,36}... | collective-permute-start | bytes 24584 | tf_op jit(solution)/shard_map/ppermute | solution.py:285
  20.2 0.0 copy-done.2
  20.2 3.9 %collective-permute-start.4 = (bf16[2,2048]{1,0:T(2,128)(2,1)S(1)}, bf16[2,2048]{1,0:T(2,128)(2,1)S(1)}, u32[]{:S(2)}, u32[]{:S(2)}) collective-permute-start(bf16[2,2048]{1,0:T(2,128)(2,1)S(1)} %slice.206), channel_id=1, source_target_pairs={{0,4},{4,8},{8,12},{12,16},{16,20},{20,24},{24,28},{28,32},{32,36}... | collective-permute-start | bytes 24584 | tf_op jit(solution)/shard_map/ppermute | solution.py:285
  24.1 0.0 copy-done.3
  24.2 0.0 copy-done.4
  24.2 0.8 sqrt_multiply_fusion
  25.0 0.0 copy-done.1
  25.0 0.0 collective-permute-done.1
  25.0 1.9 %collective-permute-start.9 = (bf16[2,2048]{1,0:T(2,128)(2,1)S(1)}, bf16[2,2048]{1,0:T(2,128)(2,1)S(1)}, u32[]{:S(2)}, u32[]{:S(2)}) collective-permute-start(bf16[2,2048]{1,0:T(2,128)(2,1)S(1)} %slice.218), channel_id=1, source_target_pairs={{0,4},{4,8},{8,12},{12,16},{16,20},{20,24},{24,28},{28,32},{32,36}... | collective-permute-start | bytes 24584 | tf_op jit(solution)/shard_map/ppermute | solution.py:285
  26.9 0.0 collective-permute-done.2
  26.9 0.1 multiply_convert_fusion.3
  27.0 0.0 collective-permute-done.3
  27.0 2.0 %multiply_add_fusion.1.gate_ref = f32[256,2048]{1,0:T(8,128)} fusion(bf16[256,2048]{1,0:T(8,128)(2,1)S(1)} %copy-done, bf16[2,2048]{1,0:T(2,128)(2,1)S(1)} %collective-permute-done.3, f32[2048]{0:T(1024)S(1)} %bitcast.34, f32[2048]{0:T(1024)S(1)} %bitcast.35, f32[2048]{0:T(1024)S(1)} %bitcast.33), kind=kLoop, calls=%fused_computation.3 | loop fusion | flops 7340032 | bytes 3178496 | tf_op jit(solution)/shard_map/add | solution.py:289
  29.1 0.0 collective-permute-done
  29.1 1.8 %pad_maximum_fusion.ext_ref = bf16[384,2048]{1,0:T(8,128)(2,1)} fusion(bf16[254,2048]{1,0:T(8,128)(2,1)S(1)} %multiply_convert_fusion.2, bf16[2,2048]{1,0:T(2,128)(2,1)S(1)} %multiply_convert_fusion.3, bf16[127,2048]{1,0:T(8,128)(2,1)S(1)} %collective-permute-done, bf16[384]{0:T(512)(128)(2,1)S(1)} %pad.8.clone), kind=kLoop, calls=%fused_computation.5 | loop fusion | flops 6291456 | bytes 3142400 | tf_op jit(solution)/shard_map/concatenate | solution.py:332
  30.8 0.0 copy-start.5
  30.8 0.0 copy-start.6
  30.8 32.4 %shard_map.140 = (bf16[256,2048]{1,0:T(8,128)(2,1)}, f32[256,128]{1,0:T(8,128)}) custom-call(bf16[384,2048]{1,0:T(8,128)(2,1)} %pad_maximum_fusion.ext_ref, f32[128,2048]{1,0:T(8,128)} %f_ref.1, f32[1,2048]{1,0:T(1,128)} %bitcast.45, f32[256,2048]{1,0:T(8,128)} %multiply_add_fusion.1.gate_ref), custom_call_target="tpu_custom_call" | custom-call | tf_op jit(solution)/shard_map/pallas_call | solution.py:57
  63.2 1.0 reduce_sum.9
  64.3 1.3 %collective-permute-start.5 = (f32[256]{0:T(256)S(1)}, f32[256]{0:T(256)S(1)}, u32[]{:S(2)}, u32[]{:S(2)}) collective-permute-start(f32[256]{0:T(256)S(1)} %reduce_sum.9), channel_id=1, source_target_pairs={{0,1},{1,2},{2,3},{3,0},{4,5},{5,6},{6,7},{7,4},{8,9},{9,10},{10,1... | collective-permute-start | bytes 3080 | tf_op jit(solution)/shard_map/ppermute | solution.py:340
  65.5 2.5 %collective-permute-start.6 = (f32[256]{0:T(256)S(1)}, f32[256]{0:T(256)S(1)}, u32[]{:S(2)}, u32[]{:S(2)}) collective-permute-start(f32[256]{0:T(256)S(1)} %reduce_sum.9), channel_id=1, source_target_pairs={{0,2},{1,3},{2,0},{3,1},{4,6},{5,7},{6,4},{7,5},{8,10},{9,11},{10,... | collective-permute-start | bytes 3080 | tf_op jit(solution)/shard_map/ppermute | solution.py:340
  68.0 1.2 collective-permute-start.7
  69.1 0.0 copy-done.5
  69.1 0.1 fusion.6
  69.2 0.0 collective-permute-done.5
  69.2 0.3 collective-permute-done.6
  69.5 1.2 %collective-permute-done.7 = f32[256]{0:T(256)S(1)} collective-permute-done((f32[256]{0:T(256)S(1)}, f32[256]{0:T(256)S(1)}, u32[]{:S(2)}, u32[]{:S(2)}) %collective-permute-start.7) | collective-permute-done | bytes 1056 | tf_op jit(solution)/shard_map/ppermute | solution.py:340
  70.7 0.0 copy-done.6
  70.7 1.5 %multiply_convert_fusion.1 = bf16[256,2048]{1,0:T(8,128)(2,1)S(1)} fusion(bf16[256,2048]{1,0:T(8,128)(2,1)} %get-tuple-element.2, f32[256]{0:T(256)S(1)} %add_rsqrt_fusion, f32[2048]{0:T(1024)S(1)} %copy-done.6), kind=kLoop, calls=%fused_computation.2 | loop fusion | flops 2097152 | bytes 2106368 | tf_op jit(solution)/shard_map/convert_element_type | solution.py:344
  72.2 6.6 %collective-permute-start.8 = (bf16[2,2048]{1,0:T(2,128)(2,1)S(1)}, bf16[2,2048]{1,0:T(2,128)(2,1)S(1)}, u32[]{:S(2)}, u32[]{:S(2)}) collective-permute-start(bf16[2,2048]{1,0:T(2,128)(2,1)S(1)} %slice.227), channel_id=1, source_target_pairs={{0,4},{4,8},{8,12},{12,16},{16,20},{20,24},{24,28},{28,32},{32,36}... | collective-permute-start | bytes 24584 | tf_op jit(solution)/shard_map/ppermute | solution.py:285
  78.8 0.0 collective-permute-done.9
  78.8 2.0 %multiply_add_fusion.gate_ref = f32[256,2048]{1,0:T(8,128)} fusion(bf16[256,2048]{1,0:T(8,128)(2,1)S(1)} %copy-done.1, bf16[2,2048]{1,0:T(2,128)(2,1)S(1)} %collective-permute-done.9, f32[2048]{0:T(1024)S(1)} %bitcast.43, f32[2048]{0:T(1024)S(1)} %bitcast.44, f32[2048]{0:T(1024)S(1)} %bitcast.42), kind=kLoop, calls=%fused_computation | loop fusion | flops 7340032 | bytes 3178496 | tf_op jit(solution)/shard_map/add | solution.py:289
  80.8 0.0 collective-permute-done.4
  80.8 0.0 collective-permute-done.8
  80.8 2.5 %multiply_convert_fusion.p_ref = bf16[256,2048]{1,0:T(8,128)(2,1)} fusion(bf16[256,2048]{1,0:T(8,128)(2,1)S(1)} %multiply_convert_fusion.1, bf16[256,2048]{1,0:T(8,128)(2,1)S(1)} %copy-done.2, bf16[2,2048]{1,0:T(2,128)(2,1)S(1)} %collective-permute-done.8, bf16[2,2048]{1,0:T(2,128)(2,1)S(1)} %collective-permute-done.4, f32[2048]{0:T(1024)S(1)} %bitcast.36, ...), kind=kLoop, calls=%fused_computation.1 | loop fusion | flops 15728640 | bytes 3211264 | tf_op jit(solution)/shard_map/convert_element_type | solution.py:351
  83.3 4.3 %shard_map.141.f_ref = f32[16,2048]{1,0:T(8,128)} custom-call(bf16[256,2048]{1,0:T(8,128)(2,1)} %multiply_convert_fusion.p_ref, f32[16,2048]{1,0:T(8,128)} %get-tuple-element.11.e_ref), custom_call_target="tpu_custom_call" | custom-call | tf_op jit(solution)/shard_map/pallas_call | solution.py:121
  87.6 24.0 %shard_map.142.s_ref = f32[16,2048]{1,0:T(8,128)} custom-call(f32[16,2048]{1,0:T(8,128)} %shard_map.141.f_ref, f32[16,2048]{1,0:T(8,128)} %r_ref.1), custom_call_target="tpu_custom_call" | custom-call | tf_op jit(solution)/shard_map/pallas_call | solution.py:267
  111.6 9.9 %shard_map.143 = bf16[256,2048]{1,0:T(8,128)(2,1)} custom-call(bf16[256,2048]{1,0:T(8,128)(2,1)} %multiply_convert_fusion.p_ref, f32[16,2048]{1,0:T(8,128)} %get-tuple-element.11.e_ref, f32[16,2048]{1,0:T(8,128)} %get-tuple-element.10.w_ref, f32[16,2048]{1,0:T(8,128)} %shard_map.142.s_ref, f32[1,2048]{1,0:T(1,128)} %bitcast.46, ...), custom_call_target="tpu_custom_call" | custom-call | tf_op jit(solution)/shard_map/pallas_call | solution.py:181
  (6 shorter events, 0.1 us)
Async XLA Ops:
  1.4 23.6 %collective-permute-start.1 = (bf16[2,2048]{1,0:T(2,128)(2,1)S(1)}, bf16[2,2048]{1,0:T(2,128)(2,1)S(1)}, u32[]{:S(2)}, u32[]{:S(2)}) collective-permute-start(bf16[2,2048]{1,0:T(2,128)(2,1)S(1)} %get-tuple-element.7), channel_id=1, source_target_pairs={{0,4},{4,8},{8,12},{12,16},{16,20},{20,24},{24,28},{28,32},{32,36}... | collective-permute-start | bytes 24584 | tf_op jit(solution)/shard_map/ppermute | solution.py:285
  6.3 20.6 %collective-permute-start.2 = (bf16[2,2048]{1,0:T(2,128)(2,1)S(1)}, bf16[2,2048]{1,0:T(2,128)(2,1)S(1)}, u32[]{:S(2)}, u32[]{:S(2)}) collective-permute-start(bf16[2,2048]{1,0:T(2,128)(2,1)S(1)} %get-tuple-element.9), channel_id=1, source_target_pairs={{0,4},{4,8},{8,12},{12,16},{16,20},{20,24},{24,28},{28,32},{32,36}... | collective-permute-start | bytes 24584 | tf_op jit(solution)/shard_map/ppermute | solution.py:285
  9.3 8.9 %copy-start = (bf16[256,2048]{1,0:T(8,128)(2,1)S(1)}, bf16[256,2048]{1,0:T(8,128)(2,1)}, u32[]{:S(2)}) copy-start(bf16[256,2048]{1,0:T(8,128)(2,1)} %param.13) | copy-start | bytes 3145732
  9.3 10.9 %copy-start.2 = (bf16[256,2048]{1,0:T(8,128)(2,1)S(1)}, bf16[256,2048]{1,0:T(8,128)(2,1)}, u32[]{:S(2)}) copy-start(bf16[256,2048]{1,0:T(8,128)(2,1)} %param.21) | copy-start | bytes 3145732
  9.3 14.8 %copy-start.3 = (f32[16,2048]{1,0:T(8,128)S(1)}, f32[16,2048]{1,0:T(8,128)}, u32[]{:S(2)}) copy-start(f32[16,2048]{1,0:T(8,128)} %r_ref.1) | copy-start | bytes 393220
  9.3 14.8 %copy-start.4 = (f32[16,2048]{1,0:T(8,128)S(1)}, f32[16,2048]{1,0:T(8,128)}, u32[]{:S(2)}) copy-start(f32[16,2048]{1,0:T(8,128)} %param.24) | copy-start | bytes 393220
  9.4 15.6 %copy-start.1 = (bf16[256,2048]{1,0:T(8,128)(2,1)S(1)}, bf16[256,2048]{1,0:T(8,128)(2,1)}, u32[]{:S(2)}) copy-start(bf16[256,2048]{1,0:T(8,128)(2,1)} %param.20) | copy-start | bytes 3145732
  14.3 14.8 %collective-permute-start = (bf16[127,2048]{1,0:T(8,128)(2,1)S(1)}, bf16[127,2048]{1,0:T(8,128)(2,1)S(1)}, u32[]{:S(2)}, u32[]{:S(2)}) collective-permute-start(bf16[127,2048]{1,0:T(8,128)(2,1)S(1)} %slice.222), channel_id=1, source_target_pairs={{0,4},{4,8},{8,12},{12,16},{16,20},{20,24},{24,28},{28,32},{32,36}... | collective-permute-start | bytes 1560584 | tf_op jit(solution)/shard_map/ppermute | solution.py:285
  18.3 8.8 %collective-permute-start.3 = (bf16[2,2048]{1,0:T(2,128)(2,1)S(1)}, bf16[2,2048]{1,0:T(2,128)(2,1)S(1)}, u32[]{:S(2)}, u32[]{:S(2)}) collective-permute-start(bf16[2,2048]{1,0:T(2,128)(2,1)S(1)} %slice.200), channel_id=1, source_target_pairs={{0,4},{4,8},{8,12},{12,16},{16,20},{20,24},{24,28},{28,32},{32,36}... | collective-permute-start | bytes 24584 | tf_op jit(solution)/shard_map/ppermute | solution.py:285
  20.2 60.6 %collective-permute-start.4 = (bf16[2,2048]{1,0:T(2,128)(2,1)S(1)}, bf16[2,2048]{1,0:T(2,128)(2,1)S(1)}, u32[]{:S(2)}, u32[]{:S(2)}) collective-permute-start(bf16[2,2048]{1,0:T(2,128)(2,1)S(1)} %slice.206), channel_id=1, source_target_pairs={{0,4},{4,8},{8,12},{12,16},{16,20},{20,24},{24,28},{28,32},{32,36}... | collective-permute-start | bytes 24584 | tf_op jit(solution)/shard_map/ppermute | solution.py:285
  25.0 53.8 %collective-permute-start.9 = (bf16[2,2048]{1,0:T(2,128)(2,1)S(1)}, bf16[2,2048]{1,0:T(2,128)(2,1)S(1)}, u32[]{:S(2)}, u32[]{:S(2)}) collective-permute-start(bf16[2,2048]{1,0:T(2,128)(2,1)S(1)} %slice.218), channel_id=1, source_target_pairs={{0,4},{4,8},{8,12},{12,16},{16,20},{20,24},{24,28},{28,32},{32,36}... | collective-permute-start | bytes 24584 | tf_op jit(solution)/shard_map/ppermute | solution.py:285
  30.8 38.3 %copy-start.5 = (f32[3,3,2048]{2,1,0:T(4,128)S(1)}, f32[3,3,2048]{2,1,0:T(4,128)}, u32[]{:S(2)}) copy-start(f32[3,3,2048]{2,1,0:T(4,128)} %param.22) | copy-start | bytes 221188
  30.8 39.9 %copy-start.6 = (f32[2048]{0:T(1024)S(1)}, f32[2048]{0:T(1024)}, u32[]{:S(2)}) copy-start(f32[2048]{0:T(1024)} %param.19) | copy-start | bytes 24580
  64.3 5.0 %collective-permute-start.5 = (f32[256]{0:T(256)S(1)}, f32[256]{0:T(256)S(1)}, u32[]{:S(2)}, u32[]{:S(2)}) collective-permute-start(f32[256]{0:T(256)S(1)} %reduce_sum.9), channel_id=1, source_target_pairs={{0,1},{1,2},{2,3},{3,0},{4,5},{5,6},{6,7},{7,4},{8,9},{9,10},{10,1... | collective-permute-start | bytes 3080 | tf_op jit(solution)/shard_map/ppermute | solution.py:340
  65.5 3.9 %collective-permute-start.6 = (f32[256]{0:T(256)S(1)}, f32[256]{0:T(256)S(1)}, u32[]{:S(2)}, u32[]{:S(2)}) collective-permute-start(f32[256]{0:T(256)S(1)} %reduce_sum.9), channel_id=1, source_target_pairs={{0,2},{1,3},{2,0},{3,1},{4,6},{5,7},{6,4},{7,5},{8,10},{9,11},{10,... | collective-permute-start | bytes 3080 | tf_op jit(solution)/shard_map/ppermute | solution.py:340
  68.0 2.7 %collective-permute-start.7 = (f32[256]{0:T(256)S(1)}, f32[256]{0:T(256)S(1)}, u32[]{:S(2)}, u32[]{:S(2)}) collective-permute-start(f32[256]{0:T(256)S(1)} %reduce_sum.9), channel_id=1, source_target_pairs={{0,3},{1,0},{2,1},{3,2},{4,7},{5,4},{6,5},{7,6},{8,11},{9,8},{10,9... | collective-permute-start | bytes 3080 | tf_op jit(solution)/shard_map/ppermute | solution.py:340
  72.2 8.6 %collective-permute-start.8 = (bf16[2,2048]{1,0:T(2,128)(2,1)S(1)}, bf16[2,2048]{1,0:T(2,128)(2,1)S(1)}, u32[]{:S(2)}, u32[]{:S(2)}) collective-permute-start(bf16[2,2048]{1,0:T(2,128)(2,1)S(1)} %slice.227), channel_id=1, source_target_pairs={{0,4},{4,8},{8,12},{12,16},{16,20},{20,24},{24,28},{28,32},{32,36}... | collective-permute-start | bytes 24584 | tf_op jit(solution)/shard_map/ppermute | solution.py:285
